TPU v7x, 32 devices: a whole 2x2x4 slice. The times are simulated.
32 devices in a mesh: row: 4 (over x, core), col: 8 (over z, y).
Axes of the slice: x: 2, y: 2, z: 4, core: 2. Of those that a mesh axis runs over, the one named last changes fastest.
Arguments:
- specimen: float32 [2, 1024, 2048], P(None, 'row', 'col'), may hold values from -6 to 6
- probe_field: float32 [2, 256, 256], replicated, may hold values from -5 to 5
- offsets: int32 [4, 8, 3, 2], P('row', 'col'), may hold values from -128 to 128
- amplitudes: float32 [4, 8, 3, 256, 256], P('row', 'col'), may hold values from 0.5 to 2.5
Outputs:
- updated: float32 [2, 1024, 2048], P(None, 'row', 'col')
Inputs may be any that keep to these rules, and one draw needn't show every extreme that they name: Window p of tile (r, c) starts at row r * 256 + offsets[r, c, p, 0] and column c * 256 + offsets[r, c, p, 1]; windows may reach past the specimen's border, where the object is zero.
All inputs are finite; a program needn't handle non-finite values.
Results may differ from a plain program's by a relative error of at most 0.0003.
Values sent between devices are 32-bit elements; how exact they have to be, the bound alone decides.
No kernel may reach another device: no remote copies, remote signals or barrier semaphores. Data moves between devices by JAX's collectives and lax.ppermute only.
A program may use at most 64 MiB of HBM per device.

v0:
```python
import functools
import math

import jax
import jax.numpy as jnp
import numpy as np
from jax import lax
from jax.experimental import pallas as pl
from jax.experimental.pallas import tpu as pltpu
from jax.sharding import PartitionSpec as P

HALO = 128
ITERS = 2
LANES = 128

smooth_term = 0.25
ridge_share = 0.1

VM = pl.BlockSpec(memory_space=pltpu.VMEM)
SM = pl.BlockSpec(memory_space=pltpu.SMEM)
F32 = jnp.float32
BF16 = jnp.bfloat16


def shape(*dims):
    return jax.ShapeDtypeStruct(dims, F32)


def to_bf16(x):
    return np.asarray(x, np.float32).astype(BF16)


def split_table(table):
    high = to_bf16(table)
    low = to_bf16(table - high.astype(np.float64))
    return high, low


@functools.lru_cache
def dft_tables(length):
    half = length // 2
    n = np.arange(half)
    left, left_back, right, right_back = [], [], [], []
    for odd in (0, 1):
        turn = ((2 * n[:, None] + odd) * n[None, :]) % length
        angle = turn * (2.0 * math.pi / length)
        cos, sin = np.cos(angle) / math.sqrt(length), -np.sin(angle) / math.sqrt(length)
        form = np.block([[cos, -sin], [sin, cos]])
        for table, rows, columns in ((form, left, right_back), (form.T, left_back, right)):
            high, low = split_table(table)
            rows.append(np.concatenate([high, low, high], axis=1))
            columns.append(np.concatenate([high, high, low], axis=0))
    place = np.zeros((length, length), np.float32)
    place[2 * n, n] = 1.0
    place[2 * n + 1, half + n] = 1.0
    pick = to_bf16(place)
    return tuple(np.stack(t) for t in (left, left_back, right, right_back)) + (
        np.concatenate([pick, pick, pick], axis=0),
        np.concatenate([pick.T, pick.T, pick.T], axis=1),
    )


def halves(x):
    high = x.astype(BF16)
    low = (x - high.astype(F32)).astype(BF16)
    return high, low


def left_product(table, x):
    high, low = halves(x)
    return jnp.dot(
        table, jnp.concatenate([high, high, low], axis=0), preferred_element_type=F32
    )


def right_product(x, table):
    high, low = halves(x)
    return jnp.dot(
        jnp.concatenate([high, low, high], axis=1), table, preferred_element_type=F32
    )


def window_masks(offsets, position, win):
    row = offsets[0, 0, position, 0] + HALO
    column = offsets[0, 0, position, 1] + HALO
    low = lax.broadcasted_iota(jnp.int32, (win, win), 0) >= row
    near = lax.broadcasted_iota(jnp.int32, (win, win), 1) >= column
    return low, near


def roll_kernel(offsets, probe, rolled):
    win = probe.shape[1]
    for position in range(rolled.shape[0]):
        row = lax.rem(offsets[0, 0, position, 0] + HALO, win)
        column = lax.rem(offsets[0, 0, position, 1] + HALO, win)
        for plane in (0, 1):
            rolled[position, plane] = pltpu.roll(
                pltpu.roll(probe[plane], column, 1), row, 0
            )


def spread(piece, low, near, upper, lower, win, first):
    above = jnp.where(low, piece, 0.0)
    below = jnp.where(low, 0.0, piece)
    for ref, block in ((upper, above), (lower, below)):
        parts = (jnp.where(near, block, 0.0), jnp.where(near, 0.0, block))
        for lanes, part in zip((slice(0, win), slice(win, None)), parts):
            ref[:, lanes] = part if first else ref[:, lanes] + part


def gradient_kernel(
    offsets, up, top, bottom, down, probe, amplitude, left, left_back, right, right_back,
    grad_up, grad_mid, grad_down, upper, lower,
):
    count, win, _ = amplitude.shape
    half = win // 2
    edge = up.shape[1]

    def patch(plane, low, near):
        first = jnp.concatenate([up[plane], top[plane]], axis=0)
        second = jnp.concatenate([bottom[plane], down[plane]], axis=0)
        return jnp.where(
            near,
            jnp.where(low, first[:, :win], second[:, :win]),
            jnp.where(low, first[:, win:], second[:, win:]),
        )

    for position in range(count):
        low, near = window_masks(offsets, position, win)
        patch_real = patch(0, low, near)
        patch_imag = patch(1, low, near)
        probe_real, probe_imag = probe[position, 0], probe[position, 1]
        real = probe_real * patch_real - probe_imag * patch_imag
        imag = probe_real * patch_imag + probe_imag * patch_real
        summed = jnp.concatenate([real[:half] + real[half:], imag[:half] + imag[half:]], axis=0)
        differ = jnp.concatenate([real[:half] - real[half:], imag[:half] - imag[half:]], axis=0)
        even = left_product(left[0], summed)
        odd = left_product(left[1], differ)
        real = jnp.concatenate([even[:half], odd[:half]], axis=0)
        imag = jnp.concatenate([even[half:], odd[half:]], axis=0)
        summed = jnp.concatenate(
            [real[:, :half] + real[:, half:], imag[:, :half] + imag[:, half:]], axis=1
        )
        differ = jnp.concatenate(
            [real[:, :half] - real[:, half:], imag[:, :half] - imag[:, half:]], axis=1
        )
        even = right_product(summed, right[0])
        odd = right_product(differ, right[1])
        even_real, even_imag = even[:, :half], even[:, half:]
        odd_real, odd_imag = odd[:, :half], odd[:, half:]
        amp = amplitude[position]
        even_factor = 1.0 - amp[:, :half] * lax.rsqrt(
            even_real * even_real + even_imag * even_imag + smooth_term
        )
        odd_factor = 1.0 - amp[:, half:] * lax.rsqrt(
            odd_real * odd_real + odd_imag * odd_imag + smooth_term
        )
        even = jnp.concatenate([even_factor * even_real, even_factor * even_imag], axis=1)
        odd = jnp.concatenate([odd_factor * odd_real, odd_factor * odd_imag], axis=1)
        even = right_product(even, right_back[0])
        odd = right_product(odd, right_back[1])
        summed, differ = even + odd, even - odd
        real = jnp.concatenate([summed[:, :half], differ[:, :half]], axis=1)
        imag = jnp.concatenate([summed[:, half:], differ[:, half:]], axis=1)
        even = left_product(left_back[0], jnp.concatenate([real[:half], imag[:half]], axis=0))
        odd = left_product(left_back[1], jnp.concatenate([real[half:], imag[half:]], axis=0))
        summed, differ = even + odd, even - odd
        real = jnp.concatenate([summed[:half], differ[:half]], axis=0)
        imag = jnp.concatenate([summed[half:], differ[half:]], axis=0)
        for plane, piece in (
            (0, probe_real * real + probe_imag * imag),
            (1, probe_real * imag - probe_imag * real),
        ):
            spread(
                piece, low, near, upper.at[plane], lower.at[plane], win, position == 0
            )
    share(upper, lower, grad_up, grad_mid, grad_down)


def share(upper, lower, out_up, out_mid, out_down):
    edge = out_up.shape[1]
    out_up[...] = upper[:, :edge, :]
    out_mid[:, :edge, :] = upper[:, edge:, :]
    out_mid[:, edge:, :] = lower[:, :edge, :]
    out_down[...] = lower[:, edge:, :]


def light_kernel(offsets, probe, light_up, light_mid, light_down, upper, lower):
    win = probe.shape[2]
    for position in range(probe.shape[0]):
        low, near = window_masks(offsets, position, win)
        real, imag = probe[position, 0], probe[position, 1]
        spread(
            real * real + imag * imag, low, near, upper.at[0], lower.at[0], win, position == 0
        )
    share(upper, lower, light_up, light_mid, light_down)


def thirds(x):
    high = x.astype(BF16)
    rest = x - high.astype(F32)
    mid = rest.astype(BF16)
    return high, mid, (rest - mid.astype(F32)).astype(BF16)


def order_kernel(amplitude, pick, pick_back, ordered):
    for position in range(ordered.shape[0]):
        block = jnp.dot(
            pick_back[...],
            jnp.concatenate(thirds(amplitude[0, 0, position]), axis=0),
            preferred_element_type=F32,
        )
        ordered[position] = jnp.dot(
            jnp.concatenate(thirds(block), axis=1), pick[...], preferred_element_type=F32
        )


def edges_kernel(specimen, head, tail):
    head[...] = specimen[:, :, :HALO]
    tail[...] = specimen[:, :, specimen.shape[2] - HALO :]


def widen_kernel(before, specimen, after, top, bottom):
    edge = top.shape[1]
    tile = specimen.shape[2]
    for index, out in enumerate((top, bottom)):
        rows = slice(index * edge, (index + 1) * edge)
        out[:, :, :HALO] = before[:, rows, :]
        out[:, :, HALO : HALO + tile] = specimen[:, rows, :]
        out[:, :, HALO + tile :] = after[:, rows, :]


def fold_rows(mid, from_above, from_below):
    edge = from_above.shape[1]
    upper = mid[:, :edge, :] + from_above[...]
    lower = mid[:, edge:, :] + from_below[...]
    return upper, lower


def fold_strips_kernel(mid, from_above, from_below, head, tail):
    edge = from_above.shape[1]
    half = head.shape[2]
    for rows, block in zip((slice(0, edge), slice(edge, None)), fold_rows(mid, from_above, from_below)):
        head[:, rows, :] = block[:, :, :half]
        tail[:, rows, :] = block[:, :, half:]


def fold_bands_kernel(mid, from_above, from_below, head, core, tail):
    edge = from_above.shape[1]
    tile = core.shape[2]
    for rows, block in zip((slice(0, edge), slice(edge, None)), fold_rows(mid, from_above, from_below)):
        head[:, rows, :] = block[:, :, :HALO]
        core[:, rows, :] = block[:, :, HALO : HALO + tile]
        tail[:, rows, :] = block[:, :, HALO + tile :]


def light_sum_kernel(head, tail, from_left, from_right, light, largest):
    left = head[0] + from_left[0]
    right = tail[0] + from_right[0]
    half = left.shape[1]
    light[:, :half] = left
    light[:, half:] = right
    best = jnp.maximum(left[:, HALO:], right[:, : half - HALO])
    rows, columns = best.shape
    found = best[:8]
    for row in range(8, rows, 8):
        found = jnp.maximum(found, best[row : row + 8])
    top = found[:, :LANES]
    for column in range(LANES, columns, LANES):
        top = jnp.maximum(top, found[:, column : column + LANES])
    largest[...] = top


def divisor_of(light, peak):
    return light + ridge_share * jnp.max(peak[...])


def update_kernel(
    place, head, tail, from_left, from_right, light, peak, old_top, old_bottom, top, bottom
):
    edge = top.shape[1]
    half = head.shape[2]
    most = ridge_share * jnp.max(peak[...])
    has_left, has_right = place[0] > 0, place[1] > 0
    lane = lax.broadcasted_iota(jnp.int32, (edge, half), 1)
    keep_left = jnp.logical_or(lane >= HALO, has_left)
    keep_right = jnp.logical_or(lane < half - HALO, has_right)
    for index, (old, out) in enumerate(((old_top, top), (old_bottom, bottom))):
        rows = slice(index * edge, (index + 1) * edge)
        for side, (own, sent, keep) in enumerate(
            ((head, from_left, keep_left), (tail, from_right, keep_right))
        ):
            lanes = slice(side * half, (side + 1) * half)
            scale = 1.0 / (light[rows, lanes] + most)
            for plane in (0, 1):
                gradient = own[plane, rows, :] + sent[plane, rows, :]
                new = old[plane, :, lanes] - gradient * scale
                out[plane, :, lanes] = jnp.where(keep, new, 0.0)


def finish_kernel(core, from_left, from_right, light, peak, old_top, old_bottom, out):
    edge = old_top.shape[1]
    tile = out.shape[2]
    inner = slice(HALO, HALO + tile)
    most = ridge_share * jnp.max(peak[...])
    for index, old in enumerate((old_top, old_bottom)):
        rows = slice(index * edge, (index + 1) * edge)
        scale = 1.0 / (light[rows, inner] + most)
        for plane in (0, 1):
            gradient = core[plane, rows, :]
            gradient = jnp.concatenate(
                [
                    gradient[:, :HALO] + from_left[plane, rows, :],
                    gradient[:, HALO : tile - HALO],
                    gradient[:, tile - HALO :] + from_right[plane, rows, :],
                ],
                axis=1,
            ) if tile > 2 * HALO else jnp.concatenate(
                [
                    gradient[:, :HALO] + from_left[plane, rows, :],
                    gradient[:, HALO:] + from_right[plane, rows, :],
                ],
                axis=1,
            )
            out[plane, rows, :] = old[plane, :, inner] - gradient * scale


def kernel_call(body, outs, specs, name, flops=0, scratch=()):
    moved = 4 * sum(math.prod(out.shape) for out in outs)
    single = len(outs) == 1
    return pl.pallas_call(
        body,
        out_shape=outs[0] if single else outs,
        in_specs=specs,
        out_specs=VM if single else (VM,) * len(outs),
        scratch_shapes=list(scratch),
        compiler_params=pltpu.CompilerParams(vmem_limit_bytes=48 * 1024 * 1024),
        cost_estimate=pl.CostEstimate(
            flops=flops, bytes_accessed=3 * moved, transcendentals=0
        ),
        name=name,
    )


def shifted(block, axis, distance):
    count = lax.axis_size(axis)
    route = [(i - distance, i) for i in range(count) if 0 <= i - distance < count]
    return lax.ppermute(block, axis, route)


def largest_of(block, axis):
    count = lax.axis_size(axis)
    reach = 1
    while reach < count:
        route = [(i, (i + reach) % count) for i in range(count)]
        block = jnp.maximum(block, lax.ppermute(block, axis, route))
        reach *= 2
    return block


def local(specimen, probe_field, offsets, amplitudes):
    tile = specimen.shape[1]
    win = probe_field.shape[1]
    span = tile + 2 * HALO
    half = span // 2
    count = offsets.shape[2]
    left, left_back, right, right_back, pick, pick_back = [
        jnp.asarray(t) for t in dft_tables(win)
    ]
    col, cols = lax.axis_index("col"), lax.axis_size("col")
    place = jnp.stack([col > 0, col < cols - 1]).astype(jnp.int32)

    head, tail = kernel_call(
        edges_kernel, [shape(2, tile, HALO)] * 2, [VM], "edges"
    )(specimen)
    before = shifted(tail, "col", 1)
    after = shifted(head, "col", -1)

    probes = kernel_call(roll_kernel, [shape(count, 2, win, win)], [SM, VM], "roll")(
        offsets, probe_field
    )
    band, middle = shape(1, HALO, span), shape(1, tile, span)
    light_up, light_mid, light_down = kernel_call(
        light_kernel,
        [band, middle, band],
        [SM, VM],
        "light",
        scratch=[pltpu.VMEM((1, win, span), F32)] * 2,
    )(offsets, probes)
    light_above = shifted(light_down, "row", 1)
    light_below = shifted(light_up, "row", -1)
    ordered = kernel_call(order_kernel, [shape(count, win, win)], [VM] * 3, "order")(
        amplitudes, pick, pick_back
    )

    top, bottom = kernel_call(
        widen_kernel, [shape(2, tile // 2, span)] * 2, [VM] * 3, "widen"
    )(before, specimen, after)
    above = shifted(bottom, "row", 1)
    below = shifted(top, "row", -1)

    light_head, light_tail = kernel_call(
        fold_strips_kernel, [shape(1, tile, half)] * 2, [VM] * 3, "light_fold"
    )(light_mid, light_above, light_below)
    light_left = shifted(light_tail, "col", 1)
    light_right = shifted(light_head, "col", -1)

    light, peak = None, None
    for iteration in range(ITERS):
        grad_up, grad_mid, grad_down = kernel_call(
            gradient_kernel,
            [shape(2, HALO, span), shape(2, tile, span), shape(2, HALO, span)],
            [SM] + [VM] * 10,
            "gradient",
            flops=count * 8 * 2 * win * 3 * win * win,
            scratch=[pltpu.VMEM((2, win, span), F32)] * 2,
        )(
            offsets, above, top, bottom, below, probes, ordered,
            left, left_back, right, right_back,
        )
        grad_above = shifted(grad_down, "row", 1)
        grad_below = shifted(grad_up, "row", -1)
        if iteration == 0:
            light, found = kernel_call(
                light_sum_kernel, [shape(tile, span), shape(8, LANES)], [VM] * 4, "light_sum"
            )(light_head, light_tail, light_left, light_right)
            peak = largest_of(largest_of(found, "row"), "col")
        if iteration + 1 < ITERS:
            grad_head, grad_tail = kernel_call(
                fold_strips_kernel, [shape(2, tile, half)] * 2, [VM] * 3, "fold"
            )(grad_mid, grad_above, grad_below)
            from_left = shifted(grad_tail, "col", 1)
            from_right = shifted(grad_head, "col", -1)
            top, bottom = kernel_call(
                update_kernel,
                [shape(2, tile // 2, span)] * 2,
                [SM] + [VM] * 8,
                "update",
            )(place, grad_head, grad_tail, from_left, from_right, light, peak, top, bottom)
            above = shifted(bottom, "row", 1)
            below = shifted(top, "row", -1)
        else:
            head, core, tail = kernel_call(
                fold_bands_kernel,
                [shape(2, tile, HALO), shape(2, tile, tile), shape(2, tile, HALO)],
                [VM] * 3,
                "fold_last",
            )(grad_mid, grad_above, grad_below)
            from_left = shifted(tail, "col", 1)
            from_right = shifted(head, "col", -1)
            return kernel_call(
                finish_kernel, [shape(2, tile, tile)], [VM] * 7, "finish"
            )(core, from_left, from_right, light, peak, top, bottom)


def solution(mesh):
    return jax.shard_map(
        local,
        mesh=mesh,
        in_specs=(
            P(None, "row", "col"),
            P(),
            P("row", "col", None, None),
            P("row", "col", None, None, None),
        ),
        out_specs=P(None, "row", "col"),
        check_vma=False,
    )
```

profile of v0, /device:TPU:1, one launch (start us, length us, event | category | flops | bytes accessed | tf_op | source)
XLA Modules:
  0.0 157.3 jit_solution(1182002339899307405)
XLA Ops:
  0.0 1.0 copy-done.2
  1.1 4.1 %collective-permute-start = (f32[2,256,128]{2,1,0:T(8,128)S(1)}, f32[2,256,128]{2,1,0:T(8,128)S(1)}, u32[]{:S(2)}, u32[]{:S(2)}) collective-permute-start(f32[2,256,128]{2,1,0:T(8,128)S(1)} %get-tuple-element.29), channel_id=1, source_target_pairs={{0,1},{1,2},{2,3},{3,4},{4,5},{5,6},{6,7},{8,9},{9,10},{10,11},{11... | collective-permute-start | bytes 786440 | tf_op jit(solution)/shard_map/ppermute | solution.py:348
  5.2 0.0 copy-start.5
  5.2 1.4 collective-permute-start.1
  6.6 3.4 %collective-permute-done.before = f32[2,256,128]{2,1,0:T(8,128)S(1)} collective-permute-done((f32[2,256,128]{2,1,0:T(8,128)S(1)}, f32[2,256,128]{2,1,0:T(8,128)S(1)}, u32[]{:S(2)}, u32[]{:S(2)}) %collective-permute-start) | collective-permute-done | bytes 262176 | tf_op jit(solution)/shard_map/ppermute | solution.py:348
  10.1 4.1 %collective-permute-done.1.after = f32[2,256,128]{2,1,0:T(8,128)S(1)} collective-permute-done((f32[2,256,128]{2,1,0:T(8,128)S(1)}, f32[2,256,128]{2,1,0:T(8,128)S(1)}, u32[]{:S(2)}, u32[]{:S(2)}) %collective-permute-start.1) | collective-permute-done | bytes 262176 | tf_op jit(solution)/shard_map/ppermute | solution.py:348
  14.2 0.1 widen.1
  14.2 6.2 %collective-permute-start.2 = (f32[2,128,512]{2,1,0:T(8,128)S(1)}, f32[2,128,512]{2,1,0:T(8,128)}, u32[]{:S(2)}, u32[]{:S(2)}) collective-permute-start(f32[2,128,512]{2,1,0:T(8,128)S(1)} %get-tuple-element.31.bottom.old_bottom), channel_id=1, source_target_pairs={{0,8},{8,16},{16,24},{1,9},{9,17},{17,25},{2,10},{10,18},{18,26},{... | collective-permute-start | bytes 1572872 | tf_op jit(solution)/shard_map/ppermute | solution.py:348
  20.4 1.9 %collective-permute-start.3 = (f32[2,128,512]{2,1,0:T(8,128)S(1)}, f32[2,128,512]{2,1,0:T(8,128)}, u32[]{:S(2)}, u32[]{:S(2)}) collective-permute-start(f32[2,128,512]{2,1,0:T(8,128)S(1)} %get-tuple-element.32.top.old_top), channel_id=1, source_target_pairs={{8,0},{16,8},{24,16},{9,1},{17,9},{25,17},{10,2},{18,10},{26,18},{... | collective-permute-start | bytes 1572872 | tf_op jit(solution)/shard_map/ppermute | solution.py:348
  22.4 0.1 copy.14.offsets
  22.5 1.2 roll.1.probe
  23.7 1.2 copy-done
  24.9 1.0 copy-done.7
  25.9 1.0 copy-done.8
  26.9 1.0 order.1.amplitude
  27.9 0.0 collective-permute-done.2.up
  27.9 3.1 %collective-permute-done.3.down = f32[2,128,512]{2,1,0:T(8,128)} collective-permute-done((f32[2,128,512]{2,1,0:T(8,128)S(1)}, f32[2,128,512]{2,1,0:T(8,128)}, u32[]{:S(2)}, u32[]{:S(2)}) %collective-permute-start.3) | collective-permute-done | bytes 524320 | tf_op jit(solution)/shard_map/ppermute | solution.py:348
  31.0 7.8 %gradient.2 = (f32[2,128,512]{2,1,0:T(8,128)S(1)}, f32[2,256,512]{2,1,0:T(8,128)}, f32[2,128,512]{2,1,0:T(8,128)S(1)}) custom-call(s32[1,1,3,2]{3,2,1,0:T(4,128)S(1)} %copy.14.offsets, f32[2,128,512]{2,1,0:T(8,128)} %collective-permute-done.2.up, f32[2,128,512]{2,1,0:T(8,128)S(1)} %get-tuple-element.32.top.old_top, ...), custom_call_target="tpu_custom_call" | custom-call | flops 2415919104 | bytes 6291456 | tf_op jit(solution)/shard_map/gradient/pallas_call | solution.py:410
  38.8 2.0 %collective-permute-start.4 = (f32[2,128,512]{2,1,0:T(8,128)S(1)}, f32[2,128,512]{2,1,0:T(8,128)S(1)}, u32[]{:S(2)}, u32[]{:S(2)}) collective-permute-start(f32[2,128,512]{2,1,0:T(8,128)S(1)} %get-tuple-element.34), channel_id=1, source_target_pairs={{0,8},{8,16},{16,24},{1,9},{9,17},{17,25},{2,10},{10,18},{18,26},{... | collective-permute-start | bytes 1572872 | tf_op jit(solution)/shard_map/ppermute | solution.py:348
  40.8 2.4 %collective-permute-start.5 = (f32[2,128,512]{2,1,0:T(8,128)S(1)}, f32[2,128,512]{2,1,0:T(8,128)S(1)}, u32[]{:S(2)}, u32[]{:S(2)}) collective-permute-start(f32[2,128,512]{2,1,0:T(8,128)S(1)} %get-tuple-element.35), channel_id=1, source_target_pairs={{8,0},{16,8},{24,16},{9,1},{17,9},{25,17},{10,2},{18,10},{26,18},{... | collective-permute-start | bytes 1572872 | tf_op jit(solution)/shard_map/ppermute | solution.py:348
  43.3 0.9 light.1
  44.2 3.1 %collective-permute-start.8 = (f32[1,128,512]{2,1,0:T(8,128)S(1)}, f32[1,128,512]{2,1,0:T(8,128)S(1)}, u32[]{:S(2)}, u32[]{:S(2)}) collective-permute-start(f32[1,128,512]{2,1,0:T(8,128)S(1)} %get-tuple-element.39), channel_id=1, source_target_pairs={{0,8},{8,16},{16,24},{1,9},{9,17},{17,25},{2,10},{10,18},{18,26},{... | collective-permute-start | bytes 786440 | tf_op jit(solution)/shard_map/ppermute | solution.py:348
  47.4 1.9 %collective-permute-start.9 = (f32[1,128,512]{2,1,0:T(8,128)S(1)}, f32[1,128,512]{2,1,0:T(8,128)S(1)}, u32[]{:S(2)}, u32[]{:S(2)}) collective-permute-start(f32[1,128,512]{2,1,0:T(8,128)S(1)} %get-tuple-element.40), channel_id=1, source_target_pairs={{8,0},{16,8},{24,16},{9,1},{17,9},{25,17},{10,2},{18,10},{26,18},{... | collective-permute-start | bytes 786440 | tf_op jit(solution)/shard_map/ppermute | solution.py:348
  49.3 0.0 collective-permute-done.4.from_above
  49.3 2.0 %collective-permute-done.5.from_below = f32[2,128,512]{2,1,0:T(8,128)S(1)} collective-permute-done((f32[2,128,512]{2,1,0:T(8,128)S(1)}, f32[2,128,512]{2,1,0:T(8,128)S(1)}, u32[]{:S(2)}, u32[]{:S(2)}) %collective-permute-start.5) | collective-permute-done | bytes 524320 | tf_op jit(solution)/shard_map/ppermute | solution.py:348
  51.4 0.2 fold.1
  51.5 1.3 collective-permute-start.7
  52.8 5.5 %collective-permute-start.6 = (f32[2,256,256]{2,1,0:T(8,128)S(1)}, f32[2,256,256]{2,1,0:T(8,128)}, u32[]{:S(2)}, u32[]{:S(2)}) collective-permute-start(f32[2,256,256]{2,1,0:T(8,128)S(1)} %get-tuple-element.37.tail), channel_id=1, source_target_pairs={{0,1},{1,2},{2,3},{3,4},{4,5},{5,6},{6,7},{8,9},{9,10},{10,11},{11... | collective-permute-start | bytes 1572872 | tf_op jit(solution)/shard_map/ppermute | solution.py:348
  58.4 0.1 light_fold.1
  58.4 1.3 collective-permute-start.11
  59.7 4.1 %collective-permute-start.10 = (f32[1,256,256]{2,1,0:T(8,128)S(1)}, f32[1,256,256]{2,1,0:T(8,128)S(1)}, u32[]{:S(2)}, u32[]{:S(2)}) collective-permute-start(f32[1,256,256]{2,1,0:T(8,128)S(1)} %get-tuple-element.42.tail), channel_id=1, source_target_pairs={{0,1},{1,2},{2,3},{3,4},{4,5},{5,6},{6,7},{8,9},{9,10},{10,11},{11... | collective-permute-start | bytes 786440 | tf_op jit(solution)/shard_map/ppermute | solution.py:348
  63.9 6.4 %collective-permute-done.11.from_right = f32[1,256,256]{2,1,0:T(8,128)S(1)} collective-permute-done((f32[1,256,256]{2,1,0:T(8,128)S(1)}, f32[1,256,256]{2,1,0:T(8,128)S(1)}, u32[]{:S(2)}, u32[]{:S(2)}) %collective-permute-start.11) | collective-permute-done | bytes 262176 | tf_op jit(solution)/shard_map/ppermute | solution.py:348
  70.2 17.7 %collective-permute-done.10.from_left = f32[1,256,256]{2,1,0:T(8,128)S(1)} collective-permute-done((f32[1,256,256]{2,1,0:T(8,128)S(1)}, f32[1,256,256]{2,1,0:T(8,128)S(1)}, u32[]{:S(2)}, u32[]{:S(2)}) %collective-permute-start.10) | collective-permute-done | bytes 262176 | tf_op jit(solution)/shard_map/ppermute | solution.py:348
  87.9 0.1 light_sum.1
  88.0 1.2 collective-permute-start.12
  89.2 0.8 collective-permute-done.12
  90.0 0.4 collective-permute-start.13
  90.4 2.1 %collective-permute-done.13 = f32[8,128]{1,0:T(8,128)S(1)} collective-permute-done((f32[8,128]{1,0:T(8,128)S(1)}, f32[8,128]{1,0:T(8,128)S(1)}, u32[]{:S(2)}, u32[]{:S(2)}) %collective-permute-start.13) | collective-permute-done | bytes 4128 | tf_op jit(solution)/shard_map/ppermute | solution.py:356
  92.4 2.2 %collective-permute-start.14 = (f32[8,128]{1,0:T(8,128)S(1)}, f32[8,128]{1,0:T(8,128)S(1)}, u32[]{:S(2)}, u32[]{:S(2)}) collective-permute-start(f32[8,128]{1,0:T(8,128)S(1)} %max.16), channel_id=1, source_target_pairs={{0,1},{1,2},{2,3},{3,4},{4,5},{5,6},{6,7},{7,0},{8,9},{9,10},{10,1... | collective-permute-start | bytes 12296 | tf_op jit(solution)/shard_map/ppermute | solution.py:356
  94.6 3.0 %collective-permute-done.14 = f32[8,128]{1,0:T(8,128)S(1)} collective-permute-done((f32[8,128]{1,0:T(8,128)S(1)}, f32[8,128]{1,0:T(8,128)S(1)}, u32[]{:S(2)}, u32[]{:S(2)}) %collective-permute-start.14) | collective-permute-done | bytes 4128 | tf_op jit(solution)/shard_map/ppermute | solution.py:356
  97.6 0.5 collective-permute-start.15
  98.1 3.8 %collective-permute-done.15 = f32[8,128]{1,0:T(8,128)S(1)} collective-permute-done((f32[8,128]{1,0:T(8,128)S(1)}, f32[8,128]{1,0:T(8,128)S(1)}, u32[]{:S(2)}, u32[]{:S(2)}) %collective-permute-start.15) | collective-permute-done | bytes 4128 | tf_op jit(solution)/shard_map/ppermute | solution.py:356
  101.9 0.0 collective-permute-start.16
  101.9 0.1 add_convert_fusion.place
  101.9 3.3 %collective-permute-done.16 = f32[8,128]{1,0:T(8,128)S(1)} collective-permute-done((f32[8,128]{1,0:T(8,128)S(1)}, f32[8,128]{1,0:T(8,128)S(1)}, u32[]{:S(2)}, u32[]{:S(2)}) %collective-permute-start.16) | collective-permute-done | bytes 4128 | tf_op jit(solution)/shard_map/ppermute | solution.py:356
  105.2 0.0 copy-start.10
  105.2 0.0 copy-start.12
  105.3 1.6 %update.1 = (f32[2,128,512]{2,1,0:T(8,128)S(1)}, f32[2,128,512]{2,1,0:T(8,128)S(1)}) custom-call(s32[2]{0:T(128)S(1)} %add_convert_fusion.place, f32[2,256,256]{2,1,0:T(8,128)S(1)} %get-tuple-element.36.head, f32[2,256,256]{2,1,0:T(8,128)S(1)} %get-tuple-element.37.tail, f32[2,256,256]{2,1,0:T(8,128)} %collective-permute-done.6.from_left, ...), custom_call_target="tpu_custom_call" | custom-call | bytes 3145728 | tf_op jit(solution)/shard_map/update/pallas_call | solution.py:434
  106.9 8.8 %collective-permute-start.17 = (f32[2,128,512]{2,1,0:T(8,128)S(1)}, f32[2,128,512]{2,1,0:T(8,128)S(1)}, u32[]{:S(2)}, u32[]{:S(2)}) collective-permute-start(f32[2,128,512]{2,1,0:T(8,128)S(1)} %get-tuple-element.45.bottom.old_bottom), channel_id=1, source_target_pairs={{0,8},{8,16},{16,24},{1,9},{9,17},{17,25},{2,10},{10,18},{18,26},{... | collective-permute-start | bytes 1572872 | tf_op jit(solution)/shard_map/ppermute | solution.py:348
  115.7 1.9 %collective-permute-start.18 = (f32[2,128,512]{2,1,0:T(8,128)S(1)}, f32[2,128,512]{2,1,0:T(8,128)S(1)}, u32[]{:S(2)}, u32[]{:S(2)}) collective-permute-start(f32[2,128,512]{2,1,0:T(8,128)S(1)} %get-tuple-element.46.top.old_top), channel_id=1, source_target_pairs={{8,0},{16,8},{24,16},{9,1},{17,9},{25,17},{10,2},{18,10},{26,18},{... | collective-permute-start | bytes 1572872 | tf_op jit(solution)/shard_map/ppermute | solution.py:348
  117.6 4.2 %collective-permute-done.17.up = f32[2,128,512]{2,1,0:T(8,128)S(1)} collective-permute-done((f32[2,128,512]{2,1,0:T(8,128)S(1)}, f32[2,128,512]{2,1,0:T(8,128)S(1)}, u32[]{:S(2)}, u32[]{:S(2)}) %collective-permute-start.17) | collective-permute-done | bytes 524320 | tf_op jit(solution)/shard_map/ppermute | solution.py:348
  121.8 4.4 %collective-permute-done.18.down = f32[2,128,512]{2,1,0:T(8,128)S(1)} collective-permute-done((f32[2,128,512]{2,1,0:T(8,128)S(1)}, f32[2,128,512]{2,1,0:T(8,128)S(1)}, u32[]{:S(2)}, u32[]{:S(2)}) %collective-permute-start.18) | collective-permute-done | bytes 524320 | tf_op jit(solution)/shard_map/ppermute | solution.py:348
  126.2 7.4 %gradient.3 = (f32[2,128,512]{2,1,0:T(8,128)S(1)}, f32[2,256,512]{2,1,0:T(8,128)}, f32[2,128,512]{2,1,0:T(8,128)S(1)}) custom-call(s32[1,1,3,2]{3,2,1,0:T(4,128)S(1)} %copy.14.offsets, f32[2,128,512]{2,1,0:T(8,128)S(1)} %collective-permute-done.17.up, f32[2,128,512]{2,1,0:T(8,128)S(1)} %get-tuple-element.46.top.old_top, ...), custom_call_target="tpu_custom_call" | custom-call | flops 2415919104 | bytes 6291456 | tf_op jit(solution)/shard_map/gradient/pallas_call | solution.py:410
  133.7 1.9 %collective-permute-start.19 = (f32[2,128,512]{2,1,0:T(8,128)S(1)}, f32[2,128,512]{2,1,0:T(8,128)S(1)}, u32[]{:S(2)}, u32[]{:S(2)}) collective-permute-start(f32[2,128,512]{2,1,0:T(8,128)S(1)} %get-tuple-element.48), channel_id=1, source_target_pairs={{0,8},{8,16},{16,24},{1,9},{9,17},{17,25},{2,10},{10,18},{18,26},{... | collective-permute-start | bytes 1572872 | tf_op jit(solution)/shard_map/ppermute | solution.py:348
  135.6 2.4 %collective-permute-start.20 = (f32[2,128,512]{2,1,0:T(8,128)S(1)}, f32[2,128,512]{2,1,0:T(8,128)S(1)}, u32[]{:S(2)}, u32[]{:S(2)}) collective-permute-start(f32[2,128,512]{2,1,0:T(8,128)S(1)} %get-tuple-element.49), channel_id=1, source_target_pairs={{8,0},{16,8},{24,16},{9,1},{17,9},{25,17},{10,2},{18,10},{26,18},{... | collective-permute-start | bytes 1572872 | tf_op jit(solution)/shard_map/ppermute | solution.py:348
  138.0 3.7 %collective-permute-done.19.from_above = f32[2,128,512]{2,1,0:T(8,128)S(1)} collective-permute-done((f32[2,128,512]{2,1,0:T(8,128)S(1)}, f32[2,128,512]{2,1,0:T(8,128)S(1)}, u32[]{:S(2)}, u32[]{:S(2)}) %collective-permute-start.19) | collective-permute-done | bytes 524320 | tf_op jit(solution)/shard_map/ppermute | solution.py:348
  141.7 4.4 %collective-permute-done.20.from_below = f32[2,128,512]{2,1,0:T(8,128)S(1)} collective-permute-done((f32[2,128,512]{2,1,0:T(8,128)S(1)}, f32[2,128,512]{2,1,0:T(8,128)S(1)}, u32[]{:S(2)}, u32[]{:S(2)}) %collective-permute-start.20) | collective-permute-done | bytes 524320 | tf_op jit(solution)/shard_map/ppermute | solution.py:348
  146.1 1.2 copy-done.4
  147.3 0.1 fold_last.1
  147.4 1.7 %collective-permute-start.21 = (f32[2,256,128]{2,1,0:T(8,128)S(1)}, f32[2,256,128]{2,1,0:T(8,128)S(1)}, u32[]{:S(2)}, u32[]{:S(2)}) collective-permute-start(f32[2,256,128]{2,1,0:T(8,128)S(1)} %get-tuple-element.51), channel_id=1, source_target_pairs={{0,1},{1,2},{2,3},{3,4},{4,5},{5,6},{6,7},{8,9},{9,10},{10,11},{11... | collective-permute-start | bytes 786440 | tf_op jit(solution)/shard_map/ppermute | solution.py:348
  149.2 1.3 collective-permute-start.22
  150.5 2.2 %collective-permute-done.21.from_left = f32[2,256,128]{2,1,0:T(8,128)S(1)} collective-permute-done((f32[2,256,128]{2,1,0:T(8,128)S(1)}, f32[2,256,128]{2,1,0:T(8,128)S(1)}, u32[]{:S(2)}, u32[]{:S(2)}) %collective-permute-start.21) | collective-permute-done | bytes 262176 | tf_op jit(solution)/shard_map/ppermute | solution.py:348
  152.7 3.6 %collective-permute-done.22.from_right = f32[2,256,128]{2,1,0:T(8,128)S(1)} collective-permute-done((f32[2,256,128]{2,1,0:T(8,128)S(1)}, f32[2,256,128]{2,1,0:T(8,128)S(1)}, u32[]{:S(2)}, u32[]{:S(2)}) %collective-permute-start.22) | collective-permute-done | bytes 262176 | tf_op jit(solution)/shard_map/ppermute | solution.py:348
  156.3 1.0 finish.1
  (30 shorter events, 0.1 us)
Async XLA Ops:
  0.0 1.0 copy-start.2
  1.0 21.3 %copy-start.13 = (s32[1,1,3,2]{2,3,1,0:T(2,128)S(1)}, s32[1,1,3,2]{2,3,1,0:T(2,128)}, u32[]{:S(2)}) copy-start(s32[1,1,3,2]{2,3,1,0:T(2,128)} %param.12) | copy-start | bytes 76
  1.0 21.4 %copy-start.6 = (f32[2,256,256]{2,1,0:T(8,128)S(1)}, f32[2,256,256]{2,1,0:T(8,128)}, u32[]{:S(2)}) copy-start(f32[2,256,256]{2,1,0:T(8,128)} %probe.1) | copy-start | bytes 1572868
  1.1 9.0 %collective-permute-start = (f32[2,256,128]{2,1,0:T(8,128)S(1)}, f32[2,256,128]{2,1,0:T(8,128)S(1)}, u32[]{:S(2)}, u32[]{:S(2)}) collective-permute-start(f32[2,256,128]{2,1,0:T(8,128)S(1)} %get-tuple-element.29), channel_id=1, source_target_pairs={{0,1},{1,2},{2,3},{3,4},{4,5},{5,6},{6,7},{8,9},{9,10},{10,11},{11... | collective-permute-start | bytes 786440 | tf_op jit(solution)/shard_map/ppermute | solution.py:348
  5.2 19.7 %copy-start.5 = (f32[1,1,3,256,256]{4,3,2,1,0:T(8,128)S(1)}, f32[1,1,3,256,256]{4,3,2,1,0:T(8,128)}, u32[]{:S(2)}) copy-start(f32[1,1,3,256,256]{4,3,2,1,0:T(8,128)} %amplitude.1) | copy-start | bytes 2359300
  5.2 8.9 %collective-permute-start.1 = (f32[2,256,128]{2,1,0:T(8,128)S(1)}, f32[2,256,128]{2,1,0:T(8,128)S(1)}, u32[]{:S(2)}, u32[]{:S(2)}) collective-permute-start(f32[2,256,128]{2,1,0:T(8,128)S(1)} %get-tuple-element.30), channel_id=1, source_target_pairs={{1,0},{2,1},{3,2},{4,3},{5,4},{6,5},{7,6},{9,8},{10,9},{11,10},{12... | collective-permute-start | bytes 786440 | tf_op jit(solution)/shard_map/ppermute | solution.py:348
  14.2 13.6 %collective-permute-start.2 = (f32[2,128,512]{2,1,0:T(8,128)S(1)}, f32[2,128,512]{2,1,0:T(8,128)}, u32[]{:S(2)}, u32[]{:S(2)}) collective-permute-start(f32[2,128,512]{2,1,0:T(8,128)S(1)} %get-tuple-element.31.bottom.old_bottom), channel_id=1, source_target_pairs={{0,8},{8,16},{16,24},{1,9},{9,17},{17,25},{2,10},{10,18},{18,26},{... | collective-permute-start | bytes 1572872 | tf_op jit(solution)/shard_map/ppermute | solution.py:348
  20.4 10.6 %collective-permute-start.3 = (f32[2,128,512]{2,1,0:T(8,128)S(1)}, f32[2,128,512]{2,1,0:T(8,128)}, u32[]{:S(2)}, u32[]{:S(2)}) collective-permute-start(f32[2,128,512]{2,1,0:T(8,128)S(1)} %get-tuple-element.32.top.old_top), channel_id=1, source_target_pairs={{8,0},{16,8},{24,16},{9,1},{17,9},{25,17},{10,2},{18,10},{26,18},{... | collective-permute-start | bytes 1572872 | tf_op jit(solution)/shard_map/ppermute | solution.py:348
  23.7 1.2 copy-start
  24.9 1.0 copy-start.7
  25.9 1.0 copy-start.8
  26.9 4.2 %copy-start.9 = (bf16[2,256,768]{2,1,0:T(8,128)(2,1)S(1)}, bf16[2,256,768]{2,1,0:T(8,128)(2,1)}, u32[]{:S(2)}) copy-start(bf16[2,256,768]{2,1,0:T(8,128)(2,1)} %constant.21.clone.left_back) | copy-start | bytes 2359300
  26.9 4.2 %copy-start.11 = (bf16[2,256,768]{2,1,0:T(8,128)(2,1)S(1)}, bf16[2,256,768]{2,1,0:T(8,128)(2,1)}, u32[]{:S(2)}) copy-start(bf16[2,256,768]{2,1,0:T(8,128)(2,1)} %constant.20.clone.left) | copy-start | bytes 2359300
  27.9 15.4 %copy-start.1 = (f32[3,2,256,256]{3,2,1,0:T(8,128)S(1)}, f32[3,2,256,256]{3,2,1,0:T(8,128)}, u32[]{:S(2)}) copy-start(f32[3,2,256,256]{3,2,1,0:T(8,128)} %copy-done) | copy-start | bytes 4718596
  38.8 12.6 %copy-start.3 = (f32[2,256,512]{2,1,0:T(8,128)S(1)}, f32[2,256,512]{2,1,0:T(8,128)}, u32[]{:S(2)}) copy-start(f32[2,256,512]{2,1,0:T(8,128)} %get-tuple-element.33.mid) | copy-start | bytes 3145732
  38.8 10.5 %collective-permute-start.4 = (f32[2,128,512]{2,1,0:T(8,128)S(1)}, f32[2,128,512]{2,1,0:T(8,128)S(1)}, u32[]{:S(2)}, u32[]{:S(2)}) collective-permute-start(f32[2,128,512]{2,1,0:T(8,128)S(1)} %get-tuple-element.34), channel_id=1, source_target_pairs={{0,8},{8,16},{16,24},{1,9},{9,17},{17,25},{2,10},{10,18},{18,26},{... | collective-permute-start | bytes 1572872 | tf_op jit(solution)/shard_map/ppermute | solution.py:348
  40.8 10.5 %collective-permute-start.5 = (f32[2,128,512]{2,1,0:T(8,128)S(1)}, f32[2,128,512]{2,1,0:T(8,128)S(1)}, u32[]{:S(2)}, u32[]{:S(2)}) collective-permute-start(f32[2,128,512]{2,1,0:T(8,128)S(1)} %get-tuple-element.35), channel_id=1, source_target_pairs={{8,0},{16,8},{24,16},{9,1},{17,9},{25,17},{10,2},{18,10},{26,18},{... | collective-permute-start | bytes 1572872 | tf_op jit(solution)/shard_map/ppermute | solution.py:348
  44.2 14.1 %collective-permute-start.8 = (f32[1,128,512]{2,1,0:T(8,128)S(1)}, f32[1,128,512]{2,1,0:T(8,128)S(1)}, u32[]{:S(2)}, u32[]{:S(2)}) collective-permute-start(f32[1,128,512]{2,1,0:T(8,128)S(1)} %get-tuple-element.39), channel_id=1, source_target_pairs={{0,8},{8,16},{16,24},{1,9},{9,17},{17,25},{2,10},{10,18},{18,26},{... | collective-permute-start | bytes 786440 | tf_op jit(solution)/shard_map/ppermute | solution.py:348
  47.4 11.0 %collective-permute-start.9 = (f32[1,128,512]{2,1,0:T(8,128)S(1)}, f32[1,128,512]{2,1,0:T(8,128)S(1)}, u32[]{:S(2)}, u32[]{:S(2)}) collective-permute-start(f32[1,128,512]{2,1,0:T(8,128)S(1)} %get-tuple-element.40), channel_id=1, source_target_pairs={{8,0},{16,8},{24,16},{9,1},{17,9},{25,17},{10,2},{18,10},{26,18},{... | collective-permute-start | bytes 786440 | tf_op jit(solution)/shard_map/ppermute | solution.py:348
  51.5 53.7 %collective-permute-start.7 = (f32[2,256,256]{2,1,0:T(8,128)S(1)}, f32[2,256,256]{2,1,0:T(8,128)}, u32[]{:S(2)}, u32[]{:S(2)}) collective-permute-start(f32[2,256,256]{2,1,0:T(8,128)S(1)} %get-tuple-element.36.head), channel_id=1, source_target_pairs={{1,0},{2,1},{3,2},{4,3},{5,4},{6,5},{7,6},{9,8},{10,9},{11,10},{12... | collective-permute-start | bytes 1572872 | tf_op jit(solution)/shard_map/ppermute | solution.py:348
  52.8 52.4 %collective-permute-start.6 = (f32[2,256,256]{2,1,0:T(8,128)S(1)}, f32[2,256,256]{2,1,0:T(8,128)}, u32[]{:S(2)}, u32[]{:S(2)}) collective-permute-start(f32[2,256,256]{2,1,0:T(8,128)S(1)} %get-tuple-element.37.tail), channel_id=1, source_target_pairs={{0,1},{1,2},{2,3},{3,4},{4,5},{5,6},{6,7},{8,9},{9,10},{10,11},{11... | collective-permute-start | bytes 1572872 | tf_op jit(solution)/shard_map/ppermute | solution.py:348
  58.4 11.8 %collective-permute-start.11 = (f32[1,256,256]{2,1,0:T(8,128)S(1)}, f32[1,256,256]{2,1,0:T(8,128)S(1)}, u32[]{:S(2)}, u32[]{:S(2)}) collective-permute-start(f32[1,256,256]{2,1,0:T(8,128)S(1)} %get-tuple-element.41.head), channel_id=1, source_target_pairs={{1,0},{2,1},{3,2},{4,3},{5,4},{6,5},{7,6},{9,8},{10,9},{11,10},{12... | collective-permute-start | bytes 786440 | tf_op jit(solution)/shard_map/ppermute | solution.py:348
  59.7 28.2 %collective-permute-start.10 = (f32[1,256,256]{2,1,0:T(8,128)S(1)}, f32[1,256,256]{2,1,0:T(8,128)S(1)}, u32[]{:S(2)}, u32[]{:S(2)}) collective-permute-start(f32[1,256,256]{2,1,0:T(8,128)S(1)} %get-tuple-element.42.tail), channel_id=1, source_target_pairs={{0,1},{1,2},{2,3},{3,4},{4,5},{5,6},{6,7},{8,9},{9,10},{10,11},{11... | collective-permute-start | bytes 786440 | tf_op jit(solution)/shard_map/ppermute | solution.py:348
  88.0 2.0 %collective-permute-start.12 = (f32[8,128]{1,0:T(8,128)S(1)}, f32[8,128]{1,0:T(8,128)S(1)}, u32[]{:S(2)}, u32[]{:S(2)}) collective-permute-start(f32[8,128]{1,0:T(8,128)S(1)} %get-tuple-element.44), channel_id=1, source_target_pairs={{0,8},{8,16},{16,24},{24,0},{1,9},{9,17},{17,25},{25,1},{2,10},{10... | collective-permute-start | bytes 12296 | tf_op jit(solution)/shard_map/ppermute | solution.py:356
  90.0 2.5 %collective-permute-start.13 = (f32[8,128]{1,0:T(8,128)S(1)}, f32[8,128]{1,0:T(8,128)S(1)}, u32[]{:S(2)}, u32[]{:S(2)}) collective-permute-start(f32[8,128]{1,0:T(8,128)S(1)} %max.15), channel_id=1, source_target_pairs={{0,16},{8,24},{16,0},{24,8},{1,17},{9,25},{17,1},{25,9},{2,18},{10... | collective-permute-start | bytes 12296 | tf_op jit(solution)/shard_map/ppermute | solution.py:356
  92.4 5.2 %collective-permute-start.14 = (f32[8,128]{1,0:T(8,128)S(1)}, f32[8,128]{1,0:T(8,128)S(1)}, u32[]{:S(2)}, u32[]{:S(2)}) collective-permute-start(f32[8,128]{1,0:T(8,128)S(1)} %max.16), channel_id=1, source_target_pairs={{0,1},{1,2},{2,3},{3,4},{4,5},{5,6},{6,7},{7,0},{8,9},{9,10},{10,1... | collective-permute-start | bytes 12296 | tf_op jit(solution)/shard_map/ppermute | solution.py:356
  97.6 4.3 %collective-permute-start.15 = (f32[8,128]{1,0:T(8,128)S(1)}, f32[8,128]{1,0:T(8,128)S(1)}, u32[]{:S(2)}, u32[]{:S(2)}) collective-permute-start(f32[8,128]{1,0:T(8,128)S(1)} %max.17), channel_id=1, source_target_pairs={{0,2},{1,3},{2,4},{3,5},{4,6},{5,7},{6,0},{7,1},{8,10},{9,11},{10,... | collective-permute-start | bytes 12296 | tf_op jit(solution)/shard_map/ppermute | solution.py:356
  101.9 3.4 %collective-permute-start.16 = (f32[8,128]{1,0:T(8,128)S(1)}, f32[8,128]{1,0:T(8,128)S(1)}, u32[]{:S(2)}, u32[]{:S(2)}) collective-permute-start(f32[8,128]{1,0:T(8,128)S(1)} %max.18), channel_id=1, source_target_pairs={{0,4},{1,5},{2,6},{3,7},{4,0},{5,1},{6,2},{7,3},{8,12},{9,13},{10,... | collective-permute-start | bytes 12296 | tf_op jit(solution)/shard_map/ppermute | solution.py:356
  105.2 21.0 %copy-start.10 = (bf16[2,256,768]{2,1,0:T(8,128)(2,1)S(1)}, bf16[2,256,768]{2,1,0:T(8,128)(2,1)}, u32[]{:S(2)}) copy-start(bf16[2,256,768]{2,1,0:T(8,128)(2,1)} %constant.21.clone.left_back) | copy-start | bytes 2359300
  105.2 21.0 %copy-start.12 = (bf16[2,256,768]{2,1,0:T(8,128)(2,1)S(1)}, bf16[2,256,768]{2,1,0:T(8,128)(2,1)}, u32[]{:S(2)}) copy-start(bf16[2,256,768]{2,1,0:T(8,128)(2,1)} %constant.20.clone.left) | copy-start | bytes 2359300
  106.9 14.9 %collective-permute-start.17 = (f32[2,128,512]{2,1,0:T(8,128)S(1)}, f32[2,128,512]{2,1,0:T(8,128)S(1)}, u32[]{:S(2)}, u32[]{:S(2)}) collective-permute-start(f32[2,128,512]{2,1,0:T(8,128)S(1)} %get-tuple-element.45.bottom.old_bottom), channel_id=1, source_target_pairs={{0,8},{8,16},{16,24},{1,9},{9,17},{17,25},{2,10},{10,18},{18,26},{... | collective-permute-start | bytes 1572872 | tf_op jit(solution)/shard_map/ppermute | solution.py:348
  115.7 10.5 %collective-permute-start.18 = (f32[2,128,512]{2,1,0:T(8,128)S(1)}, f32[2,128,512]{2,1,0:T(8,128)S(1)}, u32[]{:S(2)}, u32[]{:S(2)}) collective-permute-start(f32[2,128,512]{2,1,0:T(8,128)S(1)} %get-tuple-element.46.top.old_top), channel_id=1, source_target_pairs={{8,0},{16,8},{24,16},{9,1},{17,9},{25,17},{10,2},{18,10},{26,18},{... | collective-permute-start | bytes 1572872 | tf_op jit(solution)/shard_map/ppermute | solution.py:348
  133.7 8.0 %collective-permute-start.19 = (f32[2,128,512]{2,1,0:T(8,128)S(1)}, f32[2,128,512]{2,1,0:T(8,128)S(1)}, u32[]{:S(2)}, u32[]{:S(2)}) collective-permute-start(f32[2,128,512]{2,1,0:T(8,128)S(1)} %get-tuple-element.48), channel_id=1, source_target_pairs={{0,8},{8,16},{16,24},{1,9},{9,17},{17,25},{2,10},{10,18},{18,26},{... | collective-permute-start | bytes 1572872 | tf_op jit(solution)/shard_map/ppermute | solution.py:348
  135.6 10.5 %collective-permute-start.20 = (f32[2,128,512]{2,1,0:T(8,128)S(1)}, f32[2,128,512]{2,1,0:T(8,128)S(1)}, u32[]{:S(2)}, u32[]{:S(2)}) collective-permute-start(f32[2,128,512]{2,1,0:T(8,128)S(1)} %get-tuple-element.49), channel_id=1, source_target_pairs={{8,0},{16,8},{24,16},{9,1},{17,9},{25,17},{10,2},{18,10},{26,18},{... | collective-permute-start | bytes 1572872 | tf_op jit(solution)/shard_map/ppermute | solution.py:348
  146.1 1.2 copy-start.4
  147.4 5.3 %collective-permute-start.21 = (f32[2,256,128]{2,1,0:T(8,128)S(1)}, f32[2,256,128]{2,1,0:T(8,128)S(1)}, u32[]{:S(2)}, u32[]{:S(2)}) collective-permute-start(f32[2,256,128]{2,1,0:T(8,128)S(1)} %get-tuple-element.51), channel_id=1, source_target_pairs={{0,1},{1,2},{2,3},{3,4},{4,5},{5,6},{6,7},{8,9},{9,10},{10,11},{11... | collective-permute-start | bytes 786440 | tf_op jit(solution)/shard_map/ppermute | solution.py:348
  149.2 7.1 %collective-permute-start.22 = (f32[2,256,128]{2,1,0:T(8,128)S(1)}, f32[2,256,128]{2,1,0:T(8,128)S(1)}, u32[]{:S(2)}, u32[]{:S(2)}) collective-permute-start(f32[2,256,128]{2,1,0:T(8,128)S(1)} %get-tuple-element.52), channel_id=1, source_target_pairs={{1,0},{2,1},{3,2},{4,3},{5,4},{6,5},{7,6},{9,8},{10,9},{11,10},{12... | collective-permute-start | bytes 786440 | tf_op jit(solution)/shard_map/ppermute | solution.py:348
where the time goes:
time: 158 us; the launch traced here: 157 us
  waiting for transfers between devices  72.1 us (46%)
  starting transfers between devices  57.7 us (37%)
  Pallas kernels  21.6 us (14%)
  local copies, waits for them, and re-layouts  5.57 us (4%)
    ppermute x18, waiting for transfers between devices, shifted(): return lax.ppermute(block, axis, route)  59.2 us
    ppermute x18, starting transfers between devices, shifted(): return lax.ppermute(block, axis, route)  53.5 us
    pallas_call x2, Pallas kernels, local(): kernel_call(gradient_kernel, [shape(2, HALO, span), shape(2, tile, span),...  15.2 us
    ppermute x5, waiting for transfers between devices, largest_of(): block = jnp.maximum(block, lax.ppermute(block, axis, route))  12.9 us
    unnamed x29, local copies, waits for them, and re-layouts  5.57 us
    ppermute x5, starting transfers between devices, largest_of(): block = jnp.maximum(block, lax.ppermute(block, axis, route))  4.27 us
  transfers between devices with their start and end apart: 23, of which 17 were waited for; matrix products, arithmetic and copies ran while one was open for 0% of the time, Pallas kernels for 2%

commit v1 on v0

v1 whole, which is shorter than its diff:
```python
import functools
import math

import jax
import jax.numpy as jnp
import numpy as np
from jax import lax
from jax.experimental import pallas as pl
from jax.experimental.pallas import tpu as pltpu
from jax.sharding import PartitionSpec as P


HALO = 128
ITERS = 2
LANES = 128

smooth_term = 0.25
ridge_share = 0.1

VM = pl.BlockSpec(memory_space=pltpu.VMEM)
SM = pl.BlockSpec(memory_space=pltpu.SMEM)
F32 = jnp.float32
BF16 = jnp.bfloat16


def shape(*dims):
    return jax.ShapeDtypeStruct(dims, F32)


def to_bf16(x):
    return np.asarray(x, np.float32).astype(BF16)


def split_table(table):
    high = to_bf16(table)
    low = to_bf16(table - high.astype(np.float64))
    return high, low


@functools.lru_cache
def dft_tables(length):
    half = length // 2
    n = np.arange(half)
    forward, backward = [], []
    for odd in (0, 1):
        turn = ((2 * n[:, None] + odd) * n[None, :]) % length
        angle = turn * (2.0 * math.pi / length)
        cos, sin = np.cos(angle) / math.sqrt(length), -np.sin(angle) / math.sqrt(length)
        form = np.block([[cos, -sin], [sin, cos]])
        forward.append(np.stack(split_table(form)))
        backward.append(np.stack(split_table(form.T)))
    place = np.zeros((length, length), np.float32)
    place[2 * n, n] = 1.0
    place[2 * n + 1, half + n] = 1.0
    pick = to_bf16(place)
    return np.stack(forward), np.stack(backward), pick, np.ascontiguousarray(pick.T)


def halves(x):
    high = x.astype(BF16)
    low = (x - high.astype(F32)).astype(BF16)
    return high, low


def left_product(table, x):
    high, low = halves(x)
    return jnp.dot(
        jnp.concatenate([table[0], table[1], table[0]], axis=1),
        jnp.concatenate([high, high, low], axis=0),
        preferred_element_type=F32,
    )


def right_product(x, table):
    high, low = halves(x)
    return jnp.dot(
        jnp.concatenate([high, low, high], axis=1),
        jnp.concatenate([table[0], table[0], table[1]], axis=0),
        preferred_element_type=F32,
    )


def window_masks(offsets, position, win):
    row = offsets[0, 0, position, 0] + HALO
    column = offsets[0, 0, position, 1] + HALO
    low = lax.broadcasted_iota(jnp.int32, (win, win), 0) >= row
    near = lax.broadcasted_iota(jnp.int32, (win, win), 1) >= column
    return low, near


def roll_kernel(offsets, probe, rolled):
    win = probe.shape[1]
    for position in range(rolled.shape[0]):
        row = lax.rem(offsets[0, 0, position, 0] + HALO, win)
        column = lax.rem(offsets[0, 0, position, 1] + HALO, win)
        for plane in (0, 1):
            rolled[position, plane] = pltpu.roll(
                pltpu.roll(probe[plane], column, 1), row, 0
            )


def spread(piece, low, near, upper, lower, win, first):
    above = jnp.where(low, piece, 0.0)
    below = jnp.where(low, 0.0, piece)
    for ref, block in ((upper, above), (lower, below)):
        parts = (jnp.where(near, block, 0.0), jnp.where(near, 0.0, block))
        for lanes, part in zip((slice(0, win), slice(win, None)), parts):
            ref[:, lanes] = part if first else ref[:, lanes] + part


def gradient_kernel(
    place, offsets, near_rows, cross_rows, top, bottom, probe, amplitude, forward, backward,
    grad_near, grad_mid, grad_cross, upper, lower,
):
    count, win, _ = amplitude.shape
    half = win // 2
    is_odd = place[2] > 0

    def patch(plane, low, near):
        up = jnp.where(is_odd, near_rows[plane], cross_rows[plane])
        down = jnp.where(is_odd, cross_rows[plane], near_rows[plane])
        first = jnp.concatenate([up, top[plane]], axis=0)
        second = jnp.concatenate([bottom[plane], down], axis=0)
        return jnp.where(
            near,
            jnp.where(low, first[:, :win], second[:, :win]),
            jnp.where(low, first[:, win:], second[:, win:]),
        )

    for position in range(count):
        low, near = window_masks(offsets, position, win)
        patch_real = patch(0, low, near)
        patch_imag = patch(1, low, near)
        probe_real, probe_imag = probe[position, 0], probe[position, 1]
        real = probe_real * patch_real - probe_imag * patch_imag
        imag = probe_real * patch_imag + probe_imag * patch_real
        summed = jnp.concatenate([real[:half] + real[half:], imag[:half] + imag[half:]], axis=0)
        differ = jnp.concatenate([real[:half] - real[half:], imag[:half] - imag[half:]], axis=0)
        even = left_product(forward[0], summed)
        odd = left_product(forward[1], differ)
        real = jnp.concatenate([even[:half], odd[:half]], axis=0)
        imag = jnp.concatenate([even[half:], odd[half:]], axis=0)
        summed = jnp.concatenate(
            [real[:, :half] + real[:, half:], imag[:, :half] + imag[:, half:]], axis=1
        )
        differ = jnp.concatenate(
            [real[:, :half] - real[:, half:], imag[:, :half] - imag[:, half:]], axis=1
        )
        even = right_product(summed, backward[0])
        odd = right_product(differ, backward[1])
        even_real, even_imag = even[:, :half], even[:, half:]
        odd_real, odd_imag = odd[:, :half], odd[:, half:]
        amp = amplitude[position]
        even_factor = 1.0 - amp[:, :half] * lax.rsqrt(
            even_real * even_real + even_imag * even_imag + smooth_term
        )
        odd_factor = 1.0 - amp[:, half:] * lax.rsqrt(
            odd_real * odd_real + odd_imag * odd_imag + smooth_term
        )
        even = jnp.concatenate([even_factor * even_real, even_factor * even_imag], axis=1)
        odd = jnp.concatenate([odd_factor * odd_real, odd_factor * odd_imag], axis=1)
        even_back = right_product(even, forward[0])
        odd_back = right_product(odd, forward[1])
        summed, differ = even_back + odd_back, even_back - odd_back
        real = jnp.concatenate([summed[:, :half], differ[:, :half]], axis=1)
        imag = jnp.concatenate([summed[:, half:], differ[:, half:]], axis=1)
        even = left_product(backward[0], jnp.concatenate([real[:half], imag[:half]], axis=0))
        odd = left_product(backward[1], jnp.concatenate([real[half:], imag[half:]], axis=0))
        summed, differ = even + odd, even - odd
        real = jnp.concatenate([summed[:half], differ[:half]], axis=0)
        imag = jnp.concatenate([summed[half:], differ[half:]], axis=0)
        for plane, piece in (
            (0, probe_real * real + probe_imag * imag),
            (1, probe_real * imag - probe_imag * real),
        ):
            spread(
                piece, low, near, upper.at[plane], lower.at[plane], win, position == 0
            )
    share(is_odd, upper, lower, grad_near, grad_mid, grad_cross)


def share(is_odd, upper, lower, out_near, out_mid, out_cross):
    edge = out_near.shape[1]
    up, down = upper[:, :edge, :], lower[:, edge:, :]
    out_near[...] = jnp.where(is_odd, up, down)
    out_mid[:, :edge, :] = upper[:, edge:, :]
    out_mid[:, edge:, :] = lower[:, :edge, :]
    out_cross[...] = jnp.where(is_odd, down, up)


def light_kernel(place, offsets, probe, light_near, light_mid, light_cross, upper, lower):
    win = probe.shape[2]
    for position in range(probe.shape[0]):
        low, near = window_masks(offsets, position, win)
        real, imag = probe[position, 0], probe[position, 1]
        spread(
            real * real + imag * imag, low, near, upper.at[0], lower.at[0], win, position == 0
        )
    share(place[2] > 0, upper, lower, light_near, light_mid, light_cross)


def thirds(x):
    high = x.astype(BF16)
    rest = x - high.astype(F32)
    mid = rest.astype(BF16)
    return high, mid, (rest - mid.astype(F32)).astype(BF16)


def order_kernel(amplitude, pick, pick_back, ordered):
    rows = jnp.concatenate([pick_back[...]] * 3, axis=1)
    columns = jnp.concatenate([pick[...]] * 3, axis=0)
    for position in range(ordered.shape[0]):
        block = jnp.dot(
            rows,
            jnp.concatenate(thirds(amplitude[0, 0, position]), axis=0),
            preferred_element_type=F32,
        )
        ordered[position] = jnp.dot(
            jnp.concatenate(thirds(block), axis=1), columns, preferred_element_type=F32
        )


def edges_kernel(specimen, head, tail):
    head[...] = specimen[:, :, :HALO]
    tail[...] = specimen[:, :, specimen.shape[2] - HALO :]


def widen_kernel(place, before, specimen, after, top, bottom, near, cross):
    edge = top.shape[1]
    tile = specimen.shape[2]
    for index, out in enumerate((top, bottom)):
        rows = slice(index * edge, (index + 1) * edge)
        out[:, :, :HALO] = before[:, rows, :]
        out[:, :, HALO : HALO + tile] = specimen[:, rows, :]
        out[:, :, HALO + tile :] = after[:, rows, :]
    sides(place[2] > 0, top, bottom, near, cross)


def sides(is_odd, top, bottom, near, cross):
    near[...] = jnp.where(is_odd, top[...], bottom[...])
    cross[...] = jnp.where(is_odd, bottom[...], top[...])


def fold_rows(place, mid, near, cross):
    is_odd = place[2] > 0
    edge = near.shape[1]
    upper = mid[:, :edge, :] + jnp.where(is_odd, near[...], cross[...])
    lower = mid[:, edge:, :] + jnp.where(is_odd, cross[...], near[...])
    return (slice(0, edge), upper), (slice(edge, None), lower)


def fold_strips_kernel(place, mid, near, cross, head, tail):
    half = head.shape[2]
    for rows, block in fold_rows(place, mid, near, cross):
        head[:, rows, :] = block[:, :, :half]
        tail[:, rows, :] = block[:, :, half:]


def fold_bands_kernel(place, mid, near, cross, head, core, tail):
    tile = core.shape[2]
    for rows, block in fold_rows(place, mid, near, cross):
        head[:, rows, :] = block[:, :, :HALO]
        core[:, rows, :] = block[:, :, HALO : HALO + tile]
        tail[:, rows, :] = block[:, :, HALO + tile :]


def light_sum_kernel(head, tail, from_left, from_right, light, largest):
    left = head[0] + from_left[0]
    right = tail[0] + from_right[0]
    half = left.shape[1]
    light[:, :half] = left
    light[:, half:] = right
    best = jnp.maximum(left[:, HALO:], right[:, : half - HALO])
    rows, columns = best.shape
    found = best[:8]
    for row in range(8, rows, 8):
        found = jnp.maximum(found, best[row : row + 8])
    top = found[:, :LANES]
    for column in range(LANES, columns, LANES):
        top = jnp.maximum(top, found[:, column : column + LANES])
    largest[...] = top


def update_kernel(
    place, head, tail, from_left, from_right, light, peak, old_top, old_bottom,
    top, bottom, near, cross,
):
    edge = top.shape[1]
    half = head.shape[2]
    most = ridge_share * jnp.max(peak[...])
    has_left, has_right = place[0] > 0, place[1] > 0
    lane = lax.broadcasted_iota(jnp.int32, (edge, half), 1)
    keep_left = jnp.logical_or(lane >= HALO, has_left)
    keep_right = jnp.logical_or(lane < half - HALO, has_right)
    for index, (old, out) in enumerate(((old_top, top), (old_bottom, bottom))):
        rows = slice(index * edge, (index + 1) * edge)
        for side, (own, sent, keep) in enumerate(
            ((head, from_left, keep_left), (tail, from_right, keep_right))
        ):
            lanes = slice(side * half, (side + 1) * half)
            scale = 1.0 / (light[rows, lanes] + most)
            for plane in (0, 1):
                gradient = own[plane, rows, :] + sent[plane, rows, :]
                new = old[plane, :, lanes] - gradient * scale
                out[plane, :, lanes] = jnp.where(keep, new, 0.0)
    sides(place[2] > 0, top, bottom, near, cross)


def finish_kernel(core, from_left, from_right, light, peak, old_top, old_bottom, out):
    edge = old_top.shape[1]
    tile = out.shape[2]
    inner = slice(HALO, HALO + tile)
    most = ridge_share * jnp.max(peak[...])
    for index, old in enumerate((old_top, old_bottom)):
        rows = slice(index * edge, (index + 1) * edge)
        scale = 1.0 / (light[rows, inner] + most)
        for plane in (0, 1):
            gradient = core[plane, rows, :]
            gradient = jnp.concatenate(
                [
                    gradient[:, :HALO] + from_left[plane, rows, :],
                    gradient[:, HALO : tile - HALO],
                    gradient[:, tile - HALO :] + from_right[plane, rows, :],
                ],
                axis=1,
            ) if tile > 2 * HALO else jnp.concatenate(
                [
                    gradient[:, :HALO] + from_left[plane, rows, :],
                    gradient[:, HALO:] + from_right[plane, rows, :],
                ],
                axis=1,
            )
            out[plane, rows, :] = old[plane, :, inner] - gradient * scale


def kernel_call(body, outs, specs, flops=0, scratch=(), grant=8):
    moved = 4 * sum(math.prod(out.shape) for out in outs)
    single = len(outs) == 1
    return pl.pallas_call(
        body,
        out_shape=outs[0] if single else outs,
        in_specs=specs,
        out_specs=VM if single else (VM,) * len(outs),
        scratch_shapes=list(scratch),
        compiler_params=pltpu.CompilerParams(vmem_limit_bytes=grant * 1024 * 1024),
        cost_estimate=pl.CostEstimate(
            flops=flops, bytes_accessed=3 * moved, transcendentals=0
        ),
    )


def shifted(block, axis, distance):
    count = lax.axis_size(axis)
    route = [(i - distance, i) for i in range(count) if 0 <= i - distance < count]
    return lax.ppermute(block, axis, route)


def swapped(block, axis, first):
    count = lax.axis_size(axis)
    route = []
    for i in range(first, count - 1, 2):
        route += [(i, i + 1), (i + 1, i)]
    return lax.ppermute(block, axis, route)


def row_exchange(near, cross):
    cross = swapped(cross, "row", 1)
    near = swapped(near, "row", 0)
    return near, cross


def largest_of(block, axes):
    for axis in axes:
        count = lax.axis_size(axis)
        reach = 1
        while reach < count:
            route = [(i, (i + reach) % count) for i in range(count)]
            block = jnp.maximum(block, lax.ppermute(block, axis, route))
            reach *= 2
    return block


def steps(specimen, probe_field, offsets, amplitudes):
    tile = specimen.shape[1]
    win = probe_field.shape[1]
    span = tile + 2 * HALO
    half = span // 2
    count = offsets.shape[2]
    forward, backward, pick, pick_back = [jnp.asarray(t) for t in dft_tables(win)]
    row, col = lax.axis_index("row"), lax.axis_index("col")
    place = jnp.stack([col > 0, col < lax.axis_size("col") - 1, row % 2]).astype(jnp.int32)

    head, tail = kernel_call(edges_kernel, [shape(2, tile, HALO)] * 2, [VM])(specimen)
    before = shifted(tail, "col", 1)
    after = shifted(head, "col", -1)

    probes = kernel_call(roll_kernel, [shape(count, 2, win, win)], [SM, VM])(offsets, probe_field)
    band, middle = shape(1, HALO, span), shape(1, tile, span)
    light_near, light_mid, light_cross = kernel_call(
        light_kernel,
        [band, middle, band],
        [SM, SM, VM],
        scratch=[pltpu.VMEM((1, win, span), F32)] * 2,
    )(place, offsets, probes)
    light_near, light_cross = row_exchange(light_near, light_cross)
    ordered = kernel_call(order_kernel, [shape(count, win, win)], [VM] * 3)(
        amplitudes, pick, pick_back
    )

    block = shape(2, tile // 2, span)
    top, bottom, near, cross = kernel_call(
        widen_kernel, [block] * 4, [SM] + [VM] * 3
    )(place, before, specimen, after)
    near, cross = row_exchange(near, cross)

    light_head, light_tail = kernel_call(
        fold_strips_kernel, [shape(1, tile, half)] * 2, [SM] + [VM] * 3
    )(place, light_mid, light_near, light_cross)
    light_left = shifted(light_tail, "col", 1)
    light_right = shifted(light_head, "col", -1)

    light, peak = None, None
    for iteration in range(ITERS):
        grad_near, grad_mid, grad_cross = kernel_call(
            gradient_kernel,
            [shape(2, HALO, span), shape(2, tile, span), shape(2, HALO, span)],
            [SM] * 2 + [VM] * 8,
            flops=count * 8 * 2 * win * 3 * win * win,
            scratch=[pltpu.VMEM((2, win, span), F32)] * 2,
            grant=24,
        )(
            place, offsets, near, cross, top, bottom, probes, ordered, forward, backward
        )
        grad_near, grad_cross = row_exchange(grad_near, grad_cross)
        if iteration == 0:
            light, found = kernel_call(
                light_sum_kernel, [shape(tile, span), shape(8, LANES)], [VM] * 4
            )(light_head, light_tail, light_left, light_right)
            peak = largest_of(found, ("row", "col"))
        if iteration + 1 < ITERS:
            grad_head, grad_tail = kernel_call(
                fold_strips_kernel, [shape(2, tile, half)] * 2, [SM] + [VM] * 3
            )(place, grad_mid, grad_near, grad_cross)
            from_left = shifted(grad_tail, "col", 1)
            from_right = shifted(grad_head, "col", -1)
            top, bottom, near, cross = kernel_call(
                update_kernel, [block] * 4, [SM] + [VM] * 8
            )(place, grad_head, grad_tail, from_left, from_right, light, peak, top, bottom)
            near, cross = row_exchange(near, cross)
        else:
            head, core, tail = kernel_call(
                fold_bands_kernel,
                [shape(2, tile, HALO), shape(2, tile, tile), shape(2, tile, HALO)],
                [SM] + [VM] * 3,
            )(place, grad_mid, grad_near, grad_cross)
            from_left = shifted(tail, "col", 1)
            from_right = shifted(head, "col", -1)
            return kernel_call(
                finish_kernel, [shape(2, tile, tile)], [VM] * 7
            )(core, from_left, from_right, light, peak, top, bottom)


def solution(mesh):
    return jax.shard_map(
        steps,
        mesh=mesh,
        in_specs=(
            P(None, "row", "col"),
            P(),
            P("row", "col", None, None),
            P("row", "col", None, None, None),
        ),
        out_specs=P(None, "row", "col"),
        check_vma=False,
    )
```

time: 158 us -> 145 us (0.918)
  starting transfers between devices: 57.7 us -> 46.5 us
  local copies, waits for them, and re-layouts: 5.57 us -> 2.2 us
  waiting for transfers between devices: 72.1 us -> 74.5 us
    ppermute x18 -> x8, starting transfers between devices: 53.5 us -> 20.3 us  [shifted(): return lax.ppermute(block, axis, route)]
    ppermute x0 -> x10, waiting for transfers between devices: none -> 26.5 us  [swapped(): return lax.ppermute(block, axis, route)]
    ppermute x18 -> x8, waiting for transfers between devices: 59.2 us -> 34.8 us  [shifted(): return lax.ppermute(block, axis, route)]
    ppermute x0 -> x10, starting transfers between devices: none -> 22.8 us  [swapped(): return lax.ppermute(block, axis, route)]
    unnamed x29 -> x19, local copies, waits for them, and re-layouts: 5.57 us -> 2.2 us
  transfers between devices with their start and end apart: 23 -> 23, of which waited for: 17 -> 15; matrix products, arithmetic and copies ran while one was open for 0% -> 0% of each run, Pallas kernels for 2% -> 3%
where the time goes in v1:
time: 145 us; the launch traced here: 144 us
  waiting for transfers between devices  74.5 us (51%)
  starting transfers between devices  46.5 us (32%)
  Pallas kernels  20.9 us (14%)
  local copies, waits for them, and re-layouts  2.2 us (2%)
    ppermute x8, waiting for transfers between devices, shifted(): return lax.ppermute(block, axis, route)  34.8 us
    ppermute x10, waiting for transfers between devices, swapped(): return lax.ppermute(block, axis, route)  26.5 us
    ppermute x10, starting transfers between devices, swapped(): return lax.ppermute(block, axis, route)  22.8 us
    ppermute x8, starting transfers between devices, shifted(): return lax.ppermute(block, axis, route)  20.3 us
    ppermute x5, waiting for transfers between devices, largest_of(): block = jnp.maximum(block, lax.ppermute(block, axis, route))  13.1 us
    pallas_call x2, Pallas kernels, steps(): kernel_call(gradient_kernel, [shape(2, HALO, span), shape(2, tile, span),...  11.6 us
    ppermute x5, starting transfers between devices, largest_of(): block = jnp.maximum(block, lax.ppermute(block, axis, route))  3.3 us
  transfers between devices with their start and end apart: 23, of which 15 were waited for; matrix products, arithmetic and copies ran while one was open for 0% of the time, Pallas kernels for 3%

profile of v1, /device:TPU:1, one launch (start us, length us, event | category | flops | bytes accessed | tf_op | source)
XLA Modules:
  0.0 144.4 jit_solution(14268022156094692217)
XLA Ops:
  0.0 1.0 copy-done
  1.1 4.1 %collective-permute-start = (f32[2,256,128]{2,1,0:T(8,128)S(1)}, f32[2,256,128]{2,1,0:T(8,128)S(1)}, u32[]{:S(2)}, u32[]{:S(2)}) collective-permute-start(f32[2,256,128]{2,1,0:T(8,128)S(1)} %get-tuple-element.33), channel_id=1, source_target_pairs={{0,1},{1,2},{2,3},{3,4},{4,5},{5,6},{6,7},{8,9},{9,10},{10,11},{11... | collective-permute-start | bytes 786440 | tf_op jit(solution)/shard_map/ppermute | solution.py:355
  5.2 1.3 collective-permute-start.1
  6.5 0.1 pad_add_fusion.place
  6.6 3.4 %collective-permute-done.before = f32[2,256,128]{2,1,0:T(8,128)S(1)} collective-permute-done((f32[2,256,128]{2,1,0:T(8,128)S(1)}, f32[2,256,128]{2,1,0:T(8,128)S(1)}, u32[]{:S(2)}, u32[]{:S(2)}) %collective-permute-start) | collective-permute-done | bytes 262176 | tf_op jit(solution)/shard_map/ppermute | solution.py:355
  10.0 4.0 %collective-permute-done.1.after = f32[2,256,128]{2,1,0:T(8,128)S(1)} collective-permute-done((f32[2,256,128]{2,1,0:T(8,128)S(1)}, f32[2,256,128]{2,1,0:T(8,128)S(1)}, u32[]{:S(2)}, u32[]{:S(2)}) %collective-permute-start.1) | collective-permute-done | bytes 262176 | tf_op jit(solution)/shard_map/ppermute | solution.py:355
  14.0 1.0 copy-done.1
  15.1 1.7 %shard_map.83 = (f32[2,128,512]{2,1,0:T(8,128)S(1)}, f32[2,128,512]{2,1,0:T(8,128)S(1)}, f32[2,128,512]{2,1,0:T(8,128)}, f32[2,128,512]{2,1,0:T(8,128)}) custom-call(s32[3]{0:T(128)S(1)} %pad_add_fusion.place, f32[2,256,128]{2,1,0:T(8,128)S(1)} %collective-permute-done.before, f32[2,256,256]{2,1,0:T(8,128)S(1)} %copy-done.1, ...), custom_call_target="tpu_custom_call" | custom-call | bytes 6291456 | tf_op jit(solution)/shard_map/pallas_call | solution.py:411
  16.8 3.3 %collective-permute-start.2 = (f32[2,128,512]{2,1,0:T(8,128)}, f32[2,128,512]{2,1,0:T(8,128)}, u32[]{:S(2)}, u32[]{:S(2)}) collective-permute-start(f32[2,128,512]{2,1,0:T(8,128)} %get-tuple-element.35), channel_id=1, source_target_pairs={{0,8},{8,0},{16,24},{24,16},{1,9},{9,1},{17,25},{25,17},{2,10},{10... | collective-permute-start | bytes 1572872 | tf_op jit(solution)/shard_map/ppermute | solution.py:363
  20.1 3.0 %collective-permute-start.3 = (f32[2,128,512]{2,1,0:T(8,128)}, f32[2,128,512]{2,1,0:T(8,128)}, u32[]{:S(2)}, u32[]{:S(2)}) collective-permute-start(f32[2,128,512]{2,1,0:T(8,128)} %get-tuple-element.36), channel_id=1, source_target_pairs={{8,16},{16,8},{9,17},{17,9},{10,18},{18,10},{11,19},{19,11},{12,20... | collective-permute-start | bytes 1572872 | tf_op jit(solution)/shard_map/ppermute | solution.py:363
  23.1 0.0 copy-done.8
  23.1 0.1 copy.12.offsets
  23.2 1.2 shard_map.84.probe
  24.4 1.0 shard_map.85.amplitude
  25.5 0.0 collective-permute-done.2.near_rows
  25.5 5.4 %collective-permute-done.3.cross_rows = f32[2,128,512]{2,1,0:T(8,128)} collective-permute-done((f32[2,128,512]{2,1,0:T(8,128)}, f32[2,128,512]{2,1,0:T(8,128)}, u32[]{:S(2)}, u32[]{:S(2)}) %collective-permute-start.3) | collective-permute-done | bytes 524320 | tf_op jit(solution)/shard_map/ppermute | solution.py:363
  30.9 0.0 copy-done.6
  30.9 6.1 %shard_map.86 = (f32[2,128,512]{2,1,0:T(8,128)S(1)}, f32[2,256,512]{2,1,0:T(8,128)S(1)}, f32[2,128,512]{2,1,0:T(8,128)S(1)}) custom-call(s32[3]{0:T(128)S(1)} %pad_add_fusion.place, s32[1,1,3,2]{3,2,1,0:T(4,128)S(1)} %copy.12.offsets, f32[2,128,512]{2,1,0:T(8,128)} %collective-permute-done.2.near_rows, f32[2,128,512]{2,1,0:T(8,128)} %collective-permute-done.3.cross_rows, ...), custom_call_target="tpu_custom_call" | custom-call | flops 2415919104 | bytes 6291456 | tf_op jit(solution)/shard_map/pallas_call | solution.py:424
  37.0 0.1 collective-permute-start.4
  37.1 3.0 %collective-permute-start.5 = (f32[2,128,512]{2,1,0:T(8,128)S(1)}, f32[2,128,512]{2,1,0:T(8,128)S(1)}, u32[]{:S(2)}, u32[]{:S(2)}) collective-permute-start(f32[2,128,512]{2,1,0:T(8,128)S(1)} %get-tuple-element.41), channel_id=1, source_target_pairs={{8,16},{16,8},{9,17},{17,9},{10,18},{18,10},{11,19},{19,11},{12,20... | collective-permute-start | bytes 1572872 | tf_op jit(solution)/shard_map/ppermute | solution.py:363
  40.1 1.0 shard_map.88
  41.1 0.1 collective-permute-start.8
  41.2 2.5 %collective-permute-start.9 = (f32[1,128,512]{2,1,0:T(8,128)S(1)}, f32[1,128,512]{2,1,0:T(8,128)S(1)}, u32[]{:S(2)}, u32[]{:S(2)}) collective-permute-start(f32[1,128,512]{2,1,0:T(8,128)S(1)} %get-tuple-element.46), channel_id=1, source_target_pairs={{8,16},{16,8},{9,17},{17,9},{10,18},{18,10},{11,19},{19,11},{12,20... | collective-permute-start | bytes 786440 | tf_op jit(solution)/shard_map/ppermute | solution.py:363
  43.7 0.0 collective-permute-done.4.near
  43.7 3.9 %collective-permute-done.5.cross = f32[2,128,512]{2,1,0:T(8,128)S(1)} collective-permute-done((f32[2,128,512]{2,1,0:T(8,128)S(1)}, f32[2,128,512]{2,1,0:T(8,128)S(1)}, u32[]{:S(2)}, u32[]{:S(2)}) %collective-permute-start.5) | collective-permute-done | bytes 524320 | tf_op jit(solution)/shard_map/ppermute | solution.py:363
  47.6 0.7 shard_map.87
  48.3 1.3 collective-permute-start.7
  49.6 4.8 %collective-permute-start.6 = (f32[2,256,256]{2,1,0:T(8,128)S(1)}, f32[2,256,256]{2,1,0:T(8,128)S(1)}, u32[]{:S(2)}, u32[]{:S(2)}) collective-permute-start(f32[2,256,256]{2,1,0:T(8,128)S(1)} %get-tuple-element.43.tail), channel_id=1, source_target_pairs={{0,1},{1,2},{2,3},{3,4},{4,5},{5,6},{6,7},{8,9},{9,10},{10,11},{11... | collective-permute-start | bytes 1572872 | tf_op jit(solution)/shard_map/ppermute | solution.py:355
  54.4 0.0 collective-permute-done.8.near
  54.4 0.0 collective-permute-done.9.cross
  54.4 0.6 shard_map.89
  55.1 1.3 collective-permute-start.11
  56.4 4.9 %collective-permute-start.10 = (f32[1,256,256]{2,1,0:T(8,128)S(1)}, f32[1,256,256]{2,1,0:T(8,128)S(1)}, u32[]{:S(2)}, u32[]{:S(2)}) collective-permute-start(f32[1,256,256]{2,1,0:T(8,128)S(1)} %get-tuple-element.48.tail), channel_id=1, source_target_pairs={{0,1},{1,2},{2,3},{3,4},{4,5},{5,6},{6,7},{8,9},{9,10},{10,11},{11... | collective-permute-start | bytes 786440 | tf_op jit(solution)/shard_map/ppermute | solution.py:355
  61.3 3.9 %collective-permute-done.11.from_right = f32[1,256,256]{2,1,0:T(8,128)S(1)} collective-permute-done((f32[1,256,256]{2,1,0:T(8,128)S(1)}, f32[1,256,256]{2,1,0:T(8,128)S(1)}, u32[]{:S(2)}, u32[]{:S(2)}) %collective-permute-start.11) | collective-permute-done | bytes 262176 | tf_op jit(solution)/shard_map/ppermute | solution.py:355
  65.2 17.7 %collective-permute-done.10.from_left = f32[1,256,256]{2,1,0:T(8,128)S(1)} collective-permute-done((f32[1,256,256]{2,1,0:T(8,128)S(1)}, f32[1,256,256]{2,1,0:T(8,128)S(1)}, u32[]{:S(2)}, u32[]{:S(2)}) %collective-permute-start.10) | collective-permute-done | bytes 262176 | tf_op jit(solution)/shard_map/ppermute | solution.py:355
  82.8 0.1 shard_map.90
  82.9 0.1 collective-permute-start.12
  83.0 1.2 collective-permute-done.12
  84.1 1.1 collective-permute-start.13
  85.3 1.3 collective-permute-done.13
  86.6 2.0 %collective-permute-start.14 = (f32[8,128]{1,0:T(8,128)S(1)}, f32[8,128]{1,0:T(8,128)S(1)}, u32[]{:S(2)}, u32[]{:S(2)}) collective-permute-start(f32[8,128]{1,0:T(8,128)S(1)} %max.16), channel_id=1, source_target_pairs={{0,1},{1,2},{2,3},{3,4},{4,5},{5,6},{6,7},{7,0},{8,9},{9,10},{10,1... | collective-permute-start | bytes 12296 | tf_op jit(solution)/shard_map/ppermute | solution.py:378
  88.6 3.1 %collective-permute-done.14 = f32[8,128]{1,0:T(8,128)S(1)} collective-permute-done((f32[8,128]{1,0:T(8,128)S(1)}, f32[8,128]{1,0:T(8,128)S(1)}, u32[]{:S(2)}, u32[]{:S(2)}) %collective-permute-start.14) | collective-permute-done | bytes 4128 | tf_op jit(solution)/shard_map/ppermute | solution.py:378
  91.7 0.1 collective-permute-start.15
  91.8 4.2 %collective-permute-done.15 = f32[8,128]{1,0:T(8,128)S(1)} collective-permute-done((f32[8,128]{1,0:T(8,128)S(1)}, f32[8,128]{1,0:T(8,128)S(1)}, u32[]{:S(2)}, u32[]{:S(2)}) %collective-permute-start.15) | collective-permute-done | bytes 4128 | tf_op jit(solution)/shard_map/ppermute | solution.py:378
  96.0 0.0 collective-permute-start.16
  96.0 3.4 %collective-permute-done.16 = f32[8,128]{1,0:T(8,128)S(1)} collective-permute-done((f32[8,128]{1,0:T(8,128)S(1)}, f32[8,128]{1,0:T(8,128)S(1)}, u32[]{:S(2)}, u32[]{:S(2)}) %collective-permute-start.16) | collective-permute-done | bytes 4128 | tf_op jit(solution)/shard_map/ppermute | solution.py:378
  99.4 0.0 collective-permute-done.7.from_right
  99.4 0.0 collective-permute-done.6.from_left
  99.4 1.0 shard_map.91
  100.4 6.7 %collective-permute-start.17 = (f32[2,128,512]{2,1,0:T(8,128)S(1)}, f32[2,128,512]{2,1,0:T(8,128)S(1)}, u32[]{:S(2)}, u32[]{:S(2)}) collective-permute-start(f32[2,128,512]{2,1,0:T(8,128)S(1)} %get-tuple-element.51), channel_id=1, source_target_pairs={{0,8},{8,0},{16,24},{24,16},{1,9},{9,1},{17,25},{25,17},{2,10},{10... | collective-permute-start | bytes 1572872 | tf_op jit(solution)/shard_map/ppermute | solution.py:363
  107.1 2.1 %collective-permute-start.18 = (f32[2,128,512]{2,1,0:T(8,128)S(1)}, f32[2,128,512]{2,1,0:T(8,128)S(1)}, u32[]{:S(2)}, u32[]{:S(2)}) collective-permute-start(f32[2,128,512]{2,1,0:T(8,128)S(1)} %get-tuple-element.52), channel_id=1, source_target_pairs={{8,16},{16,8},{9,17},{17,9},{10,18},{18,10},{11,19},{19,11},{12,20... | collective-permute-start | bytes 1572872 | tf_op jit(solution)/shard_map/ppermute | solution.py:363
  109.2 0.0 collective-permute-done.17.near_rows
  109.3 8.4 %collective-permute-done.18.cross_rows = f32[2,128,512]{2,1,0:T(8,128)S(1)} collective-permute-done((f32[2,128,512]{2,1,0:T(8,128)S(1)}, f32[2,128,512]{2,1,0:T(8,128)S(1)}, u32[]{:S(2)}, u32[]{:S(2)}) %collective-permute-start.18) | collective-permute-done | bytes 524320 | tf_op jit(solution)/shard_map/ppermute | solution.py:363
  117.6 5.5 %shard_map.92 = (f32[2,128,512]{2,1,0:T(8,128)S(1)}, f32[2,256,512]{2,1,0:T(8,128)S(1)}, f32[2,128,512]{2,1,0:T(8,128)S(1)}) custom-call(s32[3]{0:T(128)S(1)} %pad_add_fusion.place, s32[1,1,3,2]{3,2,1,0:T(4,128)S(1)} %copy.12.offsets, f32[2,128,512]{2,1,0:T(8,128)S(1)} %collective-permute-done.17.near_rows, ...), custom_call_target="tpu_custom_call" | custom-call | flops 2415919104 | bytes 6291456 | tf_op jit(solution)/shard_map/pallas_call | solution.py:424
  123.2 0.1 collective-permute-start.19
  123.2 1.9 %collective-permute-start.20 = (f32[2,128,512]{2,1,0:T(8,128)S(1)}, f32[2,128,512]{2,1,0:T(8,128)S(1)}, u32[]{:S(2)}, u32[]{:S(2)}) collective-permute-start(f32[2,128,512]{2,1,0:T(8,128)S(1)} %get-tuple-element.57), channel_id=1, source_target_pairs={{8,16},{16,8},{9,17},{17,9},{10,18},{18,10},{11,19},{19,11},{12,20... | collective-permute-start | bytes 1572872 | tf_op jit(solution)/shard_map/ppermute | solution.py:363
  125.2 0.0 collective-permute-done.19.near
  125.2 8.9 %collective-permute-done.20.cross = f32[2,128,512]{2,1,0:T(8,128)S(1)} collective-permute-done((f32[2,128,512]{2,1,0:T(8,128)S(1)}, f32[2,128,512]{2,1,0:T(8,128)S(1)}, u32[]{:S(2)}, u32[]{:S(2)}) %collective-permute-start.20) | collective-permute-done | bytes 524320 | tf_op jit(solution)/shard_map/ppermute | solution.py:363
  134.0 0.8 shard_map.93
  134.8 1.4 collective-permute-start.21
  136.3 1.3 collective-permute-start.22
  137.6 2.0 %collective-permute-done.21.from_left = f32[2,256,128]{2,1,0:T(8,128)S(1)} collective-permute-done((f32[2,256,128]{2,1,0:T(8,128)S(1)}, f32[2,256,128]{2,1,0:T(8,128)S(1)}, u32[]{:S(2)}, u32[]{:S(2)}) %collective-permute-start.21) | collective-permute-done | bytes 262176 | tf_op jit(solution)/shard_map/ppermute | solution.py:355
  139.6 3.8 %collective-permute-done.22.from_right = f32[2,256,128]{2,1,0:T(8,128)S(1)} collective-permute-done((f32[2,256,128]{2,1,0:T(8,128)S(1)}, f32[2,256,128]{2,1,0:T(8,128)S(1)}, u32[]{:S(2)}, u32[]{:S(2)}) %collective-permute-start.22) | collective-permute-done | bytes 262176 | tf_op jit(solution)/shard_map/ppermute | solution.py:355
  143.4 1.0 shard_map.94
  (20 shorter events, 0.1 us)
Async XLA Ops:
  0.0 1.0 copy-start
  1.0 22.0 %copy-start.8 = (s32[1,1,3,2]{2,3,1,0:T(2,128)S(1)}, s32[1,1,3,2]{2,3,1,0:T(2,128)}, u32[]{:S(2)}) copy-start(s32[1,1,3,2]{2,3,1,0:T(2,128)} %param.10) | copy-start | bytes 76
  1.0 22.1 %copy-start.3 = (f32[2,256,256]{2,1,0:T(8,128)S(1)}, f32[2,256,256]{2,1,0:T(8,128)}, u32[]{:S(2)}) copy-start(f32[2,256,256]{2,1,0:T(8,128)} %probe.1) | copy-start | bytes 1572868
  1.1 8.9 %collective-permute-start = (f32[2,256,128]{2,1,0:T(8,128)S(1)}, f32[2,256,128]{2,1,0:T(8,128)S(1)}, u32[]{:S(2)}, u32[]{:S(2)}) collective-permute-start(f32[2,256,128]{2,1,0:T(8,128)S(1)} %get-tuple-element.33), channel_id=1, source_target_pairs={{0,1},{1,2},{2,3},{3,4},{4,5},{5,6},{6,7},{8,9},{9,10},{10,11},{11... | collective-permute-start | bytes 786440 | tf_op jit(solution)/shard_map/ppermute | solution.py:355
  5.2 8.8 %collective-permute-start.1 = (f32[2,256,128]{2,1,0:T(8,128)S(1)}, f32[2,256,128]{2,1,0:T(8,128)S(1)}, u32[]{:S(2)}, u32[]{:S(2)}) collective-permute-start(f32[2,256,128]{2,1,0:T(8,128)S(1)} %get-tuple-element.34), channel_id=1, source_target_pairs={{1,0},{2,1},{3,2},{4,3},{5,4},{6,5},{7,6},{9,8},{10,9},{11,10},{12... | collective-permute-start | bytes 786440 | tf_op jit(solution)/shard_map/ppermute | solution.py:355
  14.0 1.0 copy-start.1
  15.0 9.4 %copy-start.2 = (f32[1,1,3,256,256]{4,3,2,1,0:T(8,128)S(1)}, f32[1,1,3,256,256]{4,3,2,1,0:T(8,128)}, u32[]{:S(2)}) copy-start(f32[1,1,3,256,256]{4,3,2,1,0:T(8,128)} %amplitude.1) | copy-start | bytes 2359300
  15.1 9.4 %copy-start.4 = (bf16[256,256]{1,0:T(8,128)(2,1)S(1)}, bf16[256,256]{1,0:T(8,128)(2,1)}, u32[]{:S(2)}) copy-start(bf16[256,256]{1,0:T(8,128)(2,1)} %constant.35.clone.pick_back) | copy-start | bytes 393220
  15.1 9.4 %copy-start.5 = (bf16[256,256]{1,0:T(8,128)(2,1)S(1)}, bf16[256,256]{1,0:T(8,128)(2,1)}, u32[]{:S(2)}) copy-start(bf16[256,256]{1,0:T(8,128)(2,1)} %constant.34.clone.pick) | copy-start | bytes 393220
  16.8 8.7 %collective-permute-start.2 = (f32[2,128,512]{2,1,0:T(8,128)}, f32[2,128,512]{2,1,0:T(8,128)}, u32[]{:S(2)}, u32[]{:S(2)}) collective-permute-start(f32[2,128,512]{2,1,0:T(8,128)} %get-tuple-element.35), channel_id=1, source_target_pairs={{0,8},{8,0},{16,24},{24,16},{1,9},{9,1},{17,25},{25,17},{2,10},{10... | collective-permute-start | bytes 1572872 | tf_op jit(solution)/shard_map/ppermute | solution.py:363
  20.1 10.8 %collective-permute-start.3 = (f32[2,128,512]{2,1,0:T(8,128)}, f32[2,128,512]{2,1,0:T(8,128)}, u32[]{:S(2)}, u32[]{:S(2)}) collective-permute-start(f32[2,128,512]{2,1,0:T(8,128)} %get-tuple-element.36), channel_id=1, source_target_pairs={{8,16},{16,8},{9,17},{17,9},{10,18},{18,10},{11,19},{19,11},{12,20... | collective-permute-start | bytes 1572872 | tf_op jit(solution)/shard_map/ppermute | solution.py:363
  23.2 7.7 %copy-start.6 = (bf16[2,2,256,256]{3,2,1,0:T(8,128)(2,1)S(1)}, bf16[2,2,256,256]{3,2,1,0:T(8,128)(2,1)}, u32[]{:S(2)}) copy-start(bf16[2,2,256,256]{3,2,1,0:T(8,128)(2,1)} %constant.33.clone.backward) | copy-start | bytes 1572868
  23.2 7.7 %copy-start.7 = (bf16[2,2,256,256]{3,2,1,0:T(8,128)(2,1)S(1)}, bf16[2,2,256,256]{3,2,1,0:T(8,128)(2,1)}, u32[]{:S(2)}) copy-start(bf16[2,2,256,256]{3,2,1,0:T(8,128)(2,1)} %constant.32.clone.forward) | copy-start | bytes 1572868
  37.0 6.7 %collective-permute-start.4 = (f32[2,128,512]{2,1,0:T(8,128)S(1)}, f32[2,128,512]{2,1,0:T(8,128)S(1)}, u32[]{:S(2)}, u32[]{:S(2)}) collective-permute-start(f32[2,128,512]{2,1,0:T(8,128)S(1)} %get-tuple-element.40), channel_id=1, source_target_pairs={{0,8},{8,0},{16,24},{24,16},{1,9},{9,1},{17,25},{25,17},{2,10},{10... | collective-permute-start | bytes 1572872 | tf_op jit(solution)/shard_map/ppermute | solution.py:363
  37.1 10.5 %collective-permute-start.5 = (f32[2,128,512]{2,1,0:T(8,128)S(1)}, f32[2,128,512]{2,1,0:T(8,128)S(1)}, u32[]{:S(2)}, u32[]{:S(2)}) collective-permute-start(f32[2,128,512]{2,1,0:T(8,128)S(1)} %get-tuple-element.41), channel_id=1, source_target_pairs={{8,16},{16,8},{9,17},{17,9},{10,18},{18,10},{11,19},{19,11},{12,20... | collective-permute-start | bytes 1572872 | tf_op jit(solution)/shard_map/ppermute | solution.py:363
  41.1 13.3 %collective-permute-start.8 = (f32[1,128,512]{2,1,0:T(8,128)S(1)}, f32[1,128,512]{2,1,0:T(8,128)S(1)}, u32[]{:S(2)}, u32[]{:S(2)}) collective-permute-start(f32[1,128,512]{2,1,0:T(8,128)S(1)} %get-tuple-element.45), channel_id=1, source_target_pairs={{0,8},{8,0},{16,24},{24,16},{1,9},{9,1},{17,25},{25,17},{2,10},{10... | collective-permute-start | bytes 786440 | tf_op jit(solution)/shard_map/ppermute | solution.py:363
  41.2 13.3 %collective-permute-start.9 = (f32[1,128,512]{2,1,0:T(8,128)S(1)}, f32[1,128,512]{2,1,0:T(8,128)S(1)}, u32[]{:S(2)}, u32[]{:S(2)}) collective-permute-start(f32[1,128,512]{2,1,0:T(8,128)S(1)} %get-tuple-element.46), channel_id=1, source_target_pairs={{8,16},{16,8},{9,17},{17,9},{10,18},{18,10},{11,19},{19,11},{12,20... | collective-permute-start | bytes 786440 | tf_op jit(solution)/shard_map/ppermute | solution.py:363
  48.3 51.0 %collective-permute-start.7 = (f32[2,256,256]{2,1,0:T(8,128)S(1)}, f32[2,256,256]{2,1,0:T(8,128)S(1)}, u32[]{:S(2)}, u32[]{:S(2)}) collective-permute-start(f32[2,256,256]{2,1,0:T(8,128)S(1)} %get-tuple-element.42.head), channel_id=1, source_target_pairs={{1,0},{2,1},{3,2},{4,3},{5,4},{6,5},{7,6},{9,8},{10,9},{11,10},{12... | collective-permute-start | bytes 1572872 | tf_op jit(solution)/shard_map/ppermute | solution.py:355
  49.6 49.7 %collective-permute-start.6 = (f32[2,256,256]{2,1,0:T(8,128)S(1)}, f32[2,256,256]{2,1,0:T(8,128)S(1)}, u32[]{:S(2)}, u32[]{:S(2)}) collective-permute-start(f32[2,256,256]{2,1,0:T(8,128)S(1)} %get-tuple-element.43.tail), channel_id=1, source_target_pairs={{0,1},{1,2},{2,3},{3,4},{4,5},{5,6},{6,7},{8,9},{9,10},{10,11},{11... | collective-permute-start | bytes 1572872 | tf_op jit(solution)/shard_map/ppermute | solution.py:355
  55.1 10.1 %collective-permute-start.11 = (f32[1,256,256]{2,1,0:T(8,128)S(1)}, f32[1,256,256]{2,1,0:T(8,128)S(1)}, u32[]{:S(2)}, u32[]{:S(2)}) collective-permute-start(f32[1,256,256]{2,1,0:T(8,128)S(1)} %get-tuple-element.47.head), channel_id=1, source_target_pairs={{1,0},{2,1},{3,2},{4,3},{5,4},{6,5},{7,6},{9,8},{10,9},{11,10},{12... | collective-permute-start | bytes 786440 | tf_op jit(solution)/shard_map/ppermute | solution.py:355
  56.4 26.5 %collective-permute-start.10 = (f32[1,256,256]{2,1,0:T(8,128)S(1)}, f32[1,256,256]{2,1,0:T(8,128)S(1)}, u32[]{:S(2)}, u32[]{:S(2)}) collective-permute-start(f32[1,256,256]{2,1,0:T(8,128)S(1)} %get-tuple-element.48.tail), channel_id=1, source_target_pairs={{0,1},{1,2},{2,3},{3,4},{4,5},{5,6},{6,7},{8,9},{9,10},{10,11},{11... | collective-permute-start | bytes 786440 | tf_op jit(solution)/shard_map/ppermute | solution.py:355
  82.9 1.2 collective-permute-start.12
  84.1 2.5 %collective-permute-start.13 = (f32[8,128]{1,0:T(8,128)S(1)}, f32[8,128]{1,0:T(8,128)S(1)}, u32[]{:S(2)}, u32[]{:S(2)}) collective-permute-start(f32[8,128]{1,0:T(8,128)S(1)} %max.15), channel_id=1, source_target_pairs={{0,16},{8,24},{16,0},{24,8},{1,17},{9,25},{17,1},{25,9},{2,18},{10... | collective-permute-start | bytes 12296 | tf_op jit(solution)/shard_map/ppermute | solution.py:378
  86.6 5.2 %collective-permute-start.14 = (f32[8,128]{1,0:T(8,128)S(1)}, f32[8,128]{1,0:T(8,128)S(1)}, u32[]{:S(2)}, u32[]{:S(2)}) collective-permute-start(f32[8,128]{1,0:T(8,128)S(1)} %max.16), channel_id=1, source_target_pairs={{0,1},{1,2},{2,3},{3,4},{4,5},{5,6},{6,7},{7,0},{8,9},{9,10},{10,1... | collective-permute-start | bytes 12296 | tf_op jit(solution)/shard_map/ppermute | solution.py:378
  91.7 4.3 %collective-permute-start.15 = (f32[8,128]{1,0:T(8,128)S(1)}, f32[8,128]{1,0:T(8,128)S(1)}, u32[]{:S(2)}, u32[]{:S(2)}) collective-permute-start(f32[8,128]{1,0:T(8,128)S(1)} %max.17), channel_id=1, source_target_pairs={{0,2},{1,3},{2,4},{3,5},{4,6},{5,7},{6,0},{7,1},{8,10},{9,11},{10,... | collective-permute-start | bytes 12296 | tf_op jit(solution)/shard_map/ppermute | solution.py:378
  96.0 3.4 %collective-permute-start.16 = (f32[8,128]{1,0:T(8,128)S(1)}, f32[8,128]{1,0:T(8,128)S(1)}, u32[]{:S(2)}, u32[]{:S(2)}) collective-permute-start(f32[8,128]{1,0:T(8,128)S(1)} %max.18), channel_id=1, source_target_pairs={{0,4},{1,5},{2,6},{3,7},{4,0},{5,1},{6,2},{7,3},{8,12},{9,13},{10,... | collective-permute-start | bytes 12296 | tf_op jit(solution)/shard_map/ppermute | solution.py:378
  100.4 8.8 %collective-permute-start.17 = (f32[2,128,512]{2,1,0:T(8,128)S(1)}, f32[2,128,512]{2,1,0:T(8,128)S(1)}, u32[]{:S(2)}, u32[]{:S(2)}) collective-permute-start(f32[2,128,512]{2,1,0:T(8,128)S(1)} %get-tuple-element.51), channel_id=1, source_target_pairs={{0,8},{8,0},{16,24},{24,16},{1,9},{9,1},{17,25},{25,17},{2,10},{10... | collective-permute-start | bytes 1572872 | tf_op jit(solution)/shard_map/ppermute | solution.py:363
  107.1 10.5 %collective-permute-start.18 = (f32[2,128,512]{2,1,0:T(8,128)S(1)}, f32[2,128,512]{2,1,0:T(8,128)S(1)}, u32[]{:S(2)}, u32[]{:S(2)}) collective-permute-start(f32[2,128,512]{2,1,0:T(8,128)S(1)} %get-tuple-element.52), channel_id=1, source_target_pairs={{8,16},{16,8},{9,17},{17,9},{10,18},{18,10},{11,19},{19,11},{12,20... | collective-permute-start | bytes 1572872 | tf_op jit(solution)/shard_map/ppermute | solution.py:363
  123.2 2.0 %collective-permute-start.19 = (f32[2,128,512]{2,1,0:T(8,128)S(1)}, f32[2,128,512]{2,1,0:T(8,128)S(1)}, u32[]{:S(2)}, u32[]{:S(2)}) collective-permute-start(f32[2,128,512]{2,1,0:T(8,128)S(1)} %get-tuple-element.56), channel_id=1, source_target_pairs={{0,8},{8,0},{16,24},{24,16},{1,9},{9,1},{17,25},{25,17},{2,10},{10... | collective-permute-start | bytes 1572872 | tf_op jit(solution)/shard_map/ppermute | solution.py:363
  123.2 10.8 %collective-permute-start.20 = (f32[2,128,512]{2,1,0:T(8,128)S(1)}, f32[2,128,512]{2,1,0:T(8,128)S(1)}, u32[]{:S(2)}, u32[]{:S(2)}) collective-permute-start(f32[2,128,512]{2,1,0:T(8,128)S(1)} %get-tuple-element.57), channel_id=1, source_target_pairs={{8,16},{16,8},{9,17},{17,9},{10,18},{18,10},{11,19},{19,11},{12,20... | collective-permute-start | bytes 1572872 | tf_op jit(solution)/shard_map/ppermute | solution.py:363
  134.8 4.7 %collective-permute-start.21 = (f32[2,256,128]{2,1,0:T(8,128)S(1)}, f32[2,256,128]{2,1,0:T(8,128)S(1)}, u32[]{:S(2)}, u32[]{:S(2)}) collective-permute-start(f32[2,256,128]{2,1,0:T(8,128)S(1)} %get-tuple-element.59), channel_id=1, source_target_pairs={{0,1},{1,2},{2,3},{3,4},{4,5},{5,6},{6,7},{8,9},{9,10},{10,11},{11... | collective-permute-start | bytes 786440 | tf_op jit(solution)/shard_map/ppermute | solution.py:355
  136.3 7.1 %collective-permute-start.22 = (f32[2,256,128]{2,1,0:T(8,128)S(1)}, f32[2,256,128]{2,1,0:T(8,128)S(1)}, u32[]{:S(2)}, u32[]{:S(2)}) collective-permute-start(f32[2,256,128]{2,1,0:T(8,128)S(1)} %get-tuple-element.60), channel_id=1, source_target_pairs={{1,0},{2,1},{3,2},{4,3},{5,4},{6,5},{7,6},{9,8},{10,9},{11,10},{12... | collective-permute-start | bytes 786440 | tf_op jit(solution)/shard_map/ppermute | solution.py:355

commit v2 on v1

v2 whole, which is shorter than its diff:
```python
import functools
import math

import jax
import jax.numpy as jnp
import numpy as np
from jax import lax
from jax.experimental import pallas as pl
from jax.experimental.pallas import tpu as pltpu
from jax.sharding import PartitionSpec as P


HALO = 128
ITERS = 2
LANES = 128
ODD, HAS_LEFT, HAS_RIGHT, FLAGS = 0, 1, 2, 3

smooth_term = 0.25
ridge_share = 0.1

VM = pl.BlockSpec(memory_space=pltpu.VMEM)
SM = pl.BlockSpec(memory_space=pltpu.SMEM)
F32 = jnp.float32
BF16 = jnp.bfloat16


def shape(*dims):
    return jax.ShapeDtypeStruct(dims, F32)


def to_bf16(x):
    return np.asarray(x, np.float32).astype(BF16)


def split_table(table):
    high = to_bf16(table)
    low = to_bf16(table - high.astype(np.float64))
    return high, low


@functools.lru_cache
def dft_tables(length):
    half = length // 2
    n = np.arange(half)
    forward, backward = [], []
    for odd in (0, 1):
        turn = ((2 * n[:, None] + odd) * n[None, :]) % length
        angle = turn * (2.0 * math.pi / length)
        cos, sin = np.cos(angle) / math.sqrt(length), -np.sin(angle) / math.sqrt(length)
        form = np.block([[cos, -sin], [sin, cos]])
        forward.append(np.stack(split_table(form)))
        backward.append(np.stack(split_table(form.T)))
    place = np.zeros((length, length), np.float32)
    place[2 * n, n] = 1.0
    place[2 * n + 1, half + n] = 1.0
    pick = to_bf16(place)
    return np.stack(forward), np.stack(backward), pick, np.ascontiguousarray(pick.T)


def halves(x):
    high = x.astype(BF16)
    low = (x - high.astype(F32)).astype(BF16)
    return high, low


def left_product(table, x):
    high, low = halves(x)
    return jnp.dot(
        jnp.concatenate([table[0], table[1], table[0]], axis=1),
        jnp.concatenate([high, high, low], axis=0),
        preferred_element_type=F32,
    )


def right_product(x, table):
    high, low = halves(x)
    return jnp.dot(
        jnp.concatenate([high, low, high], axis=1),
        jnp.concatenate([table[0], table[0], table[1]], axis=0),
        preferred_element_type=F32,
    )


def window_masks(info, position, win):
    at = FLAGS + 2 * position
    low = lax.broadcasted_iota(jnp.int32, (win, win), 0) >= info[at : at + 1, :]
    near = lax.broadcasted_iota(jnp.int32, (win, win), 1) >= info[at + 1 : at + 2, :]
    return low, near


def flag(info, index):
    return info[index : index + 1, :] > 0


def roll_kernel(corners, probe, rolled):
    win = probe.shape[1]
    for position in range(rolled.shape[0]):
        row = lax.rem(corners[2 * position], win)
        column = lax.rem(corners[2 * position + 1], win)
        for plane in (0, 1):
            rolled[position, plane] = pltpu.roll(
                pltpu.roll(probe[plane], column, 1), row, 0
            )


def spread(piece, low, near, quadrants, first):
    above = jnp.where(low, piece, 0.0)
    below = jnp.where(low, 0.0, piece)
    parts = (
        jnp.where(near, above, 0.0), jnp.where(near, 0.0, above),
        jnp.where(near, below, 0.0), jnp.where(near, 0.0, below),
    )
    for index, part in enumerate(parts):
        quadrants[index] = part if first else quadrants[index] + part


def gradient_kernel(
    info, near_inner, cross_inner, near_outer, cross_outer, inner, outer, probe, amplitude,
    forward, backward,
    grad_near_inner, grad_cross_inner, grad_near_outer, grad_cross_outer,
    mid_inner, mid_outer, total,
):
    count, win, _ = amplitude.shape
    half = win // 2
    edge = near_inner.shape[1]
    odd_row = flag(info, ODD)

    def blocks(plane):
        sides = []
        for own, beside, across in (
            (inner, near_inner, cross_inner), (outer, near_outer, cross_outer)
        ):
            up = jnp.where(odd_row, beside[plane], across[plane])
            down = jnp.where(odd_row, across[plane], beside[plane])
            sides.append(
                (
                    jnp.concatenate([up, own[plane, :edge]], axis=0),
                    jnp.concatenate([own[plane, edge:], down], axis=0),
                )
            )
        out = []
        for mid, far in zip(*sides):
            out.append(jnp.concatenate([far[:, :HALO], mid[:, :half]], axis=1))
            out.append(jnp.concatenate([mid[:, half:], far[:, HALO:]], axis=1))
        return out

    def patch(plane, low, near):
        first, second, third, fourth = blocks(plane)
        return jnp.where(
            near, jnp.where(low, first, third), jnp.where(low, second, fourth)
        )

    for position in range(count):
        low, near = window_masks(info, position, win)
        patch_real = patch(0, low, near)
        patch_imag = patch(1, low, near)
        probe_real, probe_imag = probe[position, 0], probe[position, 1]
        real = probe_real * patch_real - probe_imag * patch_imag
        imag = probe_real * patch_imag + probe_imag * patch_real
        summed = jnp.concatenate([real[:half] + real[half:], imag[:half] + imag[half:]], axis=0)
        differ = jnp.concatenate([real[:half] - real[half:], imag[:half] - imag[half:]], axis=0)
        even = left_product(forward[0], summed)
        odd = left_product(forward[1], differ)
        real = jnp.concatenate([even[:half], odd[:half]], axis=0)
        imag = jnp.concatenate([even[half:], odd[half:]], axis=0)
        summed = jnp.concatenate(
            [real[:, :half] + real[:, half:], imag[:, :half] + imag[:, half:]], axis=1
        )
        differ = jnp.concatenate(
            [real[:, :half] - real[:, half:], imag[:, :half] - imag[:, half:]], axis=1
        )
        even = right_product(summed, backward[0])
        odd = right_product(differ, backward[1])
        even_real, even_imag = even[:, :half], even[:, half:]
        odd_real, odd_imag = odd[:, :half], odd[:, half:]
        amp = amplitude[position]
        even_factor = 1.0 - amp[:, :half] * lax.rsqrt(
            even_real * even_real + even_imag * even_imag + smooth_term
        )
        odd_factor = 1.0 - amp[:, half:] * lax.rsqrt(
            odd_real * odd_real + odd_imag * odd_imag + smooth_term
        )
        even = jnp.concatenate([even_factor * even_real, even_factor * even_imag], axis=1)
        odd = jnp.concatenate([odd_factor * odd_real, odd_factor * odd_imag], axis=1)
        even_back = right_product(even, forward[0])
        odd_back = right_product(odd, forward[1])
        summed, differ = even_back + odd_back, even_back - odd_back
        real = jnp.concatenate([summed[:, :half], differ[:, :half]], axis=1)
        imag = jnp.concatenate([summed[:, half:], differ[:, half:]], axis=1)
        even = left_product(backward[0], jnp.concatenate([real[:half], imag[:half]], axis=0))
        odd = left_product(backward[1], jnp.concatenate([real[half:], imag[half:]], axis=0))
        summed, differ = even + odd, even - odd
        real = jnp.concatenate([summed[:half], differ[:half]], axis=0)
        imag = jnp.concatenate([summed[half:], differ[half:]], axis=0)
        for plane, piece in (
            (0, probe_real * real + probe_imag * imag),
            (1, probe_real * imag - probe_imag * real),
        ):
            spread(piece, low, near, total.at[plane], position == 0)
    for plane in (0, 1):
        first, second, third, fourth = [total.at[plane, k] for k in range(4)]
        for take, near_out, cross_out, mid in (
            (
                lambda a, b, rows: jnp.concatenate([a[rows, half:], b[rows, :half]], axis=1),
                grad_near_inner, grad_cross_inner, mid_inner,
            ),
            (
                lambda a, b, rows: jnp.concatenate([a[rows, :HALO], b[rows, win - HALO :]], axis=1),
                grad_near_outer, grad_cross_outer, mid_outer,
            ),
        ):
            up = take(first, second, slice(0, edge))
            down = take(third, fourth, slice(win - edge, win))
            near_out[plane] = jnp.where(odd_row, up, down)
            cross_out[plane] = jnp.where(odd_row, down, up)
            mid[plane, :edge] = take(first, second, slice(edge, win))
            mid[plane, edge:] = take(third, fourth, slice(0, win - edge))


def light_kernel(own_spots, near_spots, cross_spots, odd, probe, light, largest, quadrants):
    win = probe.shape[1]
    half = win // 2
    count = own_spots.shape[0] // 6
    real, imag = probe[0], probe[1]
    intensity = real * real + imag * imag
    quadrants[...] = jnp.zeros_like(quadrants)
    is_odd = odd[0] > 0
    rows = lax.broadcasted_iota(jnp.int32, (half, win), 0)
    columns = lax.broadcasted_iota(jnp.int32, (half, win), 1)

    def spot(row_side, index):
        if row_side == 0:
            return own_spots[index]
        near, cross = near_spots[index], cross_spots[index]
        if row_side < 0:
            return jnp.where(is_odd, near, cross)
        return jnp.where(is_odd, cross, near)

    for row_side in (-1, 0, 1):
        for column_side in (-1, 0, 1):
            base = (column_side + 1) * 2 * count

            @pl.when(spot(row_side, base) > 0)
            def _():
                def one(position, carry):
                    row = spot(row_side, base + 2 * position) - 1
                    column = spot(row_side, base + 2 * position + 1) - 1
                    block = pltpu.roll(intensity, lax.rem(row, win), 0)
                    turn = lax.rem(column, win)
                    for lower in (0, 1):
                        if (row_side < 0 and lower) or (row_side > 0 and not lower):
                            continue
                        part = block[:half] if lower else block[half:]
                        part = pltpu.roll(part, turn, 1)
                        index = rows if lower else rows + half
                        if row_side < 0 or (row_side == 0 and lower):
                            keep = index < row
                        else:
                            keep = index >= row
                        part = jnp.where(keep, part, 0.0)
                        if column_side <= 0:
                            near = columns < column if column_side else columns >= column
                            quadrants[2 * lower] = quadrants[2 * lower] + jnp.where(near, part, 0.0)
                        if column_side >= 0:
                            far = columns >= column if column_side else columns < column
                            quadrants[2 * lower + 1] = quadrants[2 * lower + 1] + jnp.where(far, part, 0.0)
                    return carry

                lax.fori_loop(0, count, one, 0)

    found = None
    for lower in (0, 1):
        out = slice(lower * half, (lower + 1) * half)
        near, far = quadrants[2 * lower], quadrants[2 * lower + 1]
        light[out, :HALO] = near[:, :HALO]
        light[out, HALO : 2 * HALO] = near[:, HALO:]
        light[out, 2 * HALO :] = far
        best = jnp.maximum(near[:, HALO:], far[:, : win - HALO])
        for row in range(0, half, 8):
            block = best[row : row + 8]
            found = block if found is None else jnp.maximum(found, block)
    largest[...] = found


def thirds(x):
    high = x.astype(BF16)
    rest = x - high.astype(F32)
    mid = rest.astype(BF16)
    return high, mid, (rest - mid.astype(F32)).astype(BF16)


def order_kernel(amplitude, pick, pick_back, ordered):
    rows = jnp.concatenate([pick_back[...]] * 3, axis=1)
    columns = jnp.concatenate([pick[...]] * 3, axis=0)
    for position in range(ordered.shape[0]):
        block = jnp.dot(
            rows,
            jnp.concatenate(thirds(amplitude[0, 0, position]), axis=0),
            preferred_element_type=F32,
        )
        ordered[position] = jnp.dot(
            jnp.concatenate(thirds(block), axis=1), columns, preferred_element_type=F32
        )


def edges_kernel(specimen, head, tail):
    head[...] = specimen[:, :, :HALO]
    tail[...] = specimen[:, :, specimen.shape[2] - HALO :]


def row_sides(odd_row, plane, top, bottom, near, cross):
    near[plane] = jnp.where(odd_row, top, bottom)
    cross[plane] = jnp.where(odd_row, bottom, top)


def center_kernel(info, specimen, near, cross):
    edge = near.shape[1]
    odd_row = flag(info, ODD)
    for plane in (0, 1):
        row_sides(odd_row, plane, specimen[plane, :edge], specimen[plane, edge:], near, cross)


def corner_kernel(info, before, after, outer, near, cross):
    edge = near.shape[1]
    odd_row = flag(info, ODD)
    for plane in (0, 1):
        block = jnp.concatenate([before[plane], after[plane]], axis=1)
        outer[plane] = block
        row_sides(odd_row, plane, block[:edge], block[edge:], near, cross)


def folded(odd_row, plane, mid, near, cross):
    edge = near.shape[1]
    upper = mid[plane, :edge] + jnp.where(odd_row, near[plane], cross[plane])
    lower = mid[plane, edge:] + jnp.where(odd_row, cross[plane], near[plane])
    return jnp.concatenate([upper, lower], axis=0)


def fold_kernel(info, mid, near, cross, head, tail):
    odd_row = flag(info, ODD)
    half = head.shape[2]
    for plane in (0, 1):
        block = folded(odd_row, plane, mid, near, cross)
        head[plane] = block[:, :half]
        tail[plane] = block[:, half:]


def inner_light(light):
    return jnp.concatenate([light[:, HALO : 2 * HALO], light[:, 2 * HALO : 3 * HALO]], axis=1)


def outer_light(light):
    return jnp.concatenate([light[:, :HALO], light[:, 3 * HALO :]], axis=1)


def update_inner_kernel(
    info, head, tail, from_left, from_right, light, peak, old, new, near, cross
):
    edge = near.shape[1]
    odd_row = flag(info, ODD)
    scale = 1.0 / (inner_light(light) + ridge_share * jnp.max(peak[...]))
    for plane in (0, 1):
        gradient = jnp.concatenate(
            [head[plane] + from_left[plane], tail[plane] + from_right[plane]], axis=1
        )
        block = old[plane] - gradient * scale
        new[plane] = block
        row_sides(odd_row, plane, block[:edge], block[edge:], near, cross)


def update_outer_kernel(
    info, head, tail, from_left, from_right, light, peak, old, new, near, cross
):
    edge = near.shape[1]
    odd_row = flag(info, ODD)
    lane = lax.broadcasted_iota(jnp.int32, (1, 2 * HALO), 1)
    inside = jnp.where(lane < HALO, info[HAS_LEFT : HAS_LEFT + 1], info[HAS_RIGHT : HAS_RIGHT + 1]) > 0
    scale = 1.0 / (outer_light(light) + ridge_share * jnp.max(peak[...]))
    for plane in (0, 1):
        gradient = jnp.concatenate(
            [head[plane] + from_left[plane], tail[plane] + from_right[plane]], axis=1
        )
        block = jnp.where(inside, old[plane] - gradient * scale, 0.0)
        new[plane] = block
        row_sides(odd_row, plane, block[:edge], block[edge:], near, cross)


def finish_kernel(info, mid, near, cross, from_left, from_right, light, peak, old, out):
    odd_row = flag(info, ODD)
    scale = 1.0 / (inner_light(light) + ridge_share * jnp.max(peak[...]))
    for plane in (0, 1):
        gradient = folded(odd_row, plane, mid, near, cross) + jnp.concatenate(
            [from_left[plane], from_right[plane]], axis=1
        )
        out[plane] = old[plane] - gradient * scale


def kernel_call(body, outs, specs, flops=0, scratch=(), grant=8):
    moved = 4 * sum(math.prod(out.shape) for out in outs)
    single = len(outs) == 1
    return pl.pallas_call(
        body,
        out_shape=outs[0] if single else outs,
        in_specs=specs,
        out_specs=VM if single else (VM,) * len(outs),
        scratch_shapes=list(scratch),
        compiler_params=pltpu.CompilerParams(vmem_limit_bytes=grant * 1024 * 1024),
        cost_estimate=pl.CostEstimate(
            flops=flops, bytes_accessed=3 * moved, transcendentals=0
        ),
    )


def shifted(block, axis, distance):
    count = lax.axis_size(axis)
    route = [(i - distance, i) for i in range(count) if 0 <= i - distance < count]
    return lax.ppermute(block, axis, route)


def swapped(block, axis, first):
    count = lax.axis_size(axis)
    route = []
    for i in range(first, count - 1, 2):
        route += [(i, i + 1), (i + 1, i)]
    return lax.ppermute(block, axis, route)


def row_exchange(near, cross):
    cross = swapped(cross, "row", 1)
    near = swapped(near, "row", 0)
    return near, cross


def largest_of(block, axes):
    for axis in axes:
        count = lax.axis_size(axis)
        reach = 1
        while reach < count:
            route = [(i, (i + reach) % count) for i in range(count)]
            block = jnp.maximum(block, lax.ppermute(block, axis, route))
            reach *= 2
    return block


def steps(specimen, probe_field, offsets, amplitudes):
    tile = specimen.shape[1]
    win = probe_field.shape[1]
    span = tile + 2 * HALO
    count = offsets.shape[2]
    forward, backward, pick, pick_back = [jnp.asarray(t) for t in dft_tables(win)]
    row, col = lax.axis_index("row"), lax.axis_index("col")
    odd = row % 2
    corners = offsets.reshape(-1) + HALO
    flags = jnp.stack([odd, col > 0, col < lax.axis_size("col") - 1]).astype(jnp.int32)
    info = jnp.broadcast_to(
        jnp.concatenate([flags, corners])[:, None], (FLAGS + 2 * count, win)
    )

    spots = corners + 1
    spots_left = shifted(spots, "col", 1)
    spots_right = shifted(spots, "col", -1)

    head, tail = kernel_call(edges_kernel, [shape(2, tile, HALO)] * 2, [VM])(specimen)
    before = shifted(tail, "col", 1)
    after = shifted(head, "col", -1)

    spots = jnp.concatenate([spots_left, spots, spots_right])
    spots_near, spots_cross = row_exchange(spots, spots)

    rows_in = shape(2, tile // 2, tile)
    rows_out = shape(2, tile // 2, 2 * HALO)
    near_in, cross_in = kernel_call(center_kernel, [rows_in] * 2, [VM] * 2)(info, specimen)
    near_in, cross_in = row_exchange(near_in, cross_in)

    probes = kernel_call(roll_kernel, [shape(count, 2, win, win)], [SM, VM])(corners, probe_field)
    ordered = kernel_call(order_kernel, [shape(count, win, win)], [VM] * 3)(
        amplitudes, pick, pick_back
    )
    light, found = kernel_call(
        light_kernel,
        [shape(tile, span), shape(8, LANES)],
        [SM] * 4 + [VM],
        scratch=[pltpu.VMEM((4, win // 2, win), F32)],
    )(spots, spots_near, spots_cross, odd.astype(jnp.int32).reshape(1), probe_field)

    outer, near_out, cross_out = kernel_call(
        corner_kernel, [shape(2, tile, 2 * HALO), rows_out, rows_out], [VM] * 3
    )(info, before, after)
    near_out, cross_out = row_exchange(near_out, cross_out)
    inner = specimen

    peak = largest_of(found, ("col", "row"))
    for step in range(ITERS):
        (
            grad_near_in, grad_cross_in, grad_near_out, grad_cross_out, mid_in, mid_out
        ) = kernel_call(
            gradient_kernel,
            [rows_in] * 2 + [rows_out] * 2 + [shape(2, tile, tile), shape(2, tile, 2 * HALO)],
            [VM] * 11,
            flops=count * 8 * 2 * win * 3 * win * win,
            scratch=[pltpu.VMEM((2, 4, win, win), F32)],
            grant=24,
        )(
            info, near_in, cross_in, near_out, cross_out, inner, outer, probes, ordered,
            forward, backward,
        )
        fold_near, fold_cross = row_exchange(grad_near_out, grad_cross_out)
        head, tail = kernel_call(
            fold_kernel, [shape(2, tile, HALO)] * 2, [VM] * 4
        )(info, mid_out, fold_near, fold_cross)
        to_inner_left = shifted(tail, "col", 1)
        to_inner_right = shifted(head, "col", -1)
        fold_near, fold_cross = row_exchange(grad_near_in, grad_cross_in)
        if step + 1 == ITERS:
            return kernel_call(finish_kernel, [shape(2, tile, tile)], [VM] * 9)(
                info, mid_in, fold_near, fold_cross, to_inner_left, to_inner_right,
                light, peak, inner,
            )
        in_head, in_tail = kernel_call(
            fold_kernel, [shape(2, tile, tile // 2)] * 2, [VM] * 4
        )(info, mid_in, fold_near, fold_cross)
        to_outer_left = shifted(in_tail, "col", 1)
        to_outer_right = shifted(in_head, "col", -1)
        inner, near_in, cross_in = kernel_call(
            update_inner_kernel, [shape(2, tile, tile)] + [rows_in] * 2, [VM] * 8
        )(info, in_head, in_tail, to_inner_left, to_inner_right, light, peak, inner)
        near_in, cross_in = row_exchange(near_in, cross_in)
        outer, near_out, cross_out = kernel_call(
            update_outer_kernel, [shape(2, tile, 2 * HALO)] + [rows_out] * 2, [VM] * 8
        )(info, head, tail, to_outer_left, to_outer_right, light, peak, outer)
        near_out, cross_out = row_exchange(near_out, cross_out)


def solution(mesh):
    return jax.shard_map(
        steps,
        mesh=mesh,
        in_specs=(
            P(None, "row", "col"),
            P(),
            P("row", "col", None, None),
            P("row", "col", None, None, None),
        ),
        out_specs=P(None, "row", "col"),
        check_vma=False,
    )
```

time: 145 us -> 143 us (0.986)
  waiting for transfers between devices: 74.5 us -> 41.4 us
  starting transfers between devices: 46.5 us -> 74.4 us
    ppermute x8 -> x10, waiting for transfers between devices: 34.8 us -> 16.1 us  [shifted(): return lax.ppermute(block, axis, route)]
    ppermute x10 -> x18, waiting for transfers between devices: 26.5 us -> 14.4 us  [swapped(): return lax.ppermute(block, axis, route)]
    ppermute x5, starting transfers between devices: 3.3 us -> 15 us  [largest_of(): block = jnp.maximum(block, lax.ppermute(block, axis, route))]
    ppermute x10 -> x18, starting transfers between devices: 22.8 us -> 33.9 us  [swapped(): return lax.ppermute(block, axis, route)]
    ppermute x8 -> x10, starting transfers between devices: 20.3 us -> 25.4 us  [shifted(): return lax.ppermute(block, axis, route)]
    ppermute x5, waiting for transfers between devices: 13.1 us -> 11 us  [largest_of(): block = jnp.maximum(block, lax.ppermute(block, axis, route))]
    unnamed x19 -> x26, local copies, waits for them, and re-layouts: 2.2 us -> 3.17 us
    pallas_call x10 -> x11, Pallas kernels: 18.6 us -> 18.7 us  [the longest x2 9.15 us: steps(): kernel_call(gradient_kernel, [rows_in] * 2 + [rows_out] * 2 + [shape(2, t...]
  transfers between devices with their start and end apart: 23 -> 33, of which waited for: 15 -> 16; matrix products, arithmetic and copies ran while one was open for 0% -> 1% of each run, Pallas kernels for 3% -> 8%
where the time goes in v2:
time: 143 us; the launch traced here: 142 us
  starting transfers between devices  74.4 us (52%)
  waiting for transfers between devices  41.4 us (29%)
  Pallas kernels  21 us (15%)
  local copies, waits for them, and re-layouts  3.6 us (3%)
    ppermute x18, starting transfers between devices, swapped(): return lax.ppermute(block, axis, route)  33.9 us
    ppermute x10, starting transfers between devices, shifted(): return lax.ppermute(block, axis, route)  25.4 us
    ppermute x10, waiting for transfers between devices, shifted(): return lax.ppermute(block, axis, route)  16.1 us
    ppermute x5, starting transfers between devices, largest_of(): block = jnp.maximum(block, lax.ppermute(block, axis, route))  15 us
    ppermute x18, waiting for transfers between devices, swapped(): return lax.ppermute(block, axis, route)  14.4 us
    ppermute x5, waiting for transfers between devices, largest_of(): block = jnp.maximum(block, lax.ppermute(block, axis, route))  11 us
    pallas_call x2, Pallas kernels, steps(): kernel_call(gradient_kernel, [rows_in] * 2 + [rows_out] * 2 + [shape(2, t...  9.15 us
    pallas_call x1, Pallas kernels, steps(): kernel_call(light_kernel, [shape(tile, span), shape(8, LANES)], [SM] * 4...  3.69 us
  transfers between devices with their start and end apart: 33, of which 16 were waited for; matrix products, arithmetic and copies ran while one was open for 1% of the time, Pallas kernels for 8%

profile of v2, /device:TPU:1, one launch (start us, length us, event | category | flops | bytes accessed | tf_op | source)
XLA Modules:
  0.0 141.7 jit_solution(9807629164529809528)
XLA Ops:
  0.0 1.0 copy-done
  1.1 4.1 %collective-permute-start.2 = (f32[2,256,128]{2,1,0:T(8,128)S(1)}, f32[2,256,128]{2,1,0:T(8,128)S(1)}, u32[]{:S(2)}, u32[]{:S(2)}) collective-permute-start(f32[2,256,128]{2,1,0:T(8,128)S(1)} %get-tuple-element.40), channel_id=1, source_target_pairs={{0,1},{1,2},{2,3},{3,4},{4,5},{5,6},{6,7},{8,9},{9,10},{10,11},{11... | collective-permute-start | bytes 786440 | tf_op jit(solution)/shard_map/ppermute | solution.py:417
  5.2 1.3 collective-permute-start.3
  6.5 0.7 broadcast_add_fusion
  7.2 0.1 copy.11
  7.3 0.1 add.21.corners
  7.4 0.1 pad_add_fusion
  7.5 0.1 broadcast_in_dim.2.info
  7.5 1.0 copy-done.1
  8.6 1.0 collective-permute-start
  9.6 3.1 %collective-permute-start.1 = (f32[2,128,256]{2,1,0:T(8,128)S(1)}, f32[2,128,256]{2,1,0:T(8,128)S(1)}, u32[]{:S(2)}, u32[]{:S(2)}) collective-permute-start(f32[2,128,256]{2,1,0:T(8,128)S(1)} %get-tuple-element.39), channel_id=1, source_target_pairs={{8,16},{16,8},{9,17},{17,9},{10,18},{18,10},{11,19},{19,11},{12,20... | collective-permute-start | bytes 786440 | tf_op jit(solution)/shard_map/ppermute | solution.py:425
  12.8 1.2 collective-permute-done.3.after
  14.0 0.1 shard_map.84
  14.1 3.4 %collective-permute-start.4 = (f32[2,128,256]{2,1,0:T(8,128)S(1)}, f32[2,128,256]{2,1,0:T(8,128)S(1)}, u32[]{:S(2)}, u32[]{:S(2)}) collective-permute-start(f32[2,128,256]{2,1,0:T(8,128)S(1)} %get-tuple-element.42), channel_id=1, source_target_pairs={{0,8},{8,0},{16,24},{24,16},{1,9},{9,1},{17,25},{25,17},{2,10},{10... | collective-permute-start | bytes 786440 | tf_op jit(solution)/shard_map/ppermute | solution.py:425
  17.5 3.2 %collective-permute-start.5 = (f32[2,128,256]{2,1,0:T(8,128)S(1)}, f32[2,128,256]{2,1,0:T(8,128)S(1)}, u32[]{:S(2)}, u32[]{:S(2)}) collective-permute-start(f32[2,128,256]{2,1,0:T(8,128)S(1)} %get-tuple-element.43), channel_id=1, source_target_pairs={{8,16},{16,8},{9,17},{17,9},{10,18},{18,10},{11,19},{19,11},{12,20... | collective-permute-start | bytes 786440 | tf_op jit(solution)/shard_map/ppermute | solution.py:425
  20.7 1.2 shard_map.85.probe
  21.9 1.0 shard_map.86.amplitude
  23.0 2.3 %collective-permute-done.5.cross_outer = f32[2,128,256]{2,1,0:T(8,128)S(1)} collective-permute-done((f32[2,128,256]{2,1,0:T(8,128)S(1)}, f32[2,128,256]{2,1,0:T(8,128)S(1)}, u32[]{:S(2)}, u32[]{:S(2)}) %collective-permute-start.5) | collective-permute-done | bytes 262176 | tf_op jit(solution)/shard_map/ppermute | solution.py:425
  25.3 4.5 %shard_map.87 = (f32[2,128,256]{2,1,0:T(8,128)S(1)}, f32[2,128,256]{2,1,0:T(8,128)S(1)}, f32[2,128,256]{2,1,0:T(8,128)S(1)}, f32[2,128,256]{2,1,0:T(8,128)S(1)},...) custom-call(s32[9,256]{1,0:T(8,128)S(1)} %broadcast_in_dim.2.info, ...), custom_call_target="tpu_custom_call" | custom-call | flops 2415919104 | bytes 6291456 | tf_op jit(solution)/shard_map/pallas_call | solution.py:496
  29.9 3.1 %collective-permute-start.7 = (f32[2,128,256]{2,1,0:T(8,128)S(1)}, f32[2,128,256]{2,1,0:T(8,128)S(1)}, u32[]{:S(2)}, u32[]{:S(2)}) collective-permute-start(f32[2,128,256]{2,1,0:T(8,128)S(1)} %get-tuple-element.47), channel_id=1, source_target_pairs={{8,16},{16,8},{9,17},{17,9},{10,18},{18,10},{11,19},{19,11},{12,20... | collective-permute-start | bytes 786440 | tf_op jit(solution)/shard_map/ppermute | solution.py:425
  33.1 2.5 %collective-permute-start.9 = (f32[2,128,256]{2,1,0:T(8,128)S(1)}, f32[2,128,256]{2,1,0:T(8,128)S(1)}, u32[]{:S(2)}, u32[]{:S(2)}) collective-permute-start(f32[2,128,256]{2,1,0:T(8,128)S(1)} %get-tuple-element.52), channel_id=1, source_target_pairs={{8,16},{16,8},{9,17},{17,9},{10,18},{18,10},{11,19},{19,11},{12,20... | collective-permute-start | bytes 786440 | tf_op jit(solution)/shard_map/ppermute | solution.py:425
  35.6 2.0 %collective-permute-done.7.cross = f32[2,128,256]{2,1,0:T(8,128)S(1)} collective-permute-done((f32[2,128,256]{2,1,0:T(8,128)S(1)}, f32[2,128,256]{2,1,0:T(8,128)S(1)}, u32[]{:S(2)}, u32[]{:S(2)}) %collective-permute-start.7) | collective-permute-done | bytes 262176 | tf_op jit(solution)/shard_map/ppermute | solution.py:425
  37.6 0.9 shard_map.88
  38.5 1.3 collective-permute-start.24
  39.8 5.5 %collective-permute-start.23 = (f32[2,256,128]{2,1,0:T(8,128)}, f32[2,256,128]{2,1,0:T(8,128)}, u32[]{:S(2)}, u32[]{:S(2)}) collective-permute-start(f32[2,256,128]{2,1,0:T(8,128)} %get-tuple-element.49.tail), channel_id=1, source_target_pairs={{0,1},{1,2},{2,3},{3,4},{4,5},{5,6},{6,7},{8,9},{9,10},{10,11},{11... | collective-permute-start | bytes 786440 | tf_op jit(solution)/shard_map/ppermute | solution.py:417
  45.2 0.9 shard_map.89
  46.1 4.3 %collective-permute-start.10 = (f32[2,256,128]{2,1,0:T(8,128)}, f32[2,256,128]{2,1,0:T(8,128)}, u32[]{:S(2)}, u32[]{:S(2)}) collective-permute-start(f32[2,256,128]{2,1,0:T(8,128)} %get-tuple-element.53.tail), channel_id=1, source_target_pairs={{0,1},{1,2},{2,3},{3,4},{4,5},{5,6},{6,7},{8,9},{9,10},{10,11},{11... | collective-permute-start | bytes 786440 | tf_op jit(solution)/shard_map/ppermute | solution.py:417
  50.4 1.3 collective-permute-start.11
  51.7 0.1 copy.12
  51.8 0.1 add.24
  51.8 1.3 collective-permute-start.13
  53.1 5.4 %collective-permute-done.13 = s32[6]{0:T(128)S(1)} collective-permute-done((s32[6]{0:T(128)S(1)}, s32[6]{0:T(128)S(1)}, u32[]{:S(2)}, u32[]{:S(2)}) %collective-permute-start.13) | collective-permute-done | bytes 56 | tf_op jit(solution)/shard_map/ppermute | solution.py:417
  58.6 3.5 %collective-permute-start.12 = (s32[6]{0:T(128)S(1)}, s32[6]{0:T(128)S(1)}, u32[]{:S(2)}, u32[]{:S(2)}) collective-permute-start(s32[6]{0:T(128)S(1)} %add.24), channel_id=1, source_target_pairs={{0,1},{1,2},{2,3},{3,4},{4,5},{5,6},{6,7},{8,9},{9,10},{10,11},{11... | collective-permute-start | bytes 80 | tf_op jit(solution)/shard_map/ppermute | solution.py:417
  62.0 1.9 %collective-permute-done.12 = s32[6]{0:T(128)S(1)} collective-permute-done((s32[6]{0:T(128)S(1)}, s32[6]{0:T(128)S(1)}, u32[]{:S(2)}, u32[]{:S(2)}) %collective-permute-start.12) | collective-permute-done | bytes 56 | tf_op jit(solution)/shard_map/ppermute | solution.py:417
  63.9 0.1 pad_add_fusion.1.own_spots
  64.0 4.1 %collective-permute-start.15 = (s32[18]{0:T(128)S(1)}, s32[18]{0:T(128)S(1)}, u32[]{:S(2)}, u32[]{:S(2)}) collective-permute-start(s32[18]{0:T(128)S(1)} %pad_add_fusion.1.own_spots), channel_id=1, source_target_pairs={{8,16},{16,8},{9,17},{17,9},{10,18},{18,10},{11,19},{19,11},{12,20... | collective-permute-start | bytes 224 | tf_op jit(solution)/shard_map/ppermute | solution.py:425
  68.1 1.2 collective-permute-done.15.cross_spots
  69.3 1.2 collective-permute-done.14.near_spots
  70.5 3.7 %shard_map.90 = (f32[256,512]{1,0:T(8,128)S(1)}, f32[8,128]{1,0:T(8,128)S(1)}) custom-call(s32[18]{0:T(128)S(1)} %pad_add_fusion.1.own_spots, s32[18]{0:T(128)S(1)} %collective-permute-done.14.near_spots, s32[18]{0:T(128)S(1)} %collective-permute-done.15.cross_spots, s32[1]{0:T(128)} %bitcast.odd, f32[2,256,256]{2,1,0:T(8,128)S(1)} %copy-done.3), custom_call_target="tpu_custom_call" | custom-call | bytes 1585152 | tf_op jit(solution)/shard_map/pallas_call | solution.py:479
  74.2 6.8 %collective-permute-start.16 = (f32[8,128]{1,0:T(8,128)S(1)}, f32[8,128]{1,0:T(8,128)S(1)}, u32[]{:S(2)}, u32[]{:S(2)}) collective-permute-start(f32[8,128]{1,0:T(8,128)S(1)} %get-tuple-element.56), channel_id=1, source_target_pairs={{0,1},{1,2},{2,3},{3,4},{4,5},{5,6},{6,7},{7,0},{8,9},{9,10},{10,1... | collective-permute-start | bytes 12296 | tf_op jit(solution)/shard_map/ppermute | solution.py:440
  81.0 1.8 %collective-permute-done.16 = f32[8,128]{1,0:T(8,128)S(1)} collective-permute-done((f32[8,128]{1,0:T(8,128)S(1)}, f32[8,128]{1,0:T(8,128)S(1)}, u32[]{:S(2)}, u32[]{:S(2)}) %collective-permute-start.16) | collective-permute-done | bytes 4128 | tf_op jit(solution)/shard_map/ppermute | solution.py:440
  82.8 2.9 %collective-permute-start.17 = (f32[8,128]{1,0:T(8,128)S(1)}, f32[8,128]{1,0:T(8,128)S(1)}, u32[]{:S(2)}, u32[]{:S(2)}) collective-permute-start(f32[8,128]{1,0:T(8,128)S(1)} %max.15), channel_id=1, source_target_pairs={{0,2},{1,3},{2,4},{3,5},{4,6},{5,7},{6,0},{7,1},{8,10},{9,11},{10,... | collective-permute-start | bytes 12296 | tf_op jit(solution)/shard_map/ppermute | solution.py:440
  85.8 3.0 %collective-permute-done.17 = f32[8,128]{1,0:T(8,128)S(1)} collective-permute-done((f32[8,128]{1,0:T(8,128)S(1)}, f32[8,128]{1,0:T(8,128)S(1)}, u32[]{:S(2)}, u32[]{:S(2)}) %collective-permute-start.17) | collective-permute-done | bytes 4128 | tf_op jit(solution)/shard_map/ppermute | solution.py:440
  88.8 0.4 collective-permute-start.18
  89.3 2.9 %collective-permute-done.18 = f32[8,128]{1,0:T(8,128)S(1)} collective-permute-done((f32[8,128]{1,0:T(8,128)S(1)}, f32[8,128]{1,0:T(8,128)S(1)}, u32[]{:S(2)}, u32[]{:S(2)}) %collective-permute-start.18) | collective-permute-done | bytes 4128 | tf_op jit(solution)/shard_map/ppermute | solution.py:440
  92.2 4.8 %collective-permute-start.19 = (f32[8,128]{1,0:T(8,128)S(1)}, f32[8,128]{1,0:T(8,128)S(1)}, u32[]{:S(2)}, u32[]{:S(2)}) collective-permute-start(f32[8,128]{1,0:T(8,128)S(1)} %max.17), channel_id=1, source_target_pairs={{0,8},{8,16},{16,24},{24,0},{1,9},{9,17},{17,25},{25,1},{2,10},{10... | collective-permute-start | bytes 12296 | tf_op jit(solution)/shard_map/ppermute | solution.py:440
  97.0 0.8 collective-permute-done.19
  97.7 2.4 %collective-permute-done.20 = f32[8,128]{1,0:T(8,128)S(1)} collective-permute-done((f32[8,128]{1,0:T(8,128)S(1)}, f32[8,128]{1,0:T(8,128)S(1)}, u32[]{:S(2)}, u32[]{:S(2)}) %collective-permute-start.20) | collective-permute-done | bytes 4128 | tf_op jit(solution)/shard_map/ppermute | solution.py:440
  100.2 1.0 copy-done.6
  101.2 1.5 %shard_map.92 = (f32[2,256,256]{2,1,0:T(8,128)S(1)}, f32[2,128,256]{2,1,0:T(8,128)S(1)}, f32[2,128,256]{2,1,0:T(8,128)S(1)}) custom-call(s32[9,256]{1,0:T(8,128)S(1)} %broadcast_in_dim.2.info, f32[2,256,128]{2,1,0:T(8,128)} %get-tuple-element.54.head, f32[2,256,128]{2,1,0:T(8,128)} %get-tuple-element.53.tail, ...), custom_call_target="tpu_custom_call" | custom-call | bytes 3145728 | tf_op jit(solution)/shard_map/pallas_call | solution.py:528
  102.7 1.9 %collective-permute-start.25 = (f32[2,128,256]{2,1,0:T(8,128)S(1)}, f32[2,128,256]{2,1,0:T(8,128)S(1)}, u32[]{:S(2)}, u32[]{:S(2)}) collective-permute-start(f32[2,128,256]{2,1,0:T(8,128)S(1)} %get-tuple-element.59), channel_id=1, source_target_pairs={{0,8},{8,0},{16,24},{24,16},{1,9},{9,1},{17,25},{25,17},{2,10},{10... | collective-permute-start | bytes 786440 | tf_op jit(solution)/shard_map/ppermute | solution.py:425
  104.6 3.7 %collective-permute-start.26 = (f32[2,128,256]{2,1,0:T(8,128)S(1)}, f32[2,128,256]{2,1,0:T(8,128)S(1)}, u32[]{:S(2)}, u32[]{:S(2)}) collective-permute-start(f32[2,128,256]{2,1,0:T(8,128)S(1)} %get-tuple-element.60), channel_id=1, source_target_pairs={{8,16},{16,8},{9,17},{17,9},{10,18},{18,10},{11,19},{19,11},{12,20... | collective-permute-start | bytes 786440 | tf_op jit(solution)/shard_map/ppermute | solution.py:425
  108.3 1.4 %shard_map.91 = (f32[2,256,256]{2,1,0:T(8,128)S(1)}, f32[2,128,256]{2,1,0:T(8,128)S(1)}, f32[2,128,256]{2,1,0:T(8,128)S(1)}) custom-call(s32[9,256]{1,0:T(8,128)S(1)} %broadcast_in_dim.2.info, f32[2,256,128]{2,1,0:T(8,128)} %get-tuple-element.48.head, f32[2,256,128]{2,1,0:T(8,128)} %get-tuple-element.49.tail, ...), custom_call_target="tpu_custom_call" | custom-call | bytes 3145728 | tf_op jit(solution)/shard_map/pallas_call | solution.py:524
  109.8 2.1 %collective-permute-start.22 = (f32[2,128,256]{2,1,0:T(8,128)S(1)}, f32[2,128,256]{2,1,0:T(8,128)S(1)}, u32[]{:S(2)}, u32[]{:S(2)}) collective-permute-start(f32[2,128,256]{2,1,0:T(8,128)S(1)} %get-tuple-element.58), channel_id=1, source_target_pairs={{8,16},{16,8},{9,17},{17,9},{10,18},{18,10},{11,19},{19,11},{12,20... | collective-permute-start | bytes 786440 | tf_op jit(solution)/shard_map/ppermute | solution.py:425
  112.0 0.4 collective-permute-done.26.cross_outer
  112.3 5.2 %collective-permute-done.22.cross_inner = f32[2,128,256]{2,1,0:T(8,128)S(1)} collective-permute-done((f32[2,128,256]{2,1,0:T(8,128)S(1)}, f32[2,128,256]{2,1,0:T(8,128)S(1)}, u32[]{:S(2)}, u32[]{:S(2)}) %collective-permute-start.22) | collective-permute-done | bytes 262176 | tf_op jit(solution)/shard_map/ppermute | solution.py:425
  117.5 4.6 %shard_map.93 = (f32[2,128,256]{2,1,0:T(8,128)S(1)}, f32[2,128,256]{2,1,0:T(8,128)S(1)}, f32[2,128,256]{2,1,0:T(8,128)S(1)}, f32[2,128,256]{2,1,0:T(8,128)S(1)},...) custom-call(s32[9,256]{1,0:T(8,128)S(1)} %broadcast_in_dim.2.info, ...), custom_call_target="tpu_custom_call" | custom-call | flops 2415919104 | bytes 6291456 | tf_op jit(solution)/shard_map/pallas_call | solution.py:496
  122.2 1.9 %collective-permute-start.30 = (f32[2,128,256]{2,1,0:T(8,128)S(1)}, f32[2,128,256]{2,1,0:T(8,128)S(1)}, u32[]{:S(2)}, u32[]{:S(2)}) collective-permute-start(f32[2,128,256]{2,1,0:T(8,128)S(1)} %get-tuple-element.68), channel_id=1, source_target_pairs={{8,16},{16,8},{9,17},{17,9},{10,18},{18,10},{11,19},{19,11},{12,20... | collective-permute-start | bytes 786440 | tf_op jit(solution)/shard_map/ppermute | solution.py:425
  124.2 3.6 %collective-permute-start.28 = (f32[2,128,256]{2,1,0:T(8,128)S(1)}, f32[2,128,256]{2,1,0:T(8,128)S(1)}, u32[]{:S(2)}, u32[]{:S(2)}) collective-permute-start(f32[2,128,256]{2,1,0:T(8,128)S(1)} %get-tuple-element.65), channel_id=1, source_target_pairs={{8,16},{16,8},{9,17},{17,9},{10,18},{18,10},{11,19},{19,11},{12,20... | collective-permute-start | bytes 786440 | tf_op jit(solution)/shard_map/ppermute | solution.py:425
  127.9 2.0 %collective-permute-done.30.cross = f32[2,128,256]{2,1,0:T(8,128)S(1)} collective-permute-done((f32[2,128,256]{2,1,0:T(8,128)S(1)}, f32[2,128,256]{2,1,0:T(8,128)S(1)}, u32[]{:S(2)}, u32[]{:S(2)}) %collective-permute-start.30) | collective-permute-done | bytes 262176 | tf_op jit(solution)/shard_map/ppermute | solution.py:425
  130.0 1.7 %collective-permute-start.31 = (f32[2,256,128]{2,1,0:T(8,128)S(1)}, f32[2,256,128]{2,1,0:T(8,128)S(1)}, u32[]{:S(2)}, u32[]{:S(2)}) collective-permute-start(f32[2,256,128]{2,1,0:T(8,128)S(1)} %get-tuple-element.69), channel_id=1, source_target_pairs={{0,1},{1,2},{2,3},{3,4},{4,5},{5,6},{6,7},{8,9},{9,10},{10,11},{11... | collective-permute-start | bytes 786440 | tf_op jit(solution)/shard_map/ppermute | solution.py:417
  131.7 1.3 collective-permute-start.32
  133.0 7.6 %collective-permute-done.31.from_left = f32[2,256,128]{2,1,0:T(8,128)S(1)} collective-permute-done((f32[2,256,128]{2,1,0:T(8,128)S(1)}, f32[2,256,128]{2,1,0:T(8,128)S(1)}, u32[]{:S(2)}, u32[]{:S(2)}) %collective-permute-start.31) | collective-permute-done | bytes 262176 | tf_op jit(solution)/shard_map/ppermute | solution.py:417
  140.6 1.1 shard_map.95
  (55 shorter events, 0.6 us)
Async XLA Ops:
  0.0 1.0 copy-start
  1.0 19.6 %copy-start.3 = (f32[2,256,256]{2,1,0:T(8,128)S(1)}, f32[2,256,256]{2,1,0:T(8,128)}, u32[]{:S(2)}) copy-start(f32[2,256,256]{2,1,0:T(8,128)} %probe.3) | copy-start | bytes 1572868
  1.1 11.7 %collective-permute-start.2 = (f32[2,256,128]{2,1,0:T(8,128)S(1)}, f32[2,256,128]{2,1,0:T(8,128)S(1)}, u32[]{:S(2)}, u32[]{:S(2)}) collective-permute-start(f32[2,256,128]{2,1,0:T(8,128)S(1)} %get-tuple-element.40), channel_id=1, source_target_pairs={{0,1},{1,2},{2,3},{3,4},{4,5},{5,6},{6,7},{8,9},{9,10},{10,11},{11... | collective-permute-start | bytes 786440 | tf_op jit(solution)/shard_map/ppermute | solution.py:417
  5.2 8.8 %collective-permute-start.3 = (f32[2,256,128]{2,1,0:T(8,128)S(1)}, f32[2,256,128]{2,1,0:T(8,128)S(1)}, u32[]{:S(2)}, u32[]{:S(2)}) collective-permute-start(f32[2,256,128]{2,1,0:T(8,128)S(1)} %get-tuple-element.41), channel_id=1, source_target_pairs={{1,0},{2,1},{3,2},{4,3},{5,4},{6,5},{7,6},{9,8},{10,9},{11,10},{12... | collective-permute-start | bytes 786440 | tf_op jit(solution)/shard_map/ppermute | solution.py:417
  7.5 1.0 copy-start.1
  8.6 13.3 %copy-start.4 = (f32[1,1,3,256,256]{4,3,2,1,0:T(8,128)S(1)}, f32[1,1,3,256,256]{4,3,2,1,0:T(8,128)}, u32[]{:S(2)}) copy-start(f32[1,1,3,256,256]{4,3,2,1,0:T(8,128)} %amplitude.1) | copy-start | bytes 2359300
  8.6 13.3 %copy-start.7 = (bf16[256,256]{1,0:T(8,128)(2,1)S(1)}, bf16[256,256]{1,0:T(8,128)(2,1)}, u32[]{:S(2)}) copy-start(bf16[256,256]{1,0:T(8,128)(2,1)} %constant.40.clone.pick_back) | copy-start | bytes 393220
  8.6 13.3 %copy-start.8 = (bf16[256,256]{1,0:T(8,128)(2,1)S(1)}, bf16[256,256]{1,0:T(8,128)(2,1)}, u32[]{:S(2)}) copy-start(bf16[256,256]{1,0:T(8,128)(2,1)} %constant.39.clone.pick) | copy-start | bytes 393220
  8.6 14.3 %collective-permute-start = (f32[2,128,256]{2,1,0:T(8,128)S(1)}, f32[2,128,256]{2,1,0:T(8,128)S(1)}, u32[]{:S(2)}, u32[]{:S(2)}) collective-permute-start(f32[2,128,256]{2,1,0:T(8,128)S(1)} %get-tuple-element.38), channel_id=1, source_target_pairs={{0,8},{8,0},{16,24},{24,16},{1,9},{9,1},{17,25},{25,17},{2,10},{10... | collective-permute-start | bytes 786440 | tf_op jit(solution)/shard_map/ppermute | solution.py:425
  9.6 13.3 %collective-permute-start.1 = (f32[2,128,256]{2,1,0:T(8,128)S(1)}, f32[2,128,256]{2,1,0:T(8,128)S(1)}, u32[]{:S(2)}, u32[]{:S(2)}) collective-permute-start(f32[2,128,256]{2,1,0:T(8,128)S(1)} %get-tuple-element.39), channel_id=1, source_target_pairs={{8,16},{16,8},{9,17},{17,9},{10,18},{18,10},{11,19},{19,11},{12,20... | collective-permute-start | bytes 786440 | tf_op jit(solution)/shard_map/ppermute | solution.py:425
  14.1 11.2 %copy-start.5 = (f32[2,256,256]{2,1,0:T(8,128)}, f32[2,256,256]{2,1,0:T(8,128)S(1)}, u32[]{:S(2)}) copy-start(f32[2,256,256]{2,1,0:T(8,128)S(1)} %get-tuple-element.44.outer.old) | copy-start | bytes 1572868
  14.1 8.9 %collective-permute-start.4 = (f32[2,128,256]{2,1,0:T(8,128)S(1)}, f32[2,128,256]{2,1,0:T(8,128)S(1)}, u32[]{:S(2)}, u32[]{:S(2)}) collective-permute-start(f32[2,128,256]{2,1,0:T(8,128)S(1)} %get-tuple-element.42), channel_id=1, source_target_pairs={{0,8},{8,0},{16,24},{24,16},{1,9},{9,1},{17,25},{25,17},{2,10},{10... | collective-permute-start | bytes 786440 | tf_op jit(solution)/shard_map/ppermute | solution.py:425
  17.5 7.8 %copy-start.2 = (f32[2,256,256]{2,1,0:T(8,128)S(1)}, f32[2,256,256]{2,1,0:T(8,128)}, u32[]{:S(2)}) copy-start(f32[2,256,256]{2,1,0:T(8,128)} %old.1) | copy-start | bytes 1572868
  17.5 7.8 %copy-start.9 = (bf16[2,2,256,256]{3,2,1,0:T(8,128)(2,1)S(1)}, bf16[2,2,256,256]{3,2,1,0:T(8,128)(2,1)}, u32[]{:S(2)}) copy-start(bf16[2,2,256,256]{3,2,1,0:T(8,128)(2,1)} %constant.38.clone.backward) | copy-start | bytes 1572868
  17.5 7.8 %copy-start.11 = (bf16[2,2,256,256]{3,2,1,0:T(8,128)(2,1)S(1)}, bf16[2,2,256,256]{3,2,1,0:T(8,128)(2,1)}, u32[]{:S(2)}) copy-start(bf16[2,2,256,256]{3,2,1,0:T(8,128)(2,1)} %constant.37.clone.forward) | copy-start | bytes 1572868
  17.5 7.8 %collective-permute-start.5 = (f32[2,128,256]{2,1,0:T(8,128)S(1)}, f32[2,128,256]{2,1,0:T(8,128)S(1)}, u32[]{:S(2)}, u32[]{:S(2)}) collective-permute-start(f32[2,128,256]{2,1,0:T(8,128)S(1)} %get-tuple-element.43), channel_id=1, source_target_pairs={{8,16},{16,8},{9,17},{17,9},{10,18},{18,10},{11,19},{19,11},{12,20... | collective-permute-start | bytes 786440 | tf_op jit(solution)/shard_map/ppermute | solution.py:425
  29.9 5.7 %collective-permute-start.6 = (f32[2,128,256]{2,1,0:T(8,128)S(1)}, f32[2,128,256]{2,1,0:T(8,128)S(1)}, u32[]{:S(2)}, u32[]{:S(2)}) collective-permute-start(f32[2,128,256]{2,1,0:T(8,128)S(1)} %get-tuple-element.46), channel_id=1, source_target_pairs={{0,8},{8,0},{16,24},{24,16},{1,9},{9,1},{17,25},{25,17},{2,10},{10... | collective-permute-start | bytes 786440 | tf_op jit(solution)/shard_map/ppermute | solution.py:425
  29.9 7.7 %collective-permute-start.7 = (f32[2,128,256]{2,1,0:T(8,128)S(1)}, f32[2,128,256]{2,1,0:T(8,128)S(1)}, u32[]{:S(2)}, u32[]{:S(2)}) collective-permute-start(f32[2,128,256]{2,1,0:T(8,128)S(1)} %get-tuple-element.47), channel_id=1, source_target_pairs={{8,16},{16,8},{9,17},{17,9},{10,18},{18,10},{11,19},{19,11},{12,20... | collective-permute-start | bytes 786440 | tf_op jit(solution)/shard_map/ppermute | solution.py:425
  33.0 12.2 %collective-permute-start.8 = (f32[2,128,256]{2,1,0:T(8,128)S(1)}, f32[2,128,256]{2,1,0:T(8,128)S(1)}, u32[]{:S(2)}, u32[]{:S(2)}) collective-permute-start(f32[2,128,256]{2,1,0:T(8,128)S(1)} %get-tuple-element.51), channel_id=1, source_target_pairs={{0,8},{8,0},{16,24},{24,16},{1,9},{9,1},{17,25},{25,17},{2,10},{10... | collective-permute-start | bytes 786440 | tf_op jit(solution)/shard_map/ppermute | solution.py:425
  33.1 12.2 %collective-permute-start.9 = (f32[2,128,256]{2,1,0:T(8,128)S(1)}, f32[2,128,256]{2,1,0:T(8,128)S(1)}, u32[]{:S(2)}, u32[]{:S(2)}) collective-permute-start(f32[2,128,256]{2,1,0:T(8,128)S(1)} %get-tuple-element.52), channel_id=1, source_target_pairs={{8,16},{16,8},{9,17},{17,9},{10,18},{18,10},{11,19},{19,11},{12,20... | collective-permute-start | bytes 786440 | tf_op jit(solution)/shard_map/ppermute | solution.py:425
  38.5 61.7 %collective-permute-start.24 = (f32[2,256,128]{2,1,0:T(8,128)}, f32[2,256,128]{2,1,0:T(8,128)}, u32[]{:S(2)}, u32[]{:S(2)}) collective-permute-start(f32[2,256,128]{2,1,0:T(8,128)} %get-tuple-element.48.head), channel_id=1, source_target_pairs={{1,0},{2,1},{3,2},{4,3},{5,4},{6,5},{7,6},{9,8},{10,9},{11,10},{12... | collective-permute-start | bytes 786440 | tf_op jit(solution)/shard_map/ppermute | solution.py:417
  39.8 60.4 %collective-permute-start.23 = (f32[2,256,128]{2,1,0:T(8,128)}, f32[2,256,128]{2,1,0:T(8,128)}, u32[]{:S(2)}, u32[]{:S(2)}) collective-permute-start(f32[2,256,128]{2,1,0:T(8,128)} %get-tuple-element.49.tail), channel_id=1, source_target_pairs={{0,1},{1,2},{2,3},{3,4},{4,5},{5,6},{6,7},{8,9},{9,10},{10,11},{11... | collective-permute-start | bytes 786440 | tf_op jit(solution)/shard_map/ppermute | solution.py:417
  46.1 62.2 %collective-permute-start.10 = (f32[2,256,128]{2,1,0:T(8,128)}, f32[2,256,128]{2,1,0:T(8,128)}, u32[]{:S(2)}, u32[]{:S(2)}) collective-permute-start(f32[2,256,128]{2,1,0:T(8,128)} %get-tuple-element.53.tail), channel_id=1, source_target_pairs={{0,1},{1,2},{2,3},{3,4},{4,5},{5,6},{6,7},{8,9},{9,10},{10,11},{11... | collective-permute-start | bytes 786440 | tf_op jit(solution)/shard_map/ppermute | solution.py:417
  50.4 57.9 %collective-permute-start.11 = (f32[2,256,128]{2,1,0:T(8,128)}, f32[2,256,128]{2,1,0:T(8,128)}, u32[]{:S(2)}, u32[]{:S(2)}) collective-permute-start(f32[2,256,128]{2,1,0:T(8,128)} %get-tuple-element.54.head), channel_id=1, source_target_pairs={{1,0},{2,1},{3,2},{4,3},{5,4},{6,5},{7,6},{9,8},{10,9},{11,10},{12... | collective-permute-start | bytes 786440 | tf_op jit(solution)/shard_map/ppermute | solution.py:417
  51.8 6.7 %collective-permute-start.13 = (s32[6]{0:T(128)S(1)}, s32[6]{0:T(128)S(1)}, u32[]{:S(2)}, u32[]{:S(2)}) collective-permute-start(s32[6]{0:T(128)S(1)} %add.24), channel_id=1, source_target_pairs={{1,0},{2,1},{3,2},{4,3},{5,4},{6,5},{7,6},{9,8},{10,9},{11,10},{12... | collective-permute-start | bytes 80 | tf_op jit(solution)/shard_map/ppermute | solution.py:417
  58.6 5.3 %collective-permute-start.12 = (s32[6]{0:T(128)S(1)}, s32[6]{0:T(128)S(1)}, u32[]{:S(2)}, u32[]{:S(2)}) collective-permute-start(s32[6]{0:T(128)S(1)} %add.24), channel_id=1, source_target_pairs={{0,1},{1,2},{2,3},{3,4},{4,5},{5,6},{6,7},{8,9},{9,10},{10,11},{11... | collective-permute-start | bytes 80 | tf_op jit(solution)/shard_map/ppermute | solution.py:417
  64.0 5.3 %collective-permute-start.15 = (s32[18]{0:T(128)S(1)}, s32[18]{0:T(128)S(1)}, u32[]{:S(2)}, u32[]{:S(2)}) collective-permute-start(s32[18]{0:T(128)S(1)} %pad_add_fusion.1.own_spots), channel_id=1, source_target_pairs={{8,16},{16,8},{9,17},{17,9},{10,18},{18,10},{11,19},{19,11},{12,20... | collective-permute-start | bytes 224 | tf_op jit(solution)/shard_map/ppermute | solution.py:425
  69.3 1.2 collective-permute-start.14
  74.2 8.7 %collective-permute-start.16 = (f32[8,128]{1,0:T(8,128)S(1)}, f32[8,128]{1,0:T(8,128)S(1)}, u32[]{:S(2)}, u32[]{:S(2)}) collective-permute-start(f32[8,128]{1,0:T(8,128)S(1)} %get-tuple-element.56), channel_id=1, source_target_pairs={{0,1},{1,2},{2,3},{3,4},{4,5},{5,6},{6,7},{7,0},{8,9},{9,10},{10,1... | collective-permute-start | bytes 12296 | tf_op jit(solution)/shard_map/ppermute | solution.py:440
  82.8 6.0 %collective-permute-start.17 = (f32[8,128]{1,0:T(8,128)S(1)}, f32[8,128]{1,0:T(8,128)S(1)}, u32[]{:S(2)}, u32[]{:S(2)}) collective-permute-start(f32[8,128]{1,0:T(8,128)S(1)} %max.15), channel_id=1, source_target_pairs={{0,2},{1,3},{2,4},{3,5},{4,6},{5,7},{6,0},{7,1},{8,10},{9,11},{10,... | collective-permute-start | bytes 12296 | tf_op jit(solution)/shard_map/ppermute | solution.py:440
  88.8 3.4 %collective-permute-start.18 = (f32[8,128]{1,0:T(8,128)S(1)}, f32[8,128]{1,0:T(8,128)S(1)}, u32[]{:S(2)}, u32[]{:S(2)}) collective-permute-start(f32[8,128]{1,0:T(8,128)S(1)} %max.16), channel_id=1, source_target_pairs={{0,4},{1,5},{2,6},{3,7},{4,0},{5,1},{6,2},{7,3},{8,12},{9,13},{10,... | collective-permute-start | bytes 12296 | tf_op jit(solution)/shard_map/ppermute | solution.py:440
  92.2 5.5 %collective-permute-start.19 = (f32[8,128]{1,0:T(8,128)S(1)}, f32[8,128]{1,0:T(8,128)S(1)}, u32[]{:S(2)}, u32[]{:S(2)}) collective-permute-start(f32[8,128]{1,0:T(8,128)S(1)} %max.17), channel_id=1, source_target_pairs={{0,8},{8,16},{16,24},{24,0},{1,9},{9,17},{17,25},{25,1},{2,10},{10... | collective-permute-start | bytes 12296 | tf_op jit(solution)/shard_map/ppermute | solution.py:440
  97.7 2.5 %collective-permute-start.20 = (f32[8,128]{1,0:T(8,128)S(1)}, f32[8,128]{1,0:T(8,128)S(1)}, u32[]{:S(2)}, u32[]{:S(2)}) collective-permute-start(f32[8,128]{1,0:T(8,128)S(1)} %max.18), channel_id=1, source_target_pairs={{0,16},{8,24},{16,0},{24,8},{1,17},{9,25},{17,1},{25,9},{2,18},{10... | collective-permute-start | bytes 12296 | tf_op jit(solution)/shard_map/ppermute | solution.py:440
  100.2 1.0 copy-start.6
  102.7 14.8 %copy-start.10 = (bf16[2,2,256,256]{3,2,1,0:T(8,128)(2,1)S(1)}, bf16[2,2,256,256]{3,2,1,0:T(8,128)(2,1)}, u32[]{:S(2)}) copy-start(bf16[2,2,256,256]{3,2,1,0:T(8,128)(2,1)} %constant.38.clone.backward) | copy-start | bytes 1572868
  102.7 14.8 %copy-start.12 = (bf16[2,2,256,256]{3,2,1,0:T(8,128)(2,1)S(1)}, bf16[2,2,256,256]{3,2,1,0:T(8,128)(2,1)}, u32[]{:S(2)}) copy-start(bf16[2,2,256,256]{3,2,1,0:T(8,128)(2,1)} %constant.37.clone.forward) | copy-start | bytes 1572868
  102.7 9.2 %collective-permute-start.25 = (f32[2,128,256]{2,1,0:T(8,128)S(1)}, f32[2,128,256]{2,1,0:T(8,128)S(1)}, u32[]{:S(2)}, u32[]{:S(2)}) collective-permute-start(f32[2,128,256]{2,1,0:T(8,128)S(1)} %get-tuple-element.59), channel_id=1, source_target_pairs={{0,8},{8,0},{16,24},{24,16},{1,9},{9,1},{17,25},{25,17},{2,10},{10... | collective-permute-start | bytes 786440 | tf_op jit(solution)/shard_map/ppermute | solution.py:425
  104.6 7.7 %collective-permute-start.26 = (f32[2,128,256]{2,1,0:T(8,128)S(1)}, f32[2,128,256]{2,1,0:T(8,128)S(1)}, u32[]{:S(2)}, u32[]{:S(2)}) collective-permute-start(f32[2,128,256]{2,1,0:T(8,128)S(1)} %get-tuple-element.60), channel_id=1, source_target_pairs={{8,16},{16,8},{9,17},{17,9},{10,18},{18,10},{11,19},{19,11},{12,20... | collective-permute-start | bytes 786440 | tf_op jit(solution)/shard_map/ppermute | solution.py:425
  109.8 2.6 %collective-permute-start.21 = (f32[2,128,256]{2,1,0:T(8,128)S(1)}, f32[2,128,256]{2,1,0:T(8,128)S(1)}, u32[]{:S(2)}, u32[]{:S(2)}) collective-permute-start(f32[2,128,256]{2,1,0:T(8,128)S(1)} %get-tuple-element.57), channel_id=1, source_target_pairs={{0,8},{8,0},{16,24},{24,16},{1,9},{9,1},{17,25},{25,17},{2,10},{10... | collective-permute-start | bytes 786440 | tf_op jit(solution)/shard_map/ppermute | solution.py:425
  109.8 7.7 %collective-permute-start.22 = (f32[2,128,256]{2,1,0:T(8,128)S(1)}, f32[2,128,256]{2,1,0:T(8,128)S(1)}, u32[]{:S(2)}, u32[]{:S(2)}) collective-permute-start(f32[2,128,256]{2,1,0:T(8,128)S(1)} %get-tuple-element.58), channel_id=1, source_target_pairs={{8,16},{16,8},{9,17},{17,9},{10,18},{18,10},{11,19},{19,11},{12,20... | collective-permute-start | bytes 786440 | tf_op jit(solution)/shard_map/ppermute | solution.py:425
  122.1 5.7 %collective-permute-start.29 = (f32[2,128,256]{2,1,0:T(8,128)S(1)}, f32[2,128,256]{2,1,0:T(8,128)S(1)}, u32[]{:S(2)}, u32[]{:S(2)}) collective-permute-start(f32[2,128,256]{2,1,0:T(8,128)S(1)} %get-tuple-element.67), channel_id=1, source_target_pairs={{0,8},{8,0},{16,24},{24,16},{1,9},{9,1},{17,25},{25,17},{2,10},{10... | collective-permute-start | bytes 786440 | tf_op jit(solution)/shard_map/ppermute | solution.py:425
  122.2 7.7 %collective-permute-start.30 = (f32[2,128,256]{2,1,0:T(8,128)S(1)}, f32[2,128,256]{2,1,0:T(8,128)S(1)}, u32[]{:S(2)}, u32[]{:S(2)}) collective-permute-start(f32[2,128,256]{2,1,0:T(8,128)S(1)} %get-tuple-element.68), channel_id=1, source_target_pairs={{8,16},{16,8},{9,17},{17,9},{10,18},{18,10},{11,19},{19,11},{12,20... | collective-permute-start | bytes 786440 | tf_op jit(solution)/shard_map/ppermute | solution.py:425
  124.2 8.9 %collective-permute-start.27 = (f32[2,128,256]{2,1,0:T(8,128)S(1)}, f32[2,128,256]{2,1,0:T(8,128)S(1)}, u32[]{:S(2)}, u32[]{:S(2)}) collective-permute-start(f32[2,128,256]{2,1,0:T(8,128)S(1)} %get-tuple-element.64), channel_id=1, source_target_pairs={{0,8},{8,0},{16,24},{24,16},{1,9},{9,1},{17,25},{25,17},{2,10},{10... | collective-permute-start | bytes 786440 | tf_op jit(solution)/shard_map/ppermute | solution.py:425
  124.2 8.8 %collective-permute-start.28 = (f32[2,128,256]{2,1,0:T(8,128)S(1)}, f32[2,128,256]{2,1,0:T(8,128)S(1)}, u32[]{:S(2)}, u32[]{:S(2)}) collective-permute-start(f32[2,128,256]{2,1,0:T(8,128)S(1)} %get-tuple-element.65), channel_id=1, source_target_pairs={{8,16},{16,8},{9,17},{17,9},{10,18},{18,10},{11,19},{19,11},{12,20... | collective-permute-start | bytes 786440 | tf_op jit(solution)/shard_map/ppermute | solution.py:425
  130.0 10.6 %collective-permute-start.31 = (f32[2,256,128]{2,1,0:T(8,128)S(1)}, f32[2,256,128]{2,1,0:T(8,128)S(1)}, u32[]{:S(2)}, u32[]{:S(2)}) collective-permute-start(f32[2,256,128]{2,1,0:T(8,128)S(1)} %get-tuple-element.69), channel_id=1, source_target_pairs={{0,1},{1,2},{2,3},{3,4},{4,5},{5,6},{6,7},{8,9},{9,10},{10,11},{11... | collective-permute-start | bytes 786440 | tf_op jit(solution)/shard_map/ppermute | solution.py:417
  131.7 8.9 %collective-permute-start.32 = (f32[2,256,128]{2,1,0:T(8,128)S(1)}, f32[2,256,128]{2,1,0:T(8,128)S(1)}, u32[]{:S(2)}, u32[]{:S(2)}) collective-permute-start(f32[2,256,128]{2,1,0:T(8,128)S(1)} %get-tuple-element.70), channel_id=1, source_target_pairs={{1,0},{2,1},{3,2},{4,3},{5,4},{6,5},{7,6},{9,8},{10,9},{11,10},{12... | collective-permute-start | bytes 786440 | tf_op jit(solution)/shard_map/ppermute | solution.py:417

commit v3 on v2

v3 whole, which is shorter than its diff:
```python
import functools
import math

import jax
import jax.numpy as jnp
import numpy as np
from jax import lax
from jax.experimental import pallas as pl
from jax.experimental.pallas import tpu as pltpu
from jax.sharding import PartitionSpec as P


HALO = 128
ITERS = 2
LANES = 128
ODD, HAS_LEFT, HAS_RIGHT, FLAGS = 0, 1, 2, 3

smooth_term = 0.25
ridge_share = 0.1

VM = pl.BlockSpec(memory_space=pltpu.VMEM)
SM = pl.BlockSpec(memory_space=pltpu.SMEM)
F32 = jnp.float32
BF16 = jnp.bfloat16


def shape(*dims):
    return jax.ShapeDtypeStruct(dims, F32)


def to_bf16(x):
    return np.asarray(x, np.float32).astype(BF16)


def split_table(table):
    high = to_bf16(table)
    low = to_bf16(table - high.astype(np.float64))
    return high, low


@functools.lru_cache
def dft_tables(length):
    half = length // 2
    n = np.arange(half)
    forward, backward = [], []
    for odd in (0, 1):
        turn = ((2 * n[:, None] + odd) * n[None, :]) % length
        angle = turn * (2.0 * math.pi / length)
        cos, sin = np.cos(angle) / math.sqrt(length), -np.sin(angle) / math.sqrt(length)
        form = np.block([[cos, -sin], [sin, cos]])
        forward.append(np.stack(split_table(form)))
        backward.append(np.stack(split_table(form.T)))
    place = np.zeros((length, length), np.float32)
    place[2 * n, n] = 1.0
    place[2 * n + 1, half + n] = 1.0
    pick = to_bf16(place)
    return np.stack(forward), np.stack(backward), pick, np.ascontiguousarray(pick.T)


def halves(x):
    high = x.astype(BF16)
    low = (x - high.astype(F32)).astype(BF16)
    return high, low


def left_product(table, x):
    high, low = halves(x)
    return jnp.dot(
        jnp.concatenate([table[0], table[1], table[0]], axis=1),
        jnp.concatenate([high, high, low], axis=0),
        preferred_element_type=F32,
    )


def right_product(x, table):
    high, low = halves(x)
    return jnp.dot(
        jnp.concatenate([high, low, high], axis=1),
        jnp.concatenate([table[0], table[0], table[1]], axis=0),
        preferred_element_type=F32,
    )


def window_masks(info, position, win):
    at = FLAGS + 2 * position
    low = lax.broadcasted_iota(jnp.int32, (win, win), 0) >= info[at : at + 1, :]
    near = lax.broadcasted_iota(jnp.int32, (win, win), 1) >= info[at + 1 : at + 2, :]
    return low, near


def flag(info, index):
    return info[index : index + 1, :] > 0


def roll_kernel(corners, probe, rolled):
    win = probe.shape[1]
    for position in range(rolled.shape[0]):
        row = lax.rem(corners[2 * position], win)
        column = lax.rem(corners[2 * position + 1], win)
        for plane in (0, 1):
            rolled[position, plane] = pltpu.roll(
                pltpu.roll(probe[plane], column, 1), row, 0
            )


def spread(piece, low, near, quadrants, first):
    above = jnp.where(low, piece, 0.0)
    below = jnp.where(low, 0.0, piece)
    parts = (
        jnp.where(near, above, 0.0), jnp.where(near, 0.0, above),
        jnp.where(near, below, 0.0), jnp.where(near, 0.0, below),
    )
    for index, part in enumerate(parts):
        quadrants[index] = part if first else quadrants[index] + part


def gradient_kernel(
    info, near_rows, cross_rows, near_half, cross_half, probe, amplitude, forward, backward,
    grad_near, grad_cross, mid_near, mid_cross, area, total,
):
    count, win, _ = amplitude.shape
    half = win // 2
    odd_row = flag(info, ODD)
    for plane in (0, 1):
        for left in (0, 1):
            lanes = slice(left * win, (left + 1) * win)
            parts = [ref[plane, :, lanes] for ref in (near_rows, near_half, cross_half, cross_rows)]
            for index in range(4):
                rows = slice((index % 2) * half, (index % 2 + 1) * half)
                area[plane, 2 * (index // 2) + left, rows] = jnp.where(
                    odd_row, parts[index], parts[3 - index]
                )

    def patch(plane, low, near):
        first, second, third, fourth = [area[plane, k] for k in range(4)]
        return jnp.where(
            near, jnp.where(low, first, third), jnp.where(low, second, fourth)
        )

    for position in range(count):
        low, near = window_masks(info, position, win)
        patch_real = patch(0, low, near)
        patch_imag = patch(1, low, near)
        probe_real, probe_imag = probe[position, 0], probe[position, 1]
        real = probe_real * patch_real - probe_imag * patch_imag
        imag = probe_real * patch_imag + probe_imag * patch_real
        summed = jnp.concatenate([real[:half] + real[half:], imag[:half] + imag[half:]], axis=0)
        differ = jnp.concatenate([real[:half] - real[half:], imag[:half] - imag[half:]], axis=0)
        even = left_product(forward[0], summed)
        odd = left_product(forward[1], differ)
        real = jnp.concatenate([even[:half], odd[:half]], axis=0)
        imag = jnp.concatenate([even[half:], odd[half:]], axis=0)
        summed = jnp.concatenate(
            [real[:, :half] + real[:, half:], imag[:, :half] + imag[:, half:]], axis=1
        )
        differ = jnp.concatenate(
            [real[:, :half] - real[:, half:], imag[:, :half] - imag[:, half:]], axis=1
        )
        even = right_product(summed, backward[0])
        odd = right_product(differ, backward[1])
        even_real, even_imag = even[:, :half], even[:, half:]
        odd_real, odd_imag = odd[:, :half], odd[:, half:]
        amp = amplitude[position]
        even_factor = 1.0 - amp[:, :half] * lax.rsqrt(
            even_real * even_real + even_imag * even_imag + smooth_term
        )
        odd_factor = 1.0 - amp[:, half:] * lax.rsqrt(
            odd_real * odd_real + odd_imag * odd_imag + smooth_term
        )
        even = jnp.concatenate([even_factor * even_real, even_factor * even_imag], axis=1)
        odd = jnp.concatenate([odd_factor * odd_real, odd_factor * odd_imag], axis=1)
        even_back = right_product(even, forward[0])
        odd_back = right_product(odd, forward[1])
        summed, differ = even_back + odd_back, even_back - odd_back
        real = jnp.concatenate([summed[:, :half], differ[:, :half]], axis=1)
        imag = jnp.concatenate([summed[:, half:], differ[:, half:]], axis=1)
        even = left_product(backward[0], jnp.concatenate([real[:half], imag[:half]], axis=0))
        odd = left_product(backward[1], jnp.concatenate([real[half:], imag[half:]], axis=0))
        summed, differ = even + odd, even - odd
        real = jnp.concatenate([summed[:half], differ[:half]], axis=0)
        imag = jnp.concatenate([summed[half:], differ[half:]], axis=0)
        for plane, piece in (
            (0, probe_real * real + probe_imag * imag),
            (1, probe_real * imag - probe_imag * real),
        ):
            spread(piece, low, near, total.at[plane], position == 0)
    outs = (grad_near, mid_near, mid_cross, grad_cross)
    for plane in (0, 1):
        for left in (0, 1):
            lanes = slice(left * win, (left + 1) * win)
            parts = [
                total[plane, 2 * (k // 2) + left, (k % 2) * half : (k % 2 + 1) * half]
                for k in range(4)
            ]
            for index in range(4):
                outs[index][plane, :, lanes] = jnp.where(
                    odd_row, parts[index], parts[3 - index]
                )


def light_kernel(
    own_spots, left_spots, right_spots, info, probe, light_near, light_cross, largest, quadrants
):
    win = probe.shape[1]
    half = win // 2
    count = own_spots.shape[0] // 6
    odd_row = flag(info, ODD)
    real, imag = probe[0], probe[1]
    intensity = real * real + imag * imag
    quadrants[...] = jnp.zeros_like(quadrants)
    rows = lax.broadcasted_iota(jnp.int32, (half, win), 0)
    columns = lax.broadcasted_iota(jnp.int32, (half, win), 1)

    for row_side in (-1, 0, 1):
        for column_side, spots in ((-1, left_spots), (0, own_spots), (1, right_spots)):
            base = (row_side + 1) * 2 * count

            @pl.when(spots[base] > 0)
            def _():
                def one(position, carry):
                    row = spots[base + 2 * position] - 1
                    column = spots[base + 2 * position + 1] - 1
                    block = pltpu.roll(intensity, lax.rem(row, win), 0)
                    turn = lax.rem(column, win)
                    for lower in (0, 1):
                        if (row_side < 0 and lower) or (row_side > 0 and not lower):
                            continue
                        part = block[:half] if lower else block[half:]
                        part = pltpu.roll(part, turn, 1)
                        index = rows if lower else rows + half
                        if row_side < 0 or (row_side == 0 and lower):
                            keep = index < row
                        else:
                            keep = index >= row
                        part = jnp.where(keep, part, 0.0)
                        if column_side <= 0:
                            near = columns < column if column_side else columns >= column
                            quadrants[2 * lower] = quadrants[2 * lower] + jnp.where(near, part, 0.0)
                        if column_side >= 0:
                            far = columns >= column if column_side else columns < column
                            quadrants[2 * lower + 1] = quadrants[2 * lower + 1] + jnp.where(far, part, 0.0)
                    return carry

                lax.fori_loop(0, count, one, 0)

    found = None
    for left in (0, 1):
        lanes = slice(left * win, (left + 1) * win)
        upper, lower = quadrants[left], quadrants[2 + left]
        light_near[:, lanes] = jnp.where(odd_row, upper, lower)
        light_cross[:, lanes] = jnp.where(odd_row, lower, upper)
        best = jnp.maximum(upper, lower)
        best = best[:, : win - HALO] if left else best[:, HALO:]
        for row in range(0, half, 8):
            block = best[row : row + 8]
            found = block if found is None else jnp.maximum(found, block)
    largest[...] = found


def thirds(x):
    high = x.astype(BF16)
    rest = x - high.astype(F32)
    mid = rest.astype(BF16)
    return high, mid, (rest - mid.astype(F32)).astype(BF16)


def order_kernel(amplitude, pick, pick_back, ordered):
    rows = jnp.concatenate([pick_back[...]] * 3, axis=1)
    columns = jnp.concatenate([pick[...]] * 3, axis=0)
    for position in range(ordered.shape[0]):
        block = jnp.dot(
            rows,
            jnp.concatenate(thirds(amplitude[0, 0, position]), axis=0),
            preferred_element_type=F32,
        )
        ordered[position] = jnp.dot(
            jnp.concatenate(thirds(block), axis=1), columns, preferred_element_type=F32
        )


def edges_kernel(info, specimen, near_head, near_tail, cross_head, cross_tail):
    odd_row = info[ODD : ODD + 1, :HALO] > 0
    half = near_head.shape[1]
    for plane in (0, 1):
        for lanes, near, cross in (
            (slice(0, HALO), near_head, cross_head),
            (slice(specimen.shape[2] - HALO, None), near_tail, cross_tail),
        ):
            top, bottom = specimen[plane, :half, lanes], specimen[plane, half:, lanes]
            near[plane] = jnp.where(odd_row, top, bottom)
            cross[plane] = jnp.where(odd_row, bottom, top)


def widen_kernel(info, before, specimen, after, out, *, near):
    odd_row = flag(info, ODD)
    half, tile = out.shape[1], specimen.shape[2]
    for plane in (0, 1):
        top, bottom = specimen[plane, :half], specimen[plane, half:]
        own = jnp.where(odd_row, top, bottom) if near else jnp.where(odd_row, bottom, top)
        out[plane, :, :HALO] = before[plane]
        out[plane, :, HALO : HALO + tile] = own
        out[plane, :, HALO + tile :] = after[plane]


def fold_kernel(mid, sent, head, tail):
    side = head.shape[2]
    for plane in (0, 1):
        head[plane] = mid[plane, :, :side] + sent[plane, :, :side]
        tail[plane] = mid[plane, :, side:] + sent[plane, :, side:]


def fold_last_kernel(mid, sent, head, core, tail):
    tile = core.shape[2]
    for plane in (0, 1):
        head[plane] = mid[plane, :, :HALO] + sent[plane, :, :HALO]
        core[plane] = mid[plane, :, HALO : HALO + tile] + sent[plane, :, HALO : HALO + tile]
        tail[plane] = mid[plane, :, HALO + tile :] + sent[plane, :, HALO + tile :]


def update_kernel(info, head, tail, from_left, from_right, light, peak, old, new):
    side = head.shape[2]
    most = ridge_share * jnp.max(peak[...])
    lane = lax.broadcasted_iota(jnp.int32, (1, side), 1)
    for own, sent, inside, lanes in (
        (head, from_left, (lane >= HALO) | flag(info, HAS_LEFT), slice(0, side)),
        (tail, from_right, (lane < side - HALO) | flag(info, HAS_RIGHT), slice(side, None)),
    ):
        scale = 1.0 / (light[:, lanes] + most)
        for plane in (0, 1):
            gradient = own[plane] + sent[plane]
            new[plane, :, lanes] = jnp.where(
                inside, old[plane, :, lanes] - gradient * scale, 0.0
            )


def finish_kernel(info, *refs):
    *halves, peak, out = refs
    odd_row = flag(info, ODD)
    most = ridge_share * jnp.max(peak[...])
    half, tile = out.shape[1] // 2, out.shape[2]
    inner = slice(HALO, HALO + tile)
    for plane in (0, 1):
        news = []
        for core, from_left, from_right, light, old in (halves[:5], halves[5:]):
            sent = [from_left[plane], from_right[plane]]
            if tile > 2 * HALO:
                sent.insert(1, jnp.zeros((half, tile - 2 * HALO), F32))
            gradient = core[plane] + jnp.concatenate(sent, axis=1)
            news.append(old[plane, :, inner] - gradient / (light[:, inner] + most))
        out[plane, :half] = jnp.where(odd_row, news[0], news[1])
        out[plane, half:] = jnp.where(odd_row, news[1], news[0])


def kernel_call(body, outs, specs, flops=0, scratch=(), grant=8):
    moved = 4 * sum(math.prod(out.shape) for out in outs)
    single = len(outs) == 1
    return pl.pallas_call(
        body,
        out_shape=outs[0] if single else outs,
        in_specs=specs,
        out_specs=VM if single else (VM,) * len(outs),
        scratch_shapes=list(scratch),
        compiler_params=pltpu.CompilerParams(vmem_limit_bytes=grant * 1024 * 1024),
        cost_estimate=pl.CostEstimate(
            flops=flops, bytes_accessed=3 * moved, transcendentals=0
        ),
    )


def shifted(block, axis, distance):
    count = lax.axis_size(axis)
    route = [(i - distance, i) for i in range(count) if 0 <= i - distance < count]
    return lax.ppermute(block, axis, route)


def swapped(block, axis, first):
    count = lax.axis_size(axis)
    route = []
    for i in range(first, count - 1, 2):
        route += [(i, i + 1), (i + 1, i)]
    return lax.ppermute(block, axis, route)


def to_cross(block):
    return swapped(block, "row", 1)


def to_near(block):
    return swapped(block, "row", 0)


def to_sides(head, tail):
    right = shifted(tail, "col", 1)
    left = shifted(head, "col", -1)
    return right, left


def largest_of(block, axes):
    for axis in axes:
        count = lax.axis_size(axis)
        reach = 1
        while reach < count:
            route = [(i, (i + reach) % count) for i in range(count)]
            block = jnp.maximum(block, lax.ppermute(block, axis, route))
            reach *= 2
    return block


def steps(specimen, probe_field, offsets, amplitudes):
    tile = specimen.shape[1]
    win = probe_field.shape[1]
    side = tile // 2 + HALO
    half = tile // 2
    count = offsets.shape[2]
    forward, backward, pick, pick_back = [jnp.asarray(t) for t in dft_tables(win)]
    row, col = lax.axis_index("row"), lax.axis_index("col")
    odd = row % 2
    corners = offsets.reshape(-1) + HALO
    flags = jnp.stack([odd, col > 0, col < lax.axis_size("col") - 1]).astype(jnp.int32)
    info = jnp.broadcast_to(
        jnp.concatenate([flags, corners])[:, None], (FLAGS + 2 * count, win)
    )
    band, wide, strip = shape(2, half, HALO), shape(2, half, 2 * side), shape(2, half, side)

    near_head, near_tail, cross_head, cross_tail = kernel_call(
        edges_kernel, [band] * 4, [VM] * 2
    )(info, specimen)
    cross_sides = to_sides(cross_head, cross_tail)
    near_sides = to_sides(near_head, near_tail)

    spots = corners + 1
    spots_cross, spots_near = to_cross(spots), to_near(spots)
    spots = jnp.concatenate(
        [
            jnp.where(odd > 0, spots_near, spots_cross),
            spots,
            jnp.where(odd > 0, spots_cross, spots_near),
        ]
    )
    spots_left, spots_right = to_sides(spots, spots)

    def widened(sides, near):
        return kernel_call(
            functools.partial(widen_kernel, near=near), [wide], [VM] * 4
        )(info, sides[0], specimen, sides[1])

    cross_half = widened(cross_sides, False)
    cross_rows = to_cross(cross_half)
    near_half = widened(near_sides, True)
    near_rows = to_near(near_half)

    probes = kernel_call(roll_kernel, [shape(count, 2, win, win)], [SM, VM])(corners, probe_field)
    ordered = kernel_call(order_kernel, [shape(count, win, win)], [VM] * 3)(
        amplitudes, pick, pick_back
    )
    light_near, light_cross, found = kernel_call(
        light_kernel,
        [shape(half, 2 * side)] * 2 + [shape(8, LANES)],
        [SM] * 3 + [VM] * 2,
        scratch=[pltpu.VMEM((4, half, win), F32)],
    )(spots, spots_left, spots_right, info, probe_field)
    peak = largest_of(found, ("col", "row"))

    for step in range(ITERS):
        grad_near, grad_cross, mid_near, mid_cross = kernel_call(
            gradient_kernel,
            [wide] * 4,
            [VM] * 9,
            flops=count * 8 * 2 * win * 3 * win * win,
            scratch=[pltpu.VMEM((2, 4, win, win), F32)] * 2,
            grant=24,
        )(
            info, near_rows, cross_rows, near_half, cross_half, probes, ordered,
            forward, backward,
        )
        sent_cross = to_cross(grad_cross)
        sent_near = to_near(grad_near)
        if step + 1 < ITERS:
            halves = []
            for mid, sent, light, old in (
                (mid_cross, sent_cross, light_cross, cross_half),
                (mid_near, sent_near, light_near, near_half),
            ):
                head, tail = kernel_call(fold_kernel, [strip] * 2, [VM] * 2)(mid, sent)
                from_left, from_right = to_sides(head, tail)
                halves.append(
                    kernel_call(update_kernel, [wide], [VM] * 8)(
                        info, head, tail, from_left, from_right, light, peak, old
                    )
                )
            cross_half, near_half = halves
            cross_rows = to_cross(cross_half)
            near_rows = to_near(near_half)
        else:
            operands = []
            for mid, sent, light, old in (
                (mid_near, sent_near, light_near, near_half),
                (mid_cross, sent_cross, light_cross, cross_half),
            ):
                head, core, tail = kernel_call(
                    fold_last_kernel, [band, shape(2, half, tile), band], [VM] * 2
                )(mid, sent)
                from_left, from_right = to_sides(head, tail)
                operands += [core, from_left, from_right, light, old]
            return kernel_call(
                finish_kernel, [shape(2, tile, tile)], [VM] * 12
            )(info, *operands, peak)


def solution(mesh):
    return jax.shard_map(
        steps,
        mesh=mesh,
        in_specs=(
            P(None, "row", "col"),
            P(),
            P("row", "col", None, None),
            P("row", "col", None, None, None),
        ),
        out_specs=P(None, "row", "col"),
        check_vma=False,
    )
```

time: 143 us -> 144 us (level)
  waiting for transfers between devices: 41.4 us -> 39.1 us
  local copies, waits for them, and re-layouts: 3.6 us -> 5.19 us
  starting transfers between devices: 74.4 us -> 75.9 us
    ppermute x18 -> x10, starting transfers between devices: 33.9 us -> 22.2 us  [swapped(): return lax.ppermute(block, axis, route)]
    ppermute x10 -> x14, starting transfers between devices: 25.4 us -> 36 us  [shifted(): return lax.ppermute(block, axis, route)]
    ppermute x5, starting transfers between devices: 15 us -> 17.8 us  [largest_of(): block = jnp.maximum(block, lax.ppermute(block, axis, route))]
    ppermute x5, waiting for transfers between devices: 11 us -> 8.85 us  [largest_of(): block = jnp.maximum(block, lax.ppermute(block, axis, route))]
    unnamed x26 -> x30, local copies, waits for them, and re-layouts: 3.17 us -> 4.76 us
    pallas_call x12 -> x13, Pallas kernels: 18.8 us -> 17.9 us  [the longest x2 10.4 us: steps(): kernel_call(gradient_kernel, [wide] * 4, [VM] * 9, flops=count * 8 * 2 *...]
    ppermute x10 -> x14, waiting for transfers between devices: 16.1 us -> 15.7 us  [shifted(): return lax.ppermute(block, axis, route)]
    ppermute x18 -> x10, waiting for transfers between devices: 14.4 us -> 14.6 us  [swapped(): return lax.ppermute(block, axis, route)]
  transfers between devices with their start and end apart: 33 -> 29, of which waited for: 16 -> 14; matrix products, arithmetic and copies ran while one was open for 1% -> 0% of each run, Pallas kernels for 8% -> 6%
where the time goes in v3:
time: 144 us; the launch traced here: 142 us
  starting transfers between devices  75.9 us (53%)
  waiting for transfers between devices  39.1 us (27%)
  Pallas kernels  20.1 us (14%)
  local copies, waits for them, and re-layouts  5.19 us (4%)
    ppermute x14, starting transfers between devices, shifted(): return lax.ppermute(block, axis, route)  36 us
    ppermute x10, starting transfers between devices, swapped(): return lax.ppermute(block, axis, route)  22.2 us
    ppermute x5, starting transfers between devices, largest_of(): block = jnp.maximum(block, lax.ppermute(block, axis, route))  17.8 us
    ppermute x14, waiting for transfers between devices, shifted(): return lax.ppermute(block, axis, route)  15.7 us
    ppermute x10, waiting for transfers between devices, swapped(): return lax.ppermute(block, axis, route)  14.6 us
    pallas_call x2, Pallas kernels, steps(): kernel_call(gradient_kernel, [wide] * 4, [VM] * 9, flops=count * 8 * 2 *...  10.4 us
    ppermute x5, waiting for transfers between devices, largest_of(): block = jnp.maximum(block, lax.ppermute(block, axis, route))  8.85 us
    unnamed x30, local copies, waits for them, and re-layouts  4.76 us
  transfers between devices with their start and end apart: 29, of which 14 were waited for; matrix products, arithmetic and copies ran while one was open for 0% of the time, Pallas kernels for 6%

profile of v3, /device:TPU:1, one launch (start us, length us, event | category | flops | bytes accessed | tf_op | source)
XLA Modules:
  0.0 141.7 jit_solution(17656010048323634934)
XLA Ops:
  0.0 0.7 broadcast_add_fusion
  0.7 0.1 copy.11
  0.8 0.1 add.21.corners
  0.9 0.1 pad_add_fusion
  0.9 0.1 broadcast_in_dim.2.info
  1.0 1.0 copy-done
  2.1 4.1 %collective-permute-start = (f32[2,128,128]{2,1,0:T(8,128)S(1)}, f32[2,128,128]{2,1,0:T(8,128)S(1)}, u32[]{:S(2)}, u32[]{:S(2)}) collective-permute-start(f32[2,128,128]{2,1,0:T(8,128)S(1)} %get-tuple-element.30), channel_id=1, source_target_pairs={{0,1},{1,2},{2,3},{3,4},{4,5},{5,6},{6,7},{8,9},{9,10},{10,11},{11... | collective-permute-start | bytes 393224 | tf_op jit(solution)/shard_map/ppermute | solution.py:373
  6.2 1.3 collective-permute-start.1
  7.5 4.0 %collective-permute-start.3 = (f32[2,128,128]{2,1,0:T(8,128)S(1)}, f32[2,128,128]{2,1,0:T(8,128)S(1)}, u32[]{:S(2)}, u32[]{:S(2)}) collective-permute-start(f32[2,128,128]{2,1,0:T(8,128)S(1)} %get-tuple-element.32), channel_id=1, source_target_pairs={{0,1},{1,2},{2,3},{3,4},{4,5},{5,6},{6,7},{8,9},{9,10},{10,11},{11... | collective-permute-start | bytes 393224 | tf_op jit(solution)/shard_map/ppermute | solution.py:373
  11.5 1.3 collective-permute-start.4
  12.9 1.6 %collective-permute-start.2 = (f32[2,128,512]{2,1,0:T(8,128)S(1)}, f32[2,128,512]{2,1,0:T(8,128)S(1)}, u32[]{:S(2)}, u32[]{:S(2)}) collective-permute-start(f32[2,128,512]{2,1,0:T(8,128)S(1)} %shard_map.83.near_half.old), channel_id=1, source_target_pairs={{0,8},{8,0},{16,24},{24,16},{1,9},{9,1},{17,25},{25,17},{2,10},{10... | collective-permute-start | bytes 1572872 | tf_op jit(solution)/shard_map/ppermute | solution.py:381
  14.5 1.7 %collective-permute-done.3.before = f32[2,128,128]{2,1,0:T(8,128)S(1)} collective-permute-done((f32[2,128,128]{2,1,0:T(8,128)S(1)}, f32[2,128,128]{2,1,0:T(8,128)S(1)}, u32[]{:S(2)}, u32[]{:S(2)}) %collective-permute-start.3) | collective-permute-done | bytes 131104 | tf_op jit(solution)/shard_map/ppermute | solution.py:373
  16.2 1.7 %collective-permute-done.4.after = f32[2,128,128]{2,1,0:T(8,128)S(1)} collective-permute-done((f32[2,128,128]{2,1,0:T(8,128)S(1)}, f32[2,128,128]{2,1,0:T(8,128)S(1)}, u32[]{:S(2)}, u32[]{:S(2)}) %collective-permute-start.4) | collective-permute-done | bytes 131104 | tf_op jit(solution)/shard_map/ppermute | solution.py:373
  18.0 5.5 %collective-permute-start.5 = (f32[2,128,512]{2,1,0:T(8,128)S(1)}, f32[2,128,512]{2,1,0:T(8,128)S(1)}, u32[]{:S(2)}, u32[]{:S(2)}) collective-permute-start(f32[2,128,512]{2,1,0:T(8,128)S(1)} %shard_map.84.cross_half.old), channel_id=1, source_target_pairs={{8,16},{16,8},{9,17},{17,9},{10,18},{18,10},{11,19},{19,11},{12,20... | collective-permute-start | bytes 1572872 | tf_op jit(solution)/shard_map/ppermute | solution.py:381
  23.5 1.2 shard_map.85.probe
  24.8 1.0 shard_map.86.amplitude
  25.8 4.6 %collective-permute-done.5.cross_rows = f32[2,128,512]{2,1,0:T(8,128)S(1)} collective-permute-done((f32[2,128,512]{2,1,0:T(8,128)S(1)}, f32[2,128,512]{2,1,0:T(8,128)S(1)}, u32[]{:S(2)}, u32[]{:S(2)}) %collective-permute-start.5) | collective-permute-done | bytes 524320 | tf_op jit(solution)/shard_map/ppermute | solution.py:381
  30.4 5.6 %shard_map.87 = (f32[2,128,512]{2,1,0:T(8,128)}, f32[2,128,512]{2,1,0:T(8,128)}, f32[2,128,512]{2,1,0:T(8,128)S(1)}, f32[2,128,512]{2,1,0:T(8,128)S(1)}) custom-call(s32[9,256]{1,0:T(8,128)S(1)} %broadcast_in_dim.2.info, f32[2,128,512]{2,1,0:T(8,128)S(1)} %collective-permute-done.2.near_rows, f32[2,128,512]{2,1,0:T(8,128)S(1)} %collective-permute-done.5.cross_rows, ...), custom_call_target="tpu_custom_call" | custom-call | flops 2415919104 | bytes 6291456 | tf_op jit(solution)/shard_map/pallas_call | solution.py:465
  36.0 0.8 copy-done.5
  36.8 0.8 copy-done.7
  37.6 3.6 %collective-permute-start.19 = (f32[2,128,512]{2,1,0:T(8,128)}, f32[2,128,512]{2,1,0:T(8,128)}, u32[]{:S(2)}, u32[]{:S(2)}) collective-permute-start(f32[2,128,512]{2,1,0:T(8,128)} %get-tuple-element.41), channel_id=1, source_target_pairs={{8,16},{16,8},{9,17},{17,9},{10,18},{18,10},{11,19},{19,11},{12,20... | collective-permute-start | bytes 1572872 | tf_op jit(solution)/shard_map/ppermute | solution.py:381
  41.2 0.1 copy.12
  41.3 0.1 add.24
  41.4 1.9 %collective-permute-start.10 = (s32[6]{0:T(128)S(1)}, s32[6]{0:T(128)S(1)}, u32[]{:S(2)}, u32[]{:S(2)}) collective-permute-start(s32[6]{0:T(128)S(1)} %add.24), channel_id=1, source_target_pairs={{8,16},{16,8},{9,17},{17,9},{10,18},{18,10},{11,19},{19,11},{12,20... | collective-permute-start | bytes 80 | tf_op jit(solution)/shard_map/ppermute | solution.py:381
  43.3 0.1 collective-permute-start.9
  43.4 1.0 copy-done.8
  44.5 1.1 shard_map.88
  45.6 1.3 collective-permute-start.8
  46.9 5.2 %collective-permute-start.7 = (f32[2,128,256]{2,1,0:T(8,128)S(1)}, f32[2,128,256]{2,1,0:T(8,128)S(1)}, u32[]{:S(2)}, u32[]{:S(2)}) collective-permute-start(f32[2,128,256]{2,1,0:T(8,128)S(1)} %get-tuple-element.37.tail), channel_id=1, source_target_pairs={{0,1},{1,2},{2,3},{3,4},{4,5},{5,6},{6,7},{8,9},{9,10},{10,11},{11... | collective-permute-start | bytes 786440 | tf_op jit(solution)/shard_map/ppermute | solution.py:373
  52.1 1.0 copy-done.6
  53.1 1.1 shard_map.91
  54.2 1.3 collective-permute-start.21
  55.5 4.9 %collective-permute-start.20 = (f32[2,128,256]{2,1,0:T(8,128)S(1)}, f32[2,128,256]{2,1,0:T(8,128)S(1)}, u32[]{:S(2)}, u32[]{:S(2)}) collective-permute-start(f32[2,128,256]{2,1,0:T(8,128)S(1)} %get-tuple-element.43.tail), channel_id=1, source_target_pairs={{0,1},{1,2},{2,3},{3,4},{4,5},{5,6},{6,7},{8,9},{9,10},{10,11},{11... | collective-permute-start | bytes 786440 | tf_op jit(solution)/shard_map/ppermute | solution.py:373
  60.5 0.1 pad_add_fusion.1.own_spots
  60.5 1.3 collective-permute-start.12
  61.8 3.9 %collective-permute-done.12.right_spots = s32[18]{0:T(128)S(1)} collective-permute-done((s32[18]{0:T(128)S(1)}, s32[18]{0:T(128)S(1)}, u32[]{:S(2)}, u32[]{:S(2)}) %collective-permute-start.12) | collective-permute-done | bytes 104 | tf_op jit(solution)/shard_map/ppermute | solution.py:373
  65.7 4.2 %collective-permute-start.11 = (s32[18]{0:T(128)S(1)}, s32[18]{0:T(128)S(1)}, u32[]{:S(2)}, u32[]{:S(2)}) collective-permute-start(s32[18]{0:T(128)S(1)} %pad_add_fusion.1.own_spots), channel_id=1, source_target_pairs={{0,1},{1,2},{2,3},{3,4},{4,5},{5,6},{6,7},{8,9},{9,10},{10,11},{11... | collective-permute-start | bytes 224 | tf_op jit(solution)/shard_map/ppermute | solution.py:373
  70.0 4.0 %collective-permute-done.11.left_spots = s32[18]{0:T(128)S(1)} collective-permute-done((s32[18]{0:T(128)S(1)}, s32[18]{0:T(128)S(1)}, u32[]{:S(2)}, u32[]{:S(2)}) %collective-permute-start.11) | collective-permute-done | bytes 104 | tf_op jit(solution)/shard_map/ppermute | solution.py:373
  73.9 3.7 %shard_map.89 = (f32[128,512]{1,0:T(8,128)S(1)}, f32[128,512]{1,0:T(8,128)S(1)}, f32[8,128]{1,0:T(8,128)S(1)}) custom-call(s32[18]{0:T(128)S(1)} %pad_add_fusion.1.own_spots, s32[18]{0:T(128)S(1)} %collective-permute-done.11.left_spots, s32[18]{0:T(128)S(1)} %collective-permute-done.12.right_spots, s32[9,256]{1,0:T(8,128)S(1)} %broadcast_in_dim.2.info, ...), custom_call_target="tpu_custom_call" | custom-call | bytes 1585152 | tf_op jit(solution)/shard_map/pallas_call | solution.py:456
  77.6 5.8 %collective-permute-start.13 = (f32[8,128]{1,0:T(8,128)S(1)}, f32[8,128]{1,0:T(8,128)S(1)}, u32[]{:S(2)}, u32[]{:S(2)}) collective-permute-start(f32[8,128]{1,0:T(8,128)S(1)} %get-tuple-element.39), channel_id=1, source_target_pairs={{0,1},{1,2},{2,3},{3,4},{4,5},{5,6},{6,7},{7,0},{8,9},{9,10},{10,1... | collective-permute-start | bytes 12296 | tf_op jit(solution)/shard_map/ppermute | solution.py:404
  83.4 1.1 collective-permute-done.13
  84.5 3.6 %collective-permute-start.14 = (f32[8,128]{1,0:T(8,128)S(1)}, f32[8,128]{1,0:T(8,128)S(1)}, u32[]{:S(2)}, u32[]{:S(2)}) collective-permute-start(f32[8,128]{1,0:T(8,128)S(1)} %max.15), channel_id=1, source_target_pairs={{0,2},{1,3},{2,4},{3,5},{4,6},{5,7},{6,0},{7,1},{8,10},{9,11},{10,... | collective-permute-start | bytes 12296 | tf_op jit(solution)/shard_map/ppermute | solution.py:404
  88.2 2.3 %collective-permute-done.14 = f32[8,128]{1,0:T(8,128)S(1)} collective-permute-done((f32[8,128]{1,0:T(8,128)S(1)}, f32[8,128]{1,0:T(8,128)S(1)}, u32[]{:S(2)}, u32[]{:S(2)}) %collective-permute-start.14) | collective-permute-done | bytes 4128 | tf_op jit(solution)/shard_map/ppermute | solution.py:404
  90.5 1.1 collective-permute-start.15
  91.6 2.2 %collective-permute-done.15 = f32[8,128]{1,0:T(8,128)S(1)} collective-permute-done((f32[8,128]{1,0:T(8,128)S(1)}, f32[8,128]{1,0:T(8,128)S(1)}, u32[]{:S(2)}, u32[]{:S(2)}) %collective-permute-start.15) | collective-permute-done | bytes 4128 | tf_op jit(solution)/shard_map/ppermute | solution.py:404
  93.8 7.2 %collective-permute-start.16 = (f32[8,128]{1,0:T(8,128)S(1)}, f32[8,128]{1,0:T(8,128)S(1)}, u32[]{:S(2)}, u32[]{:S(2)}) collective-permute-start(f32[8,128]{1,0:T(8,128)S(1)} %max.17), channel_id=1, source_target_pairs={{0,8},{8,16},{16,24},{24,0},{1,9},{9,17},{17,25},{25,1},{2,10},{10... | collective-permute-start | bytes 12296 | tf_op jit(solution)/shard_map/ppermute | solution.py:404
  101.0 0.8 collective-permute-done.16
  101.8 2.4 %collective-permute-done.17 = f32[8,128]{1,0:T(8,128)S(1)} collective-permute-done((f32[8,128]{1,0:T(8,128)S(1)}, f32[8,128]{1,0:T(8,128)S(1)}, u32[]{:S(2)}, u32[]{:S(2)}) %collective-permute-start.17) | collective-permute-done | bytes 4128 | tf_op jit(solution)/shard_map/ppermute | solution.py:404
  104.2 0.2 shard_map.90.near_half.refs_4_
  104.5 1.9 %collective-permute-start.18 = (f32[2,128,512]{2,1,0:T(8,128)S(1)}, f32[2,128,512]{2,1,0:T(8,128)S(1)}, u32[]{:S(2)}, u32[]{:S(2)}) collective-permute-start(f32[2,128,512]{2,1,0:T(8,128)S(1)} %shard_map.90.near_half.refs_4_), channel_id=1, source_target_pairs={{0,8},{8,0},{16,24},{24,16},{1,9},{9,1},{17,25},{25,17},{2,10},{10... | collective-permute-start | bytes 1572872 | tf_op jit(solution)/shard_map/ppermute | solution.py:381
  106.4 0.2 shard_map.92.cross_half.refs_9_
  106.6 3.9 %collective-permute-start.22 = (f32[2,128,512]{2,1,0:T(8,128)S(1)}, f32[2,128,512]{2,1,0:T(8,128)S(1)}, u32[]{:S(2)}, u32[]{:S(2)}) collective-permute-start(f32[2,128,512]{2,1,0:T(8,128)S(1)} %shard_map.92.cross_half.refs_9_), channel_id=1, source_target_pairs={{8,16},{16,8},{9,17},{17,9},{10,18},{18,10},{11,19},{19,11},{12,20... | collective-permute-start | bytes 1572872 | tf_op jit(solution)/shard_map/ppermute | solution.py:381
  110.5 6.7 %collective-permute-done.22.cross_rows = f32[2,128,512]{2,1,0:T(8,128)S(1)} collective-permute-done((f32[2,128,512]{2,1,0:T(8,128)S(1)}, f32[2,128,512]{2,1,0:T(8,128)S(1)}, u32[]{:S(2)}, u32[]{:S(2)}) %collective-permute-start.22) | collective-permute-done | bytes 524320 | tf_op jit(solution)/shard_map/ppermute | solution.py:381
  117.2 4.7 %shard_map.93 = (f32[2,128,512]{2,1,0:T(8,128)S(1)}, f32[2,128,512]{2,1,0:T(8,128)S(1)}, f32[2,128,512]{2,1,0:T(8,128)S(1)}, f32[2,128,512]{2,1,0:T(8,128)S(1)}) custom-call(s32[9,256]{1,0:T(8,128)S(1)} %broadcast_in_dim.2.info, f32[2,128,512]{2,1,0:T(8,128)S(1)} %collective-permute-done.18.near_rows, f32[2,128,512]{2,1,0:T(8,128)S(1)} %collective-permute-done.22.cross_rows, ...), custom_call_target="tpu_custom_call" | custom-call | flops 2415919104 | bytes 6291456 | tf_op jit(solution)/shard_map/pallas_call | solution.py:465
  121.9 0.1 collective-permute-start.23
  122.0 3.6 %collective-permute-start.26 = (f32[2,128,512]{2,1,0:T(8,128)S(1)}, f32[2,128,512]{2,1,0:T(8,128)S(1)}, u32[]{:S(2)}, u32[]{:S(2)}) collective-permute-start(f32[2,128,512]{2,1,0:T(8,128)S(1)} %get-tuple-element.51), channel_id=1, source_target_pairs={{8,16},{16,8},{9,17},{17,9},{10,18},{18,10},{11,19},{19,11},{12,20... | collective-permute-start | bytes 1572872 | tf_op jit(solution)/shard_map/ppermute | solution.py:381
  125.7 2.4 %collective-permute-start.24 = (f32[2,128,128]{2,1,0:T(8,128)S(1)}, f32[2,128,128]{2,1,0:T(8,128)S(1)}, u32[]{:S(2)}, u32[]{:S(2)}) collective-permute-start(f32[2,128,128]{2,1,0:T(8,128)S(1)} %get-tuple-element.48), channel_id=1, source_target_pairs={{0,1},{1,2},{2,3},{3,4},{4,5},{5,6},{6,7},{8,9},{9,10},{10,11},{11... | collective-permute-start | bytes 393224 | tf_op jit(solution)/shard_map/ppermute | solution.py:373
  128.1 1.3 collective-permute-start.25
  129.4 3.3 %collective-permute-done.26.sent = f32[2,128,512]{2,1,0:T(8,128)S(1)} collective-permute-done((f32[2,128,512]{2,1,0:T(8,128)S(1)}, f32[2,128,512]{2,1,0:T(8,128)S(1)}, u32[]{:S(2)}, u32[]{:S(2)}) %collective-permute-start.26) | collective-permute-done | bytes 524320 | tf_op jit(solution)/shard_map/ppermute | solution.py:381
  132.8 2.1 %collective-permute-start.27 = (f32[2,128,128]{2,1,0:T(8,128)S(1)}, f32[2,128,128]{2,1,0:T(8,128)S(1)}, u32[]{:S(2)}, u32[]{:S(2)}) collective-permute-start(f32[2,128,128]{2,1,0:T(8,128)S(1)} %get-tuple-element.53), channel_id=1, source_target_pairs={{0,1},{1,2},{2,3},{3,4},{4,5},{5,6},{6,7},{8,9},{9,10},{10,11},{11... | collective-permute-start | bytes 393224 | tf_op jit(solution)/shard_map/ppermute | solution.py:373
  135.0 1.3 collective-permute-start.28
  136.3 1.0 collective-permute-done.27.refs_6_
  137.3 3.4 %collective-permute-done.28.refs_7_ = f32[2,128,128]{2,1,0:T(8,128)S(1)} collective-permute-done((f32[2,128,128]{2,1,0:T(8,128)S(1)}, f32[2,128,128]{2,1,0:T(8,128)S(1)}, u32[]{:S(2)}, u32[]{:S(2)}) %collective-permute-start.28) | collective-permute-done | bytes 131104 | tf_op jit(solution)/shard_map/ppermute | solution.py:373
  140.7 1.0 shard_map.96
  (53 shorter events, 0.4 us)
Async XLA Ops:
  1.0 1.0 copy-start
  2.1 21.5 %copy-start.1 = (f32[2,256,256]{2,1,0:T(8,128)S(1)}, f32[2,256,256]{2,1,0:T(8,128)}, u32[]{:S(2)}) copy-start(f32[2,256,256]{2,1,0:T(8,128)} %probe.3) | copy-start | bytes 1572868
  2.1 10.7 %collective-permute-start = (f32[2,128,128]{2,1,0:T(8,128)S(1)}, f32[2,128,128]{2,1,0:T(8,128)S(1)}, u32[]{:S(2)}, u32[]{:S(2)}) collective-permute-start(f32[2,128,128]{2,1,0:T(8,128)S(1)} %get-tuple-element.30), channel_id=1, source_target_pairs={{0,1},{1,2},{2,3},{3,4},{4,5},{5,6},{6,7},{8,9},{9,10},{10,11},{11... | collective-permute-start | bytes 393224 | tf_op jit(solution)/shard_map/ppermute | solution.py:373
  6.2 6.6 %collective-permute-start.1 = (f32[2,128,128]{2,1,0:T(8,128)S(1)}, f32[2,128,128]{2,1,0:T(8,128)S(1)}, u32[]{:S(2)}, u32[]{:S(2)}) collective-permute-start(f32[2,128,128]{2,1,0:T(8,128)S(1)} %get-tuple-element.31), channel_id=1, source_target_pairs={{1,0},{2,1},{3,2},{4,3},{5,4},{6,5},{7,6},{9,8},{10,9},{11,10},{12... | collective-permute-start | bytes 393224 | tf_op jit(solution)/shard_map/ppermute | solution.py:373
  7.5 8.7 %collective-permute-start.3 = (f32[2,128,128]{2,1,0:T(8,128)S(1)}, f32[2,128,128]{2,1,0:T(8,128)S(1)}, u32[]{:S(2)}, u32[]{:S(2)}) collective-permute-start(f32[2,128,128]{2,1,0:T(8,128)S(1)} %get-tuple-element.32), channel_id=1, source_target_pairs={{0,1},{1,2},{2,3},{3,4},{4,5},{5,6},{6,7},{8,9},{9,10},{10,11},{11... | collective-permute-start | bytes 393224 | tf_op jit(solution)/shard_map/ppermute | solution.py:373
  11.5 6.4 %collective-permute-start.4 = (f32[2,128,128]{2,1,0:T(8,128)S(1)}, f32[2,128,128]{2,1,0:T(8,128)S(1)}, u32[]{:S(2)}, u32[]{:S(2)}) collective-permute-start(f32[2,128,128]{2,1,0:T(8,128)S(1)} %get-tuple-element.33), channel_id=1, source_target_pairs={{1,0},{2,1},{3,2},{4,3},{5,4},{6,5},{7,6},{9,8},{10,9},{11,10},{12... | collective-permute-start | bytes 393224 | tf_op jit(solution)/shard_map/ppermute | solution.py:373
  12.9 11.8 %copy-start.2 = (f32[1,1,3,256,256]{4,3,2,1,0:T(8,128)S(1)}, f32[1,1,3,256,256]{4,3,2,1,0:T(8,128)}, u32[]{:S(2)}) copy-start(f32[1,1,3,256,256]{4,3,2,1,0:T(8,128)} %amplitude.1) | copy-start | bytes 2359300
  12.9 11.8 %copy-start.9 = (bf16[256,256]{1,0:T(8,128)(2,1)S(1)}, bf16[256,256]{1,0:T(8,128)(2,1)}, u32[]{:S(2)}) copy-start(bf16[256,256]{1,0:T(8,128)(2,1)} %constant.40.clone.pick_back) | copy-start | bytes 393220
  12.9 11.8 %copy-start.10 = (bf16[256,256]{1,0:T(8,128)(2,1)S(1)}, bf16[256,256]{1,0:T(8,128)(2,1)}, u32[]{:S(2)}) copy-start(bf16[256,256]{1,0:T(8,128)(2,1)} %constant.39.clone.pick) | copy-start | bytes 393220
  12.9 12.9 %collective-permute-start.2 = (f32[2,128,512]{2,1,0:T(8,128)S(1)}, f32[2,128,512]{2,1,0:T(8,128)S(1)}, u32[]{:S(2)}, u32[]{:S(2)}) collective-permute-start(f32[2,128,512]{2,1,0:T(8,128)S(1)} %shard_map.83.near_half.old), channel_id=1, source_target_pairs={{0,8},{8,0},{16,24},{24,16},{1,9},{9,1},{17,25},{25,17},{2,10},{10... | collective-permute-start | bytes 1572872 | tf_op jit(solution)/shard_map/ppermute | solution.py:381
  18.0 12.4 %copy-start.11 = (bf16[2,2,256,256]{3,2,1,0:T(8,128)(2,1)S(1)}, bf16[2,2,256,256]{3,2,1,0:T(8,128)(2,1)}, u32[]{:S(2)}) copy-start(bf16[2,2,256,256]{3,2,1,0:T(8,128)(2,1)} %constant.38.clone.backward) | copy-start | bytes 1572868
  18.0 12.4 %copy-start.13 = (bf16[2,2,256,256]{3,2,1,0:T(8,128)(2,1)S(1)}, bf16[2,2,256,256]{3,2,1,0:T(8,128)(2,1)}, u32[]{:S(2)}) copy-start(bf16[2,2,256,256]{3,2,1,0:T(8,128)(2,1)} %constant.37.clone.forward) | copy-start | bytes 1572868
  18.0 12.4 %collective-permute-start.5 = (f32[2,128,512]{2,1,0:T(8,128)S(1)}, f32[2,128,512]{2,1,0:T(8,128)S(1)}, u32[]{:S(2)}, u32[]{:S(2)}) collective-permute-start(f32[2,128,512]{2,1,0:T(8,128)S(1)} %shard_map.84.cross_half.old), channel_id=1, source_target_pairs={{8,16},{16,8},{9,17},{17,9},{10,18},{18,10},{11,19},{19,11},{12,20... | collective-permute-start | bytes 1572872 | tf_op jit(solution)/shard_map/ppermute | solution.py:381
  25.8 10.2 %copy-start.3 = (f32[3,256,256]{2,1,0:T(8,128)}, f32[3,256,256]{2,1,0:T(8,128)S(1)}, u32[]{:S(2)}) copy-start(f32[3,256,256]{2,1,0:T(8,128)S(1)} %shard_map.86.amplitude) | copy-start | bytes 2359300
  36.0 0.8 copy-start.5
  36.8 0.8 copy-start.7
  37.6 5.8 %collective-permute-start.6 = (f32[2,128,512]{2,1,0:T(8,128)}, f32[2,128,512]{2,1,0:T(8,128)}, u32[]{:S(2)}, u32[]{:S(2)}) collective-permute-start(f32[2,128,512]{2,1,0:T(8,128)} %get-tuple-element.35), channel_id=1, source_target_pairs={{0,8},{8,0},{16,24},{24,16},{1,9},{9,1},{17,25},{25,17},{2,10},{10... | collective-permute-start | bytes 1572872 | tf_op jit(solution)/shard_map/ppermute | solution.py:381
  37.6 14.5 %collective-permute-start.19 = (f32[2,128,512]{2,1,0:T(8,128)}, f32[2,128,512]{2,1,0:T(8,128)}, u32[]{:S(2)}, u32[]{:S(2)}) collective-permute-start(f32[2,128,512]{2,1,0:T(8,128)} %get-tuple-element.41), channel_id=1, source_target_pairs={{8,16},{16,8},{9,17},{17,9},{10,18},{18,10},{11,19},{19,11},{12,20... | collective-permute-start | bytes 1572872 | tf_op jit(solution)/shard_map/ppermute | solution.py:381
  41.4 14.1 %collective-permute-start.10 = (s32[6]{0:T(128)S(1)}, s32[6]{0:T(128)S(1)}, u32[]{:S(2)}, u32[]{:S(2)}) collective-permute-start(s32[6]{0:T(128)S(1)} %add.24), channel_id=1, source_target_pairs={{8,16},{16,8},{9,17},{17,9},{10,18},{18,10},{11,19},{19,11},{12,20... | collective-permute-start | bytes 80 | tf_op jit(solution)/shard_map/ppermute | solution.py:381
  43.3 17.1 %collective-permute-start.9 = (s32[6]{0:T(128)S(1)}, s32[6]{0:T(128)S(1)}, u32[]{:S(2)}, u32[]{:S(2)}) collective-permute-start(s32[6]{0:T(128)S(1)} %add.24), channel_id=1, source_target_pairs={{0,8},{8,0},{16,24},{24,16},{1,9},{9,1},{17,25},{25,17},{2,10},{10... | collective-permute-start | bytes 80 | tf_op jit(solution)/shard_map/ppermute | solution.py:381
  43.4 1.0 copy-start.8
  45.6 58.7 %collective-permute-start.8 = (f32[2,128,256]{2,1,0:T(8,128)S(1)}, f32[2,128,256]{2,1,0:T(8,128)S(1)}, u32[]{:S(2)}, u32[]{:S(2)}) collective-permute-start(f32[2,128,256]{2,1,0:T(8,128)S(1)} %get-tuple-element.36.head), channel_id=1, source_target_pairs={{1,0},{2,1},{3,2},{4,3},{5,4},{6,5},{7,6},{9,8},{10,9},{11,10},{12... | collective-permute-start | bytes 786440 | tf_op jit(solution)/shard_map/ppermute | solution.py:373
  46.9 57.4 %collective-permute-start.7 = (f32[2,128,256]{2,1,0:T(8,128)S(1)}, f32[2,128,256]{2,1,0:T(8,128)S(1)}, u32[]{:S(2)}, u32[]{:S(2)}) collective-permute-start(f32[2,128,256]{2,1,0:T(8,128)S(1)} %get-tuple-element.37.tail), channel_id=1, source_target_pairs={{0,1},{1,2},{2,3},{3,4},{4,5},{5,6},{6,7},{8,9},{9,10},{10,11},{11... | collective-permute-start | bytes 786440 | tf_op jit(solution)/shard_map/ppermute | solution.py:373
  52.1 1.0 copy-start.6
  54.2 52.1 %collective-permute-start.21 = (f32[2,128,256]{2,1,0:T(8,128)S(1)}, f32[2,128,256]{2,1,0:T(8,128)S(1)}, u32[]{:S(2)}, u32[]{:S(2)}) collective-permute-start(f32[2,128,256]{2,1,0:T(8,128)S(1)} %get-tuple-element.42.head), channel_id=1, source_target_pairs={{1,0},{2,1},{3,2},{4,3},{5,4},{6,5},{7,6},{9,8},{10,9},{11,10},{12... | collective-permute-start | bytes 786440 | tf_op jit(solution)/shard_map/ppermute | solution.py:373
  55.5 50.8 %collective-permute-start.20 = (f32[2,128,256]{2,1,0:T(8,128)S(1)}, f32[2,128,256]{2,1,0:T(8,128)S(1)}, u32[]{:S(2)}, u32[]{:S(2)}) collective-permute-start(f32[2,128,256]{2,1,0:T(8,128)S(1)} %get-tuple-element.43.tail), channel_id=1, source_target_pairs={{0,1},{1,2},{2,3},{3,4},{4,5},{5,6},{6,7},{8,9},{9,10},{10,11},{11... | collective-permute-start | bytes 786440 | tf_op jit(solution)/shard_map/ppermute | solution.py:373
  60.5 5.2 %collective-permute-start.12 = (s32[18]{0:T(128)S(1)}, s32[18]{0:T(128)S(1)}, u32[]{:S(2)}, u32[]{:S(2)}) collective-permute-start(s32[18]{0:T(128)S(1)} %pad_add_fusion.1.own_spots), channel_id=1, source_target_pairs={{1,0},{2,1},{3,2},{4,3},{5,4},{6,5},{7,6},{9,8},{10,9},{11,10},{12... | collective-permute-start | bytes 224 | tf_op jit(solution)/shard_map/ppermute | solution.py:373
  65.7 8.2 %collective-permute-start.11 = (s32[18]{0:T(128)S(1)}, s32[18]{0:T(128)S(1)}, u32[]{:S(2)}, u32[]{:S(2)}) collective-permute-start(s32[18]{0:T(128)S(1)} %pad_add_fusion.1.own_spots), channel_id=1, source_target_pairs={{0,1},{1,2},{2,3},{3,4},{4,5},{5,6},{6,7},{8,9},{9,10},{10,11},{11... | collective-permute-start | bytes 224 | tf_op jit(solution)/shard_map/ppermute | solution.py:373
  77.6 6.9 %collective-permute-start.13 = (f32[8,128]{1,0:T(8,128)S(1)}, f32[8,128]{1,0:T(8,128)S(1)}, u32[]{:S(2)}, u32[]{:S(2)}) collective-permute-start(f32[8,128]{1,0:T(8,128)S(1)} %get-tuple-element.39), channel_id=1, source_target_pairs={{0,1},{1,2},{2,3},{3,4},{4,5},{5,6},{6,7},{7,0},{8,9},{9,10},{10,1... | collective-permute-start | bytes 12296 | tf_op jit(solution)/shard_map/ppermute | solution.py:404
  84.5 6.0 %collective-permute-start.14 = (f32[8,128]{1,0:T(8,128)S(1)}, f32[8,128]{1,0:T(8,128)S(1)}, u32[]{:S(2)}, u32[]{:S(2)}) collective-permute-start(f32[8,128]{1,0:T(8,128)S(1)} %max.15), channel_id=1, source_target_pairs={{0,2},{1,3},{2,4},{3,5},{4,6},{5,7},{6,0},{7,1},{8,10},{9,11},{10,... | collective-permute-start | bytes 12296 | tf_op jit(solution)/shard_map/ppermute | solution.py:404
  90.5 3.4 %collective-permute-start.15 = (f32[8,128]{1,0:T(8,128)S(1)}, f32[8,128]{1,0:T(8,128)S(1)}, u32[]{:S(2)}, u32[]{:S(2)}) collective-permute-start(f32[8,128]{1,0:T(8,128)S(1)} %max.16), channel_id=1, source_target_pairs={{0,4},{1,5},{2,6},{3,7},{4,0},{5,1},{6,2},{7,3},{8,12},{9,13},{10,... | collective-permute-start | bytes 12296 | tf_op jit(solution)/shard_map/ppermute | solution.py:404
  93.8 7.9 %collective-permute-start.16 = (f32[8,128]{1,0:T(8,128)S(1)}, f32[8,128]{1,0:T(8,128)S(1)}, u32[]{:S(2)}, u32[]{:S(2)}) collective-permute-start(f32[8,128]{1,0:T(8,128)S(1)} %max.17), channel_id=1, source_target_pairs={{0,8},{8,16},{16,24},{24,0},{1,9},{9,17},{17,25},{25,1},{2,10},{10... | collective-permute-start | bytes 12296 | tf_op jit(solution)/shard_map/ppermute | solution.py:404
  101.8 2.5 %collective-permute-start.17 = (f32[8,128]{1,0:T(8,128)S(1)}, f32[8,128]{1,0:T(8,128)S(1)}, u32[]{:S(2)}, u32[]{:S(2)}) collective-permute-start(f32[8,128]{1,0:T(8,128)S(1)} %max.18), channel_id=1, source_target_pairs={{0,16},{8,24},{16,0},{24,8},{1,17},{9,25},{17,1},{25,9},{2,18},{10... | collective-permute-start | bytes 12296 | tf_op jit(solution)/shard_map/ppermute | solution.py:404
  104.5 12.7 %copy-start.4 = (f32[3,256,256]{2,1,0:T(8,128)S(1)}, f32[3,256,256]{2,1,0:T(8,128)}, u32[]{:S(2)}) copy-start(f32[3,256,256]{2,1,0:T(8,128)} %copy-done.3) | copy-start | bytes 2359300
  104.5 12.7 %copy-start.12 = (bf16[2,2,256,256]{3,2,1,0:T(8,128)(2,1)S(1)}, bf16[2,2,256,256]{3,2,1,0:T(8,128)(2,1)}, u32[]{:S(2)}) copy-start(bf16[2,2,256,256]{3,2,1,0:T(8,128)(2,1)} %constant.38.clone.backward) | copy-start | bytes 1572868
  104.5 12.7 %copy-start.14 = (bf16[2,2,256,256]{3,2,1,0:T(8,128)(2,1)S(1)}, bf16[2,2,256,256]{3,2,1,0:T(8,128)(2,1)}, u32[]{:S(2)}) copy-start(bf16[2,2,256,256]{3,2,1,0:T(8,128)(2,1)} %constant.37.clone.forward) | copy-start | bytes 1572868
  104.5 6.0 %collective-permute-start.18 = (f32[2,128,512]{2,1,0:T(8,128)S(1)}, f32[2,128,512]{2,1,0:T(8,128)S(1)}, u32[]{:S(2)}, u32[]{:S(2)}) collective-permute-start(f32[2,128,512]{2,1,0:T(8,128)S(1)} %shard_map.90.near_half.refs_4_), channel_id=1, source_target_pairs={{0,8},{8,0},{16,24},{24,16},{1,9},{9,1},{17,25},{25,17},{2,10},{10... | collective-permute-start | bytes 1572872 | tf_op jit(solution)/shard_map/ppermute | solution.py:381
  106.6 10.6 %collective-permute-start.22 = (f32[2,128,512]{2,1,0:T(8,128)S(1)}, f32[2,128,512]{2,1,0:T(8,128)S(1)}, u32[]{:S(2)}, u32[]{:S(2)}) collective-permute-start(f32[2,128,512]{2,1,0:T(8,128)S(1)} %shard_map.92.cross_half.refs_9_), channel_id=1, source_target_pairs={{8,16},{16,8},{9,17},{17,9},{10,18},{18,10},{11,19},{19,11},{12,20... | collective-permute-start | bytes 1572872 | tf_op jit(solution)/shard_map/ppermute | solution.py:381
  121.9 3.7 %collective-permute-start.23 = (f32[2,128,512]{2,1,0:T(8,128)S(1)}, f32[2,128,512]{2,1,0:T(8,128)S(1)}, u32[]{:S(2)}, u32[]{:S(2)}) collective-permute-start(f32[2,128,512]{2,1,0:T(8,128)S(1)} %get-tuple-element.46), channel_id=1, source_target_pairs={{0,8},{8,0},{16,24},{24,16},{1,9},{9,1},{17,25},{25,17},{2,10},{10... | collective-permute-start | bytes 1572872 | tf_op jit(solution)/shard_map/ppermute | solution.py:381
  122.0 10.8 %collective-permute-start.26 = (f32[2,128,512]{2,1,0:T(8,128)S(1)}, f32[2,128,512]{2,1,0:T(8,128)S(1)}, u32[]{:S(2)}, u32[]{:S(2)}) collective-permute-start(f32[2,128,512]{2,1,0:T(8,128)S(1)} %get-tuple-element.51), channel_id=1, source_target_pairs={{8,16},{16,8},{9,17},{17,9},{10,18},{18,10},{11,19},{19,11},{12,20... | collective-permute-start | bytes 1572872 | tf_op jit(solution)/shard_map/ppermute | solution.py:381
  125.7 10.6 %collective-permute-start.24 = (f32[2,128,128]{2,1,0:T(8,128)S(1)}, f32[2,128,128]{2,1,0:T(8,128)S(1)}, u32[]{:S(2)}, u32[]{:S(2)}) collective-permute-start(f32[2,128,128]{2,1,0:T(8,128)S(1)} %get-tuple-element.48), channel_id=1, source_target_pairs={{0,1},{1,2},{2,3},{3,4},{4,5},{5,6},{6,7},{8,9},{9,10},{10,11},{11... | collective-permute-start | bytes 393224 | tf_op jit(solution)/shard_map/ppermute | solution.py:373
  128.1 8.1 %collective-permute-start.25 = (f32[2,128,128]{2,1,0:T(8,128)S(1)}, f32[2,128,128]{2,1,0:T(8,128)S(1)}, u32[]{:S(2)}, u32[]{:S(2)}) collective-permute-start(f32[2,128,128]{2,1,0:T(8,128)S(1)} %get-tuple-element.49), channel_id=1, source_target_pairs={{1,0},{2,1},{3,2},{4,3},{5,4},{6,5},{7,6},{9,8},{10,9},{11,10},{12... | collective-permute-start | bytes 393224 | tf_op jit(solution)/shard_map/ppermute | solution.py:373
  132.8 4.4 %collective-permute-start.27 = (f32[2,128,128]{2,1,0:T(8,128)S(1)}, f32[2,128,128]{2,1,0:T(8,128)S(1)}, u32[]{:S(2)}, u32[]{:S(2)}) collective-permute-start(f32[2,128,128]{2,1,0:T(8,128)S(1)} %get-tuple-element.53), channel_id=1, source_target_pairs={{0,1},{1,2},{2,3},{3,4},{4,5},{5,6},{6,7},{8,9},{9,10},{10,11},{11... | collective-permute-start | bytes 393224 | tf_op jit(solution)/shard_map/ppermute | solution.py:373
  135.0 5.7 %collective-permute-start.28 = (f32[2,128,128]{2,1,0:T(8,128)S(1)}, f32[2,128,128]{2,1,0:T(8,128)S(1)}, u32[]{:S(2)}, u32[]{:S(2)}) collective-permute-start(f32[2,128,128]{2,1,0:T(8,128)S(1)} %get-tuple-element.54), channel_id=1, source_target_pairs={{1,0},{2,1},{3,2},{4,3},{5,4},{6,5},{7,6},{9,8},{10,9},{11,10},{12... | collective-permute-start | bytes 393224 | tf_op jit(solution)/shard_map/ppermute | solution.py:373

commit v4 on v3

--- a/solution.py
+++ b/solution.py
@@ -184,76 +184,64 @@
             (1, probe_real * imag - probe_imag * real),
         ):
             spread(piece, low, near, total.at[plane], position == 0)
-    outs = (grad_near, mid_near, mid_cross, grad_cross)
+    whole = slice(None)
     for plane in (0, 1):
-        for left in (0, 1):
-            lanes = slice(left * win, (left + 1) * win)
-            parts = [
-                total[plane, 2 * (k // 2) + left, (k % 2) * half : (k % 2 + 1) * half]
-                for k in range(4)
-            ]
-            for index in range(4):
-                outs[index][plane, :, lanes] = jnp.where(
-                    odd_row, parts[index], parts[3 - index]
-                )
-
-
-def light_kernel(
-    own_spots, left_spots, right_spots, info, probe, light_near, light_cross, largest, quadrants
-):
-    win = probe.shape[1]
-    half = win // 2
-    count = own_spots.shape[0] // 6
-    odd_row = flag(info, ODD)
-    real, imag = probe[0], probe[1]
-    intensity = real * real + imag * imag
-    quadrants[...] = jnp.zeros_like(quadrants)
-    rows = lax.broadcasted_iota(jnp.int32, (half, win), 0)
-    columns = lax.broadcasted_iota(jnp.int32, (half, win), 1)
-
-    for row_side in (-1, 0, 1):
-        for column_side, spots in ((-1, left_spots), (0, own_spots), (1, right_spots)):
-            base = (row_side + 1) * 2 * count
-
-            @pl.when(spots[base] > 0)
-            def _():
-                def one(position, carry):
-                    row = spots[base + 2 * position] - 1
-                    column = spots[base + 2 * position + 1] - 1
-                    block = pltpu.roll(intensity, lax.rem(row, win), 0)
-                    turn = lax.rem(column, win)
-                    for lower in (0, 1):
-                        if (row_side < 0 and lower) or (row_side > 0 and not lower):
-                            continue
-                        part = block[:half] if lower else block[half:]
-                        part = pltpu.roll(part, turn, 1)
-                        index = rows if lower else rows + half
-                        if row_side < 0 or (row_side == 0 and lower):
-                            keep = index < row
-                        else:
-                            keep = index >= row
-                        part = jnp.where(keep, part, 0.0)
-                        if column_side <= 0:
-                            near = columns < column if column_side else columns >= column
-                            quadrants[2 * lower] = quadrants[2 * lower] + jnp.where(near, part, 0.0)
-                        if column_side >= 0:
-                            far = columns >= column if column_side else columns < column
-                            quadrants[2 * lower + 1] = quadrants[2 * lower + 1] + jnp.where(far, part, 0.0)
-                    return carry
-
-                lax.fori_loop(0, count, one, 0)
-
-    found = None
+        by_halves(
+            odd_row, total, plane,
+            [(out, whole) for out in (grad_near, mid_near, mid_cross, grad_cross)],
+        )
+
+
+def by_halves(odd_row, total, plane, outs):
+    half, win = total.shape[2] // 2, total.shape[3]
     for left in (0, 1):
         lanes = slice(left * win, (left + 1) * win)
-        upper, lower = quadrants[left], quadrants[2 + left]
-        light_near[:, lanes] = jnp.where(odd_row, upper, lower)
-        light_cross[:, lanes] = jnp.where(odd_row, lower, upper)
-        best = jnp.maximum(upper, lower)
-        best = best[:, : win - HALO] if left else best[:, HALO:]
-        for row in range(0, half, 8):
-            block = best[row : row + 8]
-            found = block if found is None else jnp.maximum(found, block)
+        parts = [
+            total[plane, 2 * (k // 2) + left, (k % 2) * half : (k % 2 + 1) * half]
+            for k in range(4)
+        ]
+        for index, (out, rows) in enumerate(outs):
+            out[plane, rows, lanes] = jnp.where(odd_row, parts[index], parts[3 - index])
+
+
+def light_kernel(info, probe, light_near, light_mid, light_cross, total):
+    win = probe.shape[2]
+    half = win // 2
+    for position in range(probe.shape[0]):
+        low, near = window_masks(info, position, win)
+        real, imag = probe[position, 0], probe[position, 1]
+        spread(real * real + imag * imag, low, near, total.at[0], position == 0)
+    whole = slice(None)
+    by_halves(
+        flag(info, ODD), total, 0,
+        (
+            (light_near, whole), (light_mid, slice(0, half)),
+            (light_mid, slice(half, win)), (light_cross, whole),
+        ),
+    )
+
+
+def light_fold_kernel(mid, sent_near, sent_cross, head, tail):
+    half, side = sent_near.shape[1], head.shape[2]
+    for rows, sent in ((slice(0, half), sent_near), (slice(half, None), sent_cross)):
+        block = mid[0, rows] + sent[0]
+        head[0, rows] = block[:, :side]
+        tail[0, rows] = block[:, side:]
+
+
+def light_sum_kernel(head, tail, from_left, from_right, light_near, light_cross, largest):
+    side = head.shape[2]
+    half = light_near.shape[0]
+    left, right = head[0] + from_left[0], tail[0] + from_right[0]
+    for out, rows in ((light_near, slice(0, half)), (light_cross, slice(half, None))):
+        out[:, :side] = left[rows]
+        out[:, side:] = right[rows]
+    found = None
+    for best in (left[:, HALO:], right[:, : side - HALO]):
+        for row in range(0, best.shape[0], 8):
+            for lane in range(0, best.shape[1], LANES):
+                block = best[row : row + 8, lane : lane + LANES]
+                found = block if found is None else jnp.maximum(found, block)
     largest[...] = found
 
 
@@ -278,28 +266,24 @@
         )
 
 
-def edges_kernel(info, specimen, near_head, near_tail, cross_head, cross_tail):
-    odd_row = info[ODD : ODD + 1, :HALO] > 0
-    half = near_head.shape[1]
+def edges_kernel(specimen, head, tail):
+    head[...] = specimen[:, :, :HALO]
+    tail[...] = specimen[:, :, specimen.shape[2] - HALO :]
+
+
+def widen_kernel(info, before, specimen, after, near_half, cross_half):
+    odd_row = flag(info, ODD)
+    narrow = odd_row[:, :HALO]
+    half, tile = near_half.shape[1], specimen.shape[2]
     for plane in (0, 1):
-        for lanes, near, cross in (
-            (slice(0, HALO), near_head, cross_head),
-            (slice(specimen.shape[2] - HALO, None), near_tail, cross_tail),
+        for source, lanes, odd in (
+            (before, slice(0, HALO), narrow),
+            (specimen, slice(HALO, HALO + tile), odd_row),
+            (after, slice(HALO + tile, None), narrow),
         ):
-            top, bottom = specimen[plane, :half, lanes], specimen[plane, half:, lanes]
-            near[plane] = jnp.where(odd_row, top, bottom)
-            cross[plane] = jnp.where(odd_row, bottom, top)
-
-
-def widen_kernel(info, before, specimen, after, out, *, near):
-    odd_row = flag(info, ODD)
-    half, tile = out.shape[1], specimen.shape[2]
-    for plane in (0, 1):
-        top, bottom = specimen[plane, :half], specimen[plane, half:]
-        own = jnp.where(odd_row, top, bottom) if near else jnp.where(odd_row, bottom, top)
-        out[plane, :, :HALO] = before[plane]
-        out[plane, :, HALO : HALO + tile] = own
-        out[plane, :, HALO + tile :] = after[plane]
+            top, bottom = source[plane, :half], source[plane, half:]
+            near_half[plane, :, lanes] = jnp.where(odd, top, bottom)
+            cross_half[plane, :, lanes] = jnp.where(odd, bottom, top)
 
 
 def fold_kernel(mid, sent, head, tail):
@@ -422,43 +406,38 @@
     )
     band, wide, strip = shape(2, half, HALO), shape(2, half, 2 * side), shape(2, half, side)
 
-    near_head, near_tail, cross_head, cross_tail = kernel_call(
-        edges_kernel, [band] * 4, [VM] * 2
-    )(info, specimen)
-    cross_sides = to_sides(cross_head, cross_tail)
-    near_sides = to_sides(near_head, near_tail)
-
-    spots = corners + 1
-    spots_cross, spots_near = to_cross(spots), to_near(spots)
-    spots = jnp.concatenate(
-        [
-            jnp.where(odd > 0, spots_near, spots_cross),
-            spots,
-            jnp.where(odd > 0, spots_cross, spots_near),
-        ]
-    )
-    spots_left, spots_right = to_sides(spots, spots)
-
-    def widened(sides, near):
-        return kernel_call(
-            functools.partial(widen_kernel, near=near), [wide], [VM] * 4
-        )(info, sides[0], specimen, sides[1])
-
-    cross_half = widened(cross_sides, False)
-    cross_rows = to_cross(cross_half)
-    near_half = widened(near_sides, True)
-    near_rows = to_near(near_half)
+    head, tail = kernel_call(edges_kernel, [shape(2, tile, HALO)] * 2, [VM])(
+        specimen
+    )
+    before, after = to_sides(head, tail)
 
     probes = kernel_call(roll_kernel, [shape(count, 2, win, win)], [SM, VM])(corners, probe_field)
+    light_band = shape(1, half, 2 * side)
+    light_near, light_mid, light_cross = kernel_call(
+        light_kernel,
+        [light_band, shape(1, tile, 2 * side), light_band],
+        [VM] * 2,
+        scratch=[pltpu.VMEM((1, 4, win, win), F32)],
+    )(info, probes)
+    light_cross = to_cross(light_cross)
+    light_near = to_near(light_near)
     ordered = kernel_call(order_kernel, [shape(count, win, win)], [VM] * 3)(
         amplitudes, pick, pick_back
     )
+
+    near_half, cross_half = kernel_call(widen_kernel, [wide] * 2, [VM] * 4)(
+        info, before, specimen, after
+    )
+    cross_rows = to_cross(cross_half)
+    near_rows = to_near(near_half)
+
+    head, tail = kernel_call(
+        light_fold_kernel, [shape(1, tile, side)] * 2, [VM] * 3
+    )(light_mid, light_near, light_cross)
+    from_left, from_right = to_sides(head, tail)
     light_near, light_cross, found = kernel_call(
-        light_kernel,
-        [shape(half, 2 * side)] * 2 + [shape(8, LANES)],
-        [SM] * 3 + [VM] * 2,
-        scratch=[pltpu.VMEM((4, half, win), F32)],
-    )(spots, spots_left, spots_right, info, probe_field)
+        light_sum_kernel, [shape(half, 2 * side)] * 2 + [shape(8, LANES)], [VM] * 4
+    )(head, tail, from_left, from_right)
     peak = largest_of(found, ("col", "row"))
 
     for step in range(ITERS):

time: 144 us -> 132 us (0.917)
  starting transfers between devices: 75.9 us -> 64.3 us
  waiting for transfers between devices: 39.1 us -> 48.9 us
  Pallas kernels: 20.1 us -> 14 us
  local copies, waits for them, and re-layouts: 5.19 us -> 2.36 us
    ppermute x5, starting transfers between devices: 17.8 us -> 9.71 us  [largest_of(): block = jnp.maximum(block, lax.ppermute(block, axis, route))]
    ppermute x10, waiting for transfers between devices: 14.6 us -> 22.4 us  [swapped(): return lax.ppermute(block, axis, route)]
    ppermute x14 -> x12, starting transfers between devices: 36 us -> 32.6 us  [shifted(): return lax.ppermute(block, axis, route)]
    pallas_call x4 -> x5, Pallas kernels: 3.8 us -> 0.75 us  [the longest x1 0.48 us: steps(): kernel_call(light_kernel, [light_band, shape(1, tile, 2 * side), light_ba...]
    ppermute x5, waiting for transfers between devices: 8.85 us -> 11.7 us  [largest_of(): block = jnp.maximum(block, lax.ppermute(block, axis, route))]
    unnamed x30 -> x16, local copies, waits for them, and re-layouts: 4.76 us -> 2.11 us
    pallas_call x2, Pallas kernels: 2.2 us -> 0.12 us  [steps(): head, tail = kernel_call(fold_kernel, [strip] * 2, [VM] * 2)(mid, sent)]
    ppermute x14 -> x12, waiting for transfers between devices: 15.7 us -> 14.8 us  [shifted(): return lax.ppermute(block, axis, route)]
  transfers between devices with their start and end apart: 29 -> 27, of which waited for: 14 -> 14; matrix products, arithmetic and copies ran while one was open for 0% -> 1% of each run, Pallas kernels for 6% -> 3%
where the time goes in v4:
time: 132 us; the launch traced here: 131 us
  starting transfers between devices  64.3 us (49%)
  waiting for transfers between devices  48.9 us (37%)
  Pallas kernels  14 us (11%)
  local copies, waits for them, and re-layouts  2.36 us (2%)
    ppermute x12, starting transfers between devices, shifted(): return lax.ppermute(block, axis, route)  32.6 us
    ppermute x10, waiting for transfers between devices, swapped(): return lax.ppermute(block, axis, route)  22.4 us
    ppermute x10, starting transfers between devices, swapped(): return lax.ppermute(block, axis, route)  22 us
    ppermute x12, waiting for transfers between devices, shifted(): return lax.ppermute(block, axis, route)  14.8 us
    ppermute x5, waiting for transfers between devices, largest_of(): block = jnp.maximum(block, lax.ppermute(block, axis, route))  11.7 us
    ppermute x5, starting transfers between devices, largest_of(): block = jnp.maximum(block, lax.ppermute(block, axis, route))  9.71 us
    pallas_call x2, Pallas kernels, steps(): kernel_call(gradient_kernel, [wide] * 4, [VM] * 9, flops=count * 8 * 2 *...  9.34 us
  transfers between devices with their start and end apart: 27, of which 14 were waited for; matrix products, arithmetic and copies ran while one was open for 1% of the time, Pallas kernels for 3%

profile of v4, /device:TPU:1, one launch (start us, length us, event | category | flops | bytes accessed | tf_op | source)
XLA Modules:
  0.0 130.7 jit_solution(11143733587495873255)
XLA Ops:
  0.0 1.0 copy-done
  1.1 4.1 %collective-permute-start = (f32[2,256,128]{2,1,0:T(8,128)S(1)}, f32[2,256,128]{2,1,0:T(8,128)S(1)}, u32[]{:S(2)}, u32[]{:S(2)}) collective-permute-start(f32[2,256,128]{2,1,0:T(8,128)S(1)} %get-tuple-element.35), channel_id=1, source_target_pairs={{0,1},{1,2},{2,3},{3,4},{4,5},{5,6},{6,7},{8,9},{9,10},{10,11},{11... | collective-permute-start | bytes 786440 | tf_op jit(solution)/shard_map/ppermute | solution.py:357
  5.2 1.3 collective-permute-start.1
  6.5 0.7 broadcast_add_fusion
  7.2 0.1 copy.10
  7.3 0.1 add.11.corners
  7.4 0.1 pad_add_fusion
  7.5 2.6 %collective-permute-done.before = f32[2,256,128]{2,1,0:T(8,128)S(1)} collective-permute-done((f32[2,256,128]{2,1,0:T(8,128)S(1)}, f32[2,256,128]{2,1,0:T(8,128)S(1)}, u32[]{:S(2)}, u32[]{:S(2)}) %collective-permute-start) | collective-permute-done | bytes 262176 | tf_op jit(solution)/shard_map/ppermute | solution.py:357
  10.0 4.0 %collective-permute-done.1.after = f32[2,256,128]{2,1,0:T(8,128)S(1)} collective-permute-done((f32[2,256,128]{2,1,0:T(8,128)S(1)}, f32[2,256,128]{2,1,0:T(8,128)S(1)}, u32[]{:S(2)}, u32[]{:S(2)}) %collective-permute-start.1) | collective-permute-done | bytes 262176 | tf_op jit(solution)/shard_map/ppermute | solution.py:357
  14.0 0.1 broadcast_in_dim.2.info
  14.1 1.0 copy-done.1
  15.1 0.1 shard_map.83
  15.2 3.4 %collective-permute-start.2 = (f32[2,128,512]{2,1,0:T(8,128)S(1)}, f32[2,128,512]{2,1,0:T(8,128)S(1)}, u32[]{:S(2)}, u32[]{:S(2)}) collective-permute-start(f32[2,128,512]{2,1,0:T(8,128)S(1)} %get-tuple-element.37.near_half.old), channel_id=1, source_target_pairs={{0,8},{8,0},{16,24},{24,16},{1,9},{9,1},{17,25},{25,17},{2,10},{10... | collective-permute-start | bytes 1572872 | tf_op jit(solution)/shard_map/ppermute | solution.py:365
  18.6 3.2 %collective-permute-start.3 = (f32[2,128,512]{2,1,0:T(8,128)S(1)}, f32[2,128,512]{2,1,0:T(8,128)S(1)}, u32[]{:S(2)}, u32[]{:S(2)}) collective-permute-start(f32[2,128,512]{2,1,0:T(8,128)S(1)} %get-tuple-element.38.cross_half.old), channel_id=1, source_target_pairs={{8,16},{16,8},{9,17},{17,9},{10,18},{18,10},{11,19},{19,11},{12,20... | collective-permute-start | bytes 1572872 | tf_op jit(solution)/shard_map/ppermute | solution.py:365
  21.8 1.2 shard_map.84.probe
  23.0 1.0 shard_map.85.amplitude
  24.1 5.2 %collective-permute-done.3.cross_rows = f32[2,128,512]{2,1,0:T(8,128)S(1)} collective-permute-done((f32[2,128,512]{2,1,0:T(8,128)S(1)}, f32[2,128,512]{2,1,0:T(8,128)S(1)}, u32[]{:S(2)}, u32[]{:S(2)}) %collective-permute-start.3) | collective-permute-done | bytes 524320 | tf_op jit(solution)/shard_map/ppermute | solution.py:365
  29.2 4.7 %shard_map.86 = (f32[2,128,512]{2,1,0:T(8,128)S(1)}, f32[2,128,512]{2,1,0:T(8,128)S(1)}, f32[2,128,512]{2,1,0:T(8,128)S(1)}, f32[2,128,512]{2,1,0:T(8,128)S(1)}) custom-call(s32[9,256]{1,0:T(8,128)S(1)} %broadcast_in_dim.2.info, f32[2,128,512]{2,1,0:T(8,128)S(1)} %collective-permute-done.2.near_rows, f32[2,128,512]{2,1,0:T(8,128)S(1)} %collective-permute-done.3.cross_rows, ...), custom_call_target="tpu_custom_call" | custom-call | flops 2415919104 | bytes 6291456 | tf_op jit(solution)/shard_map/pallas_call | solution.py:444
  33.9 0.1 collective-permute-start.4
  34.0 0.5 shard_map.88
  34.5 0.6 collective-permute-start.7
  35.0 3.0 %collective-permute-start.17 = (f32[2,128,512]{2,1,0:T(8,128)S(1)}, f32[2,128,512]{2,1,0:T(8,128)S(1)}, u32[]{:S(2)}, u32[]{:S(2)}) collective-permute-start(f32[2,128,512]{2,1,0:T(8,128)S(1)} %get-tuple-element.51), channel_id=1, source_target_pairs={{8,16},{16,8},{9,17},{17,9},{10,18},{18,10},{11,19},{19,11},{12,20... | collective-permute-start | bytes 1572872 | tf_op jit(solution)/shard_map/ppermute | solution.py:365
  38.1 2.5 %collective-permute-start.8 = (f32[1,128,512]{2,1,0:T(8,128)S(1)}, f32[1,128,512]{2,1,0:T(8,128)S(1)}, u32[]{:S(2)}, u32[]{:S(2)}) collective-permute-start(f32[1,128,512]{2,1,0:T(8,128)S(1)} %get-tuple-element.45), channel_id=1, source_target_pairs={{8,16},{16,8},{9,17},{17,9},{10,18},{18,10},{11,19},{19,11},{12,20... | collective-permute-start | bytes 786440 | tf_op jit(solution)/shard_map/ppermute | solution.py:365
  40.6 0.0 collective-permute-done.7.sent_near
  40.6 7.7 %collective-permute-done.8.sent_cross = f32[1,128,512]{2,1,0:T(8,128)S(1)} collective-permute-done((f32[1,128,512]{2,1,0:T(8,128)S(1)}, f32[1,128,512]{2,1,0:T(8,128)S(1)}, u32[]{:S(2)}, u32[]{:S(2)}) %collective-permute-start.8) | collective-permute-done | bytes 262176 | tf_op jit(solution)/shard_map/ppermute | solution.py:365
  48.3 0.1 shard_map.89
  48.4 1.3 collective-permute-start.10
  49.7 4.8 %collective-permute-start.9 = (f32[1,256,256]{2,1,0:T(8,128)S(1)}, f32[1,256,256]{2,1,0:T(8,128)S(1)}, u32[]{:S(2)}, u32[]{:S(2)}) collective-permute-start(f32[1,256,256]{2,1,0:T(8,128)S(1)} %get-tuple-element.47.tail), channel_id=1, source_target_pairs={{0,1},{1,2},{2,3},{3,4},{4,5},{5,6},{6,7},{8,9},{9,10},{10,11},{11... | collective-permute-start | bytes 786440 | tf_op jit(solution)/shard_map/ppermute | solution.py:357
  54.5 0.1 shard_map.87
  54.5 1.3 collective-permute-start.6
  55.8 5.0 %collective-permute-start.5 = (f32[2,128,256]{2,1,0:T(8,128)S(1)}, f32[2,128,256]{2,1,0:T(8,128)S(1)}, u32[]{:S(2)}, u32[]{:S(2)}) collective-permute-start(f32[2,128,256]{2,1,0:T(8,128)S(1)} %get-tuple-element.42.tail), channel_id=1, source_target_pairs={{0,1},{1,2},{2,3},{3,4},{4,5},{5,6},{6,7},{8,9},{9,10},{10,11},{11... | collective-permute-start | bytes 786440 | tf_op jit(solution)/shard_map/ppermute | solution.py:357
  60.8 0.1 shard_map.92
  60.9 1.3 collective-permute-start.19
  62.2 4.9 %collective-permute-start.18 = (f32[2,128,256]{2,1,0:T(8,128)S(1)}, f32[2,128,256]{2,1,0:T(8,128)S(1)}, u32[]{:S(2)}, u32[]{:S(2)}) collective-permute-start(f32[2,128,256]{2,1,0:T(8,128)S(1)} %get-tuple-element.53.tail), channel_id=1, source_target_pairs={{0,1},{1,2},{2,3},{3,4},{4,5},{5,6},{6,7},{8,9},{9,10},{10,11},{11... | collective-permute-start | bytes 786440 | tf_op jit(solution)/shard_map/ppermute | solution.py:357
  67.1 3.8 %collective-permute-done.9.from_left = f32[1,256,256]{2,1,0:T(8,128)S(1)} collective-permute-done((f32[1,256,256]{2,1,0:T(8,128)S(1)}, f32[1,256,256]{2,1,0:T(8,128)S(1)}, u32[]{:S(2)}, u32[]{:S(2)}) %collective-permute-start.9) | collective-permute-done | bytes 262176 | tf_op jit(solution)/shard_map/ppermute | solution.py:357
  70.9 0.1 shard_map.90
  71.0 4.1 %collective-permute-start.11 = (f32[8,128]{1,0:T(8,128)S(1)}, f32[8,128]{1,0:T(8,128)S(1)}, u32[]{:S(2)}, u32[]{:S(2)}) collective-permute-start(f32[8,128]{1,0:T(8,128)S(1)} %get-tuple-element.49), channel_id=1, source_target_pairs={{0,1},{1,2},{2,3},{3,4},{4,5},{5,6},{6,7},{7,0},{8,9},{9,10},{10,1... | collective-permute-start | bytes 12296 | tf_op jit(solution)/shard_map/ppermute | solution.py:388
  75.1 2.5 %collective-permute-done.11 = f32[8,128]{1,0:T(8,128)S(1)} collective-permute-done((f32[8,128]{1,0:T(8,128)S(1)}, f32[8,128]{1,0:T(8,128)S(1)}, u32[]{:S(2)}, u32[]{:S(2)}) %collective-permute-start.11) | collective-permute-done | bytes 4128 | tf_op jit(solution)/shard_map/ppermute | solution.py:388
  77.6 2.4 %collective-permute-start.12 = (f32[8,128]{1,0:T(8,128)S(1)}, f32[8,128]{1,0:T(8,128)S(1)}, u32[]{:S(2)}, u32[]{:S(2)}) collective-permute-start(f32[8,128]{1,0:T(8,128)S(1)} %max.15), channel_id=1, source_target_pairs={{0,2},{1,3},{2,4},{3,5},{4,6},{5,7},{6,0},{7,1},{8,10},{9,11},{10,... | collective-permute-start | bytes 12296 | tf_op jit(solution)/shard_map/ppermute | solution.py:388
  80.0 3.0 %collective-permute-done.12 = f32[8,128]{1,0:T(8,128)S(1)} collective-permute-done((f32[8,128]{1,0:T(8,128)S(1)}, f32[8,128]{1,0:T(8,128)S(1)}, u32[]{:S(2)}, u32[]{:S(2)}) %collective-permute-start.12) | collective-permute-done | bytes 4128 | tf_op jit(solution)/shard_map/ppermute | solution.py:388
  83.1 0.4 collective-permute-start.13
  83.5 2.9 %collective-permute-done.13 = f32[8,128]{1,0:T(8,128)S(1)} collective-permute-done((f32[8,128]{1,0:T(8,128)S(1)}, f32[8,128]{1,0:T(8,128)S(1)}, u32[]{:S(2)}, u32[]{:S(2)}) %collective-permute-start.13) | collective-permute-done | bytes 4128 | tf_op jit(solution)/shard_map/ppermute | solution.py:388
  86.4 2.8 %collective-permute-start.14 = (f32[8,128]{1,0:T(8,128)S(1)}, f32[8,128]{1,0:T(8,128)S(1)}, u32[]{:S(2)}, u32[]{:S(2)}) collective-permute-start(f32[8,128]{1,0:T(8,128)S(1)} %max.17), channel_id=1, source_target_pairs={{0,8},{8,16},{16,24},{24,0},{1,9},{9,17},{17,25},{25,1},{2,10},{10... | collective-permute-start | bytes 12296 | tf_op jit(solution)/shard_map/ppermute | solution.py:388
  89.2 0.8 collective-permute-done.14
  90.0 0.0 collective-permute-start.15
  90.0 2.4 %collective-permute-done.15 = f32[8,128]{1,0:T(8,128)S(1)} collective-permute-done((f32[8,128]{1,0:T(8,128)S(1)}, f32[8,128]{1,0:T(8,128)S(1)}, u32[]{:S(2)}, u32[]{:S(2)}) %collective-permute-start.15) | collective-permute-done | bytes 4128 | tf_op jit(solution)/shard_map/ppermute | solution.py:388
  92.5 0.2 shard_map.91.near_half.refs_4_
  92.7 1.9 %collective-permute-start.16 = (f32[2,128,512]{2,1,0:T(8,128)S(1)}, f32[2,128,512]{2,1,0:T(8,128)S(1)}, u32[]{:S(2)}, u32[]{:S(2)}) collective-permute-start(f32[2,128,512]{2,1,0:T(8,128)S(1)} %shard_map.91.near_half.refs_4_), channel_id=1, source_target_pairs={{0,8},{8,0},{16,24},{24,16},{1,9},{9,1},{17,25},{25,17},{2,10},{10... | collective-permute-start | bytes 1572872 | tf_op jit(solution)/shard_map/ppermute | solution.py:365
  94.6 0.2 shard_map.93.cross_half.refs_9_
  94.8 3.7 %collective-permute-start.20 = (f32[2,128,512]{2,1,0:T(8,128)S(1)}, f32[2,128,512]{2,1,0:T(8,128)S(1)}, u32[]{:S(2)}, u32[]{:S(2)}) collective-permute-start(f32[2,128,512]{2,1,0:T(8,128)S(1)} %shard_map.93.cross_half.refs_9_), channel_id=1, source_target_pairs={{8,16},{16,8},{9,17},{17,9},{10,18},{18,10},{11,19},{19,11},{12,20... | collective-permute-start | bytes 1572872 | tf_op jit(solution)/shard_map/ppermute | solution.py:365
  98.6 6.7 %collective-permute-done.20.cross_rows = f32[2,128,512]{2,1,0:T(8,128)S(1)} collective-permute-done((f32[2,128,512]{2,1,0:T(8,128)S(1)}, f32[2,128,512]{2,1,0:T(8,128)S(1)}, u32[]{:S(2)}, u32[]{:S(2)}) %collective-permute-start.20) | collective-permute-done | bytes 524320 | tf_op jit(solution)/shard_map/ppermute | solution.py:365
  105.3 4.7 %shard_map.94 = (f32[2,128,512]{2,1,0:T(8,128)S(1)}, f32[2,128,512]{2,1,0:T(8,128)S(1)}, f32[2,128,512]{2,1,0:T(8,128)S(1)}, f32[2,128,512]{2,1,0:T(8,128)S(1)}) custom-call(s32[9,256]{1,0:T(8,128)S(1)} %broadcast_in_dim.2.info, f32[2,128,512]{2,1,0:T(8,128)S(1)} %collective-permute-done.16.near_rows, f32[2,128,512]{2,1,0:T(8,128)S(1)} %collective-permute-done.20.cross_rows, ...), custom_call_target="tpu_custom_call" | custom-call | flops 2415919104 | bytes 6291456 | tf_op jit(solution)/shard_map/pallas_call | solution.py:444
  110.0 0.1 collective-permute-start.21
  110.1 3.6 %collective-permute-start.24 = (f32[2,128,512]{2,1,0:T(8,128)S(1)}, f32[2,128,512]{2,1,0:T(8,128)S(1)}, u32[]{:S(2)}, u32[]{:S(2)}) collective-permute-start(f32[2,128,512]{2,1,0:T(8,128)S(1)} %get-tuple-element.61), channel_id=1, source_target_pairs={{8,16},{16,8},{9,17},{17,9},{10,18},{18,10},{11,19},{19,11},{12,20... | collective-permute-start | bytes 1572872 | tf_op jit(solution)/shard_map/ppermute | solution.py:365
  113.6 0.1 shard_map.95
  113.7 3.1 %collective-permute-start.22 = (f32[2,128,128]{2,1,0:T(8,128)S(1)}, f32[2,128,128]{2,1,0:T(8,128)S(1)}, u32[]{:S(2)}, u32[]{:S(2)}) collective-permute-start(f32[2,128,128]{2,1,0:T(8,128)S(1)} %get-tuple-element.58), channel_id=1, source_target_pairs={{0,1},{1,2},{2,3},{3,4},{4,5},{5,6},{6,7},{8,9},{9,10},{10,11},{11... | collective-permute-start | bytes 393224 | tf_op jit(solution)/shard_map/ppermute | solution.py:357
  116.8 1.3 collective-permute-start.23
  118.1 2.8 %collective-permute-done.24.sent = f32[2,128,512]{2,1,0:T(8,128)S(1)} collective-permute-done((f32[2,128,512]{2,1,0:T(8,128)S(1)}, f32[2,128,512]{2,1,0:T(8,128)S(1)}, u32[]{:S(2)}, u32[]{:S(2)}) %collective-permute-start.24) | collective-permute-done | bytes 524320 | tf_op jit(solution)/shard_map/ppermute | solution.py:365
  120.8 0.1 shard_map.96
  120.9 3.1 %collective-permute-start.25 = (f32[2,128,128]{2,1,0:T(8,128)S(1)}, f32[2,128,128]{2,1,0:T(8,128)S(1)}, u32[]{:S(2)}, u32[]{:S(2)}) collective-permute-start(f32[2,128,128]{2,1,0:T(8,128)S(1)} %get-tuple-element.63), channel_id=1, source_target_pairs={{0,1},{1,2},{2,3},{3,4},{4,5},{5,6},{6,7},{8,9},{9,10},{10,11},{11... | collective-permute-start | bytes 393224 | tf_op jit(solution)/shard_map/ppermute | solution.py:357
  124.0 1.3 collective-permute-start.26
  125.3 0.6 collective-permute-done.25.refs_6_
  125.9 3.8 %collective-permute-done.26.refs_7_ = f32[2,128,128]{2,1,0:T(8,128)S(1)} collective-permute-done((f32[2,128,128]{2,1,0:T(8,128)S(1)}, f32[2,128,128]{2,1,0:T(8,128)S(1)}, u32[]{:S(2)}, u32[]{:S(2)}) %collective-permute-start.26) | collective-permute-done | bytes 131104 | tf_op jit(solution)/shard_map/ppermute | solution.py:357
  129.7 1.0 shard_map.97
  (32 shorter events, 0.1 us)
Async XLA Ops:
  0.0 1.0 copy-start
  1.0 20.7 %copy-start.3 = (f32[2,256,256]{2,1,0:T(8,128)S(1)}, f32[2,256,256]{2,1,0:T(8,128)}, u32[]{:S(2)}) copy-start(f32[2,256,256]{2,1,0:T(8,128)} %probe.1) | copy-start | bytes 1572868
  1.1 8.9 %collective-permute-start = (f32[2,256,128]{2,1,0:T(8,128)S(1)}, f32[2,256,128]{2,1,0:T(8,128)S(1)}, u32[]{:S(2)}, u32[]{:S(2)}) collective-permute-start(f32[2,256,128]{2,1,0:T(8,128)S(1)} %get-tuple-element.35), channel_id=1, source_target_pairs={{0,1},{1,2},{2,3},{3,4},{4,5},{5,6},{6,7},{8,9},{9,10},{10,11},{11... | collective-permute-start | bytes 786440 | tf_op jit(solution)/shard_map/ppermute | solution.py:357
  5.2 8.8 %collective-permute-start.1 = (f32[2,256,128]{2,1,0:T(8,128)S(1)}, f32[2,256,128]{2,1,0:T(8,128)S(1)}, u32[]{:S(2)}, u32[]{:S(2)}) collective-permute-start(f32[2,256,128]{2,1,0:T(8,128)S(1)} %get-tuple-element.36), channel_id=1, source_target_pairs={{1,0},{2,1},{3,2},{4,3},{5,4},{6,5},{7,6},{9,8},{10,9},{11,10},{12... | collective-permute-start | bytes 786440 | tf_op jit(solution)/shard_map/ppermute | solution.py:357
  14.1 1.0 copy-start.1
  15.1 7.9 %copy-start.2 = (f32[1,1,3,256,256]{4,3,2,1,0:T(8,128)S(1)}, f32[1,1,3,256,256]{4,3,2,1,0:T(8,128)}, u32[]{:S(2)}) copy-start(f32[1,1,3,256,256]{4,3,2,1,0:T(8,128)} %amplitude.1) | copy-start | bytes 2359300
  15.1 7.9 %copy-start.4 = (bf16[256,256]{1,0:T(8,128)(2,1)S(1)}, bf16[256,256]{1,0:T(8,128)(2,1)}, u32[]{:S(2)}) copy-start(bf16[256,256]{1,0:T(8,128)(2,1)} %constant.37.clone.pick_back) | copy-start | bytes 393220
  15.1 7.9 %copy-start.5 = (bf16[256,256]{1,0:T(8,128)(2,1)S(1)}, bf16[256,256]{1,0:T(8,128)(2,1)}, u32[]{:S(2)}) copy-start(bf16[256,256]{1,0:T(8,128)(2,1)} %constant.36.clone.pick) | copy-start | bytes 393220
  15.2 8.8 %collective-permute-start.2 = (f32[2,128,512]{2,1,0:T(8,128)S(1)}, f32[2,128,512]{2,1,0:T(8,128)S(1)}, u32[]{:S(2)}, u32[]{:S(2)}) collective-permute-start(f32[2,128,512]{2,1,0:T(8,128)S(1)} %get-tuple-element.37.near_half.old), channel_id=1, source_target_pairs={{0,8},{8,0},{16,24},{24,16},{1,9},{9,1},{17,25},{25,17},{2,10},{10... | collective-permute-start | bytes 1572872 | tf_op jit(solution)/shard_map/ppermute | solution.py:365
  18.6 10.6 %copy-start.6 = (bf16[2,2,256,256]{3,2,1,0:T(8,128)(2,1)S(1)}, bf16[2,2,256,256]{3,2,1,0:T(8,128)(2,1)}, u32[]{:S(2)}) copy-start(bf16[2,2,256,256]{3,2,1,0:T(8,128)(2,1)} %constant.35.clone.backward) | copy-start | bytes 1572868
  18.6 10.6 %copy-start.7 = (bf16[2,2,256,256]{3,2,1,0:T(8,128)(2,1)S(1)}, bf16[2,2,256,256]{3,2,1,0:T(8,128)(2,1)}, u32[]{:S(2)}) copy-start(bf16[2,2,256,256]{3,2,1,0:T(8,128)(2,1)} %constant.34.clone.forward) | copy-start | bytes 1572868
  18.6 10.6 %collective-permute-start.3 = (f32[2,128,512]{2,1,0:T(8,128)S(1)}, f32[2,128,512]{2,1,0:T(8,128)S(1)}, u32[]{:S(2)}, u32[]{:S(2)}) collective-permute-start(f32[2,128,512]{2,1,0:T(8,128)S(1)} %get-tuple-element.38.cross_half.old), channel_id=1, source_target_pairs={{8,16},{16,8},{9,17},{17,9},{10,18},{18,10},{11,19},{19,11},{12,20... | collective-permute-start | bytes 1572872 | tf_op jit(solution)/shard_map/ppermute | solution.py:365
  33.9 20.6 %collective-permute-start.4 = (f32[2,128,512]{2,1,0:T(8,128)S(1)}, f32[2,128,512]{2,1,0:T(8,128)S(1)}, u32[]{:S(2)}, u32[]{:S(2)}) collective-permute-start(f32[2,128,512]{2,1,0:T(8,128)S(1)} %get-tuple-element.40), channel_id=1, source_target_pairs={{0,8},{8,0},{16,24},{24,16},{1,9},{9,1},{17,25},{25,17},{2,10},{10... | collective-permute-start | bytes 1572872 | tf_op jit(solution)/shard_map/ppermute | solution.py:365
  34.5 6.1 %collective-permute-start.7 = (f32[1,128,512]{2,1,0:T(8,128)S(1)}, f32[1,128,512]{2,1,0:T(8,128)S(1)}, u32[]{:S(2)}, u32[]{:S(2)}) collective-permute-start(f32[1,128,512]{2,1,0:T(8,128)S(1)} %get-tuple-element.44), channel_id=1, source_target_pairs={{0,8},{8,0},{16,24},{24,16},{1,9},{9,1},{17,25},{25,17},{2,10},{10... | collective-permute-start | bytes 786440 | tf_op jit(solution)/shard_map/ppermute | solution.py:365
  35.0 25.8 %collective-permute-start.17 = (f32[2,128,512]{2,1,0:T(8,128)S(1)}, f32[2,128,512]{2,1,0:T(8,128)S(1)}, u32[]{:S(2)}, u32[]{:S(2)}) collective-permute-start(f32[2,128,512]{2,1,0:T(8,128)S(1)} %get-tuple-element.51), channel_id=1, source_target_pairs={{8,16},{16,8},{9,17},{17,9},{10,18},{18,10},{11,19},{19,11},{12,20... | collective-permute-start | bytes 1572872 | tf_op jit(solution)/shard_map/ppermute | solution.py:365
  38.1 10.2 %collective-permute-start.8 = (f32[1,128,512]{2,1,0:T(8,128)S(1)}, f32[1,128,512]{2,1,0:T(8,128)S(1)}, u32[]{:S(2)}, u32[]{:S(2)}) collective-permute-start(f32[1,128,512]{2,1,0:T(8,128)S(1)} %get-tuple-element.45), channel_id=1, source_target_pairs={{8,16},{16,8},{9,17},{17,9},{10,18},{18,10},{11,19},{19,11},{12,20... | collective-permute-start | bytes 786440 | tf_op jit(solution)/shard_map/ppermute | solution.py:365
  48.4 13.8 %collective-permute-start.10 = (f32[1,256,256]{2,1,0:T(8,128)S(1)}, f32[1,256,256]{2,1,0:T(8,128)S(1)}, u32[]{:S(2)}, u32[]{:S(2)}) collective-permute-start(f32[1,256,256]{2,1,0:T(8,128)S(1)} %get-tuple-element.46.head), channel_id=1, source_target_pairs={{1,0},{2,1},{3,2},{4,3},{5,4},{6,5},{7,6},{9,8},{10,9},{11,10},{12... | collective-permute-start | bytes 786440 | tf_op jit(solution)/shard_map/ppermute | solution.py:357
  49.7 21.2 %collective-permute-start.9 = (f32[1,256,256]{2,1,0:T(8,128)S(1)}, f32[1,256,256]{2,1,0:T(8,128)S(1)}, u32[]{:S(2)}, u32[]{:S(2)}) collective-permute-start(f32[1,256,256]{2,1,0:T(8,128)S(1)} %get-tuple-element.47.tail), channel_id=1, source_target_pairs={{0,1},{1,2},{2,3},{3,4},{4,5},{5,6},{6,7},{8,9},{9,10},{10,11},{11... | collective-permute-start | bytes 786440 | tf_op jit(solution)/shard_map/ppermute | solution.py:357
  54.5 37.9 %collective-permute-start.6 = (f32[2,128,256]{2,1,0:T(8,128)S(1)}, f32[2,128,256]{2,1,0:T(8,128)S(1)}, u32[]{:S(2)}, u32[]{:S(2)}) collective-permute-start(f32[2,128,256]{2,1,0:T(8,128)S(1)} %get-tuple-element.41.head), channel_id=1, source_target_pairs={{1,0},{2,1},{3,2},{4,3},{5,4},{6,5},{7,6},{9,8},{10,9},{11,10},{12... | collective-permute-start | bytes 786440 | tf_op jit(solution)/shard_map/ppermute | solution.py:357
  55.8 36.6 %collective-permute-start.5 = (f32[2,128,256]{2,1,0:T(8,128)S(1)}, f32[2,128,256]{2,1,0:T(8,128)S(1)}, u32[]{:S(2)}, u32[]{:S(2)}) collective-permute-start(f32[2,128,256]{2,1,0:T(8,128)S(1)} %get-tuple-element.42.tail), channel_id=1, source_target_pairs={{0,1},{1,2},{2,3},{3,4},{4,5},{5,6},{6,7},{8,9},{9,10},{10,11},{11... | collective-permute-start | bytes 786440 | tf_op jit(solution)/shard_map/ppermute | solution.py:357
  60.9 33.7 %collective-permute-start.19 = (f32[2,128,256]{2,1,0:T(8,128)S(1)}, f32[2,128,256]{2,1,0:T(8,128)S(1)}, u32[]{:S(2)}, u32[]{:S(2)}) collective-permute-start(f32[2,128,256]{2,1,0:T(8,128)S(1)} %get-tuple-element.52.head), channel_id=1, source_target_pairs={{1,0},{2,1},{3,2},{4,3},{5,4},{6,5},{7,6},{9,8},{10,9},{11,10},{12... | collective-permute-start | bytes 786440 | tf_op jit(solution)/shard_map/ppermute | solution.py:357
  62.2 32.4 %collective-permute-start.18 = (f32[2,128,256]{2,1,0:T(8,128)S(1)}, f32[2,128,256]{2,1,0:T(8,128)S(1)}, u32[]{:S(2)}, u32[]{:S(2)}) collective-permute-start(f32[2,128,256]{2,1,0:T(8,128)S(1)} %get-tuple-element.53.tail), channel_id=1, source_target_pairs={{0,1},{1,2},{2,3},{3,4},{4,5},{5,6},{6,7},{8,9},{9,10},{10,11},{11... | collective-permute-start | bytes 786440 | tf_op jit(solution)/shard_map/ppermute | solution.py:357
  71.0 6.6 %collective-permute-start.11 = (f32[8,128]{1,0:T(8,128)S(1)}, f32[8,128]{1,0:T(8,128)S(1)}, u32[]{:S(2)}, u32[]{:S(2)}) collective-permute-start(f32[8,128]{1,0:T(8,128)S(1)} %get-tuple-element.49), channel_id=1, source_target_pairs={{0,1},{1,2},{2,3},{3,4},{4,5},{5,6},{6,7},{7,0},{8,9},{9,10},{10,1... | collective-permute-start | bytes 12296 | tf_op jit(solution)/shard_map/ppermute | solution.py:388
  77.6 5.4 %collective-permute-start.12 = (f32[8,128]{1,0:T(8,128)S(1)}, f32[8,128]{1,0:T(8,128)S(1)}, u32[]{:S(2)}, u32[]{:S(2)}) collective-permute-start(f32[8,128]{1,0:T(8,128)S(1)} %max.15), channel_id=1, source_target_pairs={{0,2},{1,3},{2,4},{3,5},{4,6},{5,7},{6,0},{7,1},{8,10},{9,11},{10,... | collective-permute-start | bytes 12296 | tf_op jit(solution)/shard_map/ppermute | solution.py:388
  83.1 3.4 %collective-permute-start.13 = (f32[8,128]{1,0:T(8,128)S(1)}, f32[8,128]{1,0:T(8,128)S(1)}, u32[]{:S(2)}, u32[]{:S(2)}) collective-permute-start(f32[8,128]{1,0:T(8,128)S(1)} %max.16), channel_id=1, source_target_pairs={{0,4},{1,5},{2,6},{3,7},{4,0},{5,1},{6,2},{7,3},{8,12},{9,13},{10,... | collective-permute-start | bytes 12296 | tf_op jit(solution)/shard_map/ppermute | solution.py:388
  86.4 3.6 %collective-permute-start.14 = (f32[8,128]{1,0:T(8,128)S(1)}, f32[8,128]{1,0:T(8,128)S(1)}, u32[]{:S(2)}, u32[]{:S(2)}) collective-permute-start(f32[8,128]{1,0:T(8,128)S(1)} %max.17), channel_id=1, source_target_pairs={{0,8},{8,16},{16,24},{24,0},{1,9},{9,17},{17,25},{25,1},{2,10},{10... | collective-permute-start | bytes 12296 | tf_op jit(solution)/shard_map/ppermute | solution.py:388
  90.0 2.5 %collective-permute-start.15 = (f32[8,128]{1,0:T(8,128)S(1)}, f32[8,128]{1,0:T(8,128)S(1)}, u32[]{:S(2)}, u32[]{:S(2)}) collective-permute-start(f32[8,128]{1,0:T(8,128)S(1)} %max.18), channel_id=1, source_target_pairs={{0,16},{8,24},{16,0},{24,8},{1,17},{9,25},{17,1},{25,9},{2,18},{10... | collective-permute-start | bytes 12296 | tf_op jit(solution)/shard_map/ppermute | solution.py:388
  92.7 5.8 %collective-permute-start.16 = (f32[2,128,512]{2,1,0:T(8,128)S(1)}, f32[2,128,512]{2,1,0:T(8,128)S(1)}, u32[]{:S(2)}, u32[]{:S(2)}) collective-permute-start(f32[2,128,512]{2,1,0:T(8,128)S(1)} %shard_map.91.near_half.refs_4_), channel_id=1, source_target_pairs={{0,8},{8,0},{16,24},{24,16},{1,9},{9,1},{17,25},{25,17},{2,10},{10... | collective-permute-start | bytes 1572872 | tf_op jit(solution)/shard_map/ppermute | solution.py:365
  94.8 10.5 %collective-permute-start.20 = (f32[2,128,512]{2,1,0:T(8,128)S(1)}, f32[2,128,512]{2,1,0:T(8,128)S(1)}, u32[]{:S(2)}, u32[]{:S(2)}) collective-permute-start(f32[2,128,512]{2,1,0:T(8,128)S(1)} %shard_map.93.cross_half.refs_9_), channel_id=1, source_target_pairs={{8,16},{16,8},{9,17},{17,9},{10,18},{18,10},{11,19},{19,11},{12,20... | collective-permute-start | bytes 1572872 | tf_op jit(solution)/shard_map/ppermute | solution.py:365
  110.0 3.7 %collective-permute-start.21 = (f32[2,128,512]{2,1,0:T(8,128)S(1)}, f32[2,128,512]{2,1,0:T(8,128)S(1)}, u32[]{:S(2)}, u32[]{:S(2)}) collective-permute-start(f32[2,128,512]{2,1,0:T(8,128)S(1)} %get-tuple-element.56), channel_id=1, source_target_pairs={{0,8},{8,0},{16,24},{24,16},{1,9},{9,1},{17,25},{25,17},{2,10},{10... | collective-permute-start | bytes 1572872 | tf_op jit(solution)/shard_map/ppermute | solution.py:365
  110.1 10.8 %collective-permute-start.24 = (f32[2,128,512]{2,1,0:T(8,128)S(1)}, f32[2,128,512]{2,1,0:T(8,128)S(1)}, u32[]{:S(2)}, u32[]{:S(2)}) collective-permute-start(f32[2,128,512]{2,1,0:T(8,128)S(1)} %get-tuple-element.61), channel_id=1, source_target_pairs={{8,16},{16,8},{9,17},{17,9},{10,18},{18,10},{11,19},{19,11},{12,20... | collective-permute-start | bytes 1572872 | tf_op jit(solution)/shard_map/ppermute | solution.py:365
  113.7 11.6 %collective-permute-start.22 = (f32[2,128,128]{2,1,0:T(8,128)S(1)}, f32[2,128,128]{2,1,0:T(8,128)S(1)}, u32[]{:S(2)}, u32[]{:S(2)}) collective-permute-start(f32[2,128,128]{2,1,0:T(8,128)S(1)} %get-tuple-element.58), channel_id=1, source_target_pairs={{0,1},{1,2},{2,3},{3,4},{4,5},{5,6},{6,7},{8,9},{9,10},{10,11},{11... | collective-permute-start | bytes 393224 | tf_op jit(solution)/shard_map/ppermute | solution.py:357
  116.8 8.5 %collective-permute-start.23 = (f32[2,128,128]{2,1,0:T(8,128)S(1)}, f32[2,128,128]{2,1,0:T(8,128)S(1)}, u32[]{:S(2)}, u32[]{:S(2)}) collective-permute-start(f32[2,128,128]{2,1,0:T(8,128)S(1)} %get-tuple-element.59), channel_id=1, source_target_pairs={{1,0},{2,1},{3,2},{4,3},{5,4},{6,5},{7,6},{9,8},{10,9},{11,10},{12... | collective-permute-start | bytes 393224 | tf_op jit(solution)/shard_map/ppermute | solution.py:357
  120.9 5.0 %collective-permute-start.25 = (f32[2,128,128]{2,1,0:T(8,128)S(1)}, f32[2,128,128]{2,1,0:T(8,128)S(1)}, u32[]{:S(2)}, u32[]{:S(2)}) collective-permute-start(f32[2,128,128]{2,1,0:T(8,128)S(1)} %get-tuple-element.63), channel_id=1, source_target_pairs={{0,1},{1,2},{2,3},{3,4},{4,5},{5,6},{6,7},{8,9},{9,10},{10,11},{11... | collective-permute-start | bytes 393224 | tf_op jit(solution)/shard_map/ppermute | solution.py:357
  124.0 5.7 %collective-permute-start.26 = (f32[2,128,128]{2,1,0:T(8,128)S(1)}, f32[2,128,128]{2,1,0:T(8,128)S(1)}, u32[]{:S(2)}, u32[]{:S(2)}) collective-permute-start(f32[2,128,128]{2,1,0:T(8,128)S(1)} %get-tuple-element.64), channel_id=1, source_target_pairs={{1,0},{2,1},{3,2},{4,3},{5,4},{6,5},{7,6},{9,8},{10,9},{11,10},{12... | collective-permute-start | bytes 393224 | tf_op jit(solution)/shard_map/ppermute | solution.py:357

commit v5 on v4

--- a/solution.py
+++ b/solution.py
@@ -13,7 +13,7 @@
 HALO = 128
 ITERS = 2
 LANES = 128
-ODD, HAS_LEFT, HAS_RIGHT, FLAGS = 0, 1, 2, 3
+ODD, EVEN_COL, HAS_LEFT, HAS_RIGHT, FLAGS = 0, 1, 2, 3, 4
 
 smooth_term = 0.25
 ridge_share = 0.1
@@ -221,18 +221,22 @@
     )
 
 
-def light_fold_kernel(mid, sent_near, sent_cross, head, tail):
-    half, side = sent_near.shape[1], head.shape[2]
+def light_fold_kernel(info, mid, sent_near, sent_cross, close, far):
+    even_col = flag(info, EVEN_COL)
+    half, side = sent_near.shape[1], close.shape[2]
     for rows, sent in ((slice(0, half), sent_near), (slice(half, None), sent_cross)):
         block = mid[0, rows] + sent[0]
-        head[0, rows] = block[:, :side]
-        tail[0, rows] = block[:, side:]
-
-
-def light_sum_kernel(head, tail, from_left, from_right, light_near, light_cross, largest):
-    side = head.shape[2]
+        close[0, rows], far[0, rows] = by_sides(even_col, block[:, :side], block[:, side:])
+
+
+def light_sum_kernel(
+    info, close, far, from_close, from_far, light_near, light_cross, largest
+):
+    side = close.shape[2]
     half = light_near.shape[0]
-    left, right = head[0] + from_left[0], tail[0] + from_right[0]
+    right, left = by_sides(
+        flag(info, EVEN_COL), far[0] + from_far[0], close[0] + from_close[0]
+    )
     for out, rows in ((light_near, slice(0, half)), (light_cross, slice(half, None))):
         out[:, :side] = left[rows]
         out[:, side:] = right[rows]
@@ -266,52 +270,67 @@
         )
 
 
-def edges_kernel(specimen, head, tail):
-    head[...] = specimen[:, :, :HALO]
-    tail[...] = specimen[:, :, specimen.shape[2] - HALO :]
-
-
-def widen_kernel(info, before, specimen, after, near_half, cross_half):
-    odd_row = flag(info, ODD)
-    narrow = odd_row[:, :HALO]
+def by_sides(even_col, head, tail):
+    even_col = even_col[:, : head.shape[-1]]
+    return jnp.where(even_col, tail, head), jnp.where(even_col, head, tail)
+
+
+def edges_kernel(info, specimen, close, far):
+    even_col = flag(info, EVEN_COL)
+    for plane in (0, 1):
+        close[plane], far[plane] = by_sides(
+            even_col, specimen[plane, :, :HALO], specimen[plane, :, specimen.shape[2] - HALO :]
+        )
+
+
+def widen_kernel(info, close, specimen, far, near_half, cross_half):
+    odd_row, even_col = flag(info, ODD), flag(info, EVEN_COL)
     half, tile = near_half.shape[1], specimen.shape[2]
     for plane in (0, 1):
-        for source, lanes, odd in (
-            (before, slice(0, HALO), narrow),
-            (specimen, slice(HALO, HALO + tile), odd_row),
-            (after, slice(HALO + tile, None), narrow),
+        after, before = by_sides(even_col, far[plane], close[plane])
+        for source, lanes in (
+            (before, slice(0, HALO)),
+            (specimen[plane], slice(HALO, HALO + tile)),
+            (after, slice(HALO + tile, None)),
         ):
-            top, bottom = source[plane, :half], source[plane, half:]
+            odd = odd_row[:, : source.shape[1]]
+            top, bottom = source[:half], source[half:]
             near_half[plane, :, lanes] = jnp.where(odd, top, bottom)
             cross_half[plane, :, lanes] = jnp.where(odd, bottom, top)
 
 
-def fold_kernel(mid, sent, head, tail):
-    side = head.shape[2]
-    for plane in (0, 1):
-        head[plane] = mid[plane, :, :side] + sent[plane, :, :side]
-        tail[plane] = mid[plane, :, side:] + sent[plane, :, side:]
-
-
-def fold_last_kernel(mid, sent, head, core, tail):
+def fold_kernel(info, mid, sent, close, far):
+    even_col = flag(info, EVEN_COL)
+    side = close.shape[2]
+    for plane in (0, 1):
+        block = mid[plane] + sent[plane]
+        close[plane], far[plane] = by_sides(even_col, block[:, :side], block[:, side:])
+
+
+def fold_last_kernel(info, mid, sent, close, core, far):
+    even_col = flag(info, EVEN_COL)
     tile = core.shape[2]
     for plane in (0, 1):
-        head[plane] = mid[plane, :, :HALO] + sent[plane, :, :HALO]
-        core[plane] = mid[plane, :, HALO : HALO + tile] + sent[plane, :, HALO : HALO + tile]
-        tail[plane] = mid[plane, :, HALO + tile :] + sent[plane, :, HALO + tile :]
-
-
-def update_kernel(info, head, tail, from_left, from_right, light, peak, old, new):
-    side = head.shape[2]
+        block = mid[plane] + sent[plane]
+        close[plane], far[plane] = by_sides(even_col, block[:, :HALO], block[:, HALO + tile :])
+        core[plane] = block[:, HALO : HALO + tile]
+
+
+def update_kernel(info, close, far, from_close, from_far, light, peak, old, new):
+    even_col = flag(info, EVEN_COL)
+    side = close.shape[2]
     most = ridge_share * jnp.max(peak[...])
     lane = lax.broadcasted_iota(jnp.int32, (1, side), 1)
-    for own, sent, inside, lanes in (
-        (head, from_left, (lane >= HALO) | flag(info, HAS_LEFT), slice(0, side)),
-        (tail, from_right, (lane < side - HALO) | flag(info, HAS_RIGHT), slice(side, None)),
-    ):
-        scale = 1.0 / (light[:, lanes] + most)
-        for plane in (0, 1):
-            gradient = own[plane] + sent[plane]
+    bounds = (
+        ((lane >= HALO) | flag(info, HAS_LEFT), slice(0, side)),
+        ((lane < side - HALO) | flag(info, HAS_RIGHT), slice(side, None)),
+    )
+    scales = [1.0 / (light[:, lanes] + most) for _, lanes in bounds]
+    for plane in (0, 1):
+        right, left = by_sides(
+            even_col, far[plane] + from_far[plane], close[plane] + from_close[plane]
+        )
+        for gradient, scale, (inside, lanes) in zip((left, right), scales, bounds):
             new[plane, :, lanes] = jnp.where(
                 inside, old[plane, :, lanes] - gradient * scale, 0.0
             )
@@ -319,14 +338,15 @@
 
 def finish_kernel(info, *refs):
     *halves, peak, out = refs
-    odd_row = flag(info, ODD)
+    odd_row, even_col = flag(info, ODD), flag(info, EVEN_COL)
     most = ridge_share * jnp.max(peak[...])
     half, tile = out.shape[1] // 2, out.shape[2]
     inner = slice(HALO, HALO + tile)
     for plane in (0, 1):
         news = []
-        for core, from_left, from_right, light, old in (halves[:5], halves[5:]):
-            sent = [from_left[plane], from_right[plane]]
+        for core, from_close, from_far, light, old in (halves[:5], halves[5:]):
+            right, left = by_sides(even_col, from_far[plane], from_close[plane])
+            sent = [left, right]
             if tile > 2 * HALO:
                 sent.insert(1, jnp.zeros((half, tile - 2 * HALO), F32))
             gradient = core[plane] + jnp.concatenate(sent, axis=1)
@@ -351,12 +371,6 @@
     )
 
 
-def shifted(block, axis, distance):
-    count = lax.axis_size(axis)
-    route = [(i - distance, i) for i in range(count) if 0 <= i - distance < count]
-    return lax.ppermute(block, axis, route)
-
-
 def swapped(block, axis, first):
     count = lax.axis_size(axis)
     route = []
@@ -373,10 +387,10 @@
     return swapped(block, "row", 0)
 
 
-def to_sides(head, tail):
-    right = shifted(tail, "col", 1)
-    left = shifted(head, "col", -1)
-    return right, left
+def to_sides(close, far):
+    close = swapped(close, "col", 0)
+    far = swapped(far, "col", 1)
+    return close, far
 
 
 def largest_of(block, axes):
@@ -384,7 +398,10 @@
         count = lax.axis_size(axis)
         reach = 1
         while reach < count:
-            route = [(i, (i + reach) % count) for i in range(count)]
+            if count & (count - 1) == 0:
+                route = [(i, i ^ reach) for i in range(count)]
+            else:
+                route = [(i, (i + reach) % count) for i in range(count)]
             block = jnp.maximum(block, lax.ppermute(block, axis, route))
             reach *= 2
     return block
@@ -400,16 +417,14 @@
     row, col = lax.axis_index("row"), lax.axis_index("col")
     odd = row % 2
     corners = offsets.reshape(-1) + HALO
-    flags = jnp.stack([odd, col > 0, col < lax.axis_size("col") - 1]).astype(jnp.int32)
+    flags = jnp.stack([odd, (col + 1) % 2, col > 0, col < lax.axis_size("col") - 1]).astype(jnp.int32)
     info = jnp.broadcast_to(
         jnp.concatenate([flags, corners])[:, None], (FLAGS + 2 * count, win)
     )
     band, wide, strip = shape(2, half, HALO), shape(2, half, 2 * side), shape(2, half, side)
 
-    head, tail = kernel_call(edges_kernel, [shape(2, tile, HALO)] * 2, [VM])(
-        specimen
-    )
-    before, after = to_sides(head, tail)
+    close, far = kernel_call(edges_kernel, [shape(2, tile, HALO)] * 2, [VM] * 2)(info, specimen)
+    close, far = to_sides(close, far)
 
     probes = kernel_call(roll_kernel, [shape(count, 2, win, win)], [SM, VM])(corners, probe_field)
     light_band = shape(1, half, 2 * side)
@@ -426,18 +441,18 @@
     )
 
     near_half, cross_half = kernel_call(widen_kernel, [wide] * 2, [VM] * 4)(
-        info, before, specimen, after
+        info, close, specimen, far
     )
     cross_rows = to_cross(cross_half)
     near_rows = to_near(near_half)
 
-    head, tail = kernel_call(
-        light_fold_kernel, [shape(1, tile, side)] * 2, [VM] * 3
-    )(light_mid, light_near, light_cross)
-    from_left, from_right = to_sides(head, tail)
+    close, far = kernel_call(
+        light_fold_kernel, [shape(1, tile, side)] * 2, [VM] * 4
+    )(info, light_mid, light_near, light_cross)
+    from_close, from_far = to_sides(close, far)
     light_near, light_cross, found = kernel_call(
-        light_sum_kernel, [shape(half, 2 * side)] * 2 + [shape(8, LANES)], [VM] * 4
-    )(head, tail, from_left, from_right)
+        light_sum_kernel, [shape(half, 2 * side)] * 2 + [shape(8, LANES)], [VM] * 5
+    )(info, close, far, from_close, from_far)
     peak = largest_of(found, ("col", "row"))
 
     for step in range(ITERS):
@@ -460,11 +475,11 @@
                 (mid_cross, sent_cross, light_cross, cross_half),
                 (mid_near, sent_near, light_near, near_half),
             ):
-                head, tail = kernel_call(fold_kernel, [strip] * 2, [VM] * 2)(mid, sent)
-                from_left, from_right = to_sides(head, tail)
+                close, far = kernel_call(fold_kernel, [strip] * 2, [VM] * 3)(info, mid, sent)
+                from_close, from_far = to_sides(close, far)
                 halves.append(
                     kernel_call(update_kernel, [wide], [VM] * 8)(
-                        info, head, tail, from_left, from_right, light, peak, old
+                        info, close, far, from_close, from_far, light, peak, old
                     )
                 )
             cross_half, near_half = halves
@@ -476,11 +491,11 @@
                 (mid_near, sent_near, light_near, near_half),
                 (mid_cross, sent_cross, light_cross, cross_half),
             ):
-                head, core, tail = kernel_call(
-                    fold_last_kernel, [band, shape(2, half, tile), band], [VM] * 2
-                )(mid, sent)
-                from_left, from_right = to_sides(head, tail)
-                operands += [core, from_left, from_right, light, old]
+                close, core, far = kernel_call(
+                    fold_last_kernel, [band, shape(2, half, tile), band], [VM] * 3
+                )(info, mid, sent)
+                from_close, from_far = to_sides(close, far)
+                operands += [core, from_close, from_far, light, old]
             return kernel_call(
                 finish_kernel, [shape(2, tile, tile)], [VM] * 12
             )(info, *operands, peak)

time: 132 us -> 120 us (0.909)
  the two profiles are of different devices: /device:TPU:1 before, /device:TPU:22 now
where the time goes in v5:
time: 120 us
  waiting for transfers between devices  58.9 us (49%)
  starting transfers between devices  44.4 us (37%)
  Pallas kernels  14.2 us (12%)
  local copies, waits for them, and re-layouts  1.41 us (1%)
    ppermute x22, waiting for transfers between devices, swapped(): return lax.ppermute(block, axis, route)  45.3 us
    ppermute x22, starting transfers between devices, swapped(): return lax.ppermute(block, axis, route)  40.2 us
    ppermute x5, waiting for transfers between devices, largest_of(): block = jnp.maximum(block, lax.ppermute(block, axis, route))  13.6 us
    pallas_call x2, Pallas kernels, steps(): kernel_call(gradient_kernel, [wide] * 4, [VM] * 9, flops=count * 8 * 2 *...  9.46 us
    ppermute x5, starting transfers between devices, largest_of(): block = jnp.maximum(block, lax.ppermute(block, axis, route))  4.21 us
  transfers between devices with their start and end apart: 27, of which 13 were waited for; matrix products, arithmetic and copies ran while one was open for 0% of the time, Pallas kernels for 3%

profile of v5, /device:TPU:22, one launch (start us, length us, event | category | flops | bytes accessed | tf_op | source)
XLA Modules:
  0.0 120.0 jit_solution(11724001130455342001)
XLA Ops:
  0.0 0.7 broadcast_add_fusion
  0.7 0.1 copy.10
  0.8 0.1 add.19.corners
  0.9 0.1 concatenate.3
  0.9 0.1 broadcast_in_dim.2.info
  1.0 1.0 copy-done
  2.1 0.6 collective-permute-start
  2.7 4.6 %collective-permute-start.1 = (f32[2,256,128]{2,1,0:T(8,128)S(1)}, f32[2,256,128]{2,1,0:T(8,128)S(1)}, u32[]{:S(2)}, u32[]{:S(2)}) collective-permute-start(f32[2,256,128]{2,1,0:T(8,128)S(1)} %get-tuple-element.36), channel_id=1, source_target_pairs={{1,2},{2,1},{3,4},{4,3},{5,6},{6,5},{9,10},{10,9},{11,12},{12,11},... | collective-permute-start | bytes 786440 | tf_op jit(solution)/shard_map/ppermute | solution.py:379
  7.3 8.6 %collective-permute-done.close = f32[2,256,128]{2,1,0:T(8,128)S(1)} collective-permute-done((f32[2,256,128]{2,1,0:T(8,128)S(1)}, f32[2,256,128]{2,1,0:T(8,128)S(1)}, u32[]{:S(2)}, u32[]{:S(2)}) %collective-permute-start) | collective-permute-done | bytes 262176 | tf_op jit(solution)/shard_map/ppermute | solution.py:379
  15.8 0.0 collective-permute-done.1.far
  15.8 0.1 shard_map.83
  16.0 0.1 collective-permute-start.2
  16.0 0.0 copy-start.5
  16.1 0.0 copy-start.6
  16.1 2.6 %collective-permute-start.3 = (f32[2,128,512]{2,1,0:T(8,128)S(1)}, f32[2,128,512]{2,1,0:T(8,128)S(1)}, u32[]{:S(2)}, u32[]{:S(2)}) collective-permute-start(f32[2,128,512]{2,1,0:T(8,128)S(1)} %get-tuple-element.38.cross_half.old), channel_id=1, source_target_pairs={{8,16},{16,8},{9,17},{17,9},{10,18},{18,10},{11,19},{19,11},{12,20... | collective-permute-start | bytes 1572872 | tf_op jit(solution)/shard_map/ppermute | solution.py:379
  18.7 1.2 shard_map.84.probe
  20.0 1.0 shard_map.85.amplitude
  21.0 5.7 %collective-permute-done.3.cross_rows = f32[2,128,512]{2,1,0:T(8,128)S(1)} collective-permute-done((f32[2,128,512]{2,1,0:T(8,128)S(1)}, f32[2,128,512]{2,1,0:T(8,128)S(1)}, u32[]{:S(2)}, u32[]{:S(2)}) %collective-permute-start.3) | collective-permute-done | bytes 524320 | tf_op jit(solution)/shard_map/ppermute | solution.py:379
  26.7 4.7 %shard_map.86 = (f32[2,128,512]{2,1,0:T(8,128)S(1)}, f32[2,128,512]{2,1,0:T(8,128)S(1)}, f32[2,128,512]{2,1,0:T(8,128)S(1)}, f32[2,128,512]{2,1,0:T(8,128)S(1)}) custom-call(s32[10,256]{1,0:T(8,128)S(1)} %broadcast_in_dim.2.info, f32[2,128,512]{2,1,0:T(8,128)S(1)} %collective-permute-done.2.near_rows, f32[2,128,512]{2,1,0:T(8,128)S(1)} %collective-permute-done.3.cross_rows, ...), custom_call_target="tpu_custom_call" | custom-call | flops 2415919104 | bytes 6291456 | tf_op jit(solution)/shard_map/pallas_call | solution.py:459
  31.4 0.1 collective-permute-start.4
  31.5 0.5 shard_map.88
  32.0 0.6 collective-permute-start.7
  32.6 2.5 %collective-permute-start.17 = (f32[2,128,512]{2,1,0:T(8,128)S(1)}, f32[2,128,512]{2,1,0:T(8,128)S(1)}, u32[]{:S(2)}, u32[]{:S(2)}) collective-permute-start(f32[2,128,512]{2,1,0:T(8,128)S(1)} %get-tuple-element.51), channel_id=1, source_target_pairs={{8,16},{16,8},{9,17},{17,9},{10,18},{18,10},{11,19},{19,11},{12,20... | collective-permute-start | bytes 1572872 | tf_op jit(solution)/shard_map/ppermute | solution.py:379
  35.1 3.0 %collective-permute-start.8 = (f32[1,128,512]{2,1,0:T(8,128)S(1)}, f32[1,128,512]{2,1,0:T(8,128)S(1)}, u32[]{:S(2)}, u32[]{:S(2)}) collective-permute-start(f32[1,128,512]{2,1,0:T(8,128)S(1)} %get-tuple-element.45), channel_id=1, source_target_pairs={{8,16},{16,8},{9,17},{17,9},{10,18},{18,10},{11,19},{19,11},{12,20... | collective-permute-start | bytes 786440 | tf_op jit(solution)/shard_map/ppermute | solution.py:379
  38.1 7.7 %collective-permute-done.8.sent_cross = f32[1,128,512]{2,1,0:T(8,128)S(1)} collective-permute-done((f32[1,128,512]{2,1,0:T(8,128)S(1)}, f32[1,128,512]{2,1,0:T(8,128)S(1)}, u32[]{:S(2)}, u32[]{:S(2)}) %collective-permute-start.8) | collective-permute-done | bytes 262176 | tf_op jit(solution)/shard_map/ppermute | solution.py:379
  45.9 0.1 shard_map.89
  45.9 0.6 collective-permute-start.9
  46.5 2.9 %collective-permute-start.10 = (f32[1,256,256]{2,1,0:T(8,128)S(1)}, f32[1,256,256]{2,1,0:T(8,128)S(1)}, u32[]{:S(2)}, u32[]{:S(2)}) collective-permute-start(f32[1,256,256]{2,1,0:T(8,128)S(1)} %get-tuple-element.47.far), channel_id=1, source_target_pairs={{1,2},{2,1},{3,4},{4,3},{5,6},{6,5},{9,10},{10,9},{11,12},{12,11},... | collective-permute-start | bytes 786440 | tf_op jit(solution)/shard_map/ppermute | solution.py:379
  49.5 0.0 collective-permute-done.4.sent
  49.5 0.1 shard_map.87
  49.5 0.9 collective-permute-start.5
  50.5 2.9 %collective-permute-start.6 = (f32[2,128,256]{2,1,0:T(8,128)S(1)}, f32[2,128,256]{2,1,0:T(8,128)S(1)}, u32[]{:S(2)}, u32[]{:S(2)}) collective-permute-start(f32[2,128,256]{2,1,0:T(8,128)S(1)} %get-tuple-element.42.far), channel_id=1, source_target_pairs={{1,2},{2,1},{3,4},{4,3},{5,6},{6,5},{9,10},{10,9},{11,12},{12,11},... | collective-permute-start | bytes 786440 | tf_op jit(solution)/shard_map/ppermute | solution.py:379
  53.4 0.1 shard_map.92
  53.5 1.6 %collective-permute-start.18 = (f32[2,128,256]{2,1,0:T(8,128)S(1)}, f32[2,128,256]{2,1,0:T(8,128)S(1)}, u32[]{:S(2)}, u32[]{:S(2)}) collective-permute-start(f32[2,128,256]{2,1,0:T(8,128)S(1)} %get-tuple-element.52.close), channel_id=1, source_target_pairs={{0,1},{1,0},{2,3},{3,2},{4,5},{5,4},{6,7},{7,6},{8,9},{9,8},{10,11... | collective-permute-start | bytes 786440 | tf_op jit(solution)/shard_map/ppermute | solution.py:379
  55.1 6.6 %collective-permute-done.9.from_close = f32[1,256,256]{2,1,0:T(8,128)S(1)} collective-permute-done((f32[1,256,256]{2,1,0:T(8,128)S(1)}, f32[1,256,256]{2,1,0:T(8,128)S(1)}, u32[]{:S(2)}, u32[]{:S(2)}) %collective-permute-start.9) | collective-permute-done | bytes 262176 | tf_op jit(solution)/shard_map/ppermute | solution.py:379
  61.7 2.5 %collective-permute-start.19 = (f32[2,128,256]{2,1,0:T(8,128)S(1)}, f32[2,128,256]{2,1,0:T(8,128)S(1)}, u32[]{:S(2)}, u32[]{:S(2)}) collective-permute-start(f32[2,128,256]{2,1,0:T(8,128)S(1)} %get-tuple-element.53.far), channel_id=1, source_target_pairs={{1,2},{2,1},{3,4},{4,3},{5,6},{6,5},{9,10},{10,9},{11,12},{12,11},... | collective-permute-start | bytes 786440 | tf_op jit(solution)/shard_map/ppermute | solution.py:379
  64.2 0.1 shard_map.90
  64.3 1.4 %collective-permute-start.11 = (f32[8,128]{1,0:T(8,128)S(1)}, f32[8,128]{1,0:T(8,128)S(1)}, u32[]{:S(2)}, u32[]{:S(2)}) collective-permute-start(f32[8,128]{1,0:T(8,128)S(1)} %get-tuple-element.49), channel_id=1, source_target_pairs={{0,1},{1,0},{2,3},{3,2},{4,5},{5,4},{6,7},{7,6},{8,9},{9,8},{10,11... | collective-permute-start | bytes 12296 | tf_op jit(solution)/shard_map/ppermute | solution.py:405
  65.8 3.5 %collective-permute-done.11 = f32[8,128]{1,0:T(8,128)S(1)} collective-permute-done((f32[8,128]{1,0:T(8,128)S(1)}, f32[8,128]{1,0:T(8,128)S(1)}, u32[]{:S(2)}, u32[]{:S(2)}) %collective-permute-start.11) | collective-permute-done | bytes 4128 | tf_op jit(solution)/shard_map/ppermute | solution.py:405
  69.3 1.0 collective-permute-start.12
  70.3 2.6 %collective-permute-done.12 = f32[8,128]{1,0:T(8,128)S(1)} collective-permute-done((f32[8,128]{1,0:T(8,128)S(1)}, f32[8,128]{1,0:T(8,128)S(1)}, u32[]{:S(2)}, u32[]{:S(2)}) %collective-permute-start.12) | collective-permute-done | bytes 4128 | tf_op jit(solution)/shard_map/ppermute | solution.py:405
  72.9 1.2 collective-permute-start.13
  74.1 3.3 %collective-permute-done.13 = f32[8,128]{1,0:T(8,128)S(1)} collective-permute-done((f32[8,128]{1,0:T(8,128)S(1)}, f32[8,128]{1,0:T(8,128)S(1)}, u32[]{:S(2)}, u32[]{:S(2)}) %collective-permute-start.13) | collective-permute-done | bytes 4128 | tf_op jit(solution)/shard_map/ppermute | solution.py:405
  77.4 1.2 collective-permute-done.14
  78.6 0.6 collective-permute-start.15
  79.1 3.0 %collective-permute-done.15 = f32[8,128]{1,0:T(8,128)S(1)} collective-permute-done((f32[8,128]{1,0:T(8,128)S(1)}, f32[8,128]{1,0:T(8,128)S(1)}, u32[]{:S(2)}, u32[]{:S(2)}) %collective-permute-start.15) | collective-permute-done | bytes 4128 | tf_op jit(solution)/shard_map/ppermute | solution.py:405
  82.2 0.3 shard_map.91.near_half.refs_4_
  82.4 0.1 collective-permute-start.16
  82.5 0.3 shard_map.93.cross_half.refs_9_
  82.8 2.7 %collective-permute-start.20 = (f32[2,128,512]{2,1,0:T(8,128)S(1)}, f32[2,128,512]{2,1,0:T(8,128)S(1)}, u32[]{:S(2)}, u32[]{:S(2)}) collective-permute-start(f32[2,128,512]{2,1,0:T(8,128)S(1)} %shard_map.93.cross_half.refs_9_), channel_id=1, source_target_pairs={{8,16},{16,8},{9,17},{17,9},{10,18},{18,10},{11,19},{19,11},{12,20... | collective-permute-start | bytes 1572872 | tf_op jit(solution)/shard_map/ppermute | solution.py:379
  85.6 7.7 %collective-permute-done.20.cross_rows = f32[2,128,512]{2,1,0:T(8,128)S(1)} collective-permute-done((f32[2,128,512]{2,1,0:T(8,128)S(1)}, f32[2,128,512]{2,1,0:T(8,128)S(1)}, u32[]{:S(2)}, u32[]{:S(2)}) %collective-permute-start.20) | collective-permute-done | bytes 524320 | tf_op jit(solution)/shard_map/ppermute | solution.py:379
  93.3 4.7 %shard_map.94 = (f32[2,128,512]{2,1,0:T(8,128)S(1)}, f32[2,128,512]{2,1,0:T(8,128)S(1)}, f32[2,128,512]{2,1,0:T(8,128)S(1)}, f32[2,128,512]{2,1,0:T(8,128)S(1)}) custom-call(s32[10,256]{1,0:T(8,128)S(1)} %broadcast_in_dim.2.info, f32[2,128,512]{2,1,0:T(8,128)S(1)} %collective-permute-done.16.near_rows, ...), custom_call_target="tpu_custom_call" | custom-call | flops 2415919104 | bytes 6291456 | tf_op jit(solution)/shard_map/pallas_call | solution.py:459
  98.0 0.1 collective-permute-start.21
  98.1 2.6 %collective-permute-start.24 = (f32[2,128,512]{2,1,0:T(8,128)S(1)}, f32[2,128,512]{2,1,0:T(8,128)S(1)}, u32[]{:S(2)}, u32[]{:S(2)}) collective-permute-start(f32[2,128,512]{2,1,0:T(8,128)S(1)} %get-tuple-element.61), channel_id=1, source_target_pairs={{8,16},{16,8},{9,17},{17,9},{10,18},{18,10},{11,19},{19,11},{12,20... | collective-permute-start | bytes 1572872 | tf_op jit(solution)/shard_map/ppermute | solution.py:379
  100.7 0.1 shard_map.95
  100.8 1.9 %collective-permute-start.22 = (f32[2,128,128]{2,1,0:T(8,128)S(1)}, f32[2,128,128]{2,1,0:T(8,128)S(1)}, u32[]{:S(2)}, u32[]{:S(2)}) collective-permute-start(f32[2,128,128]{2,1,0:T(8,128)S(1)} %get-tuple-element.58), channel_id=1, source_target_pairs={{0,1},{1,0},{2,3},{3,2},{4,5},{5,4},{6,7},{7,6},{8,9},{9,8},{10,11... | collective-permute-start | bytes 393224 | tf_op jit(solution)/shard_map/ppermute | solution.py:379
  102.7 2.4 %collective-permute-start.23 = (f32[2,128,128]{2,1,0:T(8,128)S(1)}, f32[2,128,128]{2,1,0:T(8,128)S(1)}, u32[]{:S(2)}, u32[]{:S(2)}) collective-permute-start(f32[2,128,128]{2,1,0:T(8,128)S(1)} %get-tuple-element.59), channel_id=1, source_target_pairs={{1,2},{2,1},{3,4},{4,3},{5,6},{6,5},{9,10},{10,9},{11,12},{12,11},... | collective-permute-start | bytes 393224 | tf_op jit(solution)/shard_map/ppermute | solution.py:379
  105.1 3.5 %collective-permute-done.24.sent = f32[2,128,512]{2,1,0:T(8,128)S(1)} collective-permute-done((f32[2,128,512]{2,1,0:T(8,128)S(1)}, f32[2,128,512]{2,1,0:T(8,128)S(1)}, u32[]{:S(2)}, u32[]{:S(2)}) %collective-permute-start.24) | collective-permute-done | bytes 524320 | tf_op jit(solution)/shard_map/ppermute | solution.py:379
  108.6 0.1 shard_map.96
  108.7 2.5 %collective-permute-start.25 = (f32[2,128,128]{2,1,0:T(8,128)S(1)}, f32[2,128,128]{2,1,0:T(8,128)S(1)}, u32[]{:S(2)}, u32[]{:S(2)}) collective-permute-start(f32[2,128,128]{2,1,0:T(8,128)S(1)} %get-tuple-element.63), channel_id=1, source_target_pairs={{0,1},{1,0},{2,3},{3,2},{4,5},{5,4},{6,7},{7,6},{8,9},{9,8},{10,11... | collective-permute-start | bytes 393224 | tf_op jit(solution)/shard_map/ppermute | solution.py:379
  111.2 2.4 %collective-permute-start.26 = (f32[2,128,128]{2,1,0:T(8,128)S(1)}, f32[2,128,128]{2,1,0:T(8,128)S(1)}, u32[]{:S(2)}, u32[]{:S(2)}) collective-permute-start(f32[2,128,128]{2,1,0:T(8,128)S(1)} %get-tuple-element.64), channel_id=1, source_target_pairs={{1,2},{2,1},{3,4},{4,3},{5,6},{6,5},{9,10},{10,9},{11,12},{12,11},... | collective-permute-start | bytes 393224 | tf_op jit(solution)/shard_map/ppermute | solution.py:379
  113.6 1.0 collective-permute-done.25.refs_6_
  114.6 4.4 %collective-permute-done.26.refs_7_ = f32[2,128,128]{2,1,0:T(8,128)S(1)} collective-permute-done((f32[2,128,128]{2,1,0:T(8,128)S(1)}, f32[2,128,128]{2,1,0:T(8,128)S(1)}, u32[]{:S(2)}, u32[]{:S(2)}) %collective-permute-start.26) | collective-permute-done | bytes 131104 | tf_op jit(solution)/shard_map/ppermute | solution.py:379
  119.0 1.0 shard_map.97
  (30 shorter events, 0.1 us)
Async XLA Ops:
  1.0 1.0 copy-start
  2.1 16.6 %copy-start.2 = (f32[2,256,256]{2,1,0:T(8,128)S(1)}, f32[2,256,256]{2,1,0:T(8,128)}, u32[]{:S(2)}) copy-start(f32[2,256,256]{2,1,0:T(8,128)} %probe.1) | copy-start | bytes 1572868
  2.1 13.7 %collective-permute-start = (f32[2,256,128]{2,1,0:T(8,128)S(1)}, f32[2,256,128]{2,1,0:T(8,128)S(1)}, u32[]{:S(2)}, u32[]{:S(2)}) collective-permute-start(f32[2,256,128]{2,1,0:T(8,128)S(1)} %get-tuple-element.35), channel_id=1, source_target_pairs={{0,1},{1,0},{2,3},{3,2},{4,5},{5,4},{6,7},{7,6},{8,9},{9,8},{10,11... | collective-permute-start | bytes 786440 | tf_op jit(solution)/shard_map/ppermute | solution.py:379
  2.7 17.2 %copy-start.1 = (f32[1,1,3,256,256]{4,3,2,1,0:T(8,128)S(1)}, f32[1,1,3,256,256]{4,3,2,1,0:T(8,128)}, u32[]{:S(2)}) copy-start(f32[1,1,3,256,256]{4,3,2,1,0:T(8,128)} %amplitude.1) | copy-start | bytes 2359300
  2.7 17.3 %copy-start.3 = (bf16[256,256]{1,0:T(8,128)(2,1)S(1)}, bf16[256,256]{1,0:T(8,128)(2,1)}, u32[]{:S(2)}) copy-start(bf16[256,256]{1,0:T(8,128)(2,1)} %constant.42.clone.pick_back) | copy-start | bytes 393220
  2.7 17.3 %copy-start.4 = (bf16[256,256]{1,0:T(8,128)(2,1)S(1)}, bf16[256,256]{1,0:T(8,128)(2,1)}, u32[]{:S(2)}) copy-start(bf16[256,256]{1,0:T(8,128)(2,1)} %constant.41.clone.pick) | copy-start | bytes 393220
  2.7 13.2 %collective-permute-start.1 = (f32[2,256,128]{2,1,0:T(8,128)S(1)}, f32[2,256,128]{2,1,0:T(8,128)S(1)}, u32[]{:S(2)}, u32[]{:S(2)}) collective-permute-start(f32[2,256,128]{2,1,0:T(8,128)S(1)} %get-tuple-element.36), channel_id=1, source_target_pairs={{1,2},{2,1},{3,4},{4,3},{5,6},{6,5},{9,10},{10,9},{11,12},{12,11},... | collective-permute-start | bytes 786440 | tf_op jit(solution)/shard_map/ppermute | solution.py:379
  16.0 5.0 %collective-permute-start.2 = (f32[2,128,512]{2,1,0:T(8,128)S(1)}, f32[2,128,512]{2,1,0:T(8,128)S(1)}, u32[]{:S(2)}, u32[]{:S(2)}) collective-permute-start(f32[2,128,512]{2,1,0:T(8,128)S(1)} %get-tuple-element.37.near_half.old), channel_id=1, source_target_pairs={{0,8},{8,0},{16,24},{24,16},{1,9},{9,1},{17,25},{25,17},{2,10},{10... | collective-permute-start | bytes 1572872 | tf_op jit(solution)/shard_map/ppermute | solution.py:379
  16.0 10.7 %copy-start.5 = (bf16[2,2,256,256]{3,2,1,0:T(8,128)(2,1)S(1)}, bf16[2,2,256,256]{3,2,1,0:T(8,128)(2,1)}, u32[]{:S(2)}) copy-start(bf16[2,2,256,256]{3,2,1,0:T(8,128)(2,1)} %constant.40.clone.backward) | copy-start | bytes 1572868
  16.1 10.6 %copy-start.6 = (bf16[2,2,256,256]{3,2,1,0:T(8,128)(2,1)S(1)}, bf16[2,2,256,256]{3,2,1,0:T(8,128)(2,1)}, u32[]{:S(2)}) copy-start(bf16[2,2,256,256]{3,2,1,0:T(8,128)(2,1)} %constant.39.clone.forward) | copy-start | bytes 1572868
  16.1 10.6 %collective-permute-start.3 = (f32[2,128,512]{2,1,0:T(8,128)S(1)}, f32[2,128,512]{2,1,0:T(8,128)S(1)}, u32[]{:S(2)}, u32[]{:S(2)}) collective-permute-start(f32[2,128,512]{2,1,0:T(8,128)S(1)} %get-tuple-element.38.cross_half.old), channel_id=1, source_target_pairs={{8,16},{16,8},{9,17},{17,9},{10,18},{18,10},{11,19},{19,11},{12,20... | collective-permute-start | bytes 1572872 | tf_op jit(solution)/shard_map/ppermute | solution.py:379
  31.4 18.0 %collective-permute-start.4 = (f32[2,128,512]{2,1,0:T(8,128)S(1)}, f32[2,128,512]{2,1,0:T(8,128)S(1)}, u32[]{:S(2)}, u32[]{:S(2)}) collective-permute-start(f32[2,128,512]{2,1,0:T(8,128)S(1)} %get-tuple-element.40), channel_id=1, source_target_pairs={{0,8},{8,0},{16,24},{24,16},{1,9},{9,1},{17,25},{25,17},{2,10},{10... | collective-permute-start | bytes 1572872 | tf_op jit(solution)/shard_map/ppermute | solution.py:379
  32.0 6.1 %collective-permute-start.7 = (f32[1,128,512]{2,1,0:T(8,128)S(1)}, f32[1,128,512]{2,1,0:T(8,128)S(1)}, u32[]{:S(2)}, u32[]{:S(2)}) collective-permute-start(f32[1,128,512]{2,1,0:T(8,128)S(1)} %get-tuple-element.44), channel_id=1, source_target_pairs={{0,8},{8,0},{16,24},{24,16},{1,9},{9,1},{17,25},{25,17},{2,10},{10... | collective-permute-start | bytes 786440 | tf_op jit(solution)/shard_map/ppermute | solution.py:379
  32.6 20.8 %collective-permute-start.17 = (f32[2,128,512]{2,1,0:T(8,128)S(1)}, f32[2,128,512]{2,1,0:T(8,128)S(1)}, u32[]{:S(2)}, u32[]{:S(2)}) collective-permute-start(f32[2,128,512]{2,1,0:T(8,128)S(1)} %get-tuple-element.51), channel_id=1, source_target_pairs={{8,16},{16,8},{9,17},{17,9},{10,18},{18,10},{11,19},{19,11},{12,20... | collective-permute-start | bytes 1572872 | tf_op jit(solution)/shard_map/ppermute | solution.py:379
  35.1 10.8 %collective-permute-start.8 = (f32[1,128,512]{2,1,0:T(8,128)S(1)}, f32[1,128,512]{2,1,0:T(8,128)S(1)}, u32[]{:S(2)}, u32[]{:S(2)}) collective-permute-start(f32[1,128,512]{2,1,0:T(8,128)S(1)} %get-tuple-element.45), channel_id=1, source_target_pairs={{8,16},{16,8},{9,17},{17,9},{10,18},{18,10},{11,19},{19,11},{12,20... | collective-permute-start | bytes 786440 | tf_op jit(solution)/shard_map/ppermute | solution.py:379
  45.9 15.8 %collective-permute-start.9 = (f32[1,256,256]{2,1,0:T(8,128)S(1)}, f32[1,256,256]{2,1,0:T(8,128)S(1)}, u32[]{:S(2)}, u32[]{:S(2)}) collective-permute-start(f32[1,256,256]{2,1,0:T(8,128)S(1)} %get-tuple-element.46.close), channel_id=1, source_target_pairs={{0,1},{1,0},{2,3},{3,2},{4,5},{5,4},{6,7},{7,6},{8,9},{9,8},{10,11... | collective-permute-start | bytes 786440 | tf_op jit(solution)/shard_map/ppermute | solution.py:379
  46.5 17.7 %collective-permute-start.10 = (f32[1,256,256]{2,1,0:T(8,128)S(1)}, f32[1,256,256]{2,1,0:T(8,128)S(1)}, u32[]{:S(2)}, u32[]{:S(2)}) collective-permute-start(f32[1,256,256]{2,1,0:T(8,128)S(1)} %get-tuple-element.47.far), channel_id=1, source_target_pairs={{1,2},{2,1},{3,4},{4,3},{5,6},{6,5},{9,10},{10,9},{11,12},{12,11},... | collective-permute-start | bytes 786440 | tf_op jit(solution)/shard_map/ppermute | solution.py:379
  49.5 32.6 %collective-permute-start.5 = (f32[2,128,256]{2,1,0:T(8,128)S(1)}, f32[2,128,256]{2,1,0:T(8,128)S(1)}, u32[]{:S(2)}, u32[]{:S(2)}) collective-permute-start(f32[2,128,256]{2,1,0:T(8,128)S(1)} %get-tuple-element.41.close), channel_id=1, source_target_pairs={{0,1},{1,0},{2,3},{3,2},{4,5},{5,4},{6,7},{7,6},{8,9},{9,8},{10,11... | collective-permute-start | bytes 786440 | tf_op jit(solution)/shard_map/ppermute | solution.py:379
  50.5 31.7 %collective-permute-start.6 = (f32[2,128,256]{2,1,0:T(8,128)S(1)}, f32[2,128,256]{2,1,0:T(8,128)S(1)}, u32[]{:S(2)}, u32[]{:S(2)}) collective-permute-start(f32[2,128,256]{2,1,0:T(8,128)S(1)} %get-tuple-element.42.far), channel_id=1, source_target_pairs={{1,2},{2,1},{3,4},{4,3},{5,6},{6,5},{9,10},{10,9},{11,12},{12,11},... | collective-permute-start | bytes 786440 | tf_op jit(solution)/shard_map/ppermute | solution.py:379
  53.5 29.1 %collective-permute-start.18 = (f32[2,128,256]{2,1,0:T(8,128)S(1)}, f32[2,128,256]{2,1,0:T(8,128)S(1)}, u32[]{:S(2)}, u32[]{:S(2)}) collective-permute-start(f32[2,128,256]{2,1,0:T(8,128)S(1)} %get-tuple-element.52.close), channel_id=1, source_target_pairs={{0,1},{1,0},{2,3},{3,2},{4,5},{5,4},{6,7},{7,6},{8,9},{9,8},{10,11... | collective-permute-start | bytes 786440 | tf_op jit(solution)/shard_map/ppermute | solution.py:379
  61.7 20.8 %collective-permute-start.19 = (f32[2,128,256]{2,1,0:T(8,128)S(1)}, f32[2,128,256]{2,1,0:T(8,128)S(1)}, u32[]{:S(2)}, u32[]{:S(2)}) collective-permute-start(f32[2,128,256]{2,1,0:T(8,128)S(1)} %get-tuple-element.53.far), channel_id=1, source_target_pairs={{1,2},{2,1},{3,4},{4,3},{5,6},{6,5},{9,10},{10,9},{11,12},{12,11},... | collective-permute-start | bytes 786440 | tf_op jit(solution)/shard_map/ppermute | solution.py:379
  64.3 4.9 %collective-permute-start.11 = (f32[8,128]{1,0:T(8,128)S(1)}, f32[8,128]{1,0:T(8,128)S(1)}, u32[]{:S(2)}, u32[]{:S(2)}) collective-permute-start(f32[8,128]{1,0:T(8,128)S(1)} %get-tuple-element.49), channel_id=1, source_target_pairs={{0,1},{1,0},{2,3},{3,2},{4,5},{5,4},{6,7},{7,6},{8,9},{9,8},{10,11... | collective-permute-start | bytes 12296 | tf_op jit(solution)/shard_map/ppermute | solution.py:405
  69.3 3.6 %collective-permute-start.12 = (f32[8,128]{1,0:T(8,128)S(1)}, f32[8,128]{1,0:T(8,128)S(1)}, u32[]{:S(2)}, u32[]{:S(2)}) collective-permute-start(f32[8,128]{1,0:T(8,128)S(1)} %max.15), channel_id=1, source_target_pairs={{0,2},{1,3},{2,0},{3,1},{4,6},{5,7},{6,4},{7,5},{8,10},{9,11},{10,... | collective-permute-start | bytes 12296 | tf_op jit(solution)/shard_map/ppermute | solution.py:405
  72.9 4.5 %collective-permute-start.13 = (f32[8,128]{1,0:T(8,128)S(1)}, f32[8,128]{1,0:T(8,128)S(1)}, u32[]{:S(2)}, u32[]{:S(2)}) collective-permute-start(f32[8,128]{1,0:T(8,128)S(1)} %max.16), channel_id=1, source_target_pairs={{0,4},{1,5},{2,6},{3,7},{4,0},{5,1},{6,2},{7,3},{8,12},{9,13},{10,... | collective-permute-start | bytes 12296 | tf_op jit(solution)/shard_map/ppermute | solution.py:405
  77.4 1.2 collective-permute-start.14
  78.6 3.6 %collective-permute-start.15 = (f32[8,128]{1,0:T(8,128)S(1)}, f32[8,128]{1,0:T(8,128)S(1)}, u32[]{:S(2)}, u32[]{:S(2)}) collective-permute-start(f32[8,128]{1,0:T(8,128)S(1)} %max.18), channel_id=1, source_target_pairs={{0,16},{8,24},{16,0},{24,8},{1,17},{9,25},{17,1},{25,9},{2,18},{10... | collective-permute-start | bytes 12296 | tf_op jit(solution)/shard_map/ppermute | solution.py:405
  82.4 3.1 %collective-permute-start.16 = (f32[2,128,512]{2,1,0:T(8,128)S(1)}, f32[2,128,512]{2,1,0:T(8,128)S(1)}, u32[]{:S(2)}, u32[]{:S(2)}) collective-permute-start(f32[2,128,512]{2,1,0:T(8,128)S(1)} %shard_map.91.near_half.refs_4_), channel_id=1, source_target_pairs={{0,8},{8,0},{16,24},{24,16},{1,9},{9,1},{17,25},{25,17},{2,10},{10... | collective-permute-start | bytes 1572872 | tf_op jit(solution)/shard_map/ppermute | solution.py:379
  82.8 10.5 %collective-permute-start.20 = (f32[2,128,512]{2,1,0:T(8,128)S(1)}, f32[2,128,512]{2,1,0:T(8,128)S(1)}, u32[]{:S(2)}, u32[]{:S(2)}) collective-permute-start(f32[2,128,512]{2,1,0:T(8,128)S(1)} %shard_map.93.cross_half.refs_9_), channel_id=1, source_target_pairs={{8,16},{16,8},{9,17},{17,9},{10,18},{18,10},{11,19},{19,11},{12,20... | collective-permute-start | bytes 1572872 | tf_op jit(solution)/shard_map/ppermute | solution.py:379
  98.0 2.7 %collective-permute-start.21 = (f32[2,128,512]{2,1,0:T(8,128)S(1)}, f32[2,128,512]{2,1,0:T(8,128)S(1)}, u32[]{:S(2)}, u32[]{:S(2)}) collective-permute-start(f32[2,128,512]{2,1,0:T(8,128)S(1)} %get-tuple-element.56), channel_id=1, source_target_pairs={{0,8},{8,0},{16,24},{24,16},{1,9},{9,1},{17,25},{25,17},{2,10},{10... | collective-permute-start | bytes 1572872 | tf_op jit(solution)/shard_map/ppermute | solution.py:379
  98.1 10.5 %collective-permute-start.24 = (f32[2,128,512]{2,1,0:T(8,128)S(1)}, f32[2,128,512]{2,1,0:T(8,128)S(1)}, u32[]{:S(2)}, u32[]{:S(2)}) collective-permute-start(f32[2,128,512]{2,1,0:T(8,128)S(1)} %get-tuple-element.61), channel_id=1, source_target_pairs={{8,16},{16,8},{9,17},{17,9},{10,18},{18,10},{11,19},{19,11},{12,20... | collective-permute-start | bytes 1572872 | tf_op jit(solution)/shard_map/ppermute | solution.py:379
  100.8 12.8 %collective-permute-start.22 = (f32[2,128,128]{2,1,0:T(8,128)S(1)}, f32[2,128,128]{2,1,0:T(8,128)S(1)}, u32[]{:S(2)}, u32[]{:S(2)}) collective-permute-start(f32[2,128,128]{2,1,0:T(8,128)S(1)} %get-tuple-element.58), channel_id=1, source_target_pairs={{0,1},{1,0},{2,3},{3,2},{4,5},{5,4},{6,7},{7,6},{8,9},{9,8},{10,11... | collective-permute-start | bytes 393224 | tf_op jit(solution)/shard_map/ppermute | solution.py:379
  102.7 10.9 %collective-permute-start.23 = (f32[2,128,128]{2,1,0:T(8,128)S(1)}, f32[2,128,128]{2,1,0:T(8,128)S(1)}, u32[]{:S(2)}, u32[]{:S(2)}) collective-permute-start(f32[2,128,128]{2,1,0:T(8,128)S(1)} %get-tuple-element.59), channel_id=1, source_target_pairs={{1,2},{2,1},{3,4},{4,3},{5,6},{6,5},{9,10},{10,9},{11,12},{12,11},... | collective-permute-start | bytes 393224 | tf_op jit(solution)/shard_map/ppermute | solution.py:379
  108.7 5.9 %collective-permute-start.25 = (f32[2,128,128]{2,1,0:T(8,128)S(1)}, f32[2,128,128]{2,1,0:T(8,128)S(1)}, u32[]{:S(2)}, u32[]{:S(2)}) collective-permute-start(f32[2,128,128]{2,1,0:T(8,128)S(1)} %get-tuple-element.63), channel_id=1, source_target_pairs={{0,1},{1,0},{2,3},{3,2},{4,5},{5,4},{6,7},{7,6},{8,9},{9,8},{10,11... | collective-permute-start | bytes 393224 | tf_op jit(solution)/shard_map/ppermute | solution.py:379
  111.2 7.7 %collective-permute-start.26 = (f32[2,128,128]{2,1,0:T(8,128)S(1)}, f32[2,128,128]{2,1,0:T(8,128)S(1)}, u32[]{:S(2)}, u32[]{:S(2)}) collective-permute-start(f32[2,128,128]{2,1,0:T(8,128)S(1)} %get-tuple-element.64), channel_id=1, source_target_pairs={{1,2},{2,1},{3,4},{4,3},{5,6},{6,5},{9,10},{10,9},{11,12},{12,11},... | collective-permute-start | bytes 393224 | tf_op jit(solution)/shard_map/ppermute | solution.py:379

commit v6 on v5

--- a/solution.py
+++ b/solution.py
@@ -114,7 +114,41 @@
         quadrants[index] = part if first else quadrants[index] + part
 
 
-def gradient_kernel(
+def load_side(ref, plane, left, win):
+    if not isinstance(ref, tuple):
+        return ref[plane, :, left * win : (left + 1) * win]
+    inner, outer = ref
+    half = win - HALO
+    if left:
+        return jnp.concatenate([inner[plane, :, half:], outer[plane, :, HALO:]], axis=1)
+    return jnp.concatenate([outer[plane, :, :HALO], inner[plane, :, :half]], axis=1)
+
+
+def store_side(ref, plane, rows, left, value):
+    win = value.shape[1]
+    if not isinstance(ref, tuple):
+        ref[plane, rows, left * win : (left + 1) * win] = value
+        return
+    inner, outer = ref
+    half = win - HALO
+    if left:
+        inner[plane, rows, half:] = value[:, :half]
+        outer[plane, rows, HALO:] = value[:, half:]
+    else:
+        outer[plane, rows, :HALO] = value[:, :HALO]
+        inner[plane, rows, :half] = value[:, HALO:]
+
+
+def gradient_kernel(*refs, first, last):
+    refs = list(refs)
+    if first:
+        refs[2:4] = [tuple(refs[2:4])]
+    if last:
+        refs[10:12] = [tuple(refs[10:12])]
+    gradient_body(*refs)
+
+
+def gradient_body(
     info, near_rows, cross_rows, near_half, cross_half, probe, amplitude, forward, backward,
     grad_near, grad_cross, mid_near, mid_cross, area, total,
 ):
@@ -123,8 +157,10 @@
     odd_row = flag(info, ODD)
     for plane in (0, 1):
         for left in (0, 1):
-            lanes = slice(left * win, (left + 1) * win)
-            parts = [ref[plane, :, lanes] for ref in (near_rows, near_half, cross_half, cross_rows)]
+            parts = [
+                load_side(ref, plane, left, win)
+                for ref in (near_rows, near_half, cross_half, cross_rows)
+            ]
             for index in range(4):
                 rows = slice((index % 2) * half, (index % 2 + 1) * half)
                 area[plane, 2 * (index // 2) + left, rows] = jnp.where(
@@ -193,15 +229,16 @@
 
 
 def by_halves(odd_row, total, plane, outs):
-    half, win = total.shape[2] // 2, total.shape[3]
+    half = total.shape[2] // 2
     for left in (0, 1):
-        lanes = slice(left * win, (left + 1) * win)
         parts = [
             total[plane, 2 * (k // 2) + left, (k % 2) * half : (k % 2 + 1) * half]
             for k in range(4)
         ]
         for index, (out, rows) in enumerate(outs):
-            out[plane, rows, lanes] = jnp.where(odd_row, parts[index], parts[3 - index])
+            store_side(
+                out, plane, rows, left, jnp.where(odd_row, parts[index], parts[3 - index])
+            )
 
 
 def light_kernel(info, probe, light_near, light_mid, light_cross, total):
@@ -275,15 +312,22 @@
     return jnp.where(even_col, tail, head), jnp.where(even_col, head, tail)
 
 
-def edges_kernel(info, specimen, close, far):
-    even_col = flag(info, EVEN_COL)
-    for plane in (0, 1):
-        close[plane], far[plane] = by_sides(
-            even_col, specimen[plane, :, :HALO], specimen[plane, :, specimen.shape[2] - HALO :]
-        )
-
-
-def widen_kernel(info, close, specimen, far, near_half, cross_half):
+def edges_kernel(specimen, close, far):
+    even_col = lax.axis_index("col") % 2 == 0
+    for plane in (0, 1):
+        head, tail = specimen[plane, :, :HALO], specimen[plane, :, specimen.shape[2] - HALO :]
+        close[plane] = jnp.where(even_col, tail, head)
+        far[plane] = jnp.where(even_col, head, tail)
+
+
+def center_kernel(info, specimen, cross):
+    odd_row = flag(info, ODD)
+    half = cross.shape[1]
+    for plane in (0, 1):
+        cross[plane] = jnp.where(odd_row, specimen[plane, half:], specimen[plane, :half])
+
+
+def widen_kernel(info, close, specimen, far, near_half, cross_half, cross_outer):
     odd_row, even_col = flag(info, ODD), flag(info, EVEN_COL)
     half, tile = near_half.shape[1], specimen.shape[2]
     for plane in (0, 1):
@@ -297,6 +341,8 @@
             top, bottom = source[:half], source[half:]
             near_half[plane, :, lanes] = jnp.where(odd, top, bottom)
             cross_half[plane, :, lanes] = jnp.where(odd, bottom, top)
+        cross_outer[plane, :, :HALO] = cross_half[plane, :, :HALO]
+        cross_outer[plane, :, HALO:] = cross_half[plane, :, HALO + tile :]
 
 
 def fold_kernel(info, mid, sent, close, far):
@@ -307,13 +353,12 @@
         close[plane], far[plane] = by_sides(even_col, block[:, :side], block[:, side:])
 
 
-def fold_last_kernel(info, mid, sent, close, core, far):
+def fold_last_kernel(info, mid, sent, close, far):
     even_col = flag(info, EVEN_COL)
-    tile = core.shape[2]
-    for plane in (0, 1):
-        block = mid[plane] + sent[plane]
-        close[plane], far[plane] = by_sides(even_col, block[:, :HALO], block[:, HALO + tile :])
-        core[plane] = block[:, HALO : HALO + tile]
+    for plane in (0, 1):
+        head = mid[plane, :, :HALO] + sent[plane, :, :HALO]
+        tail = mid[plane, :, mid.shape[2] - HALO :] + sent[plane, :, sent.shape[2] - HALO :]
+        close[plane], far[plane] = by_sides(even_col, head, tail)
 
 
 def update_kernel(info, close, far, from_close, from_far, light, peak, old, new):
@@ -344,12 +389,13 @@
     inner = slice(HALO, HALO + tile)
     for plane in (0, 1):
         news = []
-        for core, from_close, from_far, light, old in (halves[:5], halves[5:]):
+        for mid, add, from_close, from_far, light, old in (halves[:6], halves[6:]):
             right, left = by_sides(even_col, from_far[plane], from_close[plane])
             sent = [left, right]
             if tile > 2 * HALO:
                 sent.insert(1, jnp.zeros((half, tile - 2 * HALO), F32))
-            gradient = core[plane] + jnp.concatenate(sent, axis=1)
+            add = add[plane] if add.shape[2] == tile else add[plane, :, inner]
+            gradient = mid[plane, :, inner] + add + jnp.concatenate(sent, axis=1)
             news.append(old[plane, :, inner] - gradient / (light[:, inner] + most))
         out[plane, :half] = jnp.where(odd_row, news[0], news[1])
         out[plane, half:] = jnp.where(odd_row, news[1], news[0])
@@ -422,9 +468,14 @@
         jnp.concatenate([flags, corners])[:, None], (FLAGS + 2 * count, win)
     )
     band, wide, strip = shape(2, half, HALO), shape(2, half, 2 * side), shape(2, half, side)
-
-    close, far = kernel_call(edges_kernel, [shape(2, tile, HALO)] * 2, [VM] * 2)(info, specimen)
+    inner, outer = shape(2, half, tile), shape(2, half, 2 * HALO)
+
+    close, far = kernel_call(edges_kernel, [shape(2, tile, HALO)] * 2, [VM])(
+        specimen
+    )
     close, far = to_sides(close, far)
+
+    cross_inner = to_cross(kernel_call(center_kernel, [inner], [VM] * 2)(info, specimen))
 
     probes = kernel_call(roll_kernel, [shape(count, 2, win, win)], [SM, VM])(corners, probe_field)
     light_band = shape(1, half, 2 * side)
@@ -440,10 +491,10 @@
         amplitudes, pick, pick_back
     )
 
-    near_half, cross_half = kernel_call(widen_kernel, [wide] * 2, [VM] * 4)(
-        info, close, specimen, far
-    )
-    cross_rows = to_cross(cross_half)
+    near_half, cross_half, cross_outer = kernel_call(
+        widen_kernel, [wide] * 2 + [outer], [VM] * 4
+    )(info, close, specimen, far)
+    cross_rows = (cross_inner, to_cross(cross_outer))
     near_rows = to_near(near_half)
 
     close, far = kernel_call(
@@ -456,18 +507,22 @@
     peak = largest_of(found, ("col", "row"))
 
     for step in range(ITERS):
-        grad_near, grad_cross, mid_near, mid_cross = kernel_call(
-            gradient_kernel,
-            [wide] * 4,
-            [VM] * 9,
+        first, last = step == 0, step + 1 == ITERS
+        crossing = cross_rows if first else (cross_rows,)
+        grad_near, *grad_cross, mid_near, mid_cross = kernel_call(
+            functools.partial(gradient_kernel, first=first, last=last),
+            [wide] + ([inner, outer] if last else [wide]) + [wide] * 2,
+            [VM] * (9 + first),
             flops=count * 8 * 2 * win * 3 * win * win,
             scratch=[pltpu.VMEM((2, 4, win, win), F32)] * 2,
             grant=24,
         )(
-            info, near_rows, cross_rows, near_half, cross_half, probes, ordered,
+            info, near_rows, *crossing, near_half, cross_half, probes, ordered,
             forward, backward,
         )
-        sent_cross = to_cross(grad_cross)
+        sent_cross = to_cross(grad_cross[-1])
+        if last:
+            sent_inner = to_cross(grad_cross[0])
         sent_near = to_near(grad_near)
         if step + 1 < ITERS:
             halves = []
@@ -487,17 +542,15 @@
             near_rows = to_near(near_half)
         else:
             operands = []
-            for mid, sent, light, old in (
-                (mid_near, sent_near, light_near, near_half),
-                (mid_cross, sent_cross, light_cross, cross_half),
+            for mid, sent, add, light, old in (
+                (mid_near, sent_near, sent_near, light_near, near_half),
+                (mid_cross, sent_cross, sent_inner, light_cross, cross_half),
             ):
-                close, core, far = kernel_call(
-                    fold_last_kernel, [band, shape(2, half, tile), band], [VM] * 3
-                )(info, mid, sent)
+                close, far = kernel_call(fold_last_kernel, [band] * 2, [VM] * 3)(info, mid, sent)
                 from_close, from_far = to_sides(close, far)
-                operands += [core, from_close, from_far, light, old]
+                operands += [mid, add, from_close, from_far, light, old]
             return kernel_call(
-                finish_kernel, [shape(2, tile, tile)], [VM] * 12
+                finish_kernel, [shape(2, tile, tile)], [VM] * 14
             )(info, *operands, peak)
 
 

time: 120 us -> 122 us (1.017)
  the two profiles are of different devices: /device:TPU:22 before, /device:TPU:10 now
where the time goes in v6:
time: 122 us
  waiting for transfers between devices  52.3 us (43%)
  starting transfers between devices  51.8 us (42%)
  Pallas kernels  14.2 us (12%)
  local copies, waits for them, and re-layouts  2.46 us (2%)
    ppermute x24, starting transfers between devices, swapped(): return lax.ppermute(block, axis, route)  45.8 us
    ppermute x24, waiting for transfers between devices, swapped(): return lax.ppermute(block, axis, route)  40.7 us
    ppermute x5, waiting for transfers between devices, largest_of(): block = jnp.maximum(block, lax.ppermute(block, axis, route))  11.6 us
    pallas_call x2, Pallas kernels, steps(): kernel_call(functools.partial(gradient_kernel, first=first, last=last), [...  9.33 us
    ppermute x5, starting transfers between devices, largest_of(): block = jnp.maximum(block, lax.ppermute(block, axis, route))  5.96 us
  transfers between devices with their start and end apart: 29, of which 14 were waited for; matrix products, arithmetic and copies ran while one was open for 1% of the time, Pallas kernels for 3%

profile of v6, /device:TPU:10, one launch (start us, length us, event | category | flops | bytes accessed | tf_op | source)
XLA Modules:
  0.0 121.9 jit_solution(4652892137307094998)
XLA Ops:
  0.0 1.0 copy-done
  1.1 1.6 %collective-permute-start = (f32[2,256,128]{2,1,0:T(8,128)S(1)}, f32[2,256,128]{2,1,0:T(8,128)S(1)}, u32[]{:S(2)}, u32[]{:S(2)}) collective-permute-start(f32[2,256,128]{2,1,0:T(8,128)S(1)} %get-tuple-element.35), channel_id=1, source_target_pairs={{0,1},{1,0},{2,3},{3,2},{4,5},{5,4},{6,7},{7,6},{8,9},{9,8},{10,11... | collective-permute-start | bytes 786440 | tf_op jit(solution)/shard_map/ppermute | solution.py:425
  2.7 2.3 %collective-permute-start.1 = (f32[2,256,128]{2,1,0:T(8,128)S(1)}, f32[2,256,128]{2,1,0:T(8,128)S(1)}, u32[]{:S(2)}, u32[]{:S(2)}) collective-permute-start(f32[2,256,128]{2,1,0:T(8,128)S(1)} %get-tuple-element.36), channel_id=1, source_target_pairs={{1,2},{2,1},{3,4},{4,3},{5,6},{6,5},{9,10},{10,9},{11,12},{12,11},... | collective-permute-start | bytes 786440 | tf_op jit(solution)/shard_map/ppermute | solution.py:425
  5.0 0.7 broadcast_add_fusion
  5.7 0.1 copy.10
  5.8 0.1 add.19.corners
  5.9 0.1 concatenate.3
  6.0 8.9 %collective-permute-done.close = f32[2,256,128]{2,1,0:T(8,128)S(1)} collective-permute-done((f32[2,256,128]{2,1,0:T(8,128)S(1)}, f32[2,256,128]{2,1,0:T(8,128)S(1)}, u32[]{:S(2)}, u32[]{:S(2)}) %collective-permute-start) | collective-permute-done | bytes 262176 | tf_op jit(solution)/shard_map/ppermute | solution.py:425
  14.8 0.1 broadcast_in_dim.2.info.refs_0_
  14.9 1.0 copy-done.1
  15.9 0.1 shard_map.83
  16.1 0.0 copy-start.4
  16.1 0.1 collective-permute-start.2
  16.3 2.5 %collective-permute-start.3 = (f32[2,128,256]{2,1,0:T(8,128)S(1)}, f32[2,128,256]{2,1,0:T(8,128)S(1)}, u32[]{:S(2)}, u32[]{:S(2)}) collective-permute-start(f32[2,128,256]{2,1,0:T(8,128)S(1)} %shard_map.84), channel_id=1, source_target_pairs={{8,16},{16,8},{9,17},{17,9},{10,18},{18,10},{11,19},{19,11},{12,20... | collective-permute-start | bytes 786440 | tf_op jit(solution)/shard_map/ppermute | solution.py:425
  18.8 3.3 %collective-permute-start.4 = (f32[2,128,256]{2,1,0:T(8,128)S(1)}, f32[2,128,256]{2,1,0:T(8,128)S(1)}, u32[]{:S(2)}, u32[]{:S(2)}) collective-permute-start(f32[2,128,256]{2,1,0:T(8,128)S(1)} %get-tuple-element.38), channel_id=1, source_target_pairs={{8,16},{16,8},{9,17},{17,9},{10,18},{18,10},{11,19},{19,11},{12,20... | collective-permute-start | bytes 786440 | tf_op jit(solution)/shard_map/ppermute | solution.py:425
  22.1 1.2 shard_map.85.refs_6_.probe.refs_5_
  23.4 1.0 shard_map.86.refs_7_.refs_6_
  24.4 2.5 %collective-permute-done.4.refs_3_ = f32[2,128,256]{2,1,0:T(8,128)S(1)} collective-permute-done((f32[2,128,256]{2,1,0:T(8,128)S(1)}, f32[2,128,256]{2,1,0:T(8,128)S(1)}, u32[]{:S(2)}, u32[]{:S(2)}) %collective-permute-start.4) | collective-permute-done | bytes 262176 | tf_op jit(solution)/shard_map/ppermute | solution.py:425
  26.9 4.7 %shard_map.87 = (f32[2,128,512]{2,1,0:T(8,128)S(1)}, f32[2,128,512]{2,1,0:T(8,128)S(1)}, f32[2,128,512]{2,1,0:T(8,128)S(1)}, f32[2,128,512]{2,1,0:T(8,128)S(1)}) custom-call(s32[10,256]{1,0:T(8,128)S(1)} %broadcast_in_dim.2.info.refs_0_, f32[2,128,512]{2,1,0:T(8,128)S(1)} %collective-permute-done.2.refs_1_, ...), custom_call_target="tpu_custom_call" | custom-call | flops 2415919104 | bytes 6291456 | tf_op jit(solution)/shard_map/pallas_call | solution.py:512
  31.6 0.1 collective-permute-start.5
  31.7 0.5 shard_map.89
  32.1 0.6 collective-permute-start.8
  32.7 2.9 %collective-permute-start.18 = (f32[2,128,512]{2,1,0:T(8,128)S(1)}, f32[2,128,512]{2,1,0:T(8,128)S(1)}, u32[]{:S(2)}, u32[]{:S(2)}) collective-permute-start(f32[2,128,512]{2,1,0:T(8,128)S(1)} %get-tuple-element.52), channel_id=1, source_target_pairs={{8,16},{16,8},{9,17},{17,9},{10,18},{18,10},{11,19},{19,11},{12,20... | collective-permute-start | bytes 1572872 | tf_op jit(solution)/shard_map/ppermute | solution.py:425
  35.6 2.6 %collective-permute-start.9 = (f32[1,128,512]{2,1,0:T(8,128)S(1)}, f32[1,128,512]{2,1,0:T(8,128)S(1)}, u32[]{:S(2)}, u32[]{:S(2)}) collective-permute-start(f32[1,128,512]{2,1,0:T(8,128)S(1)} %get-tuple-element.46), channel_id=1, source_target_pairs={{8,16},{16,8},{9,17},{17,9},{10,18},{18,10},{11,19},{19,11},{12,20... | collective-permute-start | bytes 786440 | tf_op jit(solution)/shard_map/ppermute | solution.py:425
  38.3 7.7 %collective-permute-done.9.sent_cross = f32[1,128,512]{2,1,0:T(8,128)S(1)} collective-permute-done((f32[1,128,512]{2,1,0:T(8,128)S(1)}, f32[1,128,512]{2,1,0:T(8,128)S(1)}, u32[]{:S(2)}, u32[]{:S(2)}) %collective-permute-start.9) | collective-permute-done | bytes 262176 | tf_op jit(solution)/shard_map/ppermute | solution.py:425
  46.0 0.1 shard_map.90
  46.1 1.6 %collective-permute-start.10 = (f32[1,256,256]{2,1,0:T(8,128)S(1)}, f32[1,256,256]{2,1,0:T(8,128)S(1)}, u32[]{:S(2)}, u32[]{:S(2)}) collective-permute-start(f32[1,256,256]{2,1,0:T(8,128)S(1)} %get-tuple-element.47.close), channel_id=1, source_target_pairs={{0,1},{1,0},{2,3},{3,2},{4,5},{5,4},{6,7},{7,6},{8,9},{9,8},{10,11... | collective-permute-start | bytes 786440 | tf_op jit(solution)/shard_map/ppermute | solution.py:425
  47.6 1.9 %collective-permute-start.11 = (f32[1,256,256]{2,1,0:T(8,128)S(1)}, f32[1,256,256]{2,1,0:T(8,128)S(1)}, u32[]{:S(2)}, u32[]{:S(2)}) collective-permute-start(f32[1,256,256]{2,1,0:T(8,128)S(1)} %get-tuple-element.48.far), channel_id=1, source_target_pairs={{1,2},{2,1},{3,4},{4,3},{5,6},{6,5},{9,10},{10,9},{11,12},{12,11},... | collective-permute-start | bytes 786440 | tf_op jit(solution)/shard_map/ppermute | solution.py:425
  49.6 0.1 shard_map.88
  49.6 3.1 %collective-permute-start.6 = (f32[2,128,256]{2,1,0:T(8,128)S(1)}, f32[2,128,256]{2,1,0:T(8,128)S(1)}, u32[]{:S(2)}, u32[]{:S(2)}) collective-permute-start(f32[2,128,256]{2,1,0:T(8,128)S(1)} %get-tuple-element.42.close), channel_id=1, source_target_pairs={{0,1},{1,0},{2,3},{3,2},{4,5},{5,4},{6,7},{7,6},{8,9},{9,8},{10,11... | collective-permute-start | bytes 786440 | tf_op jit(solution)/shard_map/ppermute | solution.py:425
  52.7 1.9 %collective-permute-start.7 = (f32[2,128,256]{2,1,0:T(8,128)S(1)}, f32[2,128,256]{2,1,0:T(8,128)S(1)}, u32[]{:S(2)}, u32[]{:S(2)}) collective-permute-start(f32[2,128,256]{2,1,0:T(8,128)S(1)} %get-tuple-element.43.far), channel_id=1, source_target_pairs={{1,2},{2,1},{3,4},{4,3},{5,6},{6,5},{9,10},{10,9},{11,12},{12,11},... | collective-permute-start | bytes 786440 | tf_op jit(solution)/shard_map/ppermute | solution.py:425
  54.7 0.1 shard_map.93
  54.7 1.6 %collective-permute-start.19 = (f32[2,128,256]{2,1,0:T(8,128)S(1)}, f32[2,128,256]{2,1,0:T(8,128)S(1)}, u32[]{:S(2)}, u32[]{:S(2)}) collective-permute-start(f32[2,128,256]{2,1,0:T(8,128)S(1)} %get-tuple-element.53.close), channel_id=1, source_target_pairs={{0,1},{1,0},{2,3},{3,2},{4,5},{5,4},{6,7},{7,6},{8,9},{9,8},{10,11... | collective-permute-start | bytes 786440 | tf_op jit(solution)/shard_map/ppermute | solution.py:425
  56.3 6.5 %collective-permute-done.10.from_close = f32[1,256,256]{2,1,0:T(8,128)S(1)} collective-permute-done((f32[1,256,256]{2,1,0:T(8,128)S(1)}, f32[1,256,256]{2,1,0:T(8,128)S(1)}, u32[]{:S(2)}, u32[]{:S(2)}) %collective-permute-start.10) | collective-permute-done | bytes 262176 | tf_op jit(solution)/shard_map/ppermute | solution.py:425
  62.9 2.8 %collective-permute-start.20 = (f32[2,128,256]{2,1,0:T(8,128)S(1)}, f32[2,128,256]{2,1,0:T(8,128)S(1)}, u32[]{:S(2)}, u32[]{:S(2)}) collective-permute-start(f32[2,128,256]{2,1,0:T(8,128)S(1)} %get-tuple-element.54.far), channel_id=1, source_target_pairs={{1,2},{2,1},{3,4},{4,3},{5,6},{6,5},{9,10},{10,9},{11,12},{12,11},... | collective-permute-start | bytes 786440 | tf_op jit(solution)/shard_map/ppermute | solution.py:425
  65.7 0.1 shard_map.91
  65.8 1.1 collective-permute-start.12
  66.9 2.9 %collective-permute-done.12 = f32[8,128]{1,0:T(8,128)S(1)} collective-permute-done((f32[8,128]{1,0:T(8,128)S(1)}, f32[8,128]{1,0:T(8,128)S(1)}, u32[]{:S(2)}, u32[]{:S(2)}) %collective-permute-start.12) | collective-permute-done | bytes 4128 | tf_op jit(solution)/shard_map/ppermute | solution.py:451
  69.9 0.2 collective-permute-start.13
  70.0 3.5 %collective-permute-done.13 = f32[8,128]{1,0:T(8,128)S(1)} collective-permute-done((f32[8,128]{1,0:T(8,128)S(1)}, f32[8,128]{1,0:T(8,128)S(1)}, u32[]{:S(2)}, u32[]{:S(2)}) %collective-permute-start.13) | collective-permute-done | bytes 4128 | tf_op jit(solution)/shard_map/ppermute | solution.py:451
  73.5 3.5 %collective-permute-start.14 = (f32[8,128]{1,0:T(8,128)S(1)}, f32[8,128]{1,0:T(8,128)S(1)}, u32[]{:S(2)}, u32[]{:S(2)}) collective-permute-start(f32[8,128]{1,0:T(8,128)S(1)} %max.16), channel_id=1, source_target_pairs={{0,4},{1,5},{2,6},{3,7},{4,0},{5,1},{6,2},{7,3},{8,12},{9,13},{10,... | collective-permute-start | bytes 12296 | tf_op jit(solution)/shard_map/ppermute | solution.py:451
  77.0 1.6 %collective-permute-done.14 = f32[8,128]{1,0:T(8,128)S(1)} collective-permute-done((f32[8,128]{1,0:T(8,128)S(1)}, f32[8,128]{1,0:T(8,128)S(1)}, u32[]{:S(2)}, u32[]{:S(2)}) %collective-permute-start.14) | collective-permute-done | bytes 4128 | tf_op jit(solution)/shard_map/ppermute | solution.py:451
  78.6 1.2 collective-permute-done.15
  79.7 1.2 collective-permute-start.16
  80.9 2.4 %collective-permute-done.16 = f32[8,128]{1,0:T(8,128)S(1)} collective-permute-done((f32[8,128]{1,0:T(8,128)S(1)}, f32[8,128]{1,0:T(8,128)S(1)}, u32[]{:S(2)}, u32[]{:S(2)}) %collective-permute-start.16) | collective-permute-done | bytes 4128 | tf_op jit(solution)/shard_map/ppermute | solution.py:451
  83.3 0.3 shard_map.92.refs_3_.refs_5_
  83.6 0.1 collective-permute-start.17
  83.7 0.3 shard_map.94.refs_4_.refs_11_
  84.0 3.3 %collective-permute-start.21 = (f32[2,128,512]{2,1,0:T(8,128)S(1)}, f32[2,128,512]{2,1,0:T(8,128)S(1)}, u32[]{:S(2)}, u32[]{:S(2)}) collective-permute-start(f32[2,128,512]{2,1,0:T(8,128)S(1)} %shard_map.94.refs_4_.refs_11_), channel_id=1, source_target_pairs={{8,16},{16,8},{9,17},{17,9},{10,18},{18,10},{11,19},{19,11},{12,20... | collective-permute-start | bytes 1572872 | tf_op jit(solution)/shard_map/ppermute | solution.py:425
  87.3 7.1 %collective-permute-done.21.refs_2_ = f32[2,128,512]{2,1,0:T(8,128)S(1)} collective-permute-done((f32[2,128,512]{2,1,0:T(8,128)S(1)}, f32[2,128,512]{2,1,0:T(8,128)S(1)}, u32[]{:S(2)}, u32[]{:S(2)}) %collective-permute-start.21) | collective-permute-done | bytes 524320 | tf_op jit(solution)/shard_map/ppermute | solution.py:425
  94.5 4.7 %shard_map.95 = (f32[2,128,512]{2,1,0:T(8,128)S(1)}, f32[2,128,256]{2,1,0:T(8,128)S(1)}, f32[2,128,256]{2,1,0:T(8,128)S(1)}, f32[2,128,512]{2,1,0:T(8,128)S(1)}, f32[2,128,512]{2,1,0:T(8,128)S(1)}) custom-call(s32[10,256]{1,0:T(8,128)S(1)} %broadcast_in_dim.2.info.refs_0_, f32[2,128,512]{2,1,0:T(8,128)S(1)} %collective-permute-done.17.refs_1_, ...), custom_call_target="tpu_custom_call" | custom-call | flops 2415919104 | bytes 6291456 | tf_op jit(solution)/shard_map/pallas_call | solution.py:512
  99.2 0.1 collective-permute-start.22
  99.2 3.2 %collective-permute-start.26 = (f32[2,128,256]{2,1,0:T(8,128)S(1)}, f32[2,128,256]{2,1,0:T(8,128)S(1)}, u32[]{:S(2)}, u32[]{:S(2)}) collective-permute-start(f32[2,128,256]{2,1,0:T(8,128)S(1)} %get-tuple-element.62), channel_id=1, source_target_pairs={{8,16},{16,8},{9,17},{17,9},{10,18},{18,10},{11,19},{19,11},{12,20... | collective-permute-start | bytes 786440 | tf_op jit(solution)/shard_map/ppermute | solution.py:425
  102.4 2.4 %collective-permute-start.25 = (f32[2,128,256]{2,1,0:T(8,128)S(1)}, f32[2,128,256]{2,1,0:T(8,128)S(1)}, u32[]{:S(2)}, u32[]{:S(2)}) collective-permute-start(f32[2,128,256]{2,1,0:T(8,128)S(1)} %get-tuple-element.61), channel_id=1, source_target_pairs={{8,16},{16,8},{9,17},{17,9},{10,18},{18,10},{11,19},{19,11},{12,20... | collective-permute-start | bytes 786440 | tf_op jit(solution)/shard_map/ppermute | solution.py:425
  104.8 2.1 %collective-permute-done.26.sent = f32[2,128,256]{2,1,0:T(8,128)S(1)} collective-permute-done((f32[2,128,256]{2,1,0:T(8,128)S(1)}, f32[2,128,256]{2,1,0:T(8,128)S(1)}, u32[]{:S(2)}, u32[]{:S(2)}) %collective-permute-start.26) | collective-permute-done | bytes 262176 | tf_op jit(solution)/shard_map/ppermute | solution.py:425
  107.0 0.4 collective-permute-start.27
  107.3 4.1 %collective-permute-start.28 = (f32[2,128,128]{2,1,0:T(8,128)S(1)}, f32[2,128,128]{2,1,0:T(8,128)S(1)}, u32[]{:S(2)}, u32[]{:S(2)}) collective-permute-start(f32[2,128,128]{2,1,0:T(8,128)S(1)} %get-tuple-element.64), channel_id=1, source_target_pairs={{1,2},{2,1},{3,4},{4,3},{5,6},{6,5},{9,10},{10,9},{11,12},{12,11},... | collective-permute-start | bytes 393224 | tf_op jit(solution)/shard_map/ppermute | solution.py:425
  111.4 0.1 shard_map.96
  111.5 1.5 %collective-permute-start.23 = (f32[2,128,128]{2,1,0:T(8,128)S(1)}, f32[2,128,128]{2,1,0:T(8,128)S(1)}, u32[]{:S(2)}, u32[]{:S(2)}) collective-permute-start(f32[2,128,128]{2,1,0:T(8,128)S(1)} %get-tuple-element.58), channel_id=1, source_target_pairs={{0,1},{1,0},{2,3},{3,2},{4,5},{5,4},{6,7},{7,6},{8,9},{9,8},{10,11... | collective-permute-start | bytes 393224 | tf_op jit(solution)/shard_map/ppermute | solution.py:425
  113.0 1.9 %collective-permute-start.24 = (f32[2,128,128]{2,1,0:T(8,128)S(1)}, f32[2,128,128]{2,1,0:T(8,128)S(1)}, u32[]{:S(2)}, u32[]{:S(2)}) collective-permute-start(f32[2,128,128]{2,1,0:T(8,128)S(1)} %get-tuple-element.59), channel_id=1, source_target_pairs={{1,2},{2,1},{3,4},{4,3},{5,6},{6,5},{9,10},{10,9},{11,12},{12,11},... | collective-permute-start | bytes 393224 | tf_op jit(solution)/shard_map/ppermute | solution.py:425
  115.0 0.1 collective-permute-done.28.refs_9_
  115.1 1.4 %collective-permute-done.23.refs_2_ = f32[2,128,128]{2,1,0:T(8,128)S(1)} collective-permute-done((f32[2,128,128]{2,1,0:T(8,128)S(1)}, f32[2,128,128]{2,1,0:T(8,128)S(1)}, u32[]{:S(2)}, u32[]{:S(2)}) %collective-permute-start.23) | collective-permute-done | bytes 131104 | tf_op jit(solution)/shard_map/ppermute | solution.py:425
  116.5 4.3 %collective-permute-done.24.refs_3_ = f32[2,128,128]{2,1,0:T(8,128)S(1)} collective-permute-done((f32[2,128,128]{2,1,0:T(8,128)S(1)}, f32[2,128,128]{2,1,0:T(8,128)S(1)}, u32[]{:S(2)}, u32[]{:S(2)}) %collective-permute-start.24) | collective-permute-done | bytes 131104 | tf_op jit(solution)/shard_map/ppermute | solution.py:425
  120.8 1.1 shard_map.98
  (37 shorter events, 0.2 us)
Async XLA Ops:
  0.0 1.0 copy-start
  1.0 21.1 %copy-start.3 = (f32[2,256,256]{2,1,0:T(8,128)S(1)}, f32[2,256,256]{2,1,0:T(8,128)}, u32[]{:S(2)}) copy-start(f32[2,256,256]{2,1,0:T(8,128)} %probe.1) | copy-start | bytes 1572868
  1.1 13.7 %collective-permute-start = (f32[2,256,128]{2,1,0:T(8,128)S(1)}, f32[2,256,128]{2,1,0:T(8,128)S(1)}, u32[]{:S(2)}, u32[]{:S(2)}) collective-permute-start(f32[2,256,128]{2,1,0:T(8,128)S(1)} %get-tuple-element.35), channel_id=1, source_target_pairs={{0,1},{1,0},{2,3},{3,2},{4,5},{5,4},{6,7},{7,6},{8,9},{9,8},{10,11... | collective-permute-start | bytes 786440 | tf_op jit(solution)/shard_map/ppermute | solution.py:425
  2.7 12.1 %collective-permute-start.1 = (f32[2,256,128]{2,1,0:T(8,128)S(1)}, f32[2,256,128]{2,1,0:T(8,128)S(1)}, u32[]{:S(2)}, u32[]{:S(2)}) collective-permute-start(f32[2,256,128]{2,1,0:T(8,128)S(1)} %get-tuple-element.36), channel_id=1, source_target_pairs={{1,2},{2,1},{3,4},{4,3},{5,6},{6,5},{9,10},{10,9},{11,12},{12,11},... | collective-permute-start | bytes 786440 | tf_op jit(solution)/shard_map/ppermute | solution.py:425
  14.9 1.0 copy-start.1
  16.1 7.2 %copy-start.2 = (f32[1,1,3,256,256]{4,3,2,1,0:T(8,128)S(1)}, f32[1,1,3,256,256]{4,3,2,1,0:T(8,128)}, u32[]{:S(2)}) copy-start(f32[1,1,3,256,256]{4,3,2,1,0:T(8,128)} %amplitude.1) | copy-start | bytes 2359300
  16.1 7.2 %copy-start.4 = (bf16[256,256]{1,0:T(8,128)(2,1)S(1)}, bf16[256,256]{1,0:T(8,128)(2,1)}, u32[]{:S(2)}) copy-start(bf16[256,256]{1,0:T(8,128)(2,1)} %constant.42.clone.pick_back) | copy-start | bytes 393220
  16.1 7.2 %copy-start.5 = (bf16[256,256]{1,0:T(8,128)(2,1)S(1)}, bf16[256,256]{1,0:T(8,128)(2,1)}, u32[]{:S(2)}) copy-start(bf16[256,256]{1,0:T(8,128)(2,1)} %constant.41.clone.pick) | copy-start | bytes 393220
  16.1 10.8 %collective-permute-start.2 = (f32[2,128,512]{2,1,0:T(8,128)S(1)}, f32[2,128,512]{2,1,0:T(8,128)S(1)}, u32[]{:S(2)}, u32[]{:S(2)}) collective-permute-start(f32[2,128,512]{2,1,0:T(8,128)S(1)} %get-tuple-element.37.refs_4_.old), channel_id=1, source_target_pairs={{0,8},{8,0},{16,24},{24,16},{1,9},{9,1},{17,25},{25,17},{2,10},{10... | collective-permute-start | bytes 1572872 | tf_op jit(solution)/shard_map/ppermute | solution.py:425
  16.3 8.1 %collective-permute-start.3 = (f32[2,128,256]{2,1,0:T(8,128)S(1)}, f32[2,128,256]{2,1,0:T(8,128)S(1)}, u32[]{:S(2)}, u32[]{:S(2)}) collective-permute-start(f32[2,128,256]{2,1,0:T(8,128)S(1)} %shard_map.84), channel_id=1, source_target_pairs={{8,16},{16,8},{9,17},{17,9},{10,18},{18,10},{11,19},{19,11},{12,20... | collective-permute-start | bytes 786440 | tf_op jit(solution)/shard_map/ppermute | solution.py:425
  18.8 8.1 %copy-start.6 = (bf16[2,2,256,256]{3,2,1,0:T(8,128)(2,1)S(1)}, bf16[2,2,256,256]{3,2,1,0:T(8,128)(2,1)}, u32[]{:S(2)}) copy-start(bf16[2,2,256,256]{3,2,1,0:T(8,128)(2,1)} %constant.40.clone.refs_9_.refs_8_) | copy-start | bytes 1572868
  18.8 8.1 %copy-start.7 = (bf16[2,2,256,256]{3,2,1,0:T(8,128)(2,1)S(1)}, bf16[2,2,256,256]{3,2,1,0:T(8,128)(2,1)}, u32[]{:S(2)}) copy-start(bf16[2,2,256,256]{3,2,1,0:T(8,128)(2,1)} %constant.39.clone.refs_8_.refs_7_) | copy-start | bytes 1572868
  18.8 8.1 %collective-permute-start.4 = (f32[2,128,256]{2,1,0:T(8,128)S(1)}, f32[2,128,256]{2,1,0:T(8,128)S(1)}, u32[]{:S(2)}, u32[]{:S(2)}) collective-permute-start(f32[2,128,256]{2,1,0:T(8,128)S(1)} %get-tuple-element.38), channel_id=1, source_target_pairs={{8,16},{16,8},{9,17},{17,9},{10,18},{18,10},{11,19},{19,11},{12,20... | collective-permute-start | bytes 786440 | tf_op jit(solution)/shard_map/ppermute | solution.py:425
  31.6 18.0 %collective-permute-start.5 = (f32[2,128,512]{2,1,0:T(8,128)S(1)}, f32[2,128,512]{2,1,0:T(8,128)S(1)}, u32[]{:S(2)}, u32[]{:S(2)}) collective-permute-start(f32[2,128,512]{2,1,0:T(8,128)S(1)} %get-tuple-element.41), channel_id=1, source_target_pairs={{0,8},{8,0},{16,24},{24,16},{1,9},{9,1},{17,25},{25,17},{2,10},{10... | collective-permute-start | bytes 1572872 | tf_op jit(solution)/shard_map/ppermute | solution.py:425
  32.1 6.1 %collective-permute-start.8 = (f32[1,128,512]{2,1,0:T(8,128)S(1)}, f32[1,128,512]{2,1,0:T(8,128)S(1)}, u32[]{:S(2)}, u32[]{:S(2)}) collective-permute-start(f32[1,128,512]{2,1,0:T(8,128)S(1)} %get-tuple-element.45), channel_id=1, source_target_pairs={{0,8},{8,0},{16,24},{24,16},{1,9},{9,1},{17,25},{25,17},{2,10},{10... | collective-permute-start | bytes 786440 | tf_op jit(solution)/shard_map/ppermute | solution.py:425
  32.7 21.9 %collective-permute-start.18 = (f32[2,128,512]{2,1,0:T(8,128)S(1)}, f32[2,128,512]{2,1,0:T(8,128)S(1)}, u32[]{:S(2)}, u32[]{:S(2)}) collective-permute-start(f32[2,128,512]{2,1,0:T(8,128)S(1)} %get-tuple-element.52), channel_id=1, source_target_pairs={{8,16},{16,8},{9,17},{17,9},{10,18},{18,10},{11,19},{19,11},{12,20... | collective-permute-start | bytes 1572872 | tf_op jit(solution)/shard_map/ppermute | solution.py:425
  35.6 10.4 %collective-permute-start.9 = (f32[1,128,512]{2,1,0:T(8,128)S(1)}, f32[1,128,512]{2,1,0:T(8,128)S(1)}, u32[]{:S(2)}, u32[]{:S(2)}) collective-permute-start(f32[1,128,512]{2,1,0:T(8,128)S(1)} %get-tuple-element.46), channel_id=1, source_target_pairs={{8,16},{16,8},{9,17},{17,9},{10,18},{18,10},{11,19},{19,11},{12,20... | collective-permute-start | bytes 786440 | tf_op jit(solution)/shard_map/ppermute | solution.py:425
  46.1 16.8 %collective-permute-start.10 = (f32[1,256,256]{2,1,0:T(8,128)S(1)}, f32[1,256,256]{2,1,0:T(8,128)S(1)}, u32[]{:S(2)}, u32[]{:S(2)}) collective-permute-start(f32[1,256,256]{2,1,0:T(8,128)S(1)} %get-tuple-element.47.close), channel_id=1, source_target_pairs={{0,1},{1,0},{2,3},{3,2},{4,5},{5,4},{6,7},{7,6},{8,9},{9,8},{10,11... | collective-permute-start | bytes 786440 | tf_op jit(solution)/shard_map/ppermute | solution.py:425
  47.6 18.1 %collective-permute-start.11 = (f32[1,256,256]{2,1,0:T(8,128)S(1)}, f32[1,256,256]{2,1,0:T(8,128)S(1)}, u32[]{:S(2)}, u32[]{:S(2)}) collective-permute-start(f32[1,256,256]{2,1,0:T(8,128)S(1)} %get-tuple-element.48.far), channel_id=1, source_target_pairs={{1,2},{2,1},{3,4},{4,3},{5,6},{6,5},{9,10},{10,9},{11,12},{12,11},... | collective-permute-start | bytes 786440 | tf_op jit(solution)/shard_map/ppermute | solution.py:425
  49.6 33.7 %collective-permute-start.6 = (f32[2,128,256]{2,1,0:T(8,128)S(1)}, f32[2,128,256]{2,1,0:T(8,128)S(1)}, u32[]{:S(2)}, u32[]{:S(2)}) collective-permute-start(f32[2,128,256]{2,1,0:T(8,128)S(1)} %get-tuple-element.42.close), channel_id=1, source_target_pairs={{0,1},{1,0},{2,3},{3,2},{4,5},{5,4},{6,7},{7,6},{8,9},{9,8},{10,11... | collective-permute-start | bytes 786440 | tf_op jit(solution)/shard_map/ppermute | solution.py:425
  52.7 30.6 %collective-permute-start.7 = (f32[2,128,256]{2,1,0:T(8,128)S(1)}, f32[2,128,256]{2,1,0:T(8,128)S(1)}, u32[]{:S(2)}, u32[]{:S(2)}) collective-permute-start(f32[2,128,256]{2,1,0:T(8,128)S(1)} %get-tuple-element.43.far), channel_id=1, source_target_pairs={{1,2},{2,1},{3,4},{4,3},{5,6},{6,5},{9,10},{10,9},{11,12},{12,11},... | collective-permute-start | bytes 786440 | tf_op jit(solution)/shard_map/ppermute | solution.py:425
  54.7 29.0 %collective-permute-start.19 = (f32[2,128,256]{2,1,0:T(8,128)S(1)}, f32[2,128,256]{2,1,0:T(8,128)S(1)}, u32[]{:S(2)}, u32[]{:S(2)}) collective-permute-start(f32[2,128,256]{2,1,0:T(8,128)S(1)} %get-tuple-element.53.close), channel_id=1, source_target_pairs={{0,1},{1,0},{2,3},{3,2},{4,5},{5,4},{6,7},{7,6},{8,9},{9,8},{10,11... | collective-permute-start | bytes 786440 | tf_op jit(solution)/shard_map/ppermute | solution.py:425
  62.9 20.8 %collective-permute-start.20 = (f32[2,128,256]{2,1,0:T(8,128)S(1)}, f32[2,128,256]{2,1,0:T(8,128)S(1)}, u32[]{:S(2)}, u32[]{:S(2)}) collective-permute-start(f32[2,128,256]{2,1,0:T(8,128)S(1)} %get-tuple-element.54.far), channel_id=1, source_target_pairs={{1,2},{2,1},{3,4},{4,3},{5,6},{6,5},{9,10},{10,9},{11,12},{12,11},... | collective-permute-start | bytes 786440 | tf_op jit(solution)/shard_map/ppermute | solution.py:425
  65.8 4.1 %collective-permute-start.12 = (f32[8,128]{1,0:T(8,128)S(1)}, f32[8,128]{1,0:T(8,128)S(1)}, u32[]{:S(2)}, u32[]{:S(2)}) collective-permute-start(f32[8,128]{1,0:T(8,128)S(1)} %get-tuple-element.50), channel_id=1, source_target_pairs={{0,1},{1,0},{2,3},{3,2},{4,5},{5,4},{6,7},{7,6},{8,9},{9,8},{10,11... | collective-permute-start | bytes 12296 | tf_op jit(solution)/shard_map/ppermute | solution.py:451
  69.9 3.6 %collective-permute-start.13 = (f32[8,128]{1,0:T(8,128)S(1)}, f32[8,128]{1,0:T(8,128)S(1)}, u32[]{:S(2)}, u32[]{:S(2)}) collective-permute-start(f32[8,128]{1,0:T(8,128)S(1)} %max.15), channel_id=1, source_target_pairs={{0,2},{1,3},{2,0},{3,1},{4,6},{5,7},{6,4},{7,5},{8,10},{9,11},{10,... | collective-permute-start | bytes 12296 | tf_op jit(solution)/shard_map/ppermute | solution.py:451
  73.5 5.1 %collective-permute-start.14 = (f32[8,128]{1,0:T(8,128)S(1)}, f32[8,128]{1,0:T(8,128)S(1)}, u32[]{:S(2)}, u32[]{:S(2)}) collective-permute-start(f32[8,128]{1,0:T(8,128)S(1)} %max.16), channel_id=1, source_target_pairs={{0,4},{1,5},{2,6},{3,7},{4,0},{5,1},{6,2},{7,3},{8,12},{9,13},{10,... | collective-permute-start | bytes 12296 | tf_op jit(solution)/shard_map/ppermute | solution.py:451
  78.6 1.2 collective-permute-start.15
  79.7 3.6 %collective-permute-start.16 = (f32[8,128]{1,0:T(8,128)S(1)}, f32[8,128]{1,0:T(8,128)S(1)}, u32[]{:S(2)}, u32[]{:S(2)}) collective-permute-start(f32[8,128]{1,0:T(8,128)S(1)} %max.18), channel_id=1, source_target_pairs={{0,16},{8,24},{16,0},{24,8},{1,17},{9,25},{17,1},{25,9},{2,18},{10... | collective-permute-start | bytes 12296 | tf_op jit(solution)/shard_map/ppermute | solution.py:451
  83.6 3.7 %collective-permute-start.17 = (f32[2,128,512]{2,1,0:T(8,128)S(1)}, f32[2,128,512]{2,1,0:T(8,128)S(1)}, u32[]{:S(2)}, u32[]{:S(2)}) collective-permute-start(f32[2,128,512]{2,1,0:T(8,128)S(1)} %shard_map.92.refs_3_.refs_5_), channel_id=1, source_target_pairs={{0,8},{8,0},{16,24},{24,16},{1,9},{9,1},{17,25},{25,17},{2,10},{10... | collective-permute-start | bytes 1572872 | tf_op jit(solution)/shard_map/ppermute | solution.py:425
  84.0 10.5 %collective-permute-start.21 = (f32[2,128,512]{2,1,0:T(8,128)S(1)}, f32[2,128,512]{2,1,0:T(8,128)S(1)}, u32[]{:S(2)}, u32[]{:S(2)}) collective-permute-start(f32[2,128,512]{2,1,0:T(8,128)S(1)} %shard_map.94.refs_4_.refs_11_), channel_id=1, source_target_pairs={{8,16},{16,8},{9,17},{17,9},{10,18},{18,10},{11,19},{19,11},{12,20... | collective-permute-start | bytes 1572872 | tf_op jit(solution)/shard_map/ppermute | solution.py:425
  99.2 12.3 %collective-permute-start.22 = (f32[2,128,512]{2,1,0:T(8,128)S(1)}, f32[2,128,512]{2,1,0:T(8,128)S(1)}, u32[]{:S(2)}, u32[]{:S(2)}) collective-permute-start(f32[2,128,512]{2,1,0:T(8,128)S(1)} %get-tuple-element.57), channel_id=1, source_target_pairs={{0,8},{8,0},{16,24},{24,16},{1,9},{9,1},{17,25},{25,17},{2,10},{10... | collective-permute-start | bytes 1572872 | tf_op jit(solution)/shard_map/ppermute | solution.py:425
  99.2 7.7 %collective-permute-start.26 = (f32[2,128,256]{2,1,0:T(8,128)S(1)}, f32[2,128,256]{2,1,0:T(8,128)S(1)}, u32[]{:S(2)}, u32[]{:S(2)}) collective-permute-start(f32[2,128,256]{2,1,0:T(8,128)S(1)} %get-tuple-element.62), channel_id=1, source_target_pairs={{8,16},{16,8},{9,17},{17,9},{10,18},{18,10},{11,19},{19,11},{12,20... | collective-permute-start | bytes 786440 | tf_op jit(solution)/shard_map/ppermute | solution.py:425
  102.4 12.6 %collective-permute-start.25 = (f32[2,128,256]{2,1,0:T(8,128)S(1)}, f32[2,128,256]{2,1,0:T(8,128)S(1)}, u32[]{:S(2)}, u32[]{:S(2)}) collective-permute-start(f32[2,128,256]{2,1,0:T(8,128)S(1)} %get-tuple-element.61), channel_id=1, source_target_pairs={{8,16},{16,8},{9,17},{17,9},{10,18},{18,10},{11,19},{19,11},{12,20... | collective-permute-start | bytes 786440 | tf_op jit(solution)/shard_map/ppermute | solution.py:425
  107.0 8.0 %collective-permute-start.27 = (f32[2,128,128]{2,1,0:T(8,128)S(1)}, f32[2,128,128]{2,1,0:T(8,128)S(1)}, u32[]{:S(2)}, u32[]{:S(2)}) collective-permute-start(f32[2,128,128]{2,1,0:T(8,128)S(1)} %get-tuple-element.63), channel_id=1, source_target_pairs={{0,1},{1,0},{2,3},{3,2},{4,5},{5,4},{6,7},{7,6},{8,9},{9,8},{10,11... | collective-permute-start | bytes 393224 | tf_op jit(solution)/shard_map/ppermute | solution.py:425
  107.3 7.7 %collective-permute-start.28 = (f32[2,128,128]{2,1,0:T(8,128)S(1)}, f32[2,128,128]{2,1,0:T(8,128)S(1)}, u32[]{:S(2)}, u32[]{:S(2)}) collective-permute-start(f32[2,128,128]{2,1,0:T(8,128)S(1)} %get-tuple-element.64), channel_id=1, source_target_pairs={{1,2},{2,1},{3,4},{4,3},{5,6},{6,5},{9,10},{10,9},{11,12},{12,11},... | collective-permute-start | bytes 393224 | tf_op jit(solution)/shard_map/ppermute | solution.py:425
  111.5 5.0 %collective-permute-start.23 = (f32[2,128,128]{2,1,0:T(8,128)S(1)}, f32[2,128,128]{2,1,0:T(8,128)S(1)}, u32[]{:S(2)}, u32[]{:S(2)}) collective-permute-start(f32[2,128,128]{2,1,0:T(8,128)S(1)} %get-tuple-element.58), channel_id=1, source_target_pairs={{0,1},{1,0},{2,3},{3,2},{4,5},{5,4},{6,7},{7,6},{8,9},{9,8},{10,11... | collective-permute-start | bytes 393224 | tf_op jit(solution)/shard_map/ppermute | solution.py:425
  113.0 7.7 %collective-permute-start.24 = (f32[2,128,128]{2,1,0:T(8,128)S(1)}, f32[2,128,128]{2,1,0:T(8,128)S(1)}, u32[]{:S(2)}, u32[]{:S(2)}) collective-permute-start(f32[2,128,128]{2,1,0:T(8,128)S(1)} %get-tuple-element.59), channel_id=1, source_target_pairs={{1,2},{2,1},{3,4},{4,3},{5,6},{6,5},{9,10},{10,9},{11,12},{12,11},... | collective-permute-start | bytes 393224 | tf_op jit(solution)/shard_map/ppermute | solution.py:425

commit v7 on v6

--- a/solution.py
+++ b/solution.py
@@ -117,11 +117,13 @@
 def load_side(ref, plane, left, win):
     if not isinstance(ref, tuple):
         return ref[plane, :, left * win : (left + 1) * win]
-    inner, outer = ref
+    packed, outer = ref
     half = win - HALO
+    width = packed.shape[2] // 2
+    inner = packed[1, :, plane * width : (plane + 1) * width]
     if left:
-        return jnp.concatenate([inner[plane, :, half:], outer[plane, :, HALO:]], axis=1)
-    return jnp.concatenate([outer[plane, :, :HALO], inner[plane, :, :half]], axis=1)
+        return jnp.concatenate([inner[:, half:], outer[plane, :, HALO:]], axis=1)
+    return jnp.concatenate([outer[plane, :, :HALO], inner[:, :half]], axis=1)
 
 
 def store_side(ref, plane, rows, left, value):
@@ -241,7 +243,13 @@
             )
 
 
-def light_kernel(info, probe, light_near, light_mid, light_cross, total):
+def light_kernel(info, probe, specimen, light_near, light_mid, message, total):
+    odd_row = flag(info, ODD)
+    edge, tile = message.shape[1], specimen.shape[2]
+    for plane in (0, 1):
+        message[1, :, plane * tile : (plane + 1) * tile] = jnp.where(
+            odd_row, specimen[plane, edge:], specimen[plane, :edge]
+        )
     win = probe.shape[2]
     half = win // 2
     for position in range(probe.shape[0]):
@@ -253,7 +261,7 @@
         flag(info, ODD), total, 0,
         (
             (light_near, whole), (light_mid, slice(0, half)),
-            (light_mid, slice(half, win)), (light_cross, whole),
+            (light_mid, slice(half, win)), (message, whole),
         ),
     )
 
@@ -318,13 +326,6 @@
         head, tail = specimen[plane, :, :HALO], specimen[plane, :, specimen.shape[2] - HALO :]
         close[plane] = jnp.where(even_col, tail, head)
         far[plane] = jnp.where(even_col, head, tail)
-
-
-def center_kernel(info, specimen, cross):
-    odd_row = flag(info, ODD)
-    half = cross.shape[1]
-    for plane in (0, 1):
-        cross[plane] = jnp.where(odd_row, specimen[plane, half:], specimen[plane, :half])
 
 
 def widen_kernel(info, close, specimen, far, near_half, cross_half, cross_outer):
@@ -439,18 +440,19 @@
     return close, far
 
 
-def largest_of(block, axes):
-    for axis in axes:
-        count = lax.axis_size(axis)
-        reach = 1
-        while reach < count:
-            if count & (count - 1) == 0:
-                route = [(i, i ^ reach) for i in range(count)]
-            else:
-                route = [(i, (i + reach) % count) for i in range(count)]
-            block = jnp.maximum(block, lax.ppermute(block, axis, route))
-            reach *= 2
+def largest_of(block, axis, reaches):
+    count = lax.axis_size(axis)
+    for reach in reaches:
+        if count & (count - 1) == 0:
+            route = [(i, i ^ reach) for i in range(count)]
+        else:
+            route = [(i, (i + reach) % count) for i in range(count)]
+        block = jnp.maximum(block, lax.ppermute(block, axis, route))
     return block
+
+
+def doublings(axis):
+    return [2**k for k in range((lax.axis_size(axis) - 1).bit_length())]
 
 
 def steps(specimen, probe_field, offsets, amplitudes):
@@ -475,17 +477,15 @@
     )
     close, far = to_sides(close, far)
 
-    cross_inner = to_cross(kernel_call(center_kernel, [inner], [VM] * 2)(info, specimen))
-
     probes = kernel_call(roll_kernel, [shape(count, 2, win, win)], [SM, VM])(corners, probe_field)
     light_band = shape(1, half, 2 * side)
-    light_near, light_mid, light_cross = kernel_call(
+    light_near, light_mid, message = kernel_call(
         light_kernel,
-        [light_band, shape(1, tile, 2 * side), light_band],
-        [VM] * 2,
+        [light_band, shape(1, tile, 2 * side), wide],
+        [VM] * 3,
         scratch=[pltpu.VMEM((1, 4, win, win), F32)],
-    )(info, probes)
-    light_cross = to_cross(light_cross)
+    )(info, probes, specimen)
+    message = to_cross(message)
     light_near = to_near(light_near)
     ordered = kernel_call(order_kernel, [shape(count, win, win)], [VM] * 3)(
         amplitudes, pick, pick_back
@@ -494,17 +494,19 @@
     near_half, cross_half, cross_outer = kernel_call(
         widen_kernel, [wide] * 2 + [outer], [VM] * 4
     )(info, close, specimen, far)
-    cross_rows = (cross_inner, to_cross(cross_outer))
+    cross_rows = (message, to_cross(cross_outer))
     near_rows = to_near(near_half)
 
     close, far = kernel_call(
         light_fold_kernel, [shape(1, tile, side)] * 2, [VM] * 4
-    )(info, light_mid, light_near, light_cross)
+    )(info, light_mid, light_near, message)
     from_close, from_far = to_sides(close, far)
     light_near, light_cross, found = kernel_call(
         light_sum_kernel, [shape(half, 2 * side)] * 2 + [shape(8, LANES)], [VM] * 5
     )(info, close, far, from_close, from_far)
-    peak = largest_of(found, ("col", "row"))
+    found = largest_of(found, "col", doublings("col"))
+    found = largest_of(found, "row", doublings("row")[:0:-1])
+    peak = None
 
     for step in range(ITERS):
         first, last = step == 0, step + 1 == ITERS
@@ -532,6 +534,9 @@
             ):
                 close, far = kernel_call(fold_kernel, [strip] * 2, [VM] * 3)(info, mid, sent)
                 from_close, from_far = to_sides(close, far)
+                if peak is None:
+                    found, from_close = lax.optimization_barrier((found, from_close))
+                    peak = largest_of(found, "row", doublings("row")[:1])
                 halves.append(
                     kernel_call(update_kernel, [wide], [VM] * 8)(
                         info, close, far, from_close, from_far, light, peak, old

time: 122 us -> 121 us (level)
  starting transfers between devices: 51.8 us -> 49.8 us
    ppermute x5, waiting for transfers between devices: 11.6 us -> 19.5 us  [largest_of(): block = jnp.maximum(block, lax.ppermute(block, axis, route))]
    ppermute x24 -> x23, waiting for transfers between devices: 40.7 us -> 33.7 us  [swapped(): return lax.ppermute(block, axis, route)]
    ppermute x24 -> x23, starting transfers between devices: 45.8 us -> 43.7 us  [swapped(): return lax.ppermute(block, axis, route)]
  transfers between devices with their start and end apart: 29 -> 28, of which waited for: 14 -> 15; matrix products, arithmetic and copies ran while one was open for 1% -> 1% of each run, Pallas kernels for 3% -> 3%
where the time goes in v7:
time: 121 us
  waiting for transfers between devices  53.2 us (44%)
  starting transfers between devices  49.8 us (41%)
  Pallas kernels  14.2 us (12%)
  local copies, waits for them, and re-layouts  2.45 us (2%)
    ppermute x23, starting transfers between devices, swapped(): return lax.ppermute(block, axis, route)  43.7 us
    ppermute x23, waiting for transfers between devices, swapped(): return lax.ppermute(block, axis, route)  33.7 us
    ppermute x5, waiting for transfers between devices, largest_of(): block = jnp.maximum(block, lax.ppermute(block, axis, route))  19.5 us
    pallas_call x2, Pallas kernels, steps(): kernel_call(functools.partial(gradient_kernel, first=first, last=last), [...  9.34 us
    ppermute x5, starting transfers between devices, largest_of(): block = jnp.maximum(block, lax.ppermute(block, axis, route))  6.04 us
  transfers between devices with their start and end apart: 28, of which 15 were waited for; matrix products, arithmetic and copies ran while one was open for 1% of the time, Pallas kernels for 3%

profile of v7, /device:TPU:10, one launch (start us, length us, event | category | flops | bytes accessed | tf_op | source)
XLA Modules:
  0.0 120.7 jit_solution(7318137329631900994)
XLA Ops:
  0.0 1.0 copy-done
  1.1 1.6 %collective-permute-start = (f32[2,256,128]{2,1,0:T(8,128)S(1)}, f32[2,256,128]{2,1,0:T(8,128)S(1)}, u32[]{:S(2)}, u32[]{:S(2)}) collective-permute-start(f32[2,256,128]{2,1,0:T(8,128)S(1)} %get-tuple-element.37), channel_id=1, source_target_pairs={{0,1},{1,0},{2,3},{3,2},{4,5},{5,4},{6,7},{7,6},{8,9},{9,8},{10,11... | collective-permute-start | bytes 786440 | tf_op jit(solution)/shard_map/ppermute | solution.py:426
  2.7 2.3 %collective-permute-start.1 = (f32[2,256,128]{2,1,0:T(8,128)S(1)}, f32[2,256,128]{2,1,0:T(8,128)S(1)}, u32[]{:S(2)}, u32[]{:S(2)}) collective-permute-start(f32[2,256,128]{2,1,0:T(8,128)S(1)} %get-tuple-element.38), channel_id=1, source_target_pairs={{1,2},{2,1},{3,4},{4,3},{5,6},{6,5},{9,10},{10,9},{11,12},{12,11},... | collective-permute-start | bytes 786440 | tf_op jit(solution)/shard_map/ppermute | solution.py:426
  5.0 0.7 broadcast_add_fusion
  5.7 0.1 copy.10
  5.8 0.1 add.19.corners
  5.9 1.0 copy-done.3
  6.9 1.2 %shard_map.84.probe.refs_6_.refs_5_ = f32[3,2,256,256]{3,2,1,0:T(8,128)S(1)} custom-call(s32[6]{0:T(128)S(1)} %add.19.corners, f32[2,256,256]{2,1,0:T(8,128)S(1)} %copy-done.3), custom_call_target="tpu_custom_call" | custom-call | bytes 4718592 | tf_op jit(solution)/shard_map/pallas_call | solution.py:480
  8.1 0.1 concatenate.3
  8.2 0.1 broadcast_in_dim.2.info.refs_0_
  8.3 0.5 shard_map.85
  8.8 0.0 copy-start.6
  8.8 0.0 copy-start.7
  8.8 2.1 %collective-permute-start.3 = (f32[2,128,512]{2,1,0:T(8,128)S(1)}, f32[2,128,512]{2,1,0:T(8,128)S(1)}, u32[]{:S(2)}, u32[]{:S(2)}) collective-permute-start(f32[2,128,512]{2,1,0:T(8,128)S(1)} %get-tuple-element.40), channel_id=1, source_target_pairs={{8,16},{16,8},{9,17},{17,9},{10,18},{18,10},{11,19},{19,11},{12,20... | collective-permute-start | bytes 1572872 | tf_op jit(solution)/shard_map/ppermute | solution.py:426
  10.9 3.9 %collective-permute-done.close = f32[2,256,128]{2,1,0:T(8,128)S(1)} collective-permute-done((f32[2,256,128]{2,1,0:T(8,128)S(1)}, f32[2,256,128]{2,1,0:T(8,128)S(1)}, u32[]{:S(2)}, u32[]{:S(2)}) %collective-permute-start) | collective-permute-done | bytes 262176 | tf_op jit(solution)/shard_map/ppermute | solution.py:426
  14.8 0.1 shard_map.83
  15.0 0.1 collective-permute-start.2
  15.1 2.5 %collective-permute-start.4 = (f32[2,128,256]{2,1,0:T(8,128)S(1)}, f32[2,128,256]{2,1,0:T(8,128)S(1)}, u32[]{:S(2)}, u32[]{:S(2)}) collective-permute-start(f32[2,128,256]{2,1,0:T(8,128)S(1)} %get-tuple-element.41), channel_id=1, source_target_pairs={{8,16},{16,8},{9,17},{17,9},{10,18},{18,10},{11,19},{19,11},{12,20... | collective-permute-start | bytes 786440 | tf_op jit(solution)/shard_map/ppermute | solution.py:426
  17.6 1.0 shard_map.86.refs_7_.refs_6_
  18.7 4.1 %collective-permute-done.4.refs_3_ = f32[2,128,256]{2,1,0:T(8,128)S(1)} collective-permute-done((f32[2,128,256]{2,1,0:T(8,128)S(1)}, f32[2,128,256]{2,1,0:T(8,128)S(1)}, u32[]{:S(2)}, u32[]{:S(2)}) %collective-permute-start.4) | collective-permute-done | bytes 262176 | tf_op jit(solution)/shard_map/ppermute | solution.py:426
  22.8 0.0 collective-permute-done.3.refs_2_.sent_cross
  22.8 4.7 %shard_map.87 = (f32[2,128,512]{2,1,0:T(8,128)S(1)}, f32[2,128,512]{2,1,0:T(8,128)S(1)}, f32[2,128,512]{2,1,0:T(8,128)S(1)}, f32[2,128,512]{2,1,0:T(8,128)S(1)}) custom-call(s32[10,256]{1,0:T(8,128)S(1)} %broadcast_in_dim.2.info.refs_0_, f32[2,128,512]{2,1,0:T(8,128)S(1)} %collective-permute-done.2.refs_1_, ...), custom_call_target="tpu_custom_call" | custom-call | flops 2415919104 | bytes 6291456 | tf_op jit(solution)/shard_map/pallas_call | solution.py:514
  27.5 2.5 %collective-permute-start.15 = (f32[2,128,512]{2,1,0:T(8,128)S(1)}, f32[2,128,512]{2,1,0:T(8,128)S(1)}, u32[]{:S(2)}, u32[]{:S(2)}) collective-permute-start(f32[2,128,512]{2,1,0:T(8,128)S(1)} %get-tuple-element.54), channel_id=1, source_target_pairs={{8,16},{16,8},{9,17},{17,9},{10,18},{18,10},{11,19},{19,11},{12,20... | collective-permute-start | bytes 1572872 | tf_op jit(solution)/shard_map/ppermute | solution.py:426
  30.0 0.1 collective-permute-start.5
  30.1 0.5 collective-permute-start.8
  30.6 1.8 %collective-permute-done.8.sent_near = f32[1,128,512]{2,1,0:T(8,128)S(1)} collective-permute-done((f32[1,128,512]{2,1,0:T(8,128)S(1)}, f32[1,128,512]{2,1,0:T(8,128)S(1)}, u32[]{:S(2)}, u32[]{:S(2)}) %collective-permute-start.8) | collective-permute-done | bytes 262176 | tf_op jit(solution)/shard_map/ppermute | solution.py:426
  32.4 0.1 shard_map.89
  32.4 1.6 %collective-permute-start.9 = (f32[1,256,256]{2,1,0:T(8,128)S(1)}, f32[1,256,256]{2,1,0:T(8,128)S(1)}, u32[]{:S(2)}, u32[]{:S(2)}) collective-permute-start(f32[1,256,256]{2,1,0:T(8,128)S(1)} %get-tuple-element.49.close), channel_id=1, source_target_pairs={{0,1},{1,0},{2,3},{3,2},{4,5},{5,4},{6,7},{7,6},{8,9},{9,8},{10,11... | collective-permute-start | bytes 786440 | tf_op jit(solution)/shard_map/ppermute | solution.py:426
  34.1 1.9 %collective-permute-start.10 = (f32[1,256,256]{2,1,0:T(8,128)S(1)}, f32[1,256,256]{2,1,0:T(8,128)S(1)}, u32[]{:S(2)}, u32[]{:S(2)}) collective-permute-start(f32[1,256,256]{2,1,0:T(8,128)S(1)} %get-tuple-element.50.far), channel_id=1, source_target_pairs={{1,2},{2,1},{3,4},{4,3},{5,6},{6,5},{9,10},{10,9},{11,12},{12,11},... | collective-permute-start | bytes 786440 | tf_op jit(solution)/shard_map/ppermute | solution.py:426
  36.0 2.0 %collective-permute-done.15.sent = f32[2,128,512]{2,1,0:T(8,128)S(1)} collective-permute-done((f32[2,128,512]{2,1,0:T(8,128)S(1)}, f32[2,128,512]{2,1,0:T(8,128)S(1)}, u32[]{:S(2)}, u32[]{:S(2)}) %collective-permute-start.15) | collective-permute-done | bytes 524320 | tf_op jit(solution)/shard_map/ppermute | solution.py:426
  38.0 0.1 shard_map.91
  38.0 2.2 %collective-permute-start.16 = (f32[2,128,256]{2,1,0:T(8,128)S(1)}, f32[2,128,256]{2,1,0:T(8,128)S(1)}, u32[]{:S(2)}, u32[]{:S(2)}) collective-permute-start(f32[2,128,256]{2,1,0:T(8,128)S(1)} %get-tuple-element.55.close), channel_id=1, source_target_pairs={{0,1},{1,0},{2,3},{3,2},{4,5},{5,4},{6,7},{7,6},{8,9},{9,8},{10,11... | collective-permute-start | bytes 786440 | tf_op jit(solution)/shard_map/ppermute | solution.py:426
  40.3 1.9 %collective-permute-start.19 = (f32[2,128,256]{2,1,0:T(8,128)S(1)}, f32[2,128,256]{2,1,0:T(8,128)S(1)}, u32[]{:S(2)}, u32[]{:S(2)}) collective-permute-start(f32[2,128,256]{2,1,0:T(8,128)S(1)} %get-tuple-element.57.far), channel_id=1, source_target_pairs={{1,2},{2,1},{3,4},{4,3},{5,6},{6,5},{9,10},{10,9},{11,12},{12,11},... | collective-permute-start | bytes 786440 | tf_op jit(solution)/shard_map/ppermute | solution.py:426
  42.2 0.1 shard_map.88
  42.3 3.1 %collective-permute-start.6 = (f32[2,128,256]{2,1,0:T(8,128)S(1)}, f32[2,128,256]{2,1,0:T(8,128)S(1)}, u32[]{:S(2)}, u32[]{:S(2)}) collective-permute-start(f32[2,128,256]{2,1,0:T(8,128)S(1)} %get-tuple-element.45.close), channel_id=1, source_target_pairs={{0,1},{1,0},{2,3},{3,2},{4,5},{5,4},{6,7},{7,6},{8,9},{9,8},{10,11... | collective-permute-start | bytes 786440 | tf_op jit(solution)/shard_map/ppermute | solution.py:426
  45.3 7.5 %collective-permute-done.9.from_close = f32[1,256,256]{2,1,0:T(8,128)S(1)} collective-permute-done((f32[1,256,256]{2,1,0:T(8,128)S(1)}, f32[1,256,256]{2,1,0:T(8,128)S(1)}, u32[]{:S(2)}, u32[]{:S(2)}) %collective-permute-start.9) | collective-permute-done | bytes 262176 | tf_op jit(solution)/shard_map/ppermute | solution.py:426
  52.9 3.3 %collective-permute-start.7 = (f32[2,128,256]{2,1,0:T(8,128)S(1)}, f32[2,128,256]{2,1,0:T(8,128)S(1)}, u32[]{:S(2)}, u32[]{:S(2)}) collective-permute-start(f32[2,128,256]{2,1,0:T(8,128)S(1)} %get-tuple-element.46.far), channel_id=1, source_target_pairs={{1,2},{2,1},{3,4},{4,3},{5,6},{6,5},{9,10},{10,9},{11,12},{12,11},... | collective-permute-start | bytes 786440 | tf_op jit(solution)/shard_map/ppermute | solution.py:426
  56.3 0.1 shard_map.90
  56.3 1.6 %collective-permute-start.11 = (f32[8,128]{1,0:T(8,128)S(1)}, f32[8,128]{1,0:T(8,128)S(1)}, u32[]{:S(2)}, u32[]{:S(2)}) collective-permute-start(f32[8,128]{1,0:T(8,128)S(1)} %get-tuple-element.52), channel_id=1, source_target_pairs={{0,1},{1,0},{2,3},{3,2},{4,5},{5,4},{6,7},{7,6},{8,9},{9,8},{10,11... | collective-permute-start | bytes 12296 | tf_op jit(solution)/shard_map/ppermute | solution.py:450
  58.0 11.0 %collective-permute-done.11 = f32[8,128]{1,0:T(8,128)S(1)} collective-permute-done((f32[8,128]{1,0:T(8,128)S(1)}, f32[8,128]{1,0:T(8,128)S(1)}, u32[]{:S(2)}, u32[]{:S(2)}) %collective-permute-start.11) | collective-permute-done | bytes 4128 | tf_op jit(solution)/shard_map/ppermute | solution.py:450
  69.0 3.6 %collective-permute-done.12 = f32[8,128]{1,0:T(8,128)S(1)} collective-permute-done((f32[8,128]{1,0:T(8,128)S(1)}, f32[8,128]{1,0:T(8,128)S(1)}, u32[]{:S(2)}, u32[]{:S(2)}) %collective-permute-start.12) | collective-permute-done | bytes 4128 | tf_op jit(solution)/shard_map/ppermute | solution.py:450
  72.6 2.6 %collective-permute-start.13 = (f32[8,128]{1,0:T(8,128)S(1)}, f32[8,128]{1,0:T(8,128)S(1)}, u32[]{:S(2)}, u32[]{:S(2)}) collective-permute-start(f32[8,128]{1,0:T(8,128)S(1)} %max.16), channel_id=1, source_target_pairs={{0,4},{1,5},{2,6},{3,7},{4,0},{5,1},{6,2},{7,3},{8,12},{9,13},{10,... | collective-permute-start | bytes 12296 | tf_op jit(solution)/shard_map/ppermute | solution.py:450
  75.2 1.9 %collective-permute-done.13 = f32[8,128]{1,0:T(8,128)S(1)} collective-permute-done((f32[8,128]{1,0:T(8,128)S(1)}, f32[8,128]{1,0:T(8,128)S(1)}, u32[]{:S(2)}, u32[]{:S(2)}) %collective-permute-start.13) | collective-permute-done | bytes 4128 | tf_op jit(solution)/shard_map/ppermute | solution.py:450
  77.1 1.8 %collective-permute-start.14 = (f32[8,128]{1,0:T(8,128)S(1)}, f32[8,128]{1,0:T(8,128)S(1)}, u32[]{:S(2)}, u32[]{:S(2)}) collective-permute-start(f32[8,128]{1,0:T(8,128)S(1)} %max.17), channel_id=1, source_target_pairs={{0,16},{8,24},{16,0},{24,8},{1,17},{9,25},{17,1},{25,9},{2,18},{10... | collective-permute-start | bytes 12296 | tf_op jit(solution)/shard_map/ppermute | solution.py:450
  78.9 1.8 %collective-permute-done.14 = f32[8,128]{1,0:T(8,128)S(1)} collective-permute-done((f32[8,128]{1,0:T(8,128)S(1)}, f32[8,128]{1,0:T(8,128)S(1)}, u32[]{:S(2)}, u32[]{:S(2)}) %collective-permute-start.14) | collective-permute-done | bytes 4128 | tf_op jit(solution)/shard_map/ppermute | solution.py:450
  80.8 1.2 collective-permute-done.17
  81.9 0.3 shard_map.93.refs_4_.refs_11_
  82.2 3.7 %collective-permute-start.20 = (f32[2,128,512]{2,1,0:T(8,128)S(1)}, f32[2,128,512]{2,1,0:T(8,128)S(1)}, u32[]{:S(2)}, u32[]{:S(2)}) collective-permute-start(f32[2,128,512]{2,1,0:T(8,128)S(1)} %shard_map.93.refs_4_.refs_11_), channel_id=1, source_target_pairs={{8,16},{16,8},{9,17},{17,9},{10,18},{18,10},{11,19},{19,11},{12,20... | collective-permute-start | bytes 1572872 | tf_op jit(solution)/shard_map/ppermute | solution.py:426
  85.9 0.3 shard_map.92.refs_3_.refs_5_
  86.2 0.1 collective-permute-start.18
  86.2 6.5 %collective-permute-done.20.refs_2_ = f32[2,128,512]{2,1,0:T(8,128)S(1)} collective-permute-done((f32[2,128,512]{2,1,0:T(8,128)S(1)}, f32[2,128,512]{2,1,0:T(8,128)S(1)}, u32[]{:S(2)}, u32[]{:S(2)}) %collective-permute-start.20) | collective-permute-done | bytes 524320 | tf_op jit(solution)/shard_map/ppermute | solution.py:426
  92.7 4.7 %shard_map.94 = (f32[2,128,512]{2,1,0:T(8,128)S(1)}, f32[2,128,256]{2,1,0:T(8,128)S(1)}, f32[2,128,256]{2,1,0:T(8,128)S(1)}, f32[2,128,512]{2,1,0:T(8,128)S(1)}, f32[2,128,512]{2,1,0:T(8,128)S(1)}) custom-call(s32[10,256]{1,0:T(8,128)S(1)} %broadcast_in_dim.2.info.refs_0_, f32[2,128,512]{2,1,0:T(8,128)S(1)} %collective-permute-done.18.refs_1_, ...), custom_call_target="tpu_custom_call" | custom-call | flops 2415919104 | bytes 6291456 | tf_op jit(solution)/shard_map/pallas_call | solution.py:514
  97.4 0.1 collective-permute-start.21
  97.4 3.5 %collective-permute-start.25 = (f32[2,128,256]{2,1,0:T(8,128)S(1)}, f32[2,128,256]{2,1,0:T(8,128)S(1)}, u32[]{:S(2)}, u32[]{:S(2)}) collective-permute-start(f32[2,128,256]{2,1,0:T(8,128)S(1)} %get-tuple-element.66), channel_id=1, source_target_pairs={{8,16},{16,8},{9,17},{17,9},{10,18},{18,10},{11,19},{19,11},{12,20... | collective-permute-start | bytes 786440 | tf_op jit(solution)/shard_map/ppermute | solution.py:426
  100.9 2.1 %collective-permute-start.24 = (f32[2,128,256]{2,1,0:T(8,128)S(1)}, f32[2,128,256]{2,1,0:T(8,128)S(1)}, u32[]{:S(2)}, u32[]{:S(2)}) collective-permute-start(f32[2,128,256]{2,1,0:T(8,128)S(1)} %get-tuple-element.65), channel_id=1, source_target_pairs={{8,16},{16,8},{9,17},{17,9},{10,18},{18,10},{11,19},{19,11},{12,20... | collective-permute-start | bytes 786440 | tf_op jit(solution)/shard_map/ppermute | solution.py:426
  103.0 2.1 %collective-permute-done.25.sent = f32[2,128,256]{2,1,0:T(8,128)S(1)} collective-permute-done((f32[2,128,256]{2,1,0:T(8,128)S(1)}, f32[2,128,256]{2,1,0:T(8,128)S(1)}, u32[]{:S(2)}, u32[]{:S(2)}) %collective-permute-start.25) | collective-permute-done | bytes 262176 | tf_op jit(solution)/shard_map/ppermute | solution.py:426
  105.2 1.7 %collective-permute-start.26 = (f32[2,128,128]{2,1,0:T(8,128)S(1)}, f32[2,128,128]{2,1,0:T(8,128)S(1)}, u32[]{:S(2)}, u32[]{:S(2)}) collective-permute-start(f32[2,128,128]{2,1,0:T(8,128)S(1)} %get-tuple-element.67), channel_id=1, source_target_pairs={{0,1},{1,0},{2,3},{3,2},{4,5},{5,4},{6,7},{7,6},{8,9},{9,8},{10,11... | collective-permute-start | bytes 393224 | tf_op jit(solution)/shard_map/ppermute | solution.py:426
  106.8 1.9 %collective-permute-start.27 = (f32[2,128,128]{2,1,0:T(8,128)S(1)}, f32[2,128,128]{2,1,0:T(8,128)S(1)}, u32[]{:S(2)}, u32[]{:S(2)}) collective-permute-start(f32[2,128,128]{2,1,0:T(8,128)S(1)} %get-tuple-element.68), channel_id=1, source_target_pairs={{1,2},{2,1},{3,4},{4,3},{5,6},{6,5},{9,10},{10,9},{11,12},{12,11},... | collective-permute-start | bytes 393224 | tf_op jit(solution)/shard_map/ppermute | solution.py:426
  108.8 3.1 %collective-permute-start.22 = (f32[2,128,128]{2,1,0:T(8,128)S(1)}, f32[2,128,128]{2,1,0:T(8,128)S(1)}, u32[]{:S(2)}, u32[]{:S(2)}) collective-permute-start(f32[2,128,128]{2,1,0:T(8,128)S(1)} %get-tuple-element.62), channel_id=1, source_target_pairs={{0,1},{1,0},{2,3},{3,2},{4,5},{5,4},{6,7},{7,6},{8,9},{9,8},{10,11... | collective-permute-start | bytes 393224 | tf_op jit(solution)/shard_map/ppermute | solution.py:426
  111.9 1.9 %collective-permute-start.23 = (f32[2,128,128]{2,1,0:T(8,128)S(1)}, f32[2,128,128]{2,1,0:T(8,128)S(1)}, u32[]{:S(2)}, u32[]{:S(2)}) collective-permute-start(f32[2,128,128]{2,1,0:T(8,128)S(1)} %get-tuple-element.63), channel_id=1, source_target_pairs={{1,2},{2,1},{3,4},{4,3},{5,6},{6,5},{9,10},{10,9},{11,12},{12,11},... | collective-permute-start | bytes 393224 | tf_op jit(solution)/shard_map/ppermute | solution.py:426
  113.8 0.8 collective-permute-done.27.refs_9_
  114.7 1.3 %collective-permute-done.22.refs_2_ = f32[2,128,128]{2,1,0:T(8,128)S(1)} collective-permute-done((f32[2,128,128]{2,1,0:T(8,128)S(1)}, f32[2,128,128]{2,1,0:T(8,128)S(1)}, u32[]{:S(2)}, u32[]{:S(2)}) %collective-permute-start.22) | collective-permute-done | bytes 131104 | tf_op jit(solution)/shard_map/ppermute | solution.py:426
  116.0 3.7 %collective-permute-done.23.refs_3_ = f32[2,128,128]{2,1,0:T(8,128)S(1)} collective-permute-done((f32[2,128,128]{2,1,0:T(8,128)S(1)}, f32[2,128,128]{2,1,0:T(8,128)S(1)}, u32[]{:S(2)}, u32[]{:S(2)}) %collective-permute-start.23) | collective-permute-done | bytes 131104 | tf_op jit(solution)/shard_map/ppermute | solution.py:426
  119.6 1.1 shard_map.97
  (34 shorter events, 0.2 us)
Async XLA Ops:
  0.0 1.0 copy-start
  1.0 7.3 %copy-start.1 = (f32[2,256,256]{2,1,0:T(8,128)S(1)}, f32[2,256,256]{2,1,0:T(8,128)}, u32[]{:S(2)}) copy-start(f32[2,256,256]{2,1,0:T(8,128)} %specimen.5) | copy-start | bytes 1572868
  1.1 13.7 %collective-permute-start = (f32[2,256,128]{2,1,0:T(8,128)S(1)}, f32[2,256,128]{2,1,0:T(8,128)S(1)}, u32[]{:S(2)}, u32[]{:S(2)}) collective-permute-start(f32[2,256,128]{2,1,0:T(8,128)S(1)} %get-tuple-element.37), channel_id=1, source_target_pairs={{0,1},{1,0},{2,3},{3,2},{4,5},{5,4},{6,7},{7,6},{8,9},{9,8},{10,11... | collective-permute-start | bytes 786440 | tf_op jit(solution)/shard_map/ppermute | solution.py:426
  2.7 12.1 %collective-permute-start.1 = (f32[2,256,128]{2,1,0:T(8,128)S(1)}, f32[2,256,128]{2,1,0:T(8,128)S(1)}, u32[]{:S(2)}, u32[]{:S(2)}) collective-permute-start(f32[2,256,128]{2,1,0:T(8,128)S(1)} %get-tuple-element.38), channel_id=1, source_target_pairs={{1,2},{2,1},{3,4},{4,3},{5,6},{6,5},{9,10},{10,9},{11,12},{12,11},... | collective-permute-start | bytes 786440 | tf_op jit(solution)/shard_map/ppermute | solution.py:426
  5.9 1.0 copy-start.3
  8.3 9.3 %copy-start.2 = (f32[1,1,3,256,256]{4,3,2,1,0:T(8,128)S(1)}, f32[1,1,3,256,256]{4,3,2,1,0:T(8,128)}, u32[]{:S(2)}) copy-start(f32[1,1,3,256,256]{4,3,2,1,0:T(8,128)} %amplitude.1) | copy-start | bytes 2359300
  8.3 9.3 %copy-start.4 = (bf16[256,256]{1,0:T(8,128)(2,1)S(1)}, bf16[256,256]{1,0:T(8,128)(2,1)}, u32[]{:S(2)}) copy-start(bf16[256,256]{1,0:T(8,128)(2,1)} %constant.42.clone.pick_back) | copy-start | bytes 393220
  8.3 9.3 %copy-start.5 = (bf16[256,256]{1,0:T(8,128)(2,1)S(1)}, bf16[256,256]{1,0:T(8,128)(2,1)}, u32[]{:S(2)}) copy-start(bf16[256,256]{1,0:T(8,128)(2,1)} %constant.41.clone.pick) | copy-start | bytes 393220
  8.8 13.9 %copy-start.6 = (bf16[2,2,256,256]{3,2,1,0:T(8,128)(2,1)S(1)}, bf16[2,2,256,256]{3,2,1,0:T(8,128)(2,1)}, u32[]{:S(2)}) copy-start(bf16[2,2,256,256]{3,2,1,0:T(8,128)(2,1)} %constant.40.clone.refs_9_.refs_8_) | copy-start | bytes 1572868
  8.8 13.9 %copy-start.7 = (bf16[2,2,256,256]{3,2,1,0:T(8,128)(2,1)S(1)}, bf16[2,2,256,256]{3,2,1,0:T(8,128)(2,1)}, u32[]{:S(2)}) copy-start(bf16[2,2,256,256]{3,2,1,0:T(8,128)(2,1)} %constant.39.clone.refs_8_.refs_7_) | copy-start | bytes 1572868
  8.8 13.9 %collective-permute-start.3 = (f32[2,128,512]{2,1,0:T(8,128)S(1)}, f32[2,128,512]{2,1,0:T(8,128)S(1)}, u32[]{:S(2)}, u32[]{:S(2)}) collective-permute-start(f32[2,128,512]{2,1,0:T(8,128)S(1)} %get-tuple-element.40), channel_id=1, source_target_pairs={{8,16},{16,8},{9,17},{17,9},{10,18},{18,10},{11,19},{19,11},{12,20... | collective-permute-start | bytes 1572872 | tf_op jit(solution)/shard_map/ppermute | solution.py:426
  15.0 7.8 %collective-permute-start.2 = (f32[2,128,512]{2,1,0:T(8,128)S(1)}, f32[2,128,512]{2,1,0:T(8,128)S(1)}, u32[]{:S(2)}, u32[]{:S(2)}) collective-permute-start(f32[2,128,512]{2,1,0:T(8,128)S(1)} %get-tuple-element.39.refs_4_.old), channel_id=1, source_target_pairs={{0,8},{8,0},{16,24},{24,16},{1,9},{9,1},{17,25},{25,17},{2,10},{10... | collective-permute-start | bytes 1572872 | tf_op jit(solution)/shard_map/ppermute | solution.py:426
  15.1 7.7 %collective-permute-start.4 = (f32[2,128,256]{2,1,0:T(8,128)S(1)}, f32[2,128,256]{2,1,0:T(8,128)S(1)}, u32[]{:S(2)}, u32[]{:S(2)}) collective-permute-start(f32[2,128,256]{2,1,0:T(8,128)S(1)} %get-tuple-element.41), channel_id=1, source_target_pairs={{8,16},{16,8},{9,17},{17,9},{10,18},{18,10},{11,19},{19,11},{12,20... | collective-permute-start | bytes 786440 | tf_op jit(solution)/shard_map/ppermute | solution.py:426
  27.5 10.5 %collective-permute-start.15 = (f32[2,128,512]{2,1,0:T(8,128)S(1)}, f32[2,128,512]{2,1,0:T(8,128)S(1)}, u32[]{:S(2)}, u32[]{:S(2)}) collective-permute-start(f32[2,128,512]{2,1,0:T(8,128)S(1)} %get-tuple-element.54), channel_id=1, source_target_pairs={{8,16},{16,8},{9,17},{17,9},{10,18},{18,10},{11,19},{19,11},{12,20... | collective-permute-start | bytes 1572872 | tf_op jit(solution)/shard_map/ppermute | solution.py:426
  30.0 12.2 %collective-permute-start.5 = (f32[2,128,512]{2,1,0:T(8,128)S(1)}, f32[2,128,512]{2,1,0:T(8,128)S(1)}, u32[]{:S(2)}, u32[]{:S(2)}) collective-permute-start(f32[2,128,512]{2,1,0:T(8,128)S(1)} %get-tuple-element.44), channel_id=1, source_target_pairs={{0,8},{8,0},{16,24},{24,16},{1,9},{9,1},{17,25},{25,17},{2,10},{10... | collective-permute-start | bytes 1572872 | tf_op jit(solution)/shard_map/ppermute | solution.py:426
  30.1 2.3 %collective-permute-start.8 = (f32[1,128,512]{2,1,0:T(8,128)S(1)}, f32[1,128,512]{2,1,0:T(8,128)S(1)}, u32[]{:S(2)}, u32[]{:S(2)}) collective-permute-start(f32[1,128,512]{2,1,0:T(8,128)S(1)} %get-tuple-element.48), channel_id=1, source_target_pairs={{0,8},{8,0},{16,24},{24,16},{1,9},{9,1},{17,25},{25,17},{2,10},{10... | collective-permute-start | bytes 786440 | tf_op jit(solution)/shard_map/ppermute | solution.py:426
  32.4 20.5 %collective-permute-start.9 = (f32[1,256,256]{2,1,0:T(8,128)S(1)}, f32[1,256,256]{2,1,0:T(8,128)S(1)}, u32[]{:S(2)}, u32[]{:S(2)}) collective-permute-start(f32[1,256,256]{2,1,0:T(8,128)S(1)} %get-tuple-element.49.close), channel_id=1, source_target_pairs={{0,1},{1,0},{2,3},{3,2},{4,5},{5,4},{6,7},{7,6},{8,9},{9,8},{10,11... | collective-permute-start | bytes 786440 | tf_op jit(solution)/shard_map/ppermute | solution.py:426
  34.1 22.2 %collective-permute-start.10 = (f32[1,256,256]{2,1,0:T(8,128)S(1)}, f32[1,256,256]{2,1,0:T(8,128)S(1)}, u32[]{:S(2)}, u32[]{:S(2)}) collective-permute-start(f32[1,256,256]{2,1,0:T(8,128)S(1)} %get-tuple-element.50.far), channel_id=1, source_target_pairs={{1,2},{2,1},{3,4},{4,3},{5,6},{6,5},{9,10},{10,9},{11,12},{12,11},... | collective-permute-start | bytes 786440 | tf_op jit(solution)/shard_map/ppermute | solution.py:426
  38.0 42.7 %collective-permute-start.16 = (f32[2,128,256]{2,1,0:T(8,128)S(1)}, f32[2,128,256]{2,1,0:T(8,128)S(1)}, u32[]{:S(2)}, u32[]{:S(2)}) collective-permute-start(f32[2,128,256]{2,1,0:T(8,128)S(1)} %get-tuple-element.55.close), channel_id=1, source_target_pairs={{0,1},{1,0},{2,3},{3,2},{4,5},{5,4},{6,7},{7,6},{8,9},{9,8},{10,11... | collective-permute-start | bytes 786440 | tf_op jit(solution)/shard_map/ppermute | solution.py:426
  40.3 41.7 %collective-permute-start.19 = (f32[2,128,256]{2,1,0:T(8,128)S(1)}, f32[2,128,256]{2,1,0:T(8,128)S(1)}, u32[]{:S(2)}, u32[]{:S(2)}) collective-permute-start(f32[2,128,256]{2,1,0:T(8,128)S(1)} %get-tuple-element.57.far), channel_id=1, source_target_pairs={{1,2},{2,1},{3,4},{4,3},{5,6},{6,5},{9,10},{10,9},{11,12},{12,11},... | collective-permute-start | bytes 786440 | tf_op jit(solution)/shard_map/ppermute | solution.py:426
  42.3 43.6 %collective-permute-start.6 = (f32[2,128,256]{2,1,0:T(8,128)S(1)}, f32[2,128,256]{2,1,0:T(8,128)S(1)}, u32[]{:S(2)}, u32[]{:S(2)}) collective-permute-start(f32[2,128,256]{2,1,0:T(8,128)S(1)} %get-tuple-element.45.close), channel_id=1, source_target_pairs={{0,1},{1,0},{2,3},{3,2},{4,5},{5,4},{6,7},{7,6},{8,9},{9,8},{10,11... | collective-permute-start | bytes 786440 | tf_op jit(solution)/shard_map/ppermute | solution.py:426
  52.9 33.0 %collective-permute-start.7 = (f32[2,128,256]{2,1,0:T(8,128)S(1)}, f32[2,128,256]{2,1,0:T(8,128)S(1)}, u32[]{:S(2)}, u32[]{:S(2)}) collective-permute-start(f32[2,128,256]{2,1,0:T(8,128)S(1)} %get-tuple-element.46.far), channel_id=1, source_target_pairs={{1,2},{2,1},{3,4},{4,3},{5,6},{6,5},{9,10},{10,9},{11,12},{12,11},... | collective-permute-start | bytes 786440 | tf_op jit(solution)/shard_map/ppermute | solution.py:426
  56.3 12.7 %collective-permute-start.11 = (f32[8,128]{1,0:T(8,128)S(1)}, f32[8,128]{1,0:T(8,128)S(1)}, u32[]{:S(2)}, u32[]{:S(2)}) collective-permute-start(f32[8,128]{1,0:T(8,128)S(1)} %get-tuple-element.52), channel_id=1, source_target_pairs={{0,1},{1,0},{2,3},{3,2},{4,5},{5,4},{6,7},{7,6},{8,9},{9,8},{10,11... | collective-permute-start | bytes 12296 | tf_op jit(solution)/shard_map/ppermute | solution.py:450
  69.0 3.6 %collective-permute-start.12 = (f32[8,128]{1,0:T(8,128)S(1)}, f32[8,128]{1,0:T(8,128)S(1)}, u32[]{:S(2)}, u32[]{:S(2)}) collective-permute-start(f32[8,128]{1,0:T(8,128)S(1)} %max.15), channel_id=1, source_target_pairs={{0,2},{1,3},{2,0},{3,1},{4,6},{5,7},{6,4},{7,5},{8,10},{9,11},{10,... | collective-permute-start | bytes 12296 | tf_op jit(solution)/shard_map/ppermute | solution.py:450
  72.6 4.5 %collective-permute-start.13 = (f32[8,128]{1,0:T(8,128)S(1)}, f32[8,128]{1,0:T(8,128)S(1)}, u32[]{:S(2)}, u32[]{:S(2)}) collective-permute-start(f32[8,128]{1,0:T(8,128)S(1)} %max.16), channel_id=1, source_target_pairs={{0,4},{1,5},{2,6},{3,7},{4,0},{5,1},{6,2},{7,3},{8,12},{9,13},{10,... | collective-permute-start | bytes 12296 | tf_op jit(solution)/shard_map/ppermute | solution.py:450
  77.1 3.6 %collective-permute-start.14 = (f32[8,128]{1,0:T(8,128)S(1)}, f32[8,128]{1,0:T(8,128)S(1)}, u32[]{:S(2)}, u32[]{:S(2)}) collective-permute-start(f32[8,128]{1,0:T(8,128)S(1)} %max.17), channel_id=1, source_target_pairs={{0,16},{8,24},{16,0},{24,8},{1,17},{9,25},{17,1},{25,9},{2,18},{10... | collective-permute-start | bytes 12296 | tf_op jit(solution)/shard_map/ppermute | solution.py:450
  80.7 1.2 collective-permute-start.17
  82.2 10.5 %collective-permute-start.20 = (f32[2,128,512]{2,1,0:T(8,128)S(1)}, f32[2,128,512]{2,1,0:T(8,128)S(1)}, u32[]{:S(2)}, u32[]{:S(2)}) collective-permute-start(f32[2,128,512]{2,1,0:T(8,128)S(1)} %shard_map.93.refs_4_.refs_11_), channel_id=1, source_target_pairs={{8,16},{16,8},{9,17},{17,9},{10,18},{18,10},{11,19},{19,11},{12,20... | collective-permute-start | bytes 1572872 | tf_op jit(solution)/shard_map/ppermute | solution.py:426
  86.2 6.5 %collective-permute-start.18 = (f32[2,128,512]{2,1,0:T(8,128)S(1)}, f32[2,128,512]{2,1,0:T(8,128)S(1)}, u32[]{:S(2)}, u32[]{:S(2)}) collective-permute-start(f32[2,128,512]{2,1,0:T(8,128)S(1)} %shard_map.92.refs_3_.refs_5_), channel_id=1, source_target_pairs={{0,8},{8,0},{16,24},{24,16},{1,9},{9,1},{17,25},{25,17},{2,10},{10... | collective-permute-start | bytes 1572872 | tf_op jit(solution)/shard_map/ppermute | solution.py:426
  97.4 11.4 %collective-permute-start.21 = (f32[2,128,512]{2,1,0:T(8,128)S(1)}, f32[2,128,512]{2,1,0:T(8,128)S(1)}, u32[]{:S(2)}, u32[]{:S(2)}) collective-permute-start(f32[2,128,512]{2,1,0:T(8,128)S(1)} %get-tuple-element.61), channel_id=1, source_target_pairs={{0,8},{8,0},{16,24},{24,16},{1,9},{9,1},{17,25},{25,17},{2,10},{10... | collective-permute-start | bytes 1572872 | tf_op jit(solution)/shard_map/ppermute | solution.py:426
  97.4 7.7 %collective-permute-start.25 = (f32[2,128,256]{2,1,0:T(8,128)S(1)}, f32[2,128,256]{2,1,0:T(8,128)S(1)}, u32[]{:S(2)}, u32[]{:S(2)}) collective-permute-start(f32[2,128,256]{2,1,0:T(8,128)S(1)} %get-tuple-element.66), channel_id=1, source_target_pairs={{8,16},{16,8},{9,17},{17,9},{10,18},{18,10},{11,19},{19,11},{12,20... | collective-permute-start | bytes 786440 | tf_op jit(solution)/shard_map/ppermute | solution.py:426
  100.9 12.9 %collective-permute-start.24 = (f32[2,128,256]{2,1,0:T(8,128)S(1)}, f32[2,128,256]{2,1,0:T(8,128)S(1)}, u32[]{:S(2)}, u32[]{:S(2)}) collective-permute-start(f32[2,128,256]{2,1,0:T(8,128)S(1)} %get-tuple-element.65), channel_id=1, source_target_pairs={{8,16},{16,8},{9,17},{17,9},{10,18},{18,10},{11,19},{19,11},{12,20... | collective-permute-start | bytes 786440 | tf_op jit(solution)/shard_map/ppermute | solution.py:426
  105.2 8.7 %collective-permute-start.26 = (f32[2,128,128]{2,1,0:T(8,128)S(1)}, f32[2,128,128]{2,1,0:T(8,128)S(1)}, u32[]{:S(2)}, u32[]{:S(2)}) collective-permute-start(f32[2,128,128]{2,1,0:T(8,128)S(1)} %get-tuple-element.67), channel_id=1, source_target_pairs={{0,1},{1,0},{2,3},{3,2},{4,5},{5,4},{6,7},{7,6},{8,9},{9,8},{10,11... | collective-permute-start | bytes 393224 | tf_op jit(solution)/shard_map/ppermute | solution.py:426
  106.8 7.8 %collective-permute-start.27 = (f32[2,128,128]{2,1,0:T(8,128)S(1)}, f32[2,128,128]{2,1,0:T(8,128)S(1)}, u32[]{:S(2)}, u32[]{:S(2)}) collective-permute-start(f32[2,128,128]{2,1,0:T(8,128)S(1)} %get-tuple-element.68), channel_id=1, source_target_pairs={{1,2},{2,1},{3,4},{4,3},{5,6},{6,5},{9,10},{10,9},{11,12},{12,11},... | collective-permute-start | bytes 393224 | tf_op jit(solution)/shard_map/ppermute | solution.py:426
  108.8 7.2 %collective-permute-start.22 = (f32[2,128,128]{2,1,0:T(8,128)S(1)}, f32[2,128,128]{2,1,0:T(8,128)S(1)}, u32[]{:S(2)}, u32[]{:S(2)}) collective-permute-start(f32[2,128,128]{2,1,0:T(8,128)S(1)} %get-tuple-element.62), channel_id=1, source_target_pairs={{0,1},{1,0},{2,3},{3,2},{4,5},{5,4},{6,7},{7,6},{8,9},{9,8},{10,11... | collective-permute-start | bytes 393224 | tf_op jit(solution)/shard_map/ppermute | solution.py:426
  111.9 7.7 %collective-permute-start.23 = (f32[2,128,128]{2,1,0:T(8,128)S(1)}, f32[2,128,128]{2,1,0:T(8,128)S(1)}, u32[]{:S(2)}, u32[]{:S(2)}) collective-permute-start(f32[2,128,128]{2,1,0:T(8,128)S(1)} %get-tuple-element.63), channel_id=1, source_target_pairs={{1,2},{2,1},{3,4},{4,3},{5,6},{6,5},{9,10},{10,9},{11,12},{12,11},... | collective-permute-start | bytes 393224 | tf_op jit(solution)/shard_map/ppermute | solution.py:426

commit v8 on v6

--- a/solution.py
+++ b/solution.py
@@ -439,18 +439,19 @@
     return close, far
 
 
-def largest_of(block, axes):
-    for axis in axes:
-        count = lax.axis_size(axis)
-        reach = 1
-        while reach < count:
-            if count & (count - 1) == 0:
-                route = [(i, i ^ reach) for i in range(count)]
-            else:
-                route = [(i, (i + reach) % count) for i in range(count)]
-            block = jnp.maximum(block, lax.ppermute(block, axis, route))
-            reach *= 2
+def largest_of(block, axis, reaches):
+    count = lax.axis_size(axis)
+    for reach in reaches:
+        if count & (count - 1) == 0:
+            route = [(i, i ^ reach) for i in range(count)]
+        else:
+            route = [(i, (i + reach) % count) for i in range(count)]
+        block = jnp.maximum(block, lax.ppermute(block, axis, route))
     return block
+
+
+def doublings(axis):
+    return [2**k for k in range((lax.axis_size(axis) - 1).bit_length())]
 
 
 def steps(specimen, probe_field, offsets, amplitudes):
@@ -504,7 +505,9 @@
     light_near, light_cross, found = kernel_call(
         light_sum_kernel, [shape(half, 2 * side)] * 2 + [shape(8, LANES)], [VM] * 5
     )(info, close, far, from_close, from_far)
-    peak = largest_of(found, ("col", "row"))
+    found = largest_of(found, "col", doublings("col"))
+    found = largest_of(found, "row", doublings("row")[:0:-1])
+    peak = None
 
     for step in range(ITERS):
         first, last = step == 0, step + 1 == ITERS
@@ -532,6 +535,8 @@
             ):
                 close, far = kernel_call(fold_kernel, [strip] * 2, [VM] * 3)(info, mid, sent)
                 from_close, from_far = to_sides(close, far)
+                if peak is None:
+                    peak = largest_of(found, "row", doublings("row")[:1])
                 halves.append(
                     kernel_call(update_kernel, [wide], [VM] * 8)(
                         info, close, far, from_close, from_far, light, peak, old

time: 122 us -> 123 us (level)
  waiting for transfers between devices: 52.3 us -> 54.7 us
  starting transfers between devices: 51.8 us -> 49.5 us
    ppermute x24, waiting for transfers between devices: 40.7 us -> 42 us  [swapped(): return lax.ppermute(block, axis, route)]
where the time goes in v8:
time: 123 us; the launch traced here: 122 us
  waiting for transfers between devices  54.7 us (44%)
  starting transfers between devices  49.5 us (40%)
  Pallas kernels  14.2 us (12%)
  local copies, waits for them, and re-layouts  2.46 us (2%)
    ppermute x24, starting transfers between devices, swapped(): return lax.ppermute(block, axis, route)  44.7 us
    ppermute x24, waiting for transfers between devices, swapped(): return lax.ppermute(block, axis, route)  42 us
    ppermute x5, waiting for transfers between devices, largest_of(): block = jnp.maximum(block, lax.ppermute(block, axis, route))  12.7 us
    pallas_call x2, Pallas kernels, steps(): kernel_call(functools.partial(gradient_kernel, first=first, last=last), [...  9.34 us
    ppermute x5, starting transfers between devices, largest_of(): block = jnp.maximum(block, lax.ppermute(block, axis, route))  4.8 us
  transfers between devices with their start and end apart: 29, of which 14 were waited for; matrix products, arithmetic and copies ran while one was open for 1% of the time, Pallas kernels for 3%

profile of v8, /device:TPU:10, one launch (start us, length us, event | category | flops | bytes accessed | tf_op | source)
XLA Modules:
  0.0 122.0 jit_solution(13987631617368041999)
XLA Ops:
  0.0 1.0 copy-done
  1.1 1.6 %collective-permute-start = (f32[2,256,128]{2,1,0:T(8,128)S(1)}, f32[2,256,128]{2,1,0:T(8,128)S(1)}, u32[]{:S(2)}, u32[]{:S(2)}) collective-permute-start(f32[2,256,128]{2,1,0:T(8,128)S(1)} %get-tuple-element.35), channel_id=1, source_target_pairs={{0,1},{1,0},{2,3},{3,2},{4,5},{5,4},{6,7},{7,6},{8,9},{9,8},{10,11... | collective-permute-start | bytes 786440 | tf_op jit(solution)/shard_map/ppermute | solution.py:425
  2.7 2.3 %collective-permute-start.1 = (f32[2,256,128]{2,1,0:T(8,128)S(1)}, f32[2,256,128]{2,1,0:T(8,128)S(1)}, u32[]{:S(2)}, u32[]{:S(2)}) collective-permute-start(f32[2,256,128]{2,1,0:T(8,128)S(1)} %get-tuple-element.36), channel_id=1, source_target_pairs={{1,2},{2,1},{3,4},{4,3},{5,6},{6,5},{9,10},{10,9},{11,12},{12,11},... | collective-permute-start | bytes 786440 | tf_op jit(solution)/shard_map/ppermute | solution.py:425
  5.0 0.7 broadcast_add_fusion
  5.7 0.1 copy.10
  5.8 0.1 add.19.corners
  5.9 0.1 concatenate.3
  6.0 8.9 %collective-permute-done.close = f32[2,256,128]{2,1,0:T(8,128)S(1)} collective-permute-done((f32[2,256,128]{2,1,0:T(8,128)S(1)}, f32[2,256,128]{2,1,0:T(8,128)S(1)}, u32[]{:S(2)}, u32[]{:S(2)}) %collective-permute-start) | collective-permute-done | bytes 262176 | tf_op jit(solution)/shard_map/ppermute | solution.py:425
  14.8 0.1 broadcast_in_dim.2.info.refs_0_
  14.9 1.0 copy-done.1
  15.9 0.1 shard_map.83
  16.1 0.0 copy-start.4
  16.1 0.0 copy-start.5
  16.1 0.1 collective-permute-start.2
  16.3 2.5 %collective-permute-start.3 = (f32[2,128,256]{2,1,0:T(8,128)S(1)}, f32[2,128,256]{2,1,0:T(8,128)S(1)}, u32[]{:S(2)}, u32[]{:S(2)}) collective-permute-start(f32[2,128,256]{2,1,0:T(8,128)S(1)} %shard_map.84), channel_id=1, source_target_pairs={{8,16},{16,8},{9,17},{17,9},{10,18},{18,10},{11,19},{19,11},{12,20... | collective-permute-start | bytes 786440 | tf_op jit(solution)/shard_map/ppermute | solution.py:425
  18.8 3.3 %collective-permute-start.4 = (f32[2,128,256]{2,1,0:T(8,128)S(1)}, f32[2,128,256]{2,1,0:T(8,128)S(1)}, u32[]{:S(2)}, u32[]{:S(2)}) collective-permute-start(f32[2,128,256]{2,1,0:T(8,128)S(1)} %get-tuple-element.38), channel_id=1, source_target_pairs={{8,16},{16,8},{9,17},{17,9},{10,18},{18,10},{11,19},{19,11},{12,20... | collective-permute-start | bytes 786440 | tf_op jit(solution)/shard_map/ppermute | solution.py:425
  22.1 1.2 shard_map.85.refs_6_.probe.refs_5_
  23.4 1.0 shard_map.86.refs_7_.refs_6_
  24.4 2.5 %collective-permute-done.4.refs_3_ = f32[2,128,256]{2,1,0:T(8,128)S(1)} collective-permute-done((f32[2,128,256]{2,1,0:T(8,128)S(1)}, f32[2,128,256]{2,1,0:T(8,128)S(1)}, u32[]{:S(2)}, u32[]{:S(2)}) %collective-permute-start.4) | collective-permute-done | bytes 262176 | tf_op jit(solution)/shard_map/ppermute | solution.py:425
  26.9 4.7 %shard_map.87 = (f32[2,128,512]{2,1,0:T(8,128)S(1)}, f32[2,128,512]{2,1,0:T(8,128)S(1)}, f32[2,128,512]{2,1,0:T(8,128)S(1)}, f32[2,128,512]{2,1,0:T(8,128)S(1)}) custom-call(s32[10,256]{1,0:T(8,128)S(1)} %broadcast_in_dim.2.info.refs_0_, f32[2,128,512]{2,1,0:T(8,128)S(1)} %collective-permute-done.2.refs_1_, ...), custom_call_target="tpu_custom_call" | custom-call | flops 2415919104 | bytes 6291456 | tf_op jit(solution)/shard_map/pallas_call | solution.py:515
  31.6 0.1 collective-permute-start.5
  31.7 0.5 shard_map.89
  32.1 0.6 collective-permute-start.8
  32.7 2.9 %collective-permute-start.18 = (f32[2,128,512]{2,1,0:T(8,128)S(1)}, f32[2,128,512]{2,1,0:T(8,128)S(1)}, u32[]{:S(2)}, u32[]{:S(2)}) collective-permute-start(f32[2,128,512]{2,1,0:T(8,128)S(1)} %get-tuple-element.52), channel_id=1, source_target_pairs={{8,16},{16,8},{9,17},{17,9},{10,18},{18,10},{11,19},{19,11},{12,20... | collective-permute-start | bytes 1572872 | tf_op jit(solution)/shard_map/ppermute | solution.py:425
  35.6 2.6 %collective-permute-start.9 = (f32[1,128,512]{2,1,0:T(8,128)S(1)}, f32[1,128,512]{2,1,0:T(8,128)S(1)}, u32[]{:S(2)}, u32[]{:S(2)}) collective-permute-start(f32[1,128,512]{2,1,0:T(8,128)S(1)} %get-tuple-element.46), channel_id=1, source_target_pairs={{8,16},{16,8},{9,17},{17,9},{10,18},{18,10},{11,19},{19,11},{12,20... | collective-permute-start | bytes 786440 | tf_op jit(solution)/shard_map/ppermute | solution.py:425
  38.3 7.7 %collective-permute-done.9.sent_cross = f32[1,128,512]{2,1,0:T(8,128)S(1)} collective-permute-done((f32[1,128,512]{2,1,0:T(8,128)S(1)}, f32[1,128,512]{2,1,0:T(8,128)S(1)}, u32[]{:S(2)}, u32[]{:S(2)}) %collective-permute-start.9) | collective-permute-done | bytes 262176 | tf_op jit(solution)/shard_map/ppermute | solution.py:425
  46.0 0.1 shard_map.90
  46.1 1.6 %collective-permute-start.10 = (f32[1,256,256]{2,1,0:T(8,128)S(1)}, f32[1,256,256]{2,1,0:T(8,128)S(1)}, u32[]{:S(2)}, u32[]{:S(2)}) collective-permute-start(f32[1,256,256]{2,1,0:T(8,128)S(1)} %get-tuple-element.47.close), channel_id=1, source_target_pairs={{0,1},{1,0},{2,3},{3,2},{4,5},{5,4},{6,7},{7,6},{8,9},{9,8},{10,11... | collective-permute-start | bytes 786440 | tf_op jit(solution)/shard_map/ppermute | solution.py:425
  47.6 1.9 %collective-permute-start.11 = (f32[1,256,256]{2,1,0:T(8,128)S(1)}, f32[1,256,256]{2,1,0:T(8,128)S(1)}, u32[]{:S(2)}, u32[]{:S(2)}) collective-permute-start(f32[1,256,256]{2,1,0:T(8,128)S(1)} %get-tuple-element.48.far), channel_id=1, source_target_pairs={{1,2},{2,1},{3,4},{4,3},{5,6},{6,5},{9,10},{10,9},{11,12},{12,11},... | collective-permute-start | bytes 786440 | tf_op jit(solution)/shard_map/ppermute | solution.py:425
  49.6 0.1 shard_map.88
  49.6 3.1 %collective-permute-start.6 = (f32[2,128,256]{2,1,0:T(8,128)S(1)}, f32[2,128,256]{2,1,0:T(8,128)S(1)}, u32[]{:S(2)}, u32[]{:S(2)}) collective-permute-start(f32[2,128,256]{2,1,0:T(8,128)S(1)} %get-tuple-element.42.close), channel_id=1, source_target_pairs={{0,1},{1,0},{2,3},{3,2},{4,5},{5,4},{6,7},{7,6},{8,9},{9,8},{10,11... | collective-permute-start | bytes 786440 | tf_op jit(solution)/shard_map/ppermute | solution.py:425
  52.7 1.9 %collective-permute-start.7 = (f32[2,128,256]{2,1,0:T(8,128)S(1)}, f32[2,128,256]{2,1,0:T(8,128)S(1)}, u32[]{:S(2)}, u32[]{:S(2)}) collective-permute-start(f32[2,128,256]{2,1,0:T(8,128)S(1)} %get-tuple-element.43.far), channel_id=1, source_target_pairs={{1,2},{2,1},{3,4},{4,3},{5,6},{6,5},{9,10},{10,9},{11,12},{12,11},... | collective-permute-start | bytes 786440 | tf_op jit(solution)/shard_map/ppermute | solution.py:425
  54.7 0.1 shard_map.93
  54.7 1.6 %collective-permute-start.19 = (f32[2,128,256]{2,1,0:T(8,128)S(1)}, f32[2,128,256]{2,1,0:T(8,128)S(1)}, u32[]{:S(2)}, u32[]{:S(2)}) collective-permute-start(f32[2,128,256]{2,1,0:T(8,128)S(1)} %get-tuple-element.53.close), channel_id=1, source_target_pairs={{0,1},{1,0},{2,3},{3,2},{4,5},{5,4},{6,7},{7,6},{8,9},{9,8},{10,11... | collective-permute-start | bytes 786440 | tf_op jit(solution)/shard_map/ppermute | solution.py:425
  56.3 6.5 %collective-permute-done.10.from_close = f32[1,256,256]{2,1,0:T(8,128)S(1)} collective-permute-done((f32[1,256,256]{2,1,0:T(8,128)S(1)}, f32[1,256,256]{2,1,0:T(8,128)S(1)}, u32[]{:S(2)}, u32[]{:S(2)}) %collective-permute-start.10) | collective-permute-done | bytes 262176 | tf_op jit(solution)/shard_map/ppermute | solution.py:425
  62.9 2.8 %collective-permute-start.20 = (f32[2,128,256]{2,1,0:T(8,128)S(1)}, f32[2,128,256]{2,1,0:T(8,128)S(1)}, u32[]{:S(2)}, u32[]{:S(2)}) collective-permute-start(f32[2,128,256]{2,1,0:T(8,128)S(1)} %get-tuple-element.54.far), channel_id=1, source_target_pairs={{1,2},{2,1},{3,4},{4,3},{5,6},{6,5},{9,10},{10,9},{11,12},{12,11},... | collective-permute-start | bytes 786440 | tf_op jit(solution)/shard_map/ppermute | solution.py:425
  65.7 0.1 shard_map.91
  65.8 1.1 collective-permute-start.12
  66.9 2.9 %collective-permute-done.12 = f32[8,128]{1,0:T(8,128)S(1)} collective-permute-done((f32[8,128]{1,0:T(8,128)S(1)}, f32[8,128]{1,0:T(8,128)S(1)}, u32[]{:S(2)}, u32[]{:S(2)}) %collective-permute-start.12) | collective-permute-done | bytes 4128 | tf_op jit(solution)/shard_map/ppermute | solution.py:449
  69.9 0.2 collective-permute-start.13
  70.0 3.5 %collective-permute-done.13 = f32[8,128]{1,0:T(8,128)S(1)} collective-permute-done((f32[8,128]{1,0:T(8,128)S(1)}, f32[8,128]{1,0:T(8,128)S(1)}, u32[]{:S(2)}, u32[]{:S(2)}) %collective-permute-start.13) | collective-permute-done | bytes 4128 | tf_op jit(solution)/shard_map/ppermute | solution.py:449
  73.5 3.5 %collective-permute-start.14 = (f32[8,128]{1,0:T(8,128)S(1)}, f32[8,128]{1,0:T(8,128)S(1)}, u32[]{:S(2)}, u32[]{:S(2)}) collective-permute-start(f32[8,128]{1,0:T(8,128)S(1)} %max.16), channel_id=1, source_target_pairs={{0,4},{1,5},{2,6},{3,7},{4,0},{5,1},{6,2},{7,3},{8,12},{9,13},{10,... | collective-permute-start | bytes 12296 | tf_op jit(solution)/shard_map/ppermute | solution.py:449
  77.0 1.6 %collective-permute-done.14 = f32[8,128]{1,0:T(8,128)S(1)} collective-permute-done((f32[8,128]{1,0:T(8,128)S(1)}, f32[8,128]{1,0:T(8,128)S(1)}, u32[]{:S(2)}, u32[]{:S(2)}) %collective-permute-start.14) | collective-permute-done | bytes 4128 | tf_op jit(solution)/shard_map/ppermute | solution.py:449
  78.6 3.6 %collective-permute-done.15 = f32[8,128]{1,0:T(8,128)S(1)} collective-permute-done((f32[8,128]{1,0:T(8,128)S(1)}, f32[8,128]{1,0:T(8,128)S(1)}, u32[]{:S(2)}, u32[]{:S(2)}) %collective-permute-start.15) | collective-permute-done | bytes 4128 | tf_op jit(solution)/shard_map/ppermute | solution.py:449
  82.2 1.2 collective-permute-done.16
  83.3 0.3 shard_map.92.refs_3_.refs_5_
  83.6 0.2 collective-permute-start.17
  83.9 0.3 shard_map.94.refs_4_.refs_11_
  84.1 2.1 %collective-permute-start.21 = (f32[2,128,512]{2,1,0:T(8,128)S(1)}, f32[2,128,512]{2,1,0:T(8,128)S(1)}, u32[]{:S(2)}, u32[]{:S(2)}) collective-permute-start(f32[2,128,512]{2,1,0:T(8,128)S(1)} %shard_map.94.refs_4_.refs_11_), channel_id=1, source_target_pairs={{8,16},{16,8},{9,17},{17,9},{10,18},{18,10},{11,19},{19,11},{12,20... | collective-permute-start | bytes 1572872 | tf_op jit(solution)/shard_map/ppermute | solution.py:425
  86.2 8.4 %collective-permute-done.21.refs_2_ = f32[2,128,512]{2,1,0:T(8,128)S(1)} collective-permute-done((f32[2,128,512]{2,1,0:T(8,128)S(1)}, f32[2,128,512]{2,1,0:T(8,128)S(1)}, u32[]{:S(2)}, u32[]{:S(2)}) %collective-permute-start.21) | collective-permute-done | bytes 524320 | tf_op jit(solution)/shard_map/ppermute | solution.py:425
  94.6 4.7 %shard_map.95 = (f32[2,128,512]{2,1,0:T(8,128)S(1)}, f32[2,128,256]{2,1,0:T(8,128)S(1)}, f32[2,128,256]{2,1,0:T(8,128)S(1)}, f32[2,128,512]{2,1,0:T(8,128)S(1)}, f32[2,128,512]{2,1,0:T(8,128)S(1)}) custom-call(s32[10,256]{1,0:T(8,128)S(1)} %broadcast_in_dim.2.info.refs_0_, f32[2,128,512]{2,1,0:T(8,128)S(1)} %collective-permute-done.17.refs_1_, ...), custom_call_target="tpu_custom_call" | custom-call | flops 2415919104 | bytes 6291456 | tf_op jit(solution)/shard_map/pallas_call | solution.py:515
  99.3 0.1 collective-permute-start.22
  99.4 1.9 %collective-permute-start.26 = (f32[2,128,256]{2,1,0:T(8,128)S(1)}, f32[2,128,256]{2,1,0:T(8,128)S(1)}, u32[]{:S(2)}, u32[]{:S(2)}) collective-permute-start(f32[2,128,256]{2,1,0:T(8,128)S(1)} %get-tuple-element.62), channel_id=1, source_target_pairs={{8,16},{16,8},{9,17},{17,9},{10,18},{18,10},{11,19},{19,11},{12,20... | collective-permute-start | bytes 786440 | tf_op jit(solution)/shard_map/ppermute | solution.py:425
  101.3 3.6 %collective-permute-start.25 = (f32[2,128,256]{2,1,0:T(8,128)S(1)}, f32[2,128,256]{2,1,0:T(8,128)S(1)}, u32[]{:S(2)}, u32[]{:S(2)}) collective-permute-start(f32[2,128,256]{2,1,0:T(8,128)S(1)} %get-tuple-element.61), channel_id=1, source_target_pairs={{8,16},{16,8},{9,17},{17,9},{10,18},{18,10},{11,19},{19,11},{12,20... | collective-permute-start | bytes 786440 | tf_op jit(solution)/shard_map/ppermute | solution.py:425
  104.9 2.1 %collective-permute-done.26.sent = f32[2,128,256]{2,1,0:T(8,128)S(1)} collective-permute-done((f32[2,128,256]{2,1,0:T(8,128)S(1)}, f32[2,128,256]{2,1,0:T(8,128)S(1)}, u32[]{:S(2)}, u32[]{:S(2)}) %collective-permute-start.26) | collective-permute-done | bytes 262176 | tf_op jit(solution)/shard_map/ppermute | solution.py:425
  107.1 0.4 collective-permute-start.27
  107.5 4.1 %collective-permute-start.28 = (f32[2,128,128]{2,1,0:T(8,128)S(1)}, f32[2,128,128]{2,1,0:T(8,128)S(1)}, u32[]{:S(2)}, u32[]{:S(2)}) collective-permute-start(f32[2,128,128]{2,1,0:T(8,128)S(1)} %get-tuple-element.64), channel_id=1, source_target_pairs={{1,2},{2,1},{3,4},{4,3},{5,6},{6,5},{9,10},{10,9},{11,12},{12,11},... | collective-permute-start | bytes 393224 | tf_op jit(solution)/shard_map/ppermute | solution.py:425
  111.6 0.1 shard_map.96
  111.6 1.5 %collective-permute-start.23 = (f32[2,128,128]{2,1,0:T(8,128)S(1)}, f32[2,128,128]{2,1,0:T(8,128)S(1)}, u32[]{:S(2)}, u32[]{:S(2)}) collective-permute-start(f32[2,128,128]{2,1,0:T(8,128)S(1)} %get-tuple-element.58), channel_id=1, source_target_pairs={{0,1},{1,0},{2,3},{3,2},{4,5},{5,4},{6,7},{7,6},{8,9},{9,8},{10,11... | collective-permute-start | bytes 393224 | tf_op jit(solution)/shard_map/ppermute | solution.py:425
  113.2 1.9 %collective-permute-start.24 = (f32[2,128,128]{2,1,0:T(8,128)S(1)}, f32[2,128,128]{2,1,0:T(8,128)S(1)}, u32[]{:S(2)}, u32[]{:S(2)}) collective-permute-start(f32[2,128,128]{2,1,0:T(8,128)S(1)} %get-tuple-element.59), channel_id=1, source_target_pairs={{1,2},{2,1},{3,4},{4,3},{5,6},{6,5},{9,10},{10,9},{11,12},{12,11},... | collective-permute-start | bytes 393224 | tf_op jit(solution)/shard_map/ppermute | solution.py:425
  115.1 0.1 collective-permute-done.28.refs_9_
  115.2 1.4 %collective-permute-done.23.refs_2_ = f32[2,128,128]{2,1,0:T(8,128)S(1)} collective-permute-done((f32[2,128,128]{2,1,0:T(8,128)S(1)}, f32[2,128,128]{2,1,0:T(8,128)S(1)}, u32[]{:S(2)}, u32[]{:S(2)}) %collective-permute-start.23) | collective-permute-done | bytes 131104 | tf_op jit(solution)/shard_map/ppermute | solution.py:425
  116.6 4.3 %collective-permute-done.24.refs_3_ = f32[2,128,128]{2,1,0:T(8,128)S(1)} collective-permute-done((f32[2,128,128]{2,1,0:T(8,128)S(1)}, f32[2,128,128]{2,1,0:T(8,128)S(1)}, u32[]{:S(2)}, u32[]{:S(2)}) %collective-permute-start.24) | collective-permute-done | bytes 131104 | tf_op jit(solution)/shard_map/ppermute | solution.py:425
  120.9 1.1 shard_map.98
  (37 shorter events, 0.2 us)
Async XLA Ops:
  0.0 1.0 copy-start
  1.0 21.1 %copy-start.3 = (f32[2,256,256]{2,1,0:T(8,128)S(1)}, f32[2,256,256]{2,1,0:T(8,128)}, u32[]{:S(2)}) copy-start(f32[2,256,256]{2,1,0:T(8,128)} %probe.1) | copy-start | bytes 1572868
  1.1 13.7 %collective-permute-start = (f32[2,256,128]{2,1,0:T(8,128)S(1)}, f32[2,256,128]{2,1,0:T(8,128)S(1)}, u32[]{:S(2)}, u32[]{:S(2)}) collective-permute-start(f32[2,256,128]{2,1,0:T(8,128)S(1)} %get-tuple-element.35), channel_id=1, source_target_pairs={{0,1},{1,0},{2,3},{3,2},{4,5},{5,4},{6,7},{7,6},{8,9},{9,8},{10,11... | collective-permute-start | bytes 786440 | tf_op jit(solution)/shard_map/ppermute | solution.py:425
  2.7 12.1 %collective-permute-start.1 = (f32[2,256,128]{2,1,0:T(8,128)S(1)}, f32[2,256,128]{2,1,0:T(8,128)S(1)}, u32[]{:S(2)}, u32[]{:S(2)}) collective-permute-start(f32[2,256,128]{2,1,0:T(8,128)S(1)} %get-tuple-element.36), channel_id=1, source_target_pairs={{1,2},{2,1},{3,4},{4,3},{5,6},{6,5},{9,10},{10,9},{11,12},{12,11},... | collective-permute-start | bytes 786440 | tf_op jit(solution)/shard_map/ppermute | solution.py:425
  14.9 1.0 copy-start.1
  16.1 7.2 %copy-start.2 = (f32[1,1,3,256,256]{4,3,2,1,0:T(8,128)S(1)}, f32[1,1,3,256,256]{4,3,2,1,0:T(8,128)}, u32[]{:S(2)}) copy-start(f32[1,1,3,256,256]{4,3,2,1,0:T(8,128)} %amplitude.1) | copy-start | bytes 2359300
  16.1 7.2 %copy-start.4 = (bf16[256,256]{1,0:T(8,128)(2,1)S(1)}, bf16[256,256]{1,0:T(8,128)(2,1)}, u32[]{:S(2)}) copy-start(bf16[256,256]{1,0:T(8,128)(2,1)} %constant.42.clone.pick_back) | copy-start | bytes 393220
  16.1 7.2 %copy-start.5 = (bf16[256,256]{1,0:T(8,128)(2,1)S(1)}, bf16[256,256]{1,0:T(8,128)(2,1)}, u32[]{:S(2)}) copy-start(bf16[256,256]{1,0:T(8,128)(2,1)} %constant.41.clone.pick) | copy-start | bytes 393220
  16.1 10.8 %collective-permute-start.2 = (f32[2,128,512]{2,1,0:T(8,128)S(1)}, f32[2,128,512]{2,1,0:T(8,128)S(1)}, u32[]{:S(2)}, u32[]{:S(2)}) collective-permute-start(f32[2,128,512]{2,1,0:T(8,128)S(1)} %get-tuple-element.37.refs_4_.old), channel_id=1, source_target_pairs={{0,8},{8,0},{16,24},{24,16},{1,9},{9,1},{17,25},{25,17},{2,10},{10... | collective-permute-start | bytes 1572872 | tf_op jit(solution)/shard_map/ppermute | solution.py:425
  16.3 8.1 %collective-permute-start.3 = (f32[2,128,256]{2,1,0:T(8,128)S(1)}, f32[2,128,256]{2,1,0:T(8,128)S(1)}, u32[]{:S(2)}, u32[]{:S(2)}) collective-permute-start(f32[2,128,256]{2,1,0:T(8,128)S(1)} %shard_map.84), channel_id=1, source_target_pairs={{8,16},{16,8},{9,17},{17,9},{10,18},{18,10},{11,19},{19,11},{12,20... | collective-permute-start | bytes 786440 | tf_op jit(solution)/shard_map/ppermute | solution.py:425
  18.8 8.1 %copy-start.6 = (bf16[2,2,256,256]{3,2,1,0:T(8,128)(2,1)S(1)}, bf16[2,2,256,256]{3,2,1,0:T(8,128)(2,1)}, u32[]{:S(2)}) copy-start(bf16[2,2,256,256]{3,2,1,0:T(8,128)(2,1)} %constant.40.clone.refs_9_.refs_8_) | copy-start | bytes 1572868
  18.8 8.1 %copy-start.7 = (bf16[2,2,256,256]{3,2,1,0:T(8,128)(2,1)S(1)}, bf16[2,2,256,256]{3,2,1,0:T(8,128)(2,1)}, u32[]{:S(2)}) copy-start(bf16[2,2,256,256]{3,2,1,0:T(8,128)(2,1)} %constant.39.clone.refs_8_.refs_7_) | copy-start | bytes 1572868
  18.8 8.1 %collective-permute-start.4 = (f32[2,128,256]{2,1,0:T(8,128)S(1)}, f32[2,128,256]{2,1,0:T(8,128)S(1)}, u32[]{:S(2)}, u32[]{:S(2)}) collective-permute-start(f32[2,128,256]{2,1,0:T(8,128)S(1)} %get-tuple-element.38), channel_id=1, source_target_pairs={{8,16},{16,8},{9,17},{17,9},{10,18},{18,10},{11,19},{19,11},{12,20... | collective-permute-start | bytes 786440 | tf_op jit(solution)/shard_map/ppermute | solution.py:425
  31.6 18.0 %collective-permute-start.5 = (f32[2,128,512]{2,1,0:T(8,128)S(1)}, f32[2,128,512]{2,1,0:T(8,128)S(1)}, u32[]{:S(2)}, u32[]{:S(2)}) collective-permute-start(f32[2,128,512]{2,1,0:T(8,128)S(1)} %get-tuple-element.41), channel_id=1, source_target_pairs={{0,8},{8,0},{16,24},{24,16},{1,9},{9,1},{17,25},{25,17},{2,10},{10... | collective-permute-start | bytes 1572872 | tf_op jit(solution)/shard_map/ppermute | solution.py:425
  32.1 6.1 %collective-permute-start.8 = (f32[1,128,512]{2,1,0:T(8,128)S(1)}, f32[1,128,512]{2,1,0:T(8,128)S(1)}, u32[]{:S(2)}, u32[]{:S(2)}) collective-permute-start(f32[1,128,512]{2,1,0:T(8,128)S(1)} %get-tuple-element.45), channel_id=1, source_target_pairs={{0,8},{8,0},{16,24},{24,16},{1,9},{9,1},{17,25},{25,17},{2,10},{10... | collective-permute-start | bytes 786440 | tf_op jit(solution)/shard_map/ppermute | solution.py:425
  32.7 21.9 %collective-permute-start.18 = (f32[2,128,512]{2,1,0:T(8,128)S(1)}, f32[2,128,512]{2,1,0:T(8,128)S(1)}, u32[]{:S(2)}, u32[]{:S(2)}) collective-permute-start(f32[2,128,512]{2,1,0:T(8,128)S(1)} %get-tuple-element.52), channel_id=1, source_target_pairs={{8,16},{16,8},{9,17},{17,9},{10,18},{18,10},{11,19},{19,11},{12,20... | collective-permute-start | bytes 1572872 | tf_op jit(solution)/shard_map/ppermute | solution.py:425
  35.6 10.4 %collective-permute-start.9 = (f32[1,128,512]{2,1,0:T(8,128)S(1)}, f32[1,128,512]{2,1,0:T(8,128)S(1)}, u32[]{:S(2)}, u32[]{:S(2)}) collective-permute-start(f32[1,128,512]{2,1,0:T(8,128)S(1)} %get-tuple-element.46), channel_id=1, source_target_pairs={{8,16},{16,8},{9,17},{17,9},{10,18},{18,10},{11,19},{19,11},{12,20... | collective-permute-start | bytes 786440 | tf_op jit(solution)/shard_map/ppermute | solution.py:425
  46.1 16.8 %collective-permute-start.10 = (f32[1,256,256]{2,1,0:T(8,128)S(1)}, f32[1,256,256]{2,1,0:T(8,128)S(1)}, u32[]{:S(2)}, u32[]{:S(2)}) collective-permute-start(f32[1,256,256]{2,1,0:T(8,128)S(1)} %get-tuple-element.47.close), channel_id=1, source_target_pairs={{0,1},{1,0},{2,3},{3,2},{4,5},{5,4},{6,7},{7,6},{8,9},{9,8},{10,11... | collective-permute-start | bytes 786440 | tf_op jit(solution)/shard_map/ppermute | solution.py:425
  47.6 18.1 %collective-permute-start.11 = (f32[1,256,256]{2,1,0:T(8,128)S(1)}, f32[1,256,256]{2,1,0:T(8,128)S(1)}, u32[]{:S(2)}, u32[]{:S(2)}) collective-permute-start(f32[1,256,256]{2,1,0:T(8,128)S(1)} %get-tuple-element.48.far), channel_id=1, source_target_pairs={{1,2},{2,1},{3,4},{4,3},{5,6},{6,5},{9,10},{10,9},{11,12},{12,11},... | collective-permute-start | bytes 786440 | tf_op jit(solution)/shard_map/ppermute | solution.py:425
  49.6 33.7 %collective-permute-start.6 = (f32[2,128,256]{2,1,0:T(8,128)S(1)}, f32[2,128,256]{2,1,0:T(8,128)S(1)}, u32[]{:S(2)}, u32[]{:S(2)}) collective-permute-start(f32[2,128,256]{2,1,0:T(8,128)S(1)} %get-tuple-element.42.close), channel_id=1, source_target_pairs={{0,1},{1,0},{2,3},{3,2},{4,5},{5,4},{6,7},{7,6},{8,9},{9,8},{10,11... | collective-permute-start | bytes 786440 | tf_op jit(solution)/shard_map/ppermute | solution.py:425
  52.7 30.6 %collective-permute-start.7 = (f32[2,128,256]{2,1,0:T(8,128)S(1)}, f32[2,128,256]{2,1,0:T(8,128)S(1)}, u32[]{:S(2)}, u32[]{:S(2)}) collective-permute-start(f32[2,128,256]{2,1,0:T(8,128)S(1)} %get-tuple-element.43.far), channel_id=1, source_target_pairs={{1,2},{2,1},{3,4},{4,3},{5,6},{6,5},{9,10},{10,9},{11,12},{12,11},... | collective-permute-start | bytes 786440 | tf_op jit(solution)/shard_map/ppermute | solution.py:425
  54.7 29.1 %collective-permute-start.19 = (f32[2,128,256]{2,1,0:T(8,128)S(1)}, f32[2,128,256]{2,1,0:T(8,128)S(1)}, u32[]{:S(2)}, u32[]{:S(2)}) collective-permute-start(f32[2,128,256]{2,1,0:T(8,128)S(1)} %get-tuple-element.53.close), channel_id=1, source_target_pairs={{0,1},{1,0},{2,3},{3,2},{4,5},{5,4},{6,7},{7,6},{8,9},{9,8},{10,11... | collective-permute-start | bytes 786440 | tf_op jit(solution)/shard_map/ppermute | solution.py:425
  62.9 21.0 %collective-permute-start.20 = (f32[2,128,256]{2,1,0:T(8,128)S(1)}, f32[2,128,256]{2,1,0:T(8,128)S(1)}, u32[]{:S(2)}, u32[]{:S(2)}) collective-permute-start(f32[2,128,256]{2,1,0:T(8,128)S(1)} %get-tuple-element.54.far), channel_id=1, source_target_pairs={{1,2},{2,1},{3,4},{4,3},{5,6},{6,5},{9,10},{10,9},{11,12},{12,11},... | collective-permute-start | bytes 786440 | tf_op jit(solution)/shard_map/ppermute | solution.py:425
  65.8 4.1 %collective-permute-start.12 = (f32[8,128]{1,0:T(8,128)S(1)}, f32[8,128]{1,0:T(8,128)S(1)}, u32[]{:S(2)}, u32[]{:S(2)}) collective-permute-start(f32[8,128]{1,0:T(8,128)S(1)} %get-tuple-element.50), channel_id=1, source_target_pairs={{0,1},{1,0},{2,3},{3,2},{4,5},{5,4},{6,7},{7,6},{8,9},{9,8},{10,11... | collective-permute-start | bytes 12296 | tf_op jit(solution)/shard_map/ppermute | solution.py:449
  69.9 3.6 %collective-permute-start.13 = (f32[8,128]{1,0:T(8,128)S(1)}, f32[8,128]{1,0:T(8,128)S(1)}, u32[]{:S(2)}, u32[]{:S(2)}) collective-permute-start(f32[8,128]{1,0:T(8,128)S(1)} %max.15), channel_id=1, source_target_pairs={{0,2},{1,3},{2,0},{3,1},{4,6},{5,7},{6,4},{7,5},{8,10},{9,11},{10,... | collective-permute-start | bytes 12296 | tf_op jit(solution)/shard_map/ppermute | solution.py:449
  73.5 5.1 %collective-permute-start.14 = (f32[8,128]{1,0:T(8,128)S(1)}, f32[8,128]{1,0:T(8,128)S(1)}, u32[]{:S(2)}, u32[]{:S(2)}) collective-permute-start(f32[8,128]{1,0:T(8,128)S(1)} %max.16), channel_id=1, source_target_pairs={{0,4},{1,5},{2,6},{3,7},{4,0},{5,1},{6,2},{7,3},{8,12},{9,13},{10,... | collective-permute-start | bytes 12296 | tf_op jit(solution)/shard_map/ppermute | solution.py:449
  78.6 3.6 %collective-permute-start.15 = (f32[8,128]{1,0:T(8,128)S(1)}, f32[8,128]{1,0:T(8,128)S(1)}, u32[]{:S(2)}, u32[]{:S(2)}) collective-permute-start(f32[8,128]{1,0:T(8,128)S(1)} %max.17), channel_id=1, source_target_pairs={{0,16},{8,24},{16,0},{24,8},{1,17},{9,25},{17,1},{25,9},{2,18},{10... | collective-permute-start | bytes 12296 | tf_op jit(solution)/shard_map/ppermute | solution.py:449
  82.2 1.2 collective-permute-start.16
  83.6 2.6 %collective-permute-start.17 = (f32[2,128,512]{2,1,0:T(8,128)S(1)}, f32[2,128,512]{2,1,0:T(8,128)S(1)}, u32[]{:S(2)}, u32[]{:S(2)}) collective-permute-start(f32[2,128,512]{2,1,0:T(8,128)S(1)} %shard_map.92.refs_3_.refs_5_), channel_id=1, source_target_pairs={{0,8},{8,0},{16,24},{24,16},{1,9},{9,1},{17,25},{25,17},{2,10},{10... | collective-permute-start | bytes 1572872 | tf_op jit(solution)/shard_map/ppermute | solution.py:425
  84.1 10.5 %collective-permute-start.21 = (f32[2,128,512]{2,1,0:T(8,128)S(1)}, f32[2,128,512]{2,1,0:T(8,128)S(1)}, u32[]{:S(2)}, u32[]{:S(2)}) collective-permute-start(f32[2,128,512]{2,1,0:T(8,128)S(1)} %shard_map.94.refs_4_.refs_11_), channel_id=1, source_target_pairs={{8,16},{16,8},{9,17},{17,9},{10,18},{18,10},{11,19},{19,11},{12,20... | collective-permute-start | bytes 1572872 | tf_op jit(solution)/shard_map/ppermute | solution.py:425
  99.3 12.3 %collective-permute-start.22 = (f32[2,128,512]{2,1,0:T(8,128)S(1)}, f32[2,128,512]{2,1,0:T(8,128)S(1)}, u32[]{:S(2)}, u32[]{:S(2)}) collective-permute-start(f32[2,128,512]{2,1,0:T(8,128)S(1)} %get-tuple-element.57), channel_id=1, source_target_pairs={{0,8},{8,0},{16,24},{24,16},{1,9},{9,1},{17,25},{25,17},{2,10},{10... | collective-permute-start | bytes 1572872 | tf_op jit(solution)/shard_map/ppermute | solution.py:425
  99.4 7.7 %collective-permute-start.26 = (f32[2,128,256]{2,1,0:T(8,128)S(1)}, f32[2,128,256]{2,1,0:T(8,128)S(1)}, u32[]{:S(2)}, u32[]{:S(2)}) collective-permute-start(f32[2,128,256]{2,1,0:T(8,128)S(1)} %get-tuple-element.62), channel_id=1, source_target_pairs={{8,16},{16,8},{9,17},{17,9},{10,18},{18,10},{11,19},{19,11},{12,20... | collective-permute-start | bytes 786440 | tf_op jit(solution)/shard_map/ppermute | solution.py:425
  101.3 13.8 %collective-permute-start.25 = (f32[2,128,256]{2,1,0:T(8,128)S(1)}, f32[2,128,256]{2,1,0:T(8,128)S(1)}, u32[]{:S(2)}, u32[]{:S(2)}) collective-permute-start(f32[2,128,256]{2,1,0:T(8,128)S(1)} %get-tuple-element.61), channel_id=1, source_target_pairs={{8,16},{16,8},{9,17},{17,9},{10,18},{18,10},{11,19},{19,11},{12,20... | collective-permute-start | bytes 786440 | tf_op jit(solution)/shard_map/ppermute | solution.py:425
  107.1 8.0 %collective-permute-start.27 = (f32[2,128,128]{2,1,0:T(8,128)S(1)}, f32[2,128,128]{2,1,0:T(8,128)S(1)}, u32[]{:S(2)}, u32[]{:S(2)}) collective-permute-start(f32[2,128,128]{2,1,0:T(8,128)S(1)} %get-tuple-element.63), channel_id=1, source_target_pairs={{0,1},{1,0},{2,3},{3,2},{4,5},{5,4},{6,7},{7,6},{8,9},{9,8},{10,11... | collective-permute-start | bytes 393224 | tf_op jit(solution)/shard_map/ppermute | solution.py:425
  107.5 7.7 %collective-permute-start.28 = (f32[2,128,128]{2,1,0:T(8,128)S(1)}, f32[2,128,128]{2,1,0:T(8,128)S(1)}, u32[]{:S(2)}, u32[]{:S(2)}) collective-permute-start(f32[2,128,128]{2,1,0:T(8,128)S(1)} %get-tuple-element.64), channel_id=1, source_target_pairs={{1,2},{2,1},{3,4},{4,3},{5,6},{6,5},{9,10},{10,9},{11,12},{12,11},... | collective-permute-start | bytes 393224 | tf_op jit(solution)/shard_map/ppermute | solution.py:425
  111.6 5.0 %collective-permute-start.23 = (f32[2,128,128]{2,1,0:T(8,128)S(1)}, f32[2,128,128]{2,1,0:T(8,128)S(1)}, u32[]{:S(2)}, u32[]{:S(2)}) collective-permute-start(f32[2,128,128]{2,1,0:T(8,128)S(1)} %get-tuple-element.58), channel_id=1, source_target_pairs={{0,1},{1,0},{2,3},{3,2},{4,5},{5,4},{6,7},{7,6},{8,9},{9,8},{10,11... | collective-permute-start | bytes 393224 | tf_op jit(solution)/shard_map/ppermute | solution.py:425
  113.2 7.7 %collective-permute-start.24 = (f32[2,128,128]{2,1,0:T(8,128)S(1)}, f32[2,128,128]{2,1,0:T(8,128)S(1)}, u32[]{:S(2)}, u32[]{:S(2)}) collective-permute-start(f32[2,128,128]{2,1,0:T(8,128)S(1)} %get-tuple-element.59), channel_id=1, source_target_pairs={{1,2},{2,1},{3,4},{4,3},{5,6},{6,5},{9,10},{10,9},{11,12},{12,11},... | collective-permute-start | bytes 393224 | tf_op jit(solution)/shard_map/ppermute | solution.py:425
